TPU v7x, 256 devices: a whole 4x4x8 slice. The times are simulated.
256 devices in a mesh: ctx: 32 (over x, y, core), section: 8 (over z).
Axes of the slice: x: 4, y: 4, z: 8, core: 2. Of those that a mesh axis runs over, the one named last changes fastest.
Arguments:
- queries: bfloat16 [8, 8192, 2560], P('section', 'ctx'), may hold values from -7 to 7
- keys: bfloat16 [8, 8192, 2560], P('section', 'ctx'), may hold values from -7 to 7
- values: bfloat16 [8, 8192, 2560], P('section', 'ctx'), may hold values from -6 to 6
- out_grad: bfloat16 [8, 8192, 2560], P('section', 'ctx'), may hold values from -6 to 6
- key_blocks: int32 [8, 32, 20, 4], P('section'), may hold values from 0 to 63, as said below
- list_lengths: int32 [8, 32, 20], P('section'), may hold values from 1 to 4, as said below
Outputs:
- handed_queries: bfloat16 [8, 8192, 2560], P('section', 'ctx')
- handed_keys: bfloat16 [8, 8192, 2560], P('section', 'ctx')
- handed_values: bfloat16 [8, 8192, 2560], P('section', 'ctx')
Inputs may be any that keep to these rules, and one draw needn't show every extreme that they name: `key_blocks`: within one list the key blocks lie in the shards of distinct indices of ctx (key block b lies in shard b // 2), so they are distinct. For each section, the used entries of the lists of the 1 query group of one index of ctx name at most 3 key blocks in any one shard, and in every section some index of ctx names exactly 3 in some shard. `list_lengths`: in every section, all lists of the query groups of some index of ctx have length 4.
All inputs are finite; a program needn't handle non-finite values.
Results may differ from a plain program's by a relative error of at most 0.017.
The roundings to bfloat16 on the way count: a program that leaves them out, or rounds other values in their place, can miss the bound.
Values may be sent and summed in bfloat16 or wider, within the bound.
No kernel may reach another device: no remote copies, remote signals or barrier semaphores. Data moves between devices by JAX's collectives and lax.ppermute only.
A program may use at most 128 MiB of HBM per device.

v0:
```python
import math

import jax
import jax.numpy as jnp
from jax import lax
from jax.sharding import PartitionSpec as P

head_batch = 4


def shifted(value, axis, steps):
    count = lax.axis_size(axis)
    pairs = [(source, (source + steps) % count) for source in range(count)]
    return lax.ppermute(value, axis, pairs)


def attend(query_tile, grad_tile, pair_tiles, is_used, softmax_scale):
    tile_count, list_count, _, block_rows, head_dim = pair_tiles.shape
    key_flat = pair_tiles[:, :, 0].reshape(tile_count, list_count * block_rows, head_dim)
    value_flat = pair_tiles[:, :, 1].reshape(tile_count, list_count * block_rows, head_dim)
    scores = (
        jnp.einsum("nqd,nkd->nqk", query_tile, key_flat, preferred_element_type=jnp.float32)
        * softmax_scale
    )
    key_mask = jnp.repeat(is_used, block_rows, axis=1)[:, None, :]
    scores = jnp.where(key_mask, scores, -jnp.inf)
    row_max = jnp.max(scores, axis=-1, keepdims=True)
    exp_scores = jnp.exp(scores - row_max)
    weights = exp_scores / jnp.sum(exp_scores, axis=-1, keepdims=True)
    weights_low = weights.astype(jnp.bfloat16)
    attn_out = jnp.einsum(
        "nqk,nkd->nqd", weights_low, value_flat, preferred_element_type=jnp.float32
    )
    row_delta = jnp.sum(grad_tile.astype(jnp.float32) * attn_out, axis=-1, keepdims=True)
    dweights = jnp.einsum("nqd,nkd->nqk", grad_tile, value_flat, preferred_element_type=jnp.float32)
    dscores = (weights * (dweights - row_delta)).astype(jnp.bfloat16)
    query_grad = (
        jnp.einsum("nqk,nkd->nqd", dscores, key_flat, preferred_element_type=jnp.float32)
        * softmax_scale
    ).astype(jnp.bfloat16)
    key_terms = (
        jnp.einsum("nqk,nqd->nkd", dscores, query_tile, preferred_element_type=jnp.float32)
        * softmax_scale
    ).astype(jnp.bfloat16)
    value_terms = jnp.einsum(
        "nqk,nqd->nkd", weights_low, grad_tile, preferred_element_type=jnp.float32
    ).astype(jnp.bfloat16)
    shape = (tile_count, list_count, block_rows, head_dim)
    return (query_grad, key_terms.reshape(shape), value_terms.reshape(shape))


def local(queries, keys, values, out_grad, key_blocks, list_lengths):
    ctx_count = lax.axis_size("ctx")
    my_index = lax.axis_index("ctx")
    row_count = queries.shape[1]
    head_count = list_lengths.shape[2]
    head_dim = queries.shape[2] // head_count
    list_size = key_blocks.shape[3]
    group_count = key_blocks.shape[1] // ctx_count
    group_rows = row_count // group_count
    block_rows = group_rows // 2
    own_blocks = row_count // block_rows
    entries = group_count * head_count * list_size
    capacity = (entries + ctx_count - 1) // ctx_count
    dump_slot = ctx_count * capacity
    softmax_scale = 1.0 / math.sqrt(head_dim)
    chosen = key_blocks[0].reshape(ctx_count, entries)
    is_used = (
        jnp.arange(list_size, dtype=jnp.int32)[None, None, :] < list_lengths[0][:, :, None]
    ).reshape(ctx_count, entries)
    holder = chosen // own_blocks
    peers = jnp.arange(ctx_count, dtype=jnp.int32)
    owner_table = ((holder[:, :, None] == peers[None, None, :]) & is_used[:, :, None]).astype(
        jnp.int32
    )
    slot_rank = jnp.sum((jnp.cumsum(owner_table, axis=1) - 1) * owner_table, axis=2)
    head_of = jnp.arange(entries, dtype=jnp.int32) // list_size % head_count
    local_tile = head_of[None, :] * own_blocks + chosen % own_blocks
    is_mine = (holder == my_index) & is_used
    send_slot = jnp.where(is_mine, peers[:, None] * capacity + slot_rank, dump_slot).reshape(-1)
    tile_table = (
        jnp.zeros((dump_slot + 1,), jnp.int32).at[send_slot].set(local_tile.reshape(-1))[:dump_slot]
    )
    slot_filled = jnp.zeros((dump_slot + 1,), jnp.int32).at[send_slot].set(1)[:dump_slot] > 0
    local_pairs = jnp.stack([keys[0], values[0]], axis=0).reshape(
        2, own_blocks, block_rows, head_count, head_dim
    )
    local_pairs = local_pairs.transpose(3, 1, 0, 2, 4).reshape(
        head_count * own_blocks, 2, block_rows, head_dim
    )
    outgoing = jnp.where(
        slot_filled[:, None, None, None], local_pairs[tile_table], jnp.zeros((), jnp.bfloat16)
    )
    outgoing = outgoing.reshape(ctx_count, capacity, 2, block_rows, head_dim)
    fetched = lax.all_to_all(outgoing, "ctx", split_axis=0, concat_axis=0, tiled=True)
    my_holder = lax.dynamic_index_in_dim(holder, my_index, 0, keepdims=False)
    my_slot = lax.dynamic_index_in_dim(slot_rank, my_index, 0, keepdims=False)
    my_used = lax.dynamic_index_in_dim(is_used, my_index, 0, keepdims=False)
    recv_slot = jnp.where(my_used, my_holder * capacity + my_slot, 0)
    arrived = fetched.reshape(dump_slot, 2, block_rows, head_dim)[recv_slot]
    batches = group_count * head_count // head_batch
    arrived = arrived.reshape(batches, head_batch, list_size, 2, block_rows, head_dim)
    used_here = my_used.reshape(batches, head_batch, list_size)
    query_items = (
        queries[0].reshape(group_count, group_rows, head_count, head_dim).transpose(0, 2, 1, 3)
    )
    query_items = query_items.reshape(batches, head_batch, group_rows, head_dim)
    grad_items = (
        out_grad[0].reshape(group_count, group_rows, head_count, head_dim).transpose(0, 2, 1, 3)
    )
    grad_items = grad_items.reshape(batches, head_batch, group_rows, head_dim)

    def run_batch(inputs):
        return attend(inputs[0], inputs[1], inputs[2], inputs[3], softmax_scale)

    query_parts, key_terms, value_terms = lax.map(
        run_batch, (query_items, grad_items, arrived, used_here)
    )
    query_grad = (
        query_parts.reshape(group_count, head_count, group_rows, head_dim)
        .transpose(0, 2, 1, 3)
        .reshape(row_count, head_count * head_dim)
    )
    partials = jnp.stack([key_terms, value_terms], axis=3).reshape(entries, 2, block_rows, head_dim)
    back_slot = jnp.where(my_used, my_holder * capacity + my_slot, dump_slot)
    returning = (
        jnp.zeros((dump_slot + 1, 2, block_rows, head_dim), jnp.bfloat16)
        .at[back_slot]
        .set(partials)[:dump_slot]
    )
    returning = returning.reshape(ctx_count, capacity, 2, block_rows, head_dim)
    returned = lax.all_to_all(returning, "ctx", split_axis=0, concat_axis=0, tiled=True)
    tile_ids = jnp.arange(head_count * own_blocks, dtype=jnp.int32)
    selector = ((tile_table[None, :] == tile_ids[:, None]) & slot_filled[None, :]).astype(
        jnp.bfloat16
    )
    summed = jnp.dot(
        selector,
        returned.reshape(dump_slot, 2 * block_rows * head_dim),
        preferred_element_type=jnp.float32,
    ).astype(jnp.bfloat16)
    summed = summed.reshape(head_count, own_blocks, 2, block_rows, head_dim).transpose(
        2, 1, 3, 0, 4
    )
    summed = summed.reshape(2, row_count, head_count * head_dim)
    key_grad = summed[0]
    value_grad = summed[1]
    handed_queries, handed_keys, handed_values = shifted(
        (query_grad, key_grad, value_grad), "section", -1
    )
    return (handed_queries[None], handed_keys[None], handed_values[None])


def solution(mesh):
    placed = (
        P("section", "ctx", None),
        P("section", "ctx", None),
        P("section", "ctx", None),
        P("section", "ctx", None),
        P("section", None, None, None),
        P("section", None, None),
    )
    return jax.shard_map(
        local,
        mesh=mesh,
        in_specs=placed,
        out_specs=(P("section", "ctx", None), P("section", "ctx", None), P("section", "ctx", None)),
        check_vma=False,
    )
```

profile of v0, /device:TPU:8, one launch (start us, length us, event | category | flops | bytes accessed | tf_op | source)
XLA Modules:
  0.0 455.8 jit_solution(8976415171700205891)
XLA Ops:
  3.7 3.1 pad_maximum_fusion.1
  6.8 4.2 reshape.402
  11.0 4.2 copy.155
  15.2 6.0 %copy.137 = bf16[20,2,2,128,128]{4,3,2,1,0:T(8,128)(2,1)S(1)} copy(bf16[20,2,2,128,128]{3,1,4,0,2:T(2,128)(2,1)} %bitcast.181) | data formatting | bytes 5242880 | tf_op jit(solution)/shard_map/transpose | solution.py:88
  21.3 2.8 select_reduce_fusion
  25.0 9.9 %scatter_custom_fusion.1 = s32[97]{0:T(128)S(1)} fusion(s32[2560]{0:T(1024)S(1)} %fusion.53, s32[2560]{0:T(1024)S(1)} %fusion.52, s32[]{:T(128)} %copy.201), kind=kCustom, calls=%fused_computation.105 | custom fusion | bytes 392 | tf_op jit(solution)/shard_map/scatter | solution.py:82
  34.9 9.9 %scatter_custom_fusion = s32[97]{0:T(128)S(1)} fusion(s32[2560]{0:T(1024)S(1)} %fusion.53, s32[2560]{0:T(1024)S(1)} %broadcast.314, s32[]{:T(128)} %copy.201), kind=kCustom, calls=%fused_computation.107 | custom fusion | bytes 392 | tf_op jit(solution)/shard_map/scatter | solution.py:84
  45.0 6.0 %gather_fusion = bf16[96,2,128,128]{3,2,1,0:T(8,128)(2,1)} fusion(bf16[40,2,128,128]{3,2,1,0:T(8,128)(2,1)S(1)} %bitcast.169, s32[1024]{0:T(1024)S(1)} %pad_clamp_fusion.1), kind=kCustom, calls=%fused_computation | custom fusion | bytes 12583296 | tf_op jit(solution)/shard_map/gather | solution.py:92
  51.0 5.9 %broadcast_select_fusion = bf16[32,3,2,128,128]{4,3,2,1,0:T(8,128)(2,1)} fusion(bf16[32,3,2,128,128]{4,3,2,1,0:T(8,128)(2,1)} %bitcast.171, pred[32,3]{1,0:T(8,128)(4,1)S(1)} %gt.8), kind=kLoop, calls=%fused_computation.46 | loop fusion | flops 3145728 | bytes 12583008 | tf_op jit(solution)/shard_map/jit(_where)/select_n | solution.py:91
  56.9 7.7 %all-to-all-start = ((bf16[32,3,2,128,128]{4,3,2,1,0:T(8,128)(2,1)}), bf16[32,3,2,128,128]{4,3,2,1,0:T(8,128)(2,1)}, u32[]{:S(2)}, u32[]{:S(2)}) async-start(bf16[32,3,2,128,128]{4,3,2,1,0:T(8,128)(2,1)} %broadcast_select_fusion), calls=%async_computation | async-start | bytes 12582912 | tf_op jit(solution)/shard_map/all_to_all | solution.py:95
  68.1 84.8 %all-to-all-done = bf16[32,3,2,128,128]{4,3,2,1,0:T(8,128)(2,1)} async-done(((bf16[32,3,2,128,128]{4,3,2,1,0:T(8,128)(2,1)}), bf16[32,3,2,128,128]{4,3,2,1,0:T(8,128)(2,1)}, u32[]{:S(2)}, u32[]{:S(2)}) %all-to-all-start) | async-done | bytes 6291488 | tf_op jit(solution)/shard_map/all_to_all | solution.py:95
  152.9 8.5 %gather_fusion.1 = bf16[80,2,128,128]{3,2,1,0:T(8,128)(2,1)} fusion(bf16[96,2,128,128]{3,2,1,0:T(8,128)(2,1)} %bitcast.18, s32[1024]{0:T(1024)S(1)} %pad_clamp_fusion), kind=kCustom, calls=%fused_computation.1 | custom fusion | bytes 10486080 | tf_op jit(solution)/shard_map/gather | solution.py:100
  161.4 80.1 %while.14 = (s32[]{:T(128)}, bf16[5,4,256,128]{2,3,1,0:T(8,128)(2,1)}, bf16[5,4,4,128,128]{4,3,2,1,0:T(8,128)(2,1)}, bf16[5,4,4,128,128]{4,3,2,1,0:T(8,128)(2,1)...) while((s32[]{:T(128)}, ...), condition=%wide.region_8.9_spmd, body=%wide.region_4.8_spmd.sunk | while | flops 1084623360 | bytes 22057144 | solution.py:116
  164.0 3.2 fusion.119
  169.2 2.2 multiply_convert_fusion.2
  172.7 2.1 convolution_convert_fusion.3
  180.1 3.2 fusion.119
  185.3 2.2 multiply_convert_fusion.2
  188.7 2.1 convolution_convert_fusion.3
  196.1 3.2 fusion.119
  199.3 2.0 fusion.120
  201.3 2.2 multiply_convert_fusion.2
  204.8 2.1 convolution_convert_fusion.3
  212.1 3.2 fusion.119
  215.3 2.0 fusion.120
  217.3 2.2 multiply_convert_fusion.2
  220.8 2.1 convolution_convert_fusion.3
  228.1 3.2 fusion.119
  231.3 2.0 fusion.120
  233.3 2.2 multiply_convert_fusion.2
  236.8 2.1 convolution_convert_fusion.3
  241.5 5.4 %pad_maximum_fusion = bf16[80,2,128,128]{3,2,1,0:T(8,128)(2,1)} fusion(bf16[80,1,128,128]{3,2,1,0:T(8,128)(2,1)} %bitcast.188, bf16[80,1,128,128]{3,2,1,0:T(8,128)(2,1)} %bitcast.187), kind=kLoop, calls=%fused_computation.47 | loop fusion | flops 2621440 | bytes 10485760 | tf_op jit(solution)/shard_map/stack | solution.py:124
  246.9 4.3 broadcast_in_dim.91
  251.2 14.7 %scatter_fusion = bf16[97,2,128,128]{3,2,1,0:T(8,128)(2,1)} fusion(bf16[97,2,128,128]{3,2,1,0:T(8,128)(2,1)} %broadcast_in_dim.91, s32[80]{0:T(128)S(1)} %fusion.59, bf16[80,2,128,128]{3,2,1,0:T(8,128)(2,1)} %pad_maximum_fusion), kind=kCustom, calls=%fused_computation.4 | custom fusion | bytes 15728960 | tf_op jit(solution)/shard_map/scatter | solution.py:129
  265.9 8.1 %slice.34 = bf16[96,2,128,128]{3,2,1,0:T(8,128)(2,1)} slice(bf16[97,2,128,128]{3,2,1,0:T(8,128)(2,1)} %scatter_fusion), slice={[0:96], [0:2], [0:128], [0:128]} | slice | bytes 12582912 | tf_op jit(solution)/shard_map/slice | solution.py:127
  274.0 4.7 %all-to-all-start.1 = ((bf16[32,3,2,128,128]{4,3,2,1,0:T(8,128)(2,1)}), bf16[32,3,2,128,128]{4,3,2,1,0:T(8,128)(2,1)}, u32[]{:S(2)}, u32[]{:S(2)}) async-start(bf16[32,3,2,128,128]{4,3,2,1,0:T(8,128)(2,1)} %bitcast.170), calls=%async_computation.1 | async-start | bytes 12582912 | tf_op jit(solution)/shard_map/all_to_all | solution.py:132
  278.7 6.0 %collective-permute-start = (bf16[256,2560]{0,1:T(8,128)(2,1)}, bf16[256,2560]{0,1:T(8,128)(2,1)}, u32[]{:S(2)}, u32[]{:S(2)}) collective-permute-start(bf16[256,2560]{0,1:T(8,128)(2,1)} %bitcast.26), channel_id=1, source_target_pairs={{0,7},{1,0},{2,1},{3,2},{4,3},{5,4},{6,5},{7,6},{8,15},{9,8},{10,9... | collective-permute-start | bytes 3932168 | tf_op jit(solution)/shard_map/ppermute | solution.py:14
  284.6 82.4 %all-to-all-done.1 = bf16[32,3,2,128,128]{4,3,2,1,0:T(8,128)(2,1)} async-done(((bf16[32,3,2,128,128]{4,3,2,1,0:T(8,128)(2,1)}), bf16[32,3,2,128,128]{4,3,2,1,0:T(8,128)(2,1)}, u32[]{:S(2)}, u32[]{:S(2)}) %all-to-all-start.1) | async-done | bytes 6291488 | tf_op jit(solution)/shard_map/all_to_all | solution.py:132
  367.0 10.3 %reshape.359 = bf16[96,32768]{1,0:T(8,128)(2,1)} reshape(bf16[32,3,2,128,128]{4,3,2,1,0:T(8,128)(2,1)} %all-to-all-done.1) | data formatting | bytes 12582912 | tf_op jit(solution)/shard_map/reshape | solution.py:139
  377.3 3.7 fusion.40
  381.1 2.1 copy.164
  383.2 5.9 %copy.146 = bf16[20,2,2,128,128]{3,1,4,0,2:T(2,128)(2,1)S(1)} copy(bf16[20,2,2,128,128]{4,3,2,1,0:T(8,128)(2,1)} %bitcast.182) | data formatting | bytes 5242880 | tf_op jit(solution)/shard_map/reshape | solution.py:142
  389.1 2.3 fusion.68
  391.7 5.7 %collective-permute-start.1 = (bf16[256,2560]{0,1:T(8,128)(2,1)S(1)}, bf16[256,2560]{0,1:T(8,128)(2,1)S(1)}, u32[]{:S(2)}, u32[]{:S(2)}) collective-permute-start(bf16[256,2560]{0,1:T(8,128)(2,1)S(1)} %bitcast.189), channel_id=1, source_target_pairs={{0,7},{1,0},{2,1},{3,2},{4,3},{5,4},{6,5},{7,6},{8,15},{9,8},{10,9... | collective-permute-start | bytes 3932168 | tf_op jit(solution)/shard_map/ppermute | solution.py:14
  399.6 2.4 copy.147
  402.0 24.6 %collective-permute-done.1 = bf16[256,2560]{0,1:T(8,128)(2,1)S(1)} collective-permute-done((bf16[256,2560]{0,1:T(8,128)(2,1)S(1)}, bf16[256,2560]{0,1:T(8,128)(2,1)S(1)}, u32[]{:S(2)}, u32[]{:S(2)}) %collective-permute-start.1) | collective-permute-done | bytes 1310752 | tf_op jit(solution)/shard_map/ppermute | solution.py:14
  428.1 25.2 %collective-permute-done.2 = bf16[256,2560]{0,1:T(8,128)(2,1)} collective-permute-done((bf16[256,2560]{0,1:T(8,128)(2,1)}, bf16[256,2560]{0,1:T(8,128)(2,1)}, u32[]{:S(2)}, u32[]{:S(2)}) %collective-permute-start.2) | collective-permute-done | bytes 1310752 | tf_op jit(solution)/shard_map/ppermute | solution.py:14
  453.4 2.4 copy.149
  (114 shorter events, 48.1 us)
Async XLA Ops:
  0.6 3.1 copy-start
  15.2 6.0 %copy-start.3 = (s32[1,32,20,4]{1,3,2,0:T(4,128)S(1)}, s32[1,32,20,4]{1,3,2,0:T(4,128)}, u32[]{:S(2)}) copy-start(s32[1,32,20,4]{1,3,2,0:T(4,128)} %param.12) | copy-start | bytes 30724
  56.9 8.1 %copy-start.1 = (bf16[1,256,2560]{2,1,0:T(8,128)(2,1)S(1)}, bf16[1,256,2560]{2,1,0:T(8,128)(2,1)}, u32[]{:S(2)}) copy-start(bf16[1,256,2560]{2,1,0:T(8,128)(2,1)} %param.8) | copy-start | bytes 3932164
  56.9 96.0 %all-to-all-start = ((bf16[32,3,2,128,128]{4,3,2,1,0:T(8,128)(2,1)}), bf16[32,3,2,128,128]{4,3,2,1,0:T(8,128)(2,1)}, u32[]{:S(2)}, u32[]{:S(2)}) async-start(bf16[32,3,2,128,128]{4,3,2,1,0:T(8,128)(2,1)} %broadcast_select_fusion), calls=%async_computation | async-start | bytes 12582912 | tf_op jit(solution)/shard_map/all_to_all | solution.py:95
  64.6 1.8 copy-start.2
  274.0 93.0 %all-to-all-start.1 = ((bf16[32,3,2,128,128]{4,3,2,1,0:T(8,128)(2,1)}), bf16[32,3,2,128,128]{4,3,2,1,0:T(8,128)(2,1)}, u32[]{:S(2)}, u32[]{:S(2)}) async-start(bf16[32,3,2,128,128]{4,3,2,1,0:T(8,128)(2,1)} %bitcast.170), calls=%async_computation.1 | async-start | bytes 12582912 | tf_op jit(solution)/shard_map/all_to_all | solution.py:132
  278.7 121.0 %collective-permute-start = (bf16[256,2560]{0,1:T(8,128)(2,1)}, bf16[256,2560]{0,1:T(8,128)(2,1)}, u32[]{:S(2)}, u32[]{:S(2)}) collective-permute-start(bf16[256,2560]{0,1:T(8,128)(2,1)} %bitcast.26), channel_id=1, source_target_pairs={{0,7},{1,0},{2,1},{3,2},{4,3},{5,4},{6,5},{7,6},{8,15},{9,8},{10,9... | collective-permute-start | bytes 3932168 | tf_op jit(solution)/shard_map/ppermute | solution.py:14
  391.7 34.9 %collective-permute-start.1 = (bf16[256,2560]{0,1:T(8,128)(2,1)S(1)}, bf16[256,2560]{0,1:T(8,128)(2,1)S(1)}, u32[]{:S(2)}, u32[]{:S(2)}) collective-permute-start(bf16[256,2560]{0,1:T(8,128)(2,1)S(1)} %bitcast.189), channel_id=1, source_target_pairs={{0,7},{1,0},{2,1},{3,2},{4,3},{5,4},{6,5},{7,6},{8,15},{9,8},{10,9... | collective-permute-start | bytes 3932168 | tf_op jit(solution)/shard_map/ppermute | solution.py:14
  398.6 54.8 %collective-permute-start.2 = (bf16[256,2560]{0,1:T(8,128)(2,1)}, bf16[256,2560]{0,1:T(8,128)(2,1)}, u32[]{:S(2)}, u32[]{:S(2)}) collective-permute-start(bf16[256,2560]{0,1:T(8,128)(2,1)} %bitcast.117), channel_id=1, source_target_pairs={{0,7},{1,0},{2,1},{3,2},{4,3},{5,4},{6,5},{7,6},{8,15},{9,8},{10,9... | collective-permute-start | bytes 3932168 | tf_op jit(solution)/shard_map/ppermute | solution.py:14
where the time goes:
time: 458 us; the launch traced here: 456 us
  waiting for transfers between devices  217 us (47%)
  local copies, waits for them, and re-layouts  134 us (29%)
  matrix products  60.6 us (13%)
  starting transfers between devices  25.1 us (5%)
  other arithmetic  17.7 us (4%)
    all_to_all x1, waiting for transfers between devices, local(): lax.all_to_all(outgoing, 'ctx', split_axis=0, concat_axis=0, tiled=True)  84.8 us
    all_to_all x1, waiting for transfers between devices, local(): lax.all_to_all(returning, 'ctx', split_axis=0, concat_axis=0, tiled=True)  82.4 us
    ppermute x3, waiting for transfers between devices, shifted(): return lax.ppermute(value, axis, pairs)  49.8 us
    sub x5, matrix products, attend(): exp_scores = jnp.exp(scores - row_max)  15.8 us
    scatter x1, local copies, waits for them, and re-layouts, local(): returning = jnp.zeros((dump_slot + 1, 2, block_rows, head_dim), jnp.bfloa...  14.7 us
    unnamed x17, local copies, waits for them, and re-layouts  13.8 us
    ppermute x3, starting transfers between devices, shifted(): return lax.ppermute(value, axis, pairs)  12.7 us
    dot_general x5, matrix products, attend(): jnp.einsum('nqd,nkd->nqk', grad_tile, value_flat, preferred_element_type=...  10.8 us
  transfers between devices with their start and end apart: 5, of which 4 were waited for; matrix products, arithmetic and copies ran while one was open for 7% of the time, Pallas kernels for 0%

commit v1 on v0

v1 whole, which is shorter than its diff:
```python
import functools
import math

import jax
import jax.numpy as jnp
from jax import lax
from jax.experimental import pallas as pl
from jax.experimental.pallas import tpu as pltpu
from jax.sharding import PartitionSpec as P

HEAD_BITS = 8
VMEM = pl.BlockSpec(memory_space=pltpu.VMEM)
SMEM = pl.BlockSpec(memory_space=pltpu.SMEM)
PARAMS = pltpu.CompilerParams(vmem_limit_bytes=56 * 1024 * 1024)
NT = (((1,), (1,)), ((), ()))
NN = (((1,), (0,)), ((), ()))
TN = (((0,), (0,)), ((), ()))


def shifted(value, axis, steps):
    count = lax.axis_size(axis)
    pairs = [(source, (source + steps) % count) for source in range(count)]
    return lax.ppermute(value, axis, pairs)


def exchanged(value):
    return lax.all_to_all(value, "ctx", split_axis=0, concat_axis=0, tiled=True)


def tile_of(code, rows, cols):
    block = lax.shift_right_logical(code, HEAD_BITS)
    head = lax.bitwise_and(code, (1 << HEAD_BITS) - 1)
    return (
        pl.ds(pl.multiple_of(block * rows, rows), rows),
        pl.ds(pl.multiple_of(head * cols, cols), cols),
    )


def pack_kernel(codes, source, packed):
    slots, rows, cols = packed.shape

    def one(slot, carry):
        packed[slot] = source[tile_of(jnp.maximum(codes[slot], 0), rows, cols)]
        return carry

    lax.fori_loop(0, slots, one, 0, unroll=4)


def sum_kernel(codes, terms, total, wide):
    slots, rows, cols = terms.shape
    wide[...] = jnp.zeros_like(wide)

    def one(slot, carry):
        code = codes[slot]

        @pl.when(code >= 0)
        def _():
            where = tile_of(code, rows, cols)
            wide[where] += terms[slot].astype(jnp.float32)

        return carry

    lax.fori_loop(0, slots, one, 0, unroll=4)
    total[...] = wide[...].astype(total.dtype)


def softmax_rows(query, key, used_rows, scale):
    scores = lax.dot_general(key, query, NT, preferred_element_type=jnp.float32) * scale
    row = lax.broadcasted_iota(jnp.int32, scores.shape, 0)
    scores = jnp.where(row < used_rows, scores, -jnp.inf)
    exp_scores = jnp.exp(scores - jnp.max(scores, axis=0, keepdims=True))
    return exp_scores * (1.0 / jnp.sum(exp_scores, axis=0, keepdims=True))


def listed(places, head, list_size, tiles):
    where = [jnp.maximum(places[head * list_size + item], 0) for item in range(list_size)]
    return jnp.concatenate([tiles[place] for place in where], axis=0)


def put_terms(places, head, list_size, terms, out):
    rows = terms.shape[0] // list_size
    for item in range(list_size):
        place = places[head * list_size + item]

        @pl.when(place >= 0)
        def _():
            out[place] = terms[item * rows : (item + 1) * rows]


def value_kernel(list_size, scale, places, lengths, queries, grads, keys, terms):
    rows, cols = keys.shape[1:]

    def one(head, carry):
        columns = pl.ds(pl.multiple_of(head * cols, cols), cols)
        key = listed(places, head, list_size, keys)
        weights = softmax_rows(queries[:, columns], key, lengths[head] * rows, scale)
        made = lax.dot_general(
            weights.astype(jnp.bfloat16),
            grads[:, columns],
            NN,
            preferred_element_type=jnp.float32,
        )
        put_terms(places, head, list_size, made.astype(jnp.bfloat16), terms)
        return carry

    lax.fori_loop(0, lengths.shape[0], one, 0)


def key_kernel(
    list_size, scale, places, lengths, queries, grads, keys, values, query_grad, terms
):
    rows, cols = keys.shape[1:]

    def one(head, carry):
        columns = pl.ds(pl.multiple_of(head * cols, cols), cols)
        query = queries[:, columns]
        key = listed(places, head, list_size, keys)
        value = listed(places, head, list_size, values)
        weights = softmax_rows(query, key, lengths[head] * rows, scale)
        weights_low = weights.astype(jnp.bfloat16).astype(jnp.float32)
        dweights = lax.dot_general(
            value, grads[:, columns], NT, preferred_element_type=jnp.float32
        )
        row_delta = jnp.sum(weights_low * dweights, axis=0, keepdims=True)
        dscores = (weights * (dweights - row_delta)).astype(jnp.bfloat16)
        made = lax.dot_general(dscores, query, NN, preferred_element_type=jnp.float32)
        put_terms(places, head, list_size, (made * scale).astype(jnp.bfloat16), terms)
        flipped = lax.dot_general(key, dscores, TN, preferred_element_type=jnp.float32)
        query_grad[:, columns] = (flipped * scale).T.astype(jnp.bfloat16)
        return carry

    lax.fori_loop(0, lengths.shape[0], one, 0)


def local(queries, keys, values, out_grad, key_blocks, list_lengths):
    ctx_count = lax.axis_size("ctx")
    my_index = lax.axis_index("ctx")
    row_count, column_count = queries.shape[1:]
    head_count = list_lengths.shape[2]
    head_dim = column_count // head_count
    list_size = key_blocks.shape[3]
    block_rows = row_count // 2
    entries = head_count * list_size
    capacity = (entries + ctx_count - 1) // ctx_count
    slots = ctx_count * capacity
    scale = 1.0 / math.sqrt(head_dim)

    chosen = key_blocks[0]
    lengths = list_lengths[0]
    items = jnp.arange(list_size, dtype=jnp.int32)
    heads = jnp.arange(head_count, dtype=jnp.int32)
    peers = jnp.arange(ctx_count, dtype=jnp.int32)
    is_used = items[None, None, :] < lengths[:, :, None]
    is_mine = is_used & ((chosen >> 1) == my_index)
    hit = jnp.sum(jnp.where(is_mine, 1 + (chosen & 1), 0), axis=2)
    rank = jnp.sum(
        jnp.where((heads[None, None, :] < heads[None, :, None]) & (hit[:, None, :] > 0), 1, 0),
        axis=2,
    )
    code = ((hit - 1) << HEAD_BITS) + heads[None, :]
    ranks = jnp.arange(capacity, dtype=jnp.int32)
    codes = jnp.max(
        jnp.where(
            (hit[:, None, :] > 0) & (rank[:, None, :] == ranks[None, :, None]),
            code[:, None, :],
            -1,
        ),
        axis=2,
    ).reshape(slots)

    my_lengths = lax.dynamic_index_in_dim(lengths, my_index, 0, keepdims=False)
    my_chosen = lax.dynamic_index_in_dim(chosen, my_index, 0, keepdims=False)
    my_used = items[None, :] < my_lengths[:, None]
    my_holder = jnp.where(my_used, my_chosen >> 1, -1)
    earlier = (heads[None, None, :, None] < heads[:, None, None, None]) & (
        my_holder[None, None, :, :] == my_holder[:, :, None, None]
    )
    my_rank = jnp.sum(jnp.where(earlier, 1, 0), axis=(2, 3))
    places = jnp.where(my_used, my_holder * capacity + my_rank, -1).reshape(entries)

    packed_shape = jax.ShapeDtypeStruct((slots, block_rows, head_dim), jnp.bfloat16)
    flat_shape = jax.ShapeDtypeStruct((row_count, column_count), jnp.bfloat16)
    sent_shape = (ctx_count, capacity, block_rows, head_dim)

    def pack(name, source):
        packed = pl.pallas_call(
            pack_kernel,
            out_shape=packed_shape,
            in_specs=[SMEM, VMEM],
            out_specs=VMEM,
            compiler_params=PARAMS,
            name=name,
        )(codes, source)
        return exchanged(packed.reshape(sent_shape)).reshape(packed_shape.shape)

    def add_up(name, terms):
        returned = exchanged(terms.reshape(sent_shape)).reshape(packed_shape.shape)
        return pl.pallas_call(
            sum_kernel,
            out_shape=flat_shape,
            in_specs=[SMEM, VMEM],
            out_specs=VMEM,
            scratch_shapes=[pltpu.VMEM((row_count, column_count), jnp.float32)],
            compiler_params=PARAMS,
            name=name,
        )(codes, returned)

    fetched_keys = pack("pack_keys", keys[0])
    fetched_values = pack("pack_values", values[0])
    value_terms = pl.pallas_call(
        functools.partial(value_kernel, list_size, scale),
        out_shape=packed_shape,
        in_specs=[SMEM, SMEM, VMEM, VMEM, VMEM],
        out_specs=VMEM,
        compiler_params=PARAMS,
        name="value_terms",
    )(places, my_lengths, queries[0], out_grad[0], fetched_keys)
    query_grad, key_terms = pl.pallas_call(
        functools.partial(key_kernel, list_size, scale),
        out_shape=(flat_shape, packed_shape),
        in_specs=[SMEM, SMEM, VMEM, VMEM, VMEM, VMEM],
        out_specs=(VMEM, VMEM),
        compiler_params=PARAMS,
        name="key_terms",
    )(places, my_lengths, queries[0], out_grad[0], fetched_keys, fetched_values)
    value_grad = add_up("sum_values", value_terms)
    key_grad = add_up("sum_keys", key_terms)
    handed_queries = shifted(query_grad, "section", -1)
    handed_values = shifted(value_grad, "section", -1)
    handed_keys = shifted(key_grad, "section", -1)
    return (handed_queries[None], handed_keys[None], handed_values[None])


def solution(mesh):
    placed = (
        P("section", "ctx", None),
        P("section", "ctx", None),
        P("section", "ctx", None),
        P("section", "ctx", None),
        P("section", None, None, None),
        P("section", None, None),
    )
    return jax.shard_map(
        local,
        mesh=mesh,
        in_specs=placed,
        out_specs=(P("section", "ctx", None), P("section", "ctx", None), P("section", "ctx", None)),
        check_vma=False,
    )
```

time: 458 us -> 247 us (0.54)
  local copies, waits for them, and re-layouts: 134 us -> 9.28 us
  waiting for transfers between devices: 217 us -> 134 us
  Pallas kernels: 0 us -> 62.8 us
  matrix products: 60.6 us -> 0 us
  other arithmetic: 17.7 us -> 3.74 us
  starting transfers between devices: 25.1 us -> 36.3 us
    all_to_all x2 -> x4, waiting for transfers between devices: 167 us -> 93 us  [exchanged(): return lax.all_to_all(value, 'ctx', split_axis=0, concat_axis=0, tiled=True)]
    pallas_call x0 -> x6, Pallas kernels: none -> 62.8 us  [the longest x1 27.3 us: local(): pl.pallas_call(functools.partial(key_kernel, list_size, scale), out_shape...]
    dot_general x26 -> x0, matrix products: 44.8 us -> none  [the longest x5 10.8 us: attend(): jnp.einsum('nqd,nkd->nqk', grad_tile, value_flat, preferred_element_type=...]
    scatter x3 -> x0, local copies, waits for them, and re-layouts: 34.5 us -> none  [the longest x1 14.7 us: local(): returning = jnp.zeros((dump_slot + 1, 2, block_rows, head_dim), jnp.bfloa...]
    reshape x5 -> x1, local copies, waits for them, and re-layouts: 24.7 us -> 0.69 us  [local(): codes = jnp.max(jnp.where((hit[:, None, :] > 0) & (rank[:, None, :] == ra...]
    sub x5 -> x0, matrix products: 15.8 us -> none  [attend(): exp_scores = jnp.exp(scores - row_max)]
    gather x2 -> x0, local copies, waits for them, and re-layouts: 14.5 us -> none  [the longest x1 8.51 us: local(): arrived = fetched.reshape(dump_slot, 2, block_rows, head_dim)[recv_slot]]
    another operation x5 -> x0, other arithmetic: 11.3 us -> none  [the longest x1 5.43 us: local(): jnp.stack([key_terms, value_terms], axis=3)]
  transfers between devices with their start and end apart: 5 -> 7, of which waited for: 4 -> 6; matrix products, arithmetic and copies ran while one was open for 7% -> 2% of each run, Pallas kernels for 0% -> 24%
where the time goes in v1:
time: 247 us; the launch traced here: 246 us
  waiting for transfers between devices  134 us (54%)
  Pallas kernels  62.8 us (25%)
  starting transfers between devices  36.3 us (15%)
  local copies, waits for them, and re-layouts  9.28 us (4%)
  other arithmetic  3.74 us (2%)
    all_to_all x4, waiting for transfers between devices, exchanged(): return lax.all_to_all(value, 'ctx', split_axis=0, concat_axis=0, tiled=True)  93 us
    ppermute x3, waiting for transfers between devices, shifted(): return lax.ppermute(value, axis, pairs)  40.6 us
    pallas_call x1, Pallas kernels, local(): pl.pallas_call(functools.partial(key_kernel, list_size, scale), out_shape...  27.3 us
    all_to_all x4, starting transfers between devices, exchanged(): return lax.all_to_all(value, 'ctx', split_axis=0, concat_axis=0, tiled=True)  23.4 us
    pallas_call x1, Pallas kernels, local(): pl.pallas_call(functools.partial(value_kernel, list_size, scale), out_sha...  18.1 us
    ppermute x3, starting transfers between devices, shifted(): return lax.ppermute(value, axis, pairs)  12.9 us
    pallas_call x2, Pallas kernels, add_up(): pl.pallas_call(sum_kernel, out_shape=flat_shape, in_specs=[SMEM, VMEM], o...  9.43 us
    pallas_call x2, Pallas kernels, pack(): pl.pallas_call(pack_kernel, out_shape=packed_shape, in_specs=[SMEM, VMEM]...  7.98 us
  transfers between devices with their start and end apart: 7, of which 6 were waited for; matrix products, arithmetic and copies ran while one was open for 2% of the time, Pallas kernels for 24%

profile of v1, /device:TPU:8, one launch (start us, length us, event | category | flops | bytes accessed | tf_op | source)
XLA Modules:
  0.0 246.5 jit_solution(6389718395753153380)
XLA Ops:
  0.7 0.7 copy.34
  1.4 0.8 fusion
  2.2 0.2 select_reduce_fusion
  2.4 0.1 copy.31
  2.5 0.7 reshape.166.codes
  3.2 4.0 %pack_keys.1 = bf16[96,128,128]{2,1,0:T(8,128)(2,1)} custom-call(s32[96]{0:T(128)} %reshape.166.codes, bf16[256,2560]{1,0:T(8,128)(2,1)} %bitcast.40), custom_call_target="tpu_custom_call" | custom-call | tf_op jit(solution)/shard_map/pack_keys/pallas_call | solution.py:186
  7.2 7.5 %all-to-all-start = ((bf16[32,3,128,128]{3,2,1,0:T(8,128)(2,1)}), bf16[32,3,128,128]{3,2,1,0:T(8,128)(2,1)S(1)}, u32[]{:S(2)}, u32[]{:S(2)}) async-start(bf16[32,3,128,128]{3,2,1,0:T(8,128)(2,1)} %bitcast.34), calls=%async_computation | async-start | bytes 6291456 | tf_op jit(solution)/shard_map/all_to_all | solution.py:27
  14.7 4.0 %pack_values.1 = bf16[96,128,128]{2,1,0:T(8,128)(2,1)} custom-call(s32[96]{0:T(128)} %reshape.166.codes, bf16[256,2560]{1,0:T(8,128)(2,1)} %bitcast.41), custom_call_target="tpu_custom_call" | custom-call | tf_op jit(solution)/shard_map/pack_values/pallas_call | solution.py:186
  18.7 35.5 %all-to-all-done = bf16[32,3,128,128]{3,2,1,0:T(8,128)(2,1)S(1)} async-done(((bf16[32,3,128,128]{3,2,1,0:T(8,128)(2,1)}), bf16[32,3,128,128]{3,2,1,0:T(8,128)(2,1)S(1)}, u32[]{:S(2)}, u32[]{:S(2)}) %all-to-all-start) | async-done | bytes 3145760 | tf_op jit(solution)/shard_map/all_to_all | solution.py:27
  54.2 0.0 copy-start
  54.2 0.0 copy-start.2
  54.2 1.7 copy-done
  55.9 5.3 %all-to-all-start.1 = ((bf16[32,3,128,128]{3,2,1,0:T(8,128)(2,1)}), bf16[32,3,128,128]{3,2,1,0:T(8,128)(2,1)}, u32[]{:S(2)}, u32[]{:S(2)}) async-start(bf16[32,3,128,128]{3,2,1,0:T(8,128)(2,1)} %bitcast.31), calls=%async_computation.1 | async-start | bytes 6291456 | tf_op jit(solution)/shard_map/all_to_all | solution.py:27
  61.2 0.0 copy-done.3
  61.2 0.5 dynamic-slice_reduce_fusion.lengths
  61.8 0.0 copy-start.4
  61.8 0.1 copy.27
  61.9 0.1 lt.98
  62.0 0.0 copy-done.2
  62.0 0.5 fusion.5
  62.5 0.1 shift_right_arithmetic.24
  62.6 0.1 copy.29
  62.7 0.1 fusion.1
  62.8 0.1 copy.28
  62.9 0.1 copy.30
  63.0 1.6 select_reduce_fusion.1
  64.6 0.1 reduce_sum.30
  64.7 0.5 add_select_fusion.places
  65.2 0.0 copy-done.4
  65.2 18.1 %value_terms.1 = bf16[96,128,128]{2,1,0:T(8,128)(2,1)} custom-call(s32[80]{0:T(128)} %add_select_fusion.places, s32[20]{0:T(128)} %copy-done.4, bf16[256,2560]{1,0:T(8,128)(2,1)} %bitcast.35, bf16[256,2560]{1,0:T(8,128)(2,1)} %bitcast.37, bf16[96,128,128]{2,1,0:T(8,128)(2,1)} %bitcast.29), custom_call_target="tpu_custom_call" | custom-call | tf_op jit(solution)/shard_map/value_terms/pallas_call | solution.py:210
  83.3 17.5 %all-to-all-done.1 = bf16[32,3,128,128]{3,2,1,0:T(8,128)(2,1)} async-done(((bf16[32,3,128,128]{3,2,1,0:T(8,128)(2,1)}), bf16[32,3,128,128]{3,2,1,0:T(8,128)(2,1)}, u32[]{:S(2)}, u32[]{:S(2)}) %all-to-all-start.1) | async-done | bytes 3145760 | tf_op jit(solution)/shard_map/all_to_all | solution.py:27
  100.8 5.2 %all-to-all-start.3 = ((bf16[32,3,128,128]{3,2,1,0:T(8,128)(2,1)}), bf16[32,3,128,128]{3,2,1,0:T(8,128)(2,1)S(1)}, u32[]{:S(2)}, u32[]{:S(2)}) async-start(bf16[32,3,128,128]{3,2,1,0:T(8,128)(2,1)} %bitcast.33), calls=%async_computation.3 | async-start | bytes 6291456 | tf_op jit(solution)/shard_map/all_to_all | solution.py:27
  106.0 27.3 %key_terms.1 = (bf16[256,2560]{1,0:T(8,128)(2,1)}, bf16[96,128,128]{2,1,0:T(8,128)(2,1)}) custom-call(s32[80]{0:T(128)} %add_select_fusion.places, s32[20]{0:T(128)} %copy-done.4, bf16[256,2560]{1,0:T(8,128)(2,1)} %bitcast.36, bf16[256,2560]{1,0:T(8,128)(2,1)} %bitcast.38, bf16[96,128,128]{2,1,0:T(8,128)(2,1)} %bitcast.30, bf16[96,128,128]{2,1,0:T(8,128)(2,1)} %bitcast.11.values), custom_call_target="tpu_custom_call" | custom-call | tf_op jit(solution)/shard_map/key_terms/pallas_call | solution.py:218
  133.3 12.2 %all-to-all-done.3 = bf16[32,3,128,128]{3,2,1,0:T(8,128)(2,1)S(1)} async-done(((bf16[32,3,128,128]{3,2,1,0:T(8,128)(2,1)}), bf16[32,3,128,128]{3,2,1,0:T(8,128)(2,1)S(1)}, u32[]{:S(2)}, u32[]{:S(2)}) %all-to-all-start.3) | async-done | bytes 3145760 | tf_op jit(solution)/shard_map/all_to_all | solution.py:27
  145.5 1.7 copy-done.1
  147.2 5.3 %all-to-all-start.2 = ((bf16[32,3,128,128]{3,2,1,0:T(8,128)(2,1)}), bf16[32,3,128,128]{3,2,1,0:T(8,128)(2,1)}, u32[]{:S(2)}, u32[]{:S(2)}) async-start(bf16[32,3,128,128]{3,2,1,0:T(8,128)(2,1)} %bitcast.39), calls=%async_computation.2 | async-start | bytes 6291456 | tf_op jit(solution)/shard_map/all_to_all | solution.py:27
  152.5 5.9 %collective-permute-start = (bf16[256,2560]{1,0:T(8,128)(2,1)}, bf16[256,2560]{1,0:T(8,128)(2,1)S(1)}, u32[]{:S(2)}, u32[]{:S(2)}) collective-permute-start(bf16[256,2560]{1,0:T(8,128)(2,1)} %get-tuple-element.5), channel_id=1, source_target_pairs={{0,7},{1,0},{2,1},{3,2},{4,3},{5,4},{6,5},{7,6},{8,15},{9,8},{10,9... | collective-permute-start | bytes 3932168 | tf_op jit(solution)/shard_map/ppermute | solution.py:23
  158.5 4.7 %sum_values.1 = bf16[256,2560]{1,0:T(8,128)(2,1)} custom-call(s32[96]{0:T(128)} %reshape.166.codes, bf16[96,128,128]{2,1,0:T(8,128)(2,1)} %bitcast.32), custom_call_target="tpu_custom_call" | custom-call | tf_op jit(solution)/shard_map/sum_values/pallas_call | solution.py:198
  163.2 1.1 collective-permute-start.2
  164.3 27.8 %all-to-all-done.2 = bf16[32,3,128,128]{3,2,1,0:T(8,128)(2,1)} async-done(((bf16[32,3,128,128]{3,2,1,0:T(8,128)(2,1)}), bf16[32,3,128,128]{3,2,1,0:T(8,128)(2,1)}, u32[]{:S(2)}, u32[]{:S(2)}) %all-to-all-start.2) | async-done | bytes 3145760 | tf_op jit(solution)/shard_map/all_to_all | solution.py:27
  192.1 4.7 %sum_keys.1 = bf16[256,2560]{1,0:T(8,128)(2,1)} custom-call(s32[96]{0:T(128)} %reshape.166.codes, bf16[96,128,128]{2,1,0:T(8,128)(2,1)} %bitcast.14.terms), custom_call_target="tpu_custom_call" | custom-call | tf_op jit(solution)/shard_map/sum_keys/pallas_call | solution.py:198
  196.8 5.9 %collective-permute-start.1 = (bf16[256,2560]{1,0:T(8,128)(2,1)}, bf16[256,2560]{1,0:T(8,128)(2,1)S(1)}, u32[]{:S(2)}, u32[]{:S(2)}) collective-permute-start(bf16[256,2560]{1,0:T(8,128)(2,1)} %sum_keys.1), channel_id=1, source_target_pairs={{0,7},{1,0},{2,1},{3,2},{4,3},{5,4},{6,5},{7,6},{8,15},{9,8},{10,9... | collective-permute-start | bytes 3932168 | tf_op jit(solution)/shard_map/ppermute | solution.py:23
  202.7 0.0 collective-permute-done
  202.7 13.3 %collective-permute-done.2 = bf16[256,2560]{1,0:T(8,128)(2,1)S(1)} collective-permute-done((bf16[256,2560]{1,0:T(8,128)(2,1)}, bf16[256,2560]{1,0:T(8,128)(2,1)S(1)}, u32[]{:S(2)}, u32[]{:S(2)}) %collective-permute-start.2) | collective-permute-done | bytes 1310752 | tf_op jit(solution)/shard_map/ppermute | solution.py:23
  216.0 27.3 %collective-permute-done.1 = bf16[256,2560]{1,0:T(8,128)(2,1)S(1)} collective-permute-done((bf16[256,2560]{1,0:T(8,128)(2,1)}, bf16[256,2560]{1,0:T(8,128)(2,1)S(1)}, u32[]{:S(2)}, u32[]{:S(2)}) %collective-permute-start.1) | collective-permute-done | bytes 1310752 | tf_op jit(solution)/shard_map/ppermute | solution.py:23
  243.3 1.1 copy.38
  244.4 1.1 copy.39
  245.4 1.1 copy.40
  (8 shorter events, 0.1 us)
Async XLA Ops:
  7.2 47.0 %all-to-all-start = ((bf16[32,3,128,128]{3,2,1,0:T(8,128)(2,1)}), bf16[32,3,128,128]{3,2,1,0:T(8,128)(2,1)S(1)}, u32[]{:S(2)}, u32[]{:S(2)}) async-start(bf16[32,3,128,128]{3,2,1,0:T(8,128)(2,1)} %bitcast.34), calls=%async_computation | async-start | bytes 6291456 | tf_op jit(solution)/shard_map/all_to_all | solution.py:27
  54.2 1.7 copy-start
  54.2 7.0 %copy-start.3 = (s32[1,32,20]{1,0,2:T(1,128)S(1)}, s32[1,32,20]{1,0,2:T(1,128)}, u32[]{:S(2)}) copy-start(s32[1,32,20]{1,0,2:T(1,128)} %param.11) | copy-start | bytes 7684
  54.2 7.8 %copy-start.2 = (s32[1,32,20,4]{1,3,2,0:T(4,128)S(1)}, s32[1,32,20,4]{1,3,2,0:T(4,128)}, u32[]{:S(2)}) copy-start(s32[1,32,20,4]{1,3,2,0:T(4,128)} %param.10) | copy-start | bytes 30724
  55.9 44.9 %all-to-all-start.1 = ((bf16[32,3,128,128]{3,2,1,0:T(8,128)(2,1)}), bf16[32,3,128,128]{3,2,1,0:T(8,128)(2,1)}, u32[]{:S(2)}, u32[]{:S(2)}) async-start(bf16[32,3,128,128]{3,2,1,0:T(8,128)(2,1)} %bitcast.31), calls=%async_computation.1 | async-start | bytes 6291456 | tf_op jit(solution)/shard_map/all_to_all | solution.py:27
  61.8 3.5 %copy-start.4 = (s32[20]{0:T(128)}, s32[20]{0:T(128)S(1)}, u32[]{:S(2)}) copy-start(s32[20]{0:T(128)S(1)} %dynamic-slice_reduce_fusion.lengths) | copy-start | bytes 244
  100.8 44.8 %all-to-all-start.3 = ((bf16[32,3,128,128]{3,2,1,0:T(8,128)(2,1)}), bf16[32,3,128,128]{3,2,1,0:T(8,128)(2,1)S(1)}, u32[]{:S(2)}, u32[]{:S(2)}) async-start(bf16[32,3,128,128]{3,2,1,0:T(8,128)(2,1)} %bitcast.33), calls=%async_computation.3 | async-start | bytes 6291456 | tf_op jit(solution)/shard_map/all_to_all | solution.py:27
  145.5 1.7 copy-start.1
  147.2 44.9 %all-to-all-start.2 = ((bf16[32,3,128,128]{3,2,1,0:T(8,128)(2,1)}), bf16[32,3,128,128]{3,2,1,0:T(8,128)(2,1)}, u32[]{:S(2)}, u32[]{:S(2)}) async-start(bf16[32,3,128,128]{3,2,1,0:T(8,128)(2,1)} %bitcast.39), calls=%async_computation.2 | async-start | bytes 6291456 | tf_op jit(solution)/shard_map/all_to_all | solution.py:27
  152.5 50.2 %collective-permute-start = (bf16[256,2560]{1,0:T(8,128)(2,1)}, bf16[256,2560]{1,0:T(8,128)(2,1)S(1)}, u32[]{:S(2)}, u32[]{:S(2)}) collective-permute-start(bf16[256,2560]{1,0:T(8,128)(2,1)} %get-tuple-element.5), channel_id=1, source_target_pairs={{0,7},{1,0},{2,1},{3,2},{4,3},{5,4},{6,5},{7,6},{8,15},{9,8},{10,9... | collective-permute-start | bytes 3932168 | tf_op jit(solution)/shard_map/ppermute | solution.py:23
  163.2 52.8 %collective-permute-start.2 = (bf16[256,2560]{1,0:T(8,128)(2,1)}, bf16[256,2560]{1,0:T(8,128)(2,1)S(1)}, u32[]{:S(2)}, u32[]{:S(2)}) collective-permute-start(bf16[256,2560]{1,0:T(8,128)(2,1)} %sum_values.1), channel_id=1, source_target_pairs={{0,7},{1,0},{2,1},{3,2},{4,3},{5,4},{6,5},{7,6},{8,15},{9,8},{10,9... | collective-permute-start | bytes 3932168 | tf_op jit(solution)/shard_map/ppermute | solution.py:23
  196.8 46.5 %collective-permute-start.1 = (bf16[256,2560]{1,0:T(8,128)(2,1)}, bf16[256,2560]{1,0:T(8,128)(2,1)S(1)}, u32[]{:S(2)}, u32[]{:S(2)}) collective-permute-start(bf16[256,2560]{1,0:T(8,128)(2,1)} %sum_keys.1), channel_id=1, source_target_pairs={{0,7},{1,0},{2,1},{3,2},{4,3},{5,4},{6,5},{7,6},{8,15},{9,8},{10,9... | collective-permute-start | bytes 3932168 | tf_op jit(solution)/shard_map/ppermute | solution.py:23

commit v2 on v1

v2 whole, which is shorter than its diff:
```python
import functools
import math

import jax
import jax.numpy as jnp
from jax import lax
from jax.experimental import pallas as pl
from jax.experimental.pallas import tpu as pltpu
from jax.sharding import PartitionSpec as P

HEAD_BITS = 8
VMEM = pl.BlockSpec(memory_space=pltpu.VMEM)
SMEM = pl.BlockSpec(memory_space=pltpu.SMEM)
PARAMS = pltpu.CompilerParams(vmem_limit_bytes=56 * 1024 * 1024)
NT = (((1,), (1,)), ((), ()))
NN = (((1,), (0,)), ((), ()))
TN = (((0,), (0,)), ((), ()))


def shifted(value, axis, steps):
    count = lax.axis_size(axis)
    pairs = [(source, (source + steps) % count) for source in range(count)]
    return lax.ppermute(value, axis, pairs)


def tile_of(code, rows, cols):
    block = lax.shift_right_logical(code, HEAD_BITS)
    head = lax.bitwise_and(code, (1 << HEAD_BITS) - 1)
    return (
        pl.ds(pl.multiple_of(block * rows, rows), rows),
        pl.ds(pl.multiple_of(head * cols, cols), cols),
    )


def pack_kernel(codes, source, packed):
    slots, rows, cols = packed.shape

    def one(slot, carry):
        packed[slot] = source[tile_of(jnp.maximum(codes[slot], 0), rows, cols)]
        return carry

    lax.fori_loop(0, slots, one, 0, unroll=4)


def add_terms(codes, terms, wide):
    slots, rows, cols = terms.shape
    wide[...] = jnp.zeros_like(wide)

    def one(slot, carry):
        code = codes[slot]

        @pl.when(code >= 0)
        def _():
            wide[tile_of(code, rows, cols)] += terms[slot].astype(jnp.float32)

        return carry

    lax.fori_loop(0, slots, one, 0, unroll=4)


def sum_kernel(codes, terms, total, wide):
    add_terms(codes, terms, wide)
    total[...] = wide[...].astype(total.dtype)


def join_kernel(codes, head_part, terms, total, wide):
    add_terms(codes, terms, wide)
    tail_rows = terms.shape[1]
    head_rows = total.shape[0] // 2 - tail_rows
    for block in range(2):
        start = block * (head_rows + tail_rows)
        total[start : start + head_rows] = head_part[block * head_rows : (block + 1) * head_rows]
        total[start + head_rows : start + head_rows + tail_rows] = wide[
            block * tail_rows : (block + 1) * tail_rows
        ].astype(total.dtype)


def weights_of(query, key, length, list_size, scale):
    scores = lax.dot_general(key, query, NT, preferred_element_type=jnp.float32)
    row_max = jnp.max(scores, axis=0, keepdims=True)
    exp_scores = jnp.exp2((scores - row_max) * (scale * math.log2(math.e)))
    rows = key.shape[0] // list_size
    parts = [exp_scores[item * rows : (item + 1) * rows] for item in range(list_size)]
    kept = [jnp.where(item < length, 1.0, 0.0).astype(jnp.float32) for item in range(list_size)]
    total = sum(keep * jnp.sum(part, axis=0, keepdims=True) for keep, part in zip(kept, parts))
    inverse = 1.0 / total
    return [part * (inverse * keep) for keep, part in zip(kept, parts)]


def listed(places, head, list_size, tiles):
    return jnp.concatenate(
        [tiles[places[head * list_size + item]] for item in range(list_size)], axis=0
    )


def put_terms(places, head, list_size, length, terms, outs):
    rows = terms.shape[0] // list_size
    for item in range(list_size):

        @pl.when(item < length)
        def _():
            place = places[head * list_size + item]
            start = item * rows
            for out in outs:
                count = out.shape[1]
                out[place] = terms[start : start + count]
                start += count


def value_kernel(list_size, scale, places, lengths, queries, grads, keys, *terms):
    cols = keys.shape[2]

    def one(head, carry):
        columns = pl.ds(pl.multiple_of(head * cols, cols), cols)
        key = listed(places, head, list_size, keys)
        weights = weights_of(queries[:, columns], key, lengths[head], list_size, scale)
        weights_low = jnp.concatenate([part.astype(jnp.bfloat16) for part in weights], axis=0)
        made = lax.dot_general(
            weights_low, grads[:, columns], NN, preferred_element_type=jnp.float32
        )
        put_terms(places, head, list_size, lengths[head], made.astype(jnp.bfloat16), terms)
        return carry

    lax.fori_loop(0, lengths.shape[0], one, 0, unroll=4)


def key_kernel(
    list_size, scale, places, lengths, queries, grads, keys, values, query_grad, terms
):
    rows, cols = keys.shape[1:]

    def one(head, carry):
        columns = pl.ds(pl.multiple_of(head * cols, cols), cols)
        query = queries[:, columns]
        key = listed(places, head, list_size, keys)
        value = listed(places, head, list_size, values)
        weights = weights_of(query, key, lengths[head], list_size, scale)
        weights_low = [part.astype(jnp.bfloat16).astype(jnp.float32) for part in weights]
        joined = lax.dot_general(
            value, grads[:, columns], NT, preferred_element_type=jnp.float32
        )
        dweights = [joined[item * rows : (item + 1) * rows] for item in range(list_size)]
        row_delta = sum(
            jnp.sum(low * part, axis=0, keepdims=True)
            for low, part in zip(weights_low, dweights)
        )
        dscores = jnp.concatenate(
            [
                (weight * (part - row_delta)).astype(jnp.bfloat16)
                for weight, part in zip(weights, dweights)
            ],
            axis=0,
        )
        made = lax.dot_general(dscores, query, NN, preferred_element_type=jnp.float32)
        made = (made * scale).astype(jnp.bfloat16)
        put_terms(places, head, list_size, lengths[head], made, [terms])
        flipped = lax.dot_general(key, dscores, TN, preferred_element_type=jnp.float32)
        query_grad[:, columns] = (flipped * scale).astype(jnp.bfloat16).T
        return carry

    lax.fori_loop(0, lengths.shape[0], one, 0, unroll=4)


def local(queries, keys, values, out_grad, key_blocks, list_lengths):
    ctx_count = lax.axis_size("ctx")
    my_index = lax.axis_index("ctx")
    row_count, column_count = queries.shape[1:]
    head_count = list_lengths.shape[2]
    head_dim = column_count // head_count
    list_size = key_blocks.shape[3]
    block_rows = row_count // 2
    entries = head_count * list_size
    capacity = (entries + ctx_count - 1) // ctx_count
    slots = ctx_count * capacity
    scale = 1.0 / math.sqrt(head_dim)

    chosen = key_blocks[0]
    lengths = list_lengths[0]
    items = jnp.arange(list_size, dtype=jnp.int32)
    heads = jnp.arange(head_count, dtype=jnp.int32)
    peers = jnp.arange(ctx_count, dtype=jnp.int32)
    is_used = items[None, None, :] < lengths[:, :, None]
    is_mine = is_used & ((chosen >> 1) == my_index)
    hit = jnp.sum(jnp.where(is_mine, 1 + (chosen & 1), 0), axis=2)
    rank = jnp.sum(
        jnp.where((heads[None, None, :] < heads[None, :, None]) & (hit[:, None, :] > 0), 1, 0),
        axis=2,
    )
    code = ((hit - 1) << HEAD_BITS) + heads[None, :]
    ranks = jnp.arange(capacity, dtype=jnp.int32)
    codes = jnp.max(
        jnp.where(
            (hit[:, None, :] > 0) & (rank[:, None, :] == ranks[None, :, None]),
            code[:, None, :],
            -1,
        ),
        axis=2,
    ).reshape(slots)

    my_lengths = lax.dynamic_index_in_dim(lengths, my_index, 0, keepdims=False)
    my_chosen = lax.dynamic_index_in_dim(chosen, my_index, 0, keepdims=False)
    my_used = items[None, :] < my_lengths[:, None]
    my_holder = jnp.where(my_used, my_chosen >> 1, -1)
    earlier = (heads[None, None, :, None] < heads[:, None, None, None]) & (
        my_holder[None, None, :, :] == my_holder[:, :, None, None]
    )
    my_rank = jnp.sum(jnp.where(earlier, 1, 0), axis=(2, 3))
    places = my_holder * capacity + my_rank
    places = jnp.where(my_used, places, places[:, :1]).reshape(entries)

    first_rows = block_rows // 2
    last_rows = block_rows - first_rows
    flat_shape = jax.ShapeDtypeStruct((row_count, column_count), jnp.bfloat16)

    def packed_shape(rows):
        return jax.ShapeDtypeStruct((slots, rows, head_dim), jnp.bfloat16)

    def exchanged(packed):
        parts = packed.reshape(ctx_count, capacity, *packed.shape[1:])
        parts = lax.all_to_all(parts, "ctx", split_axis=0, concat_axis=0, tiled=True)
        return parts.reshape(packed.shape)

    def pack(name, source):
        return exchanged(
            pl.pallas_call(
                pack_kernel,
                out_shape=packed_shape(block_rows),
                in_specs=[SMEM, VMEM],
                out_specs=VMEM,
                compiler_params=PARAMS,
                name=name,
            )(codes, source)
        )

    def add_up(name, returned):
        rows = 2 * returned.shape[1]
        return pl.pallas_call(
            sum_kernel,
            out_shape=jax.ShapeDtypeStruct((rows, column_count), jnp.bfloat16),
            in_specs=[SMEM, VMEM],
            out_specs=VMEM,
            scratch_shapes=[pltpu.VMEM((rows, column_count), jnp.float32)],
            compiler_params=PARAMS,
            name=name,
        )(codes, returned)

    fetched_keys = pack("pack_keys", keys[0])
    fetched_values = pack("pack_values", values[0])
    first_terms, last_terms = pl.pallas_call(
        functools.partial(value_kernel, list_size, scale),
        out_shape=(packed_shape(first_rows), packed_shape(last_rows)),
        in_specs=[SMEM, SMEM, VMEM, VMEM, VMEM],
        out_specs=(VMEM, VMEM),
        compiler_params=PARAMS,
        name="value_terms",
    )(places, my_lengths, queries[0], out_grad[0], fetched_keys)
    handed_terms = shifted(last_terms, "section", -1)
    handed_codes = shifted(codes, "section", -1)
    query_grad, key_terms = pl.pallas_call(
        functools.partial(key_kernel, list_size, scale),
        out_shape=(flat_shape, packed_shape(block_rows)),
        in_specs=[SMEM, SMEM, VMEM, VMEM, VMEM, VMEM],
        out_specs=(VMEM, VMEM),
        compiler_params=PARAMS,
        name="key_terms",
    )(places, my_lengths, queries[0], out_grad[0], fetched_keys, fetched_values)
    handed_queries = shifted(query_grad, "section", -1)
    first_values = add_up("sum_values", exchanged(first_terms))
    handed_first = shifted(first_values, "section", -1)
    key_terms, handed_terms, handed_codes = lax.optimization_barrier(
        (key_terms, handed_terms, handed_codes)
    )
    returned_keys = exchanged(key_terms)
    returned_keys, handed_queries, handed_first = lax.optimization_barrier(
        (returned_keys, handed_queries, handed_first)
    )
    key_grad = add_up("sum_keys", returned_keys)
    handed_keys = shifted(key_grad, "section", -1)
    handed_values = pl.pallas_call(
        join_kernel,
        out_shape=flat_shape,
        in_specs=[SMEM, VMEM, VMEM],
        out_specs=VMEM,
        scratch_shapes=[pltpu.VMEM((2 * last_rows, column_count), jnp.float32)],
        compiler_params=PARAMS,
        name="join_values",
    )(handed_codes, handed_first, exchanged(handed_terms))
    return (handed_queries[None], handed_keys[None], handed_values[None])


def solution(mesh):
    placed = (
        P("section", "ctx", None),
        P("section", "ctx", None),
        P("section", "ctx", None),
        P("section", "ctx", None),
        P("section", None, None, None),
        P("section", None, None),
    )
    return jax.shard_map(
        local,
        mesh=mesh,
        in_specs=placed,
        out_specs=(P("section", "ctx", None), P("section", "ctx", None), P("section", "ctx", None)),
        check_vma=False,
    )
```

time: 247 us -> 232 us (0.939)
  waiting for transfers between devices: 134 us -> 107 us
  starting transfers between devices: 36.3 us -> 45.7 us
    ppermute x3 -> x5, waiting for transfers between devices: 40.6 us -> 10.5 us  [shifted(): return lax.ppermute(value, axis, pairs)]
    all_to_all x4 -> x5, starting transfers between devices: 23.4 us -> 30.8 us  [exchanged(): lax.all_to_all(parts, 'ctx', split_axis=0, concat_axis=0, tiled=True)]
    pallas_call x1, Pallas kernels: 27.3 us -> 23.9 us  [local(): pl.pallas_call(functools.partial(key_kernel, list_size, scale), out_shape...]
    all_to_all x4 -> x5, waiting for transfers between devices: 93 us -> 96.3 us  [exchanged(): lax.all_to_all(parts, 'ctx', split_axis=0, concat_axis=0, tiled=True)]
    pallas_call x4 -> x5, Pallas kernels: 17.4 us -> 20.6 us  [the longest x2 8.47 us: add_up(): pl.pallas_call(sum_kernel, out_shape=jax.ShapeDtypeStruct((rows, column_c...]
    unnamed x14 -> x21, local copies, waits for them, and re-layouts: 7.27 us -> 9.24 us
    ppermute x3 -> x5, starting transfers between devices: 12.9 us -> 14.8 us  [shifted(): return lax.ppermute(value, axis, pairs)]
  transfers between devices with their start and end apart: 7 -> 10, of which waited for: 6 -> 5; matrix products, arithmetic and copies ran while one was open for 2% -> 2% of each run, Pallas kernels for 24% -> 25%
where the time goes in v2:
time: 232 us; the launch traced here: 231 us
  waiting for transfers between devices  107 us (46%)
  Pallas kernels  62.1 us (27%)
  starting transfers between devices  45.7 us (20%)
  local copies, waits for them, and re-layouts  11.3 us (5%)
  other arithmetic  4 us (2%)
    all_to_all x5, waiting for transfers between devices, exchanged(): lax.all_to_all(parts, 'ctx', split_axis=0, concat_axis=0, tiled=True)  96.3 us
    all_to_all x5, starting transfers between devices, exchanged(): lax.all_to_all(parts, 'ctx', split_axis=0, concat_axis=0, tiled=True)  30.8 us
    pallas_call x1, Pallas kernels, local(): pl.pallas_call(functools.partial(key_kernel, list_size, scale), out_shape...  23.9 us
    pallas_call x1, Pallas kernels, local(): pl.pallas_call(functools.partial(value_kernel, list_size, scale), out_sha...  17.6 us
    ppermute x5, starting transfers between devices, shifted(): return lax.ppermute(value, axis, pairs)  14.8 us
    ppermute x5, waiting for transfers between devices, shifted(): return lax.ppermute(value, axis, pairs)  10.5 us
    unnamed x21, local copies, waits for them, and re-layouts  9.24 us
    pallas_call x2, Pallas kernels, add_up(): pl.pallas_call(sum_kernel, out_shape=jax.ShapeDtypeStruct((rows, column_c...  8.47 us
  transfers between devices with their start and end apart: 10, of which 5 were waited for; matrix products, arithmetic and copies ran while one was open for 2% of the time, Pallas kernels for 25%

profile of v2, /device:TPU:8, one launch (start us, length us, event | category | flops | bytes accessed | tf_op | source)
XLA Modules:
  0.0 230.8 jit_solution(1589939872276764309)
XLA Ops:
  0.7 0.7 copy.40
  1.4 0.8 fusion
  2.2 0.2 select_reduce_fusion
  2.4 0.1 copy.37
  2.5 0.7 reshape.173.codes
  3.2 4.0 %pack_keys.1 = bf16[96,128,128]{2,1,0:T(8,128)(2,1)} custom-call(s32[96]{0:T(128)} %reshape.173.codes, bf16[256,2560]{1,0:T(8,128)(2,1)} %bitcast.43), custom_call_target="tpu_custom_call" | custom-call | tf_op jit(solution)/shard_map/pack_keys/pallas_call | solution.py:225
  7.2 7.5 %all-to-all-start = ((bf16[32,3,128,128]{3,2,1,0:T(8,128)(2,1)}), bf16[32,3,128,128]{3,2,1,0:T(8,128)(2,1)S(1)}, u32[]{:S(2)}, u32[]{:S(2)}) async-start(bf16[32,3,128,128]{3,2,1,0:T(8,128)(2,1)} %bitcast.34), calls=%async_computation | async-start | bytes 6291456 | tf_op jit(solution)/shard_map/all_to_all | solution.py:220
  14.7 4.0 %pack_values.1 = bf16[96,128,128]{2,1,0:T(8,128)(2,1)} custom-call(s32[96]{0:T(128)} %reshape.173.codes, bf16[256,2560]{1,0:T(8,128)(2,1)} %bitcast.44), custom_call_target="tpu_custom_call" | custom-call | tf_op jit(solution)/shard_map/pack_values/pallas_call | solution.py:225
  18.7 35.5 %all-to-all-done = bf16[32,3,128,128]{3,2,1,0:T(8,128)(2,1)S(1)} async-done(((bf16[32,3,128,128]{3,2,1,0:T(8,128)(2,1)}), bf16[32,3,128,128]{3,2,1,0:T(8,128)(2,1)S(1)}, u32[]{:S(2)}, u32[]{:S(2)}) %all-to-all-start) | async-done | bytes 3145760 | tf_op jit(solution)/shard_map/all_to_all | solution.py:220
  54.2 1.7 copy-done
  55.9 5.3 %all-to-all-start.1 = ((bf16[32,3,128,128]{3,2,1,0:T(8,128)(2,1)}), bf16[32,3,128,128]{3,2,1,0:T(8,128)(2,1)}, u32[]{:S(2)}, u32[]{:S(2)}) async-start(bf16[32,3,128,128]{3,2,1,0:T(8,128)(2,1)} %bitcast.32), calls=%async_computation.1 | async-start | bytes 6291456 | tf_op jit(solution)/shard_map/all_to_all | solution.py:220
  61.2 0.5 dynamic-slice_reduce_fusion.lengths
  61.8 0.1 iota_compare_fusion.4
  61.8 0.1 lt.98
  61.9 0.5 fusion.6
  62.4 0.1 shift_right_arithmetic.24
  62.5 0.1 copy.35
  62.6 0.1 fusion.1
  62.7 0.1 copy.34
  62.9 0.1 copy.36
  63.0 0.1 broadcast_select_fusion
  63.0 1.6 select_reduce_fusion.1
  64.6 0.1 reduce_sum.30
  64.7 0.1 fusion.5
  64.9 0.1 broadcast_in_dim.83
  65.0 0.5 add_select_fusion.places
  65.6 17.6 %value_terms.1 = (bf16[96,64,128]{2,1,0:T(8,128)(2,1)}, bf16[96,64,128]{2,1,0:T(8,128)(2,1)}) custom-call(s32[80]{0:T(128)} %add_select_fusion.places, s32[20]{0:T(128)} %copy-done.6, bf16[256,2560]{1,0:T(8,128)(2,1)} %bitcast.36, bf16[256,2560]{1,0:T(8,128)(2,1)} %bitcast.38, bf16[96,128,128]{2,1,0:T(8,128)(2,1)} %bitcast.30), custom_call_target="tpu_custom_call" | custom-call | tf_op jit(solution)/shard_map/value_terms/pallas_call | solution.py:249
  83.2 5.9 %collective-permute-start = (bf16[96,64,128]{2,1,0:T(8,128)(2,1)}, bf16[96,64,128]{2,1,0:T(8,128)(2,1)S(1)}, u32[]{:S(2)}, u32[]{:S(2)}) collective-permute-start(bf16[96,64,128]{2,1,0:T(8,128)(2,1)} %get-tuple-element.14), channel_id=1, source_target_pairs={{0,7},{1,0},{2,1},{3,2},{4,3},{5,4},{6,5},{7,6},{8,15},{9,8},{10,9... | collective-permute-start | bytes 4718600 | tf_op jit(solution)/shard_map/ppermute | solution.py:23
  89.1 11.7 %all-to-all-done.1 = bf16[32,3,128,128]{3,2,1,0:T(8,128)(2,1)} async-done(((bf16[32,3,128,128]{3,2,1,0:T(8,128)(2,1)}), bf16[32,3,128,128]{3,2,1,0:T(8,128)(2,1)}, u32[]{:S(2)}, u32[]{:S(2)}) %all-to-all-start.1) | async-done | bytes 3145760 | tf_op jit(solution)/shard_map/all_to_all | solution.py:220
  100.8 5.4 %all-to-all-start.3 = ((bf16[32,3,64,128]{3,2,1,0:T(8,128)(2,1)}), bf16[32,3,64,128]{3,2,1,0:T(8,128)(2,1)S(1)}, u32[]{:S(2)}, u32[]{:S(2)}) async-start(bf16[32,3,64,128]{3,2,1,0:T(8,128)(2,1)} %bitcast.42), calls=%async_computation.3 | async-start | bytes 3145728 | tf_op jit(solution)/shard_map/all_to_all | solution.py:220
  106.2 5.9 %collective-permute-start.1 = (s32[96]{0:T(128)S(1)}, s32[96]{0:T(128)S(1)}, u32[]{:S(2)}, u32[]{:S(2)}) collective-permute-start(s32[96]{0:T(128)S(1)} %copy-done.7), channel_id=1, source_target_pairs={{0,7},{1,0},{2,1},{3,2},{4,3},{5,4},{6,5},{7,6},{8,15},{9,8},{10,9... | collective-permute-start | bytes 1160 | tf_op jit(solution)/shard_map/ppermute | solution.py:23
  112.1 23.9 %key_terms.1 = (bf16[256,2560]{1,0:T(8,128)(2,1)}, bf16[96,128,128]{2,1,0:T(8,128)(2,1)}) custom-call(s32[80]{0:T(128)} %add_select_fusion.places, s32[20]{0:T(128)} %copy-done.6, bf16[256,2560]{1,0:T(8,128)(2,1)} %bitcast.37, bf16[256,2560]{1,0:T(8,128)(2,1)} %bitcast.39, bf16[96,128,128]{2,1,0:T(8,128)(2,1)} %bitcast.31, bf16[96,128,128]{2,1,0:T(8,128)(2,1)} %bitcast.11.values), custom_call_target="tpu_custom_call" | custom-call | tf_op jit(solution)/shard_map/key_terms/pallas_call | solution.py:259
  136.1 1.1 copy-done.3
  137.2 0.5 copy-done.2
  137.7 7.3 %all-to-all-start.2 = ((bf16[32,3,128,128]{3,2,1,0:T(8,128)(2,1)}), bf16[32,3,128,128]{3,2,1,0:T(8,128)(2,1)S(1)}, u32[]{:S(2)}, u32[]{:S(2)}) async-start(bf16[32,3,128,128]{3,2,1,0:T(8,128)(2,1)} %bitcast.40), calls=%async_computation.2 | async-start | bytes 6291456 | tf_op jit(solution)/shard_map/all_to_all | solution.py:220
  145.1 1.1 collective-permute-start.2
  146.2 3.7 %sum_values.1 = bf16[128,2560]{1,0:T(8,128)(2,1)} custom-call(s32[96]{0:T(128)} %reshape.173.codes, bf16[96,64,128]{2,1,0:T(8,128)(2,1)} %bitcast.35), custom_call_target="tpu_custom_call" | custom-call | tf_op jit(solution)/shard_map/sum_values/pallas_call | solution.py:237
  149.9 1.0 collective-permute-start.3
  150.9 33.7 %all-to-all-done.2 = bf16[32,3,128,128]{3,2,1,0:T(8,128)(2,1)S(1)} async-done(((bf16[32,3,128,128]{3,2,1,0:T(8,128)(2,1)}), bf16[32,3,128,128]{3,2,1,0:T(8,128)(2,1)S(1)}, u32[]{:S(2)}, u32[]{:S(2)}) %all-to-all-start.2) | async-done | bytes 3145760 | tf_op jit(solution)/shard_map/all_to_all | solution.py:220
  184.6 1.6 copy-done.1
  186.2 5.3 %all-to-all-start.4 = ((bf16[32,3,64,128]{3,2,1,0:T(8,128)(2,1)}), bf16[32,3,64,128]{3,2,1,0:T(8,128)(2,1)}, u32[]{:S(2)}, u32[]{:S(2)}) async-start(bf16[32,3,64,128]{3,2,1,0:T(8,128)(2,1)} %bitcast.41), calls=%async_computation.4 | async-start | bytes 3145728 | tf_op jit(solution)/shard_map/all_to_all | solution.py:220
  191.6 4.8 %sum_keys.1 = bf16[256,2560]{1,0:T(8,128)(2,1)} custom-call(s32[96]{0:T(128)} %reshape.173.codes, bf16[96,128,128]{2,1,0:T(8,128)(2,1)} %bitcast.33), custom_call_target="tpu_custom_call" | custom-call | tf_op jit(solution)/shard_map/sum_keys/pallas_call | solution.py:237
  196.3 1.0 collective-permute-start.4
  197.3 15.3 %all-to-all-done.4 = bf16[32,3,64,128]{3,2,1,0:T(8,128)(2,1)} async-done(((bf16[32,3,64,128]{3,2,1,0:T(8,128)(2,1)}), bf16[32,3,64,128]{3,2,1,0:T(8,128)(2,1)}, u32[]{:S(2)}, u32[]{:S(2)}) %all-to-all-start.4) | async-done | bytes 1572896 | tf_op jit(solution)/shard_map/all_to_all | solution.py:220
  212.6 4.2 %join_values.1 = bf16[256,2560]{1,0:T(8,128)(2,1)} custom-call(s32[96]{0:T(128)} %copy-done.8, bf16[128,2560]{1,0:T(8,128)(2,1)} %collective-permute-done.3.head_part, bf16[96,64,128]{2,1,0:T(8,128)(2,1)} %bitcast.19.terms), custom_call_target="tpu_custom_call" | custom-call | tf_op jit(solution)/shard_map/join_values/pallas_call | solution.py:279
  216.8 10.5 %collective-permute-done.4 = bf16[256,2560]{1,0:T(8,128)(2,1)S(1)} collective-permute-done((bf16[256,2560]{1,0:T(8,128)(2,1)}, bf16[256,2560]{1,0:T(8,128)(2,1)S(1)}, u32[]{:S(2)}, u32[]{:S(2)}) %collective-permute-start.4) | collective-permute-done | bytes 1310752 | tf_op jit(solution)/shard_map/ppermute | solution.py:23
  227.3 2.5 %copy.43 = bf16[1,256,2560]{2,1,0:T(8,128)(2,1)} copy(bf16[1,256,2560]{2,1,0:T(8,128)(2,1)} %bitcast.16) | data formatting | bytes 2621440
  229.7 1.1 copy.44
  (24 shorter events, 0.2 us)
Async XLA Ops:
  7.2 47.0 %all-to-all-start = ((bf16[32,3,128,128]{3,2,1,0:T(8,128)(2,1)}), bf16[32,3,128,128]{3,2,1,0:T(8,128)(2,1)S(1)}, u32[]{:S(2)}, u32[]{:S(2)}) async-start(bf16[32,3,128,128]{3,2,1,0:T(8,128)(2,1)} %bitcast.34), calls=%async_computation | async-start | bytes 6291456 | tf_op jit(solution)/shard_map/all_to_all | solution.py:220
  54.2 1.7 copy-start
  54.2 7.0 %copy-start.5 = (s32[1,32,20]{1,0,2:T(1,128)S(1)}, s32[1,32,20]{1,0,2:T(1,128)}, u32[]{:S(2)}) copy-start(s32[1,32,20]{1,0,2:T(1,128)} %param.11) | copy-start | bytes 7684
  54.2 7.7 %copy-start.4 = (s32[1,32,20,4]{1,3,2,0:T(4,128)S(1)}, s32[1,32,20,4]{1,3,2,0:T(4,128)}, u32[]{:S(2)}) copy-start(s32[1,32,20,4]{1,3,2,0:T(4,128)} %param.10) | copy-start | bytes 30724
  55.9 44.9 %all-to-all-start.1 = ((bf16[32,3,128,128]{3,2,1,0:T(8,128)(2,1)}), bf16[32,3,128,128]{3,2,1,0:T(8,128)(2,1)}, u32[]{:S(2)}, u32[]{:S(2)}) async-start(bf16[32,3,128,128]{3,2,1,0:T(8,128)(2,1)} %bitcast.32), calls=%async_computation.1 | async-start | bytes 6291456 | tf_op jit(solution)/shard_map/all_to_all | solution.py:220
  61.8 3.8 %copy-start.6 = (s32[20]{0:T(128)}, s32[20]{0:T(128)S(1)}, u32[]{:S(2)}) copy-start(s32[20]{0:T(128)S(1)} %dynamic-slice_reduce_fusion.lengths) | copy-start | bytes 244
  83.2 52.8 %collective-permute-start = (bf16[96,64,128]{2,1,0:T(8,128)(2,1)}, bf16[96,64,128]{2,1,0:T(8,128)(2,1)S(1)}, u32[]{:S(2)}, u32[]{:S(2)}) collective-permute-start(bf16[96,64,128]{2,1,0:T(8,128)(2,1)} %get-tuple-element.14), channel_id=1, source_target_pairs={{0,7},{1,0},{2,1},{3,2},{4,3},{5,4},{6,5},{7,6},{8,15},{9,8},{10,9... | collective-permute-start | bytes 4718600 | tf_op jit(solution)/shard_map/ppermute | solution.py:23
  100.8 5.4 %copy-start.7 = (s32[96]{0:T(128)S(1)}, s32[96]{0:T(128)}, u32[]{:S(2)}) copy-start(s32[96]{0:T(128)} %reshape.173.codes) | copy-start | bytes 1156
  100.8 35.3 %all-to-all-start.3 = ((bf16[32,3,64,128]{3,2,1,0:T(8,128)(2,1)}), bf16[32,3,64,128]{3,2,1,0:T(8,128)(2,1)S(1)}, u32[]{:S(2)}, u32[]{:S(2)}) async-start(bf16[32,3,64,128]{3,2,1,0:T(8,128)(2,1)} %bitcast.42), calls=%async_computation.3 | async-start | bytes 3145728 | tf_op jit(solution)/shard_map/all_to_all | solution.py:220
  106.2 29.9 %collective-permute-start.1 = (s32[96]{0:T(128)S(1)}, s32[96]{0:T(128)S(1)}, u32[]{:S(2)}, u32[]{:S(2)}) collective-permute-start(s32[96]{0:T(128)S(1)} %copy-done.7), channel_id=1, source_target_pairs={{0,7},{1,0},{2,1},{3,2},{4,3},{5,4},{6,5},{7,6},{8,15},{9,8},{10,9... | collective-permute-start | bytes 1160 | tf_op jit(solution)/shard_map/ppermute | solution.py:23
  136.0 1.7 copy-start.8
  136.0 1.2 copy-start.3
  136.1 1.7 copy-start.2
  137.7 46.8 %all-to-all-start.2 = ((bf16[32,3,128,128]{3,2,1,0:T(8,128)(2,1)}), bf16[32,3,128,128]{3,2,1,0:T(8,128)(2,1)S(1)}, u32[]{:S(2)}, u32[]{:S(2)}) async-start(bf16[32,3,128,128]{3,2,1,0:T(8,128)(2,1)} %bitcast.40), calls=%async_computation.2 | async-start | bytes 6291456 | tf_op jit(solution)/shard_map/all_to_all | solution.py:220
  145.1 46.5 %collective-permute-start.2 = (bf16[256,2560]{1,0:T(8,128)(2,1)}, bf16[256,2560]{1,0:T(8,128)(2,1)}, u32[]{:S(2)}, u32[]{:S(2)}) collective-permute-start(bf16[256,2560]{1,0:T(8,128)(2,1)} %get-tuple-element.16), channel_id=1, source_target_pairs={{0,7},{1,0},{2,1},{3,2},{4,3},{5,4},{6,5},{7,6},{8,15},{9,8},{10,9... | collective-permute-start | bytes 3932168 | tf_op jit(solution)/shard_map/ppermute | solution.py:23
  149.9 41.7 %collective-permute-start.3 = (bf16[128,2560]{1,0:T(8,128)(2,1)}, bf16[128,2560]{1,0:T(8,128)(2,1)}, u32[]{:S(2)}, u32[]{:S(2)}) collective-permute-start(bf16[128,2560]{1,0:T(8,128)(2,1)} %sum_values.1), channel_id=1, source_target_pairs={{0,7},{1,0},{2,1},{3,2},{4,3},{5,4},{6,5},{7,6},{8,15},{9,8},{10,9... | collective-permute-start | bytes 1966088 | tf_op jit(solution)/shard_map/ppermute | solution.py:23
  184.6 1.7 copy-start.1
  186.2 26.4 %all-to-all-start.4 = ((bf16[32,3,64,128]{3,2,1,0:T(8,128)(2,1)}), bf16[32,3,64,128]{3,2,1,0:T(8,128)(2,1)}, u32[]{:S(2)}, u32[]{:S(2)}) async-start(bf16[32,3,64,128]{3,2,1,0:T(8,128)(2,1)} %bitcast.41), calls=%async_computation.4 | async-start | bytes 3145728 | tf_op jit(solution)/shard_map/all_to_all | solution.py:220
  196.3 30.9 %collective-permute-start.4 = (bf16[256,2560]{1,0:T(8,128)(2,1)}, bf16[256,2560]{1,0:T(8,128)(2,1)S(1)}, u32[]{:S(2)}, u32[]{:S(2)}) collective-permute-start(bf16[256,2560]{1,0:T(8,128)(2,1)} %sum_keys.1), channel_id=1, source_target_pairs={{0,7},{1,0},{2,1},{3,2},{4,3},{5,4},{6,5},{7,6},{8,15},{9,8},{10,9... | collective-permute-start | bytes 3932168 | tf_op jit(solution)/shard_map/ppermute | solution.py:23

commit v3 on v2

v3 whole, which is shorter than its diff:
```python
import functools
import math

import jax
import jax.numpy as jnp
from jax import lax
from jax.experimental import pallas as pl
from jax.experimental.pallas import tpu as pltpu
from jax.sharding import PartitionSpec as P

HEAD_BITS = 8
VMEM = pl.BlockSpec(memory_space=pltpu.VMEM)
SMEM = pl.BlockSpec(memory_space=pltpu.SMEM)
ANY = pl.BlockSpec(memory_space=pl.ANY)
PARAMS = pltpu.CompilerParams(vmem_limit_bytes=56 * 1024 * 1024)
NT = (((1,), (1,)), ((), ()))
NN = (((1,), (0,)), ((), ()))
TN = (((0,), (0,)), ((), ()))
copy = pltpu.make_async_copy


def shifted(value, axis, steps):
    count = lax.axis_size(axis)
    pairs = [(source, (source + steps) % count) for source in range(count)]
    return lax.ppermute(value, axis, pairs)


def tile_of(code, rows, cols):
    block = lax.shift_right_logical(code, HEAD_BITS)
    head = lax.bitwise_and(code, (1 << HEAD_BITS) - 1)
    return (
        pl.ds(pl.multiple_of(block * rows, rows), rows),
        pl.ds(pl.multiple_of(head * cols, cols), cols),
    )


def pack_kernel(codes, source, packed):
    slots, rows, cols = packed.shape

    def one(slot, carry):
        packed[slot] = source[tile_of(jnp.maximum(codes[slot], 0), rows, cols)]
        return carry

    lax.fori_loop(0, slots, one, 0, unroll=4)


def add_slots(codes, terms, wide, first, count):
    rows, cols = terms.shape[1:]
    for item in range(count):
        slot = first + item
        code = codes[slot]
        code = jnp.where(code < 0, 2 << HEAD_BITS, code)
        wide[tile_of(code, rows, cols)] += terms[slot].astype(jnp.float32)


def add_terms(codes, terms, wide, parts):
    wide[...] = jnp.zeros_like(wide)
    step = terms.shape[0] // parts

    def one_part(part, carry):
        add_slots(codes, terms, wide, part * step, step)
        return carry

    lax.fori_loop(0, parts, one_part, 0)


def send_columns(ready, total, sent, parts, fill):
    width = total.shape[1] // parts
    copies = []
    for part in range(parts):
        columns = pl.ds(part * width, width)
        fill(columns)
        copies.append(copy(ready.at[:, columns], total.at[:, columns], sent.at[part]))
        copies[-1].start()
    for one in copies:
        one.wait()


def sum_kernel(parts, codes, terms, total, wide, ready, sent):
    add_terms(codes, terms, wide, parts)
    rows = total.shape[0]

    def fill(columns):
        ready[:, columns] = wide[:rows, columns].astype(ready.dtype)

    send_columns(ready, total, sent, sent.shape[0], fill)


def join_kernel(
    parts, codes, keys, head_part, terms, key_out, total, wide, ready, head, sent, got, put
):
    head_copy = copy(head_part, head, got)
    head_copy.start()
    key_copy = copy(keys, key_out, put)
    key_copy.start()
    add_terms(codes, terms, wide, parts)
    head_copy.wait()
    tail_rows = terms.shape[1]
    head_rows = total.shape[0] // 2 - tail_rows

    def fill(columns):
        for block in range(2):
            start = block * (head_rows + tail_rows)
            middle = start + head_rows
            ready[start:middle, columns] = head[
                block * head_rows : (block + 1) * head_rows, columns
            ]
            ready[middle : middle + tail_rows, columns] = wide[
                block * tail_rows : (block + 1) * tail_rows, columns
            ].astype(ready.dtype)

    send_columns(ready, total, sent, sent.shape[0], fill)
    key_copy.wait()


def place_kernel(source, out):
    out[...] = source[...]


def weights_of(query, key, length, list_size, scale):
    scores = lax.dot_general(key, query, NT, preferred_element_type=jnp.float32)
    row_max = jnp.max(scores, axis=0, keepdims=True)
    exp_scores = jnp.exp2((scores - row_max) * (scale * math.log2(math.e)))
    rows = key.shape[0] // list_size
    parts = [exp_scores[item * rows : (item + 1) * rows] for item in range(list_size)]
    kept = [jnp.where(item < length, 1.0, 0.0).astype(jnp.float32) for item in range(list_size)]
    total = sum(keep * jnp.sum(part, axis=0, keepdims=True) for keep, part in zip(kept, parts))
    inverse = 1.0 / total
    return [part * (inverse * keep) for keep, part in zip(kept, parts)]


class Grouped:
    def __init__(self, places, lengths, list_size, group, cols):
        self.places, self.lengths = places, lengths
        self.list_size, self.group, self.cols = list_size, group, cols
        self.groups = lengths.shape[0] // group

    def head(self, head):
        return pl.ds(pl.multiple_of(head * self.cols, self.cols), self.cols)

    def wide(self, index, source, held, sems):
        width = self.group * self.cols
        columns = pl.ds(pl.multiple_of(index * width, width), width)
        return copy(source.at[:, columns], held.at[:, columns], sems.at[index])

    def fetches(self, index, sources, tiles):
        made = [self.wide(index, *source) for source in sources]
        count = self.group * self.list_size
        for item in range(count):
            entry = index * count + item
            for source, held, sems in tiles:
                made.append(
                    copy(source.at[self.places[entry]], held.at[entry], sems.at[entry])
                )
        return made

    def puts(self, entry, made, outs, sems):
        start, copies = 0, []
        for which, out in enumerate(outs):
            count = out.shape[1]
            copies.append(
                copy(
                    made.at[entry, pl.ds(start, count)],
                    out.at[self.places[entry]],
                    sems.at[which, entry],
                )
            )
            start += count
        return copies

    def each_put(self, head, made, outs, sems, act):
        for item in range(self.list_size):

            @pl.when(item < self.lengths[head])
            def _():
                for one in self.puts(head * self.list_size + item, made, outs, sems):
                    act(one)

    def run(self, sources, tiles, made, outs, sems, compute, finish=None):
        def start(index):
            for one in self.fetches(index, sources, tiles):
                one.start()

        start(0)

        def one_group(index, carry):
            @pl.when(index + 1 < self.groups)
            def _():
                start(index + 1)

            for one in self.fetches(index, sources, tiles):
                one.wait()
            for item in range(self.group):
                head = index * self.group + item
                terms = compute(head)
                entries = pl.ds(head * self.list_size, self.list_size)
                made[entries] = terms.reshape(self.list_size, -1, self.cols)
                self.each_put(head, made, outs, sems, lambda one: one.start())
            if finish is not None:
                finish(index).start()
            return carry

        lax.fori_loop(0, self.groups, one_group, 0)

        def last(head, carry):
            self.each_put(head, made, outs, sems, lambda one: one.wait())
            return carry

        lax.fori_loop(0, self.lengths.shape[0], last, 0)
        if finish is not None:
            for index in range(self.groups):
                finish(index).wait()


def value_kernel(
    list_size, group, scale, places, lengths, queries, grads, keys, first, last,
    query_held, grad_held, key_held, made, query_sem, grad_sem, key_sem, out_sem,
):
    cols = keys.shape[2]
    walk = Grouped(places, lengths, list_size, group, cols)

    def compute(head):
        columns = walk.head(head)
        key = key_held[pl.ds(head * list_size, list_size)].reshape(-1, cols)
        weights = weights_of(query_held[:, columns], key, lengths[head], list_size, scale)
        weights_low = jnp.concatenate([part.astype(jnp.bfloat16) for part in weights], axis=0)
        return lax.dot_general(
            weights_low, grad_held[:, columns], NN, preferred_element_type=jnp.float32
        ).astype(jnp.bfloat16)

    walk.run(
        [(queries, query_held, query_sem), (grads, grad_held, grad_sem)],
        [(keys, key_held, key_sem)],
        made,
        [first, last],
        out_sem,
        compute,
    )


def key_kernel(
    list_size, group, scale, places, lengths, queries, grads, keys, values, query_grad, terms,
    query_held, grad_held, key_held, value_held, made, query_made,
    query_sem, grad_sem, key_sem, value_sem, out_sem, query_out_sem,
):
    rows, cols = keys.shape[1:]
    walk = Grouped(places, lengths, list_size, group, cols)

    def compute(head):
        columns = walk.head(head)
        entries = pl.ds(head * list_size, list_size)
        query = query_held[:, columns]
        key = key_held[entries].reshape(-1, cols)
        value = value_held[entries].reshape(-1, cols)
        weights = weights_of(query, key, lengths[head], list_size, scale)
        weights_low = [part.astype(jnp.bfloat16).astype(jnp.float32) for part in weights]
        joined = lax.dot_general(
            value, grad_held[:, columns], NT, preferred_element_type=jnp.float32
        )
        dweights = [joined[item * rows : (item + 1) * rows] for item in range(list_size)]
        row_delta = sum(
            jnp.sum(low * part, axis=0, keepdims=True)
            for low, part in zip(weights_low, dweights)
        )
        dscores = jnp.concatenate(
            [
                (weight * (part - row_delta)).astype(jnp.bfloat16)
                for weight, part in zip(weights, dweights)
            ],
            axis=0,
        )
        flipped = lax.dot_general(key, dscores, TN, preferred_element_type=jnp.float32)
        query_made[:, columns] = (flipped * scale).astype(jnp.bfloat16).T
        made_terms = lax.dot_general(dscores, query, NN, preferred_element_type=jnp.float32)
        return (made_terms * scale).astype(jnp.bfloat16)

    def finish(index):
        width = group * cols
        columns = pl.ds(pl.multiple_of(index * width, width), width)
        return copy(
            query_made.at[:, columns], query_grad.at[:, columns], query_out_sem.at[index]
        )

    walk.run(
        [(queries, query_held, query_sem), (grads, grad_held, grad_sem)],
        [(keys, key_held, key_sem), (values, value_held, value_sem)],
        made,
        [terms],
        out_sem,
        compute,
        finish,
    )


def local(queries, keys, values, out_grad, key_blocks, list_lengths):
    ctx_count = lax.axis_size("ctx")
    my_index = lax.axis_index("ctx")
    row_count, column_count = queries.shape[1:]
    head_count = list_lengths.shape[2]
    head_dim = column_count // head_count
    list_size = key_blocks.shape[3]
    block_rows = row_count // 2
    entries = head_count * list_size
    capacity = (entries + ctx_count - 1) // ctx_count
    slots = ctx_count * capacity
    scale = 1.0 / math.sqrt(head_dim)
    group = 4 if head_count % 4 == 0 else 1
    groups = head_count // group

    chosen = key_blocks[0]
    lengths = list_lengths[0]
    items = jnp.arange(list_size, dtype=jnp.int32)
    heads = jnp.arange(head_count, dtype=jnp.int32)
    is_used = items[None, None, :] < lengths[:, :, None]
    is_mine = is_used & ((chosen >> 1) == my_index)
    hit = jnp.sum(jnp.where(is_mine, 1 + (chosen & 1), 0), axis=2)
    rank = jnp.sum(
        jnp.where((heads[None, None, :] < heads[None, :, None]) & (hit[:, None, :] > 0), 1, 0),
        axis=2,
    )
    code = ((hit - 1) << HEAD_BITS) + heads[None, :]
    ranks = jnp.arange(capacity, dtype=jnp.int32)
    codes = jnp.max(
        jnp.where(
            (hit[:, None, :] > 0) & (rank[:, None, :] == ranks[None, :, None]),
            code[:, None, :],
            -1,
        ),
        axis=2,
    ).reshape(slots)

    my_lengths = lax.dynamic_index_in_dim(lengths, my_index, 0, keepdims=False)
    my_chosen = lax.dynamic_index_in_dim(chosen, my_index, 0, keepdims=False)
    my_used = items[None, :] < my_lengths[:, None]
    my_holder = jnp.where(my_used, my_chosen >> 1, -1)
    earlier = (heads[None, None, :, None] < heads[:, None, None, None]) & (
        my_holder[None, None, :, :] == my_holder[:, :, None, None]
    )
    my_rank = jnp.sum(jnp.where(earlier, 1, 0), axis=(2, 3))
    places = my_holder * capacity + my_rank
    places = jnp.where(my_used, places, places[:, :1]).reshape(entries)

    first_rows = block_rows // 2
    last_rows = block_rows - first_rows
    add_parts = 8 if slots % 8 == 0 else 1
    send_parts = 5 if head_count % 5 == 0 else 1
    flat_shape = jax.ShapeDtypeStruct((row_count, column_count), jnp.bfloat16)
    dma = pltpu.SemaphoreType.DMA

    def vmem(*shape):
        return pltpu.VMEM(shape, jnp.bfloat16)

    def packed_shape(rows):
        return jax.ShapeDtypeStruct((slots, rows, head_dim), jnp.bfloat16)

    def exchanged(packed):
        parts = packed.reshape(ctx_count, capacity, *packed.shape[1:])
        parts = lax.all_to_all(parts, "ctx", split_axis=0, concat_axis=0, tiled=True)
        return parts.reshape(packed.shape)

    def pack(name, source):
        return pl.pallas_call(
            pack_kernel,
            out_shape=packed_shape(block_rows),
            in_specs=[SMEM, VMEM],
            out_specs=VMEM,
            compiler_params=PARAMS,
            name=name,
        )(codes, source)

    def near(value):
        return pltpu.with_memory_space_constraint(value, pltpu.VMEM)

    def wide_sum(rows):
        return pltpu.VMEM((3 * rows, column_count), jnp.float32)

    def add_up(name, returned):
        rows = returned.shape[1]
        return pl.pallas_call(
            functools.partial(sum_kernel, add_parts),
            out_shape=jax.ShapeDtypeStruct((2 * rows, column_count), jnp.bfloat16),
            in_specs=[SMEM, VMEM],
            out_specs=ANY,
            scratch_shapes=[wide_sum(rows), vmem(2 * rows, column_count), dma((send_parts,))],
            compiler_params=PARAMS,
            name=name,
        )(codes, returned)

    flat = vmem(row_count, column_count)
    tiles = vmem(entries, block_rows, head_dim)
    wide_sem, tile_sem = dma((groups,)), dma((entries,))
    fetched_keys = exchanged(pack("pack_keys", keys[0]))
    handed_codes = shifted(codes, "section", -1)
    packed_values, handed_codes = lax.optimization_barrier(
        (pack("pack_values", values[0]), handed_codes)
    )
    fetched_values = exchanged(packed_values)
    first_terms, last_terms = pl.pallas_call(
        functools.partial(value_kernel, list_size, group, scale),
        out_shape=(packed_shape(first_rows), packed_shape(last_rows)),
        in_specs=[SMEM, SMEM, ANY, ANY, ANY],
        out_specs=(ANY, ANY),
        scratch_shapes=[flat, flat, tiles, tiles]
        + [wide_sem, wide_sem, tile_sem, dma((2, entries))],
        compiler_params=PARAMS,
        name="value_terms",
    )(places, my_lengths, queries[0], out_grad[0], fetched_keys)
    handed_terms = shifted(last_terms, "section", -1)
    query_grad, key_terms = pl.pallas_call(
        functools.partial(key_kernel, list_size, group, scale),
        out_shape=(flat_shape, packed_shape(block_rows)),
        in_specs=[SMEM, SMEM, ANY, ANY, ANY, ANY],
        out_specs=(ANY, ANY),
        scratch_shapes=[flat, flat, tiles, tiles, tiles, flat]
        + [wide_sem, wide_sem, tile_sem, tile_sem, dma((1, entries)), wide_sem],
        compiler_params=PARAMS,
        name="key_terms",
    )(places, my_lengths, queries[0], out_grad[0], fetched_keys, fetched_values)
    handed_queries = shifted(query_grad, "section", -1)
    first_values = add_up("sum_values", exchanged(first_terms))
    handed_first = shifted(first_values, "section", -1)
    key_terms, handed_terms = lax.optimization_barrier((key_terms, handed_terms))
    returned_keys = exchanged(key_terms)
    handed_queries = pl.pallas_call(
        place_kernel,
        out_shape=flat_shape,
        in_specs=[VMEM],
        out_specs=VMEM,
        compiler_params=PARAMS,
        name="place_queries",
    )(near(handed_queries))
    returned_keys, handed_queries, handed_first = lax.optimization_barrier(
        (returned_keys, handed_queries, handed_first)
    )
    key_grad = add_up("sum_keys", near(returned_keys))
    key_grad, handed_terms = lax.optimization_barrier((key_grad, handed_terms))
    handed_keys = shifted(key_grad, "section", -1)
    handed_keys, handed_values = pl.pallas_call(
        functools.partial(join_kernel, add_parts),
        out_shape=(flat_shape, flat_shape),
        in_specs=[SMEM, VMEM, ANY, VMEM],
        out_specs=(ANY, ANY),
        scratch_shapes=[wide_sum(last_rows), flat, vmem(2 * first_rows, column_count)]
        + [dma((send_parts,)), dma, dma],
        compiler_params=PARAMS,
        name="join_values",
    )(handed_codes, near(handed_keys), handed_first, near(exchanged(handed_terms)))
    return (handed_queries[None], handed_keys[None], handed_values[None])


def solution(mesh):
    placed = (
        P("section", "ctx", None),
        P("section", "ctx", None),
        P("section", "ctx", None),
        P("section", "ctx", None),
        P("section", None, None, None),
        P("section", None, None),
    )
    return jax.shard_map(
        local,
        mesh=mesh,
        in_specs=placed,
        out_specs=(P("section", "ctx", None), P("section", "ctx", None), P("section", "ctx", None)),
        check_vma=False,
    )
```

time: 232 us -> 231 us (level)
  Pallas kernels: 62.1 us -> 49 us
  waiting for transfers between devices: 107 us -> 116 us
  starting transfers between devices: 45.7 us -> 54.4 us
  local copies, waits for them, and re-layouts: 11.3 us -> 5.65 us
    ppermute x5, waiting for transfers between devices: 10.5 us -> 65.7 us  [shifted(): return lax.ppermute(value, axis, pairs)]
    all_to_all x5, waiting for transfers between devices: 96.3 us -> 50 us  [exchanged(): lax.all_to_all(parts, 'ctx', split_axis=0, concat_axis=0, tiled=True)]
    pallas_call x5 -> x6, Pallas kernels: 54.2 us -> 41 us  [the longest x1 18.4 us: local(): pl.pallas_call(functools.partial(key_kernel, list_size, group, scale), ou...]
    ppermute x5, starting transfers between devices: 14.8 us -> 22.6 us  [shifted(): return lax.ppermute(value, axis, pairs)]
    unnamed x21 -> x17, local copies, waits for them, and re-layouts: 9.24 us -> 3.57 us
  transfers between devices with their start and end apart: 10 -> 10, of which waited for: 5 -> 6; matrix products, arithmetic and copies ran while one was open for 2% -> 2% of each run, Pallas kernels for 25% -> 17%
where the time goes in v3:
time: 231 us; the launch traced here: 230 us
  waiting for transfers between devices  116 us (50%)
  starting transfers between devices  54.4 us (24%)
  Pallas kernels  49 us (21%)
  local copies, waits for them, and re-layouts  5.65 us (2%)
  other arithmetic  4 us (2%)
    ppermute x5, waiting for transfers between devices, shifted(): return lax.ppermute(value, axis, pairs)  65.7 us
    all_to_all x5, waiting for transfers between devices, exchanged(): lax.all_to_all(parts, 'ctx', split_axis=0, concat_axis=0, tiled=True)  50 us
    all_to_all x5, starting transfers between devices, exchanged(): lax.all_to_all(parts, 'ctx', split_axis=0, concat_axis=0, tiled=True)  31.8 us
    ppermute x5, starting transfers between devices, shifted(): return lax.ppermute(value, axis, pairs)  22.6 us
    pallas_call x1, Pallas kernels, local(): pl.pallas_call(functools.partial(key_kernel, list_size, group, scale), ou...  18.4 us
    pallas_call x1, Pallas kernels, local(): pl.pallas_call(functools.partial(value_kernel, list_size, group, scale),...  11.7 us
    pallas_call x2, Pallas kernels, pack(): pl.pallas_call(pack_kernel, out_shape=packed_shape(block_rows), in_specs=...  7.95 us
    pallas_call x2, Pallas kernels, add_up(): pl.pallas_call(functools.partial(sum_kernel, add_parts), out_shape=jax.Sh...  6.5 us
  transfers between devices with their start and end apart: 10, of which 6 were waited for; matrix products, arithmetic and copies ran while one was open for 2% of the time, Pallas kernels for 17%

profile of v3, /device:TPU:8, one launch (start us, length us, event | category | flops | bytes accessed | tf_op | source)
XLA Modules:
  0.0 229.8 jit_solution(15943277235184852274)
XLA Ops:
  0.7 0.7 copy.40
  1.4 0.8 fusion
  2.2 0.2 select_reduce_fusion
  2.4 0.1 copy.37
  2.5 0.7 reshape.173.codes
  3.2 4.0 %pack_keys.1 = bf16[96,128,128]{2,1,0:T(8,128)(2,1)} custom-call(s32[96]{0:T(128)} %reshape.173.codes, bf16[256,2560]{1,0:T(8,128)(2,1)} %bitcast.44), custom_call_target="tpu_custom_call" | custom-call | tf_op jit(solution)/shard_map/pack_keys/pallas_call | solution.py:362
  7.2 7.7 %all-to-all-start = ((bf16[32,3,128,128]{3,2,1,0:T(8,128)(2,1)}), bf16[32,3,128,128]{3,2,1,0:T(8,128)(2,1)S(1)}, u32[]{:S(2)}, u32[]{:S(2)}) async-start(bf16[32,3,128,128]{3,2,1,0:T(8,128)(2,1)} %bitcast.35), calls=%async_computation | async-start | bytes 6291456 | tf_op jit(solution)/shard_map/all_to_all | solution.py:358
  14.9 5.9 %collective-permute-start = (s32[96]{0:T(128)S(1)}, s32[96]{0:T(128)S(1)}, u32[]{:S(2)}, u32[]{:S(2)}) collective-permute-start(s32[96]{0:T(128)S(1)} %copy-done.6), channel_id=1, source_target_pairs={{0,7},{1,0},{2,1},{3,2},{4,3},{5,4},{6,5},{7,6},{8,15},{9,8},{10,9... | collective-permute-start | bytes 1160 | tf_op jit(solution)/shard_map/ppermute | solution.py:25
  20.8 4.0 %pack_values.1 = bf16[96,128,128]{2,1,0:T(8,128)(2,1)} custom-call(s32[96]{0:T(128)} %reshape.173.codes, bf16[256,2560]{1,0:T(8,128)(2,1)} %bitcast.45), custom_call_target="tpu_custom_call" | custom-call | tf_op jit(solution)/shard_map/pack_values/pallas_call | solution.py:362
  24.8 0.0 collective-permute-done.codes
  24.8 29.6 %all-to-all-done = bf16[32,3,128,128]{3,2,1,0:T(8,128)(2,1)S(1)} async-done(((bf16[32,3,128,128]{3,2,1,0:T(8,128)(2,1)}), bf16[32,3,128,128]{3,2,1,0:T(8,128)(2,1)S(1)}, u32[]{:S(2)}, u32[]{:S(2)}) %all-to-all-start) | async-done | bytes 3145760 | tf_op jit(solution)/shard_map/all_to_all | solution.py:358
  54.4 1.7 copy-done
  56.1 5.3 %all-to-all-start.1 = ((bf16[32,3,128,128]{3,2,1,0:T(8,128)(2,1)}), bf16[32,3,128,128]{3,2,1,0:T(8,128)(2,1)}, u32[]{:S(2)}, u32[]{:S(2)}) async-start(bf16[32,3,128,128]{3,2,1,0:T(8,128)(2,1)} %bitcast.34), calls=%async_computation.1 | async-start | bytes 6291456 | tf_op jit(solution)/shard_map/all_to_all | solution.py:358
  61.4 0.5 dynamic-slice_reduce_fusion.lengths
  61.9 0.1 iota_compare_fusion.4
  62.0 0.1 lt.98
  62.1 0.5 fusion.6
  62.6 0.1 shift_right_arithmetic.24
  62.7 0.1 copy.35
  62.8 0.1 fusion.1
  62.9 0.1 copy.34
  63.0 0.1 copy.36
  63.1 0.1 broadcast_select_fusion
  63.2 1.6 select_reduce_fusion.1
  64.8 0.1 reduce_sum.30
  64.9 0.1 fusion.5
  65.0 0.1 broadcast_in_dim.82
  65.1 0.1 broadcast_in_dim.83
  65.2 0.5 add_select_fusion.places
  65.7 11.7 %value_terms.1 = (bf16[96,64,128]{2,1,0:T(8,128)(2,1)}, bf16[96,64,128]{2,1,0:T(8,128)(2,1)}) custom-call(s32[80]{0:T(128)} %add_select_fusion.places, s32[20]{0:T(128)} %copy-done.5, bf16[256,2560]{1,0:T(8,128)(2,1)} %bitcast.37, bf16[256,2560]{1,0:T(8,128)(2,1)} %bitcast.39, bf16[96,128,128]{2,1,0:T(8,128)(2,1)} %bitcast.32), custom_call_target="tpu_custom_call" | custom-call | tf_op jit(solution)/shard_map/value_terms/pallas_call | solution.py:398
  77.4 5.7 %collective-permute-start.1 = (bf16[96,64,128]{2,1,0:T(8,128)(2,1)}, bf16[96,64,128]{2,1,0:T(8,128)(2,1)S(1)}, u32[]{:S(2)}, u32[]{:S(2)}) collective-permute-start(bf16[96,64,128]{2,1,0:T(8,128)(2,1)} %get-tuple-element.20), channel_id=1, source_target_pairs={{0,7},{1,0},{2,1},{3,2},{4,3},{5,4},{6,5},{7,6},{8,15},{9,8},{10,9... | collective-permute-start | bytes 4718600 | tf_op jit(solution)/shard_map/ppermute | solution.py:25
  83.1 17.8 %all-to-all-done.1 = bf16[32,3,128,128]{3,2,1,0:T(8,128)(2,1)} async-done(((bf16[32,3,128,128]{3,2,1,0:T(8,128)(2,1)}), bf16[32,3,128,128]{3,2,1,0:T(8,128)(2,1)}, u32[]{:S(2)}, u32[]{:S(2)}) %all-to-all-start.1) | async-done | bytes 3145760 | tf_op jit(solution)/shard_map/all_to_all | solution.py:358
  100.9 5.2 %all-to-all-start.3 = ((bf16[32,3,64,128]{3,2,1,0:T(8,128)(2,1)}), bf16[32,3,64,128]{3,2,1,0:T(8,128)(2,1)S(1)}, u32[]{:S(2)}, u32[]{:S(2)}) async-start(bf16[32,3,64,128]{3,2,1,0:T(8,128)(2,1)} %bitcast.43), calls=%async_computation.3 | async-start | bytes 3145728 | tf_op jit(solution)/shard_map/all_to_all | solution.py:358
  106.2 18.4 %key_terms.1 = (bf16[256,2560]{1,0:T(8,128)(2,1)}, bf16[96,128,128]{2,1,0:T(8,128)(2,1)}) custom-call(s32[80]{0:T(128)} %add_select_fusion.places, s32[20]{0:T(128)} %copy-done.5, bf16[256,2560]{1,0:T(8,128)(2,1)} %bitcast.38, bf16[256,2560]{1,0:T(8,128)(2,1)} %bitcast.40, bf16[96,128,128]{2,1,0:T(8,128)(2,1)} %bitcast.33, bf16[96,128,128]{2,1,0:T(8,128)(2,1)} %bitcast.11.values), custom_call_target="tpu_custom_call" | custom-call | tf_op jit(solution)/shard_map/key_terms/pallas_call | solution.py:409
  124.6 2.6 %all-to-all-done.3 = bf16[32,3,64,128]{3,2,1,0:T(8,128)(2,1)S(1)} async-done(((bf16[32,3,64,128]{3,2,1,0:T(8,128)(2,1)}), bf16[32,3,64,128]{3,2,1,0:T(8,128)(2,1)S(1)}, u32[]{:S(2)}, u32[]{:S(2)}) %all-to-all-start.3) | async-done | bytes 1572896 | tf_op jit(solution)/shard_map/all_to_all | solution.py:358
  127.2 1.2 copy-done.1
  128.4 6.0 %all-to-all-start.2 = ((bf16[32,3,128,128]{3,2,1,0:T(8,128)(2,1)}), bf16[32,3,128,128]{3,2,1,0:T(8,128)(2,1)S(1)}, u32[]{:S(2)}, u32[]{:S(2)}) async-start(bf16[32,3,128,128]{3,2,1,0:T(8,128)(2,1)} %bitcast.41), calls=%async_computation.2 | async-start | bytes 6291456 | tf_op jit(solution)/shard_map/all_to_all | solution.py:358
  134.4 5.9 %collective-permute-start.2 = (bf16[256,2560]{1,0:T(8,128)(2,1)}, bf16[256,2560]{1,0:T(8,128)(2,1)S(1)}, u32[]{:S(2)}, u32[]{:S(2)}) collective-permute-start(bf16[256,2560]{1,0:T(8,128)(2,1)} %get-tuple-element.22), channel_id=1, source_target_pairs={{0,7},{1,0},{2,1},{3,2},{4,3},{5,4},{6,5},{7,6},{8,15},{9,8},{10,9... | collective-permute-start | bytes 3932168 | tf_op jit(solution)/shard_map/ppermute | solution.py:25
  140.4 3.2 %sum_values.1 = bf16[128,2560]{1,0:T(8,128)(2,1)} custom-call(s32[96]{0:T(128)} %reshape.173.codes, bf16[96,64,128]{2,1,0:T(8,128)(2,1)} %bitcast.36), custom_call_target="tpu_custom_call" | custom-call | tf_op jit(solution)/shard_map/sum_values/pallas_call | solution.py:379
  143.6 1.3 collective-permute-start.3
  144.9 24.9 %collective-permute-done.2.source = bf16[256,2560]{1,0:T(8,128)(2,1)S(1)} collective-permute-done((bf16[256,2560]{1,0:T(8,128)(2,1)}, bf16[256,2560]{1,0:T(8,128)(2,1)S(1)}, u32[]{:S(2)}, u32[]{:S(2)}) %collective-permute-start.2) | collective-permute-done | bytes 1310752 | tf_op jit(solution)/shard_map/ppermute | solution.py:25
  169.8 1.1 place_queries.1
  171.0 12.1 %collective-permute-done.3.head_part = bf16[128,2560]{1,0:T(8,128)(2,1)} collective-permute-done((bf16[128,2560]{1,0:T(8,128)(2,1)}, bf16[128,2560]{1,0:T(8,128)(2,1)}, u32[]{:S(2)}, u32[]{:S(2)}) %collective-permute-start.3) | collective-permute-done | bytes 655392 | tf_op jit(solution)/shard_map/ppermute | solution.py:25
  183.1 3.3 %sum_keys.1 = bf16[256,2560]{1,0:T(8,128)(2,1)} custom-call(s32[96]{0:T(128)} %reshape.173.codes, bf16[96,128,128]{2,1,0:T(8,128)(2,1)S(1)} %bitcast.30), custom_call_target="tpu_custom_call" | custom-call | tf_op jit(solution)/shard_map/sum_keys/pallas_call | solution.py:379
  186.3 7.5 %all-to-all-start.4 = ((bf16[32,3,64,128]{3,2,1,0:T(8,128)(2,1)}), bf16[32,3,64,128]{3,2,1,0:T(8,128)(2,1)S(1)}, u32[]{:S(2)}, u32[]{:S(2)}) async-start(bf16[32,3,64,128]{3,2,1,0:T(8,128)(2,1)} %bitcast.42), calls=%async_computation.4 | async-start | bytes 3145728 | tf_op jit(solution)/shard_map/all_to_all | solution.py:358
  193.8 3.8 %collective-permute-start.4 = (bf16[256,2560]{1,0:T(8,128)(2,1)}, bf16[256,2560]{1,0:T(8,128)(2,1)S(1)}, u32[]{:S(2)}, u32[]{:S(2)}) collective-permute-start(bf16[256,2560]{1,0:T(8,128)(2,1)} %sum_keys.1), channel_id=1, source_target_pairs={{0,7},{1,0},{2,1},{3,2},{4,3},{5,4},{6,5},{7,6},{8,15},{9,8},{10,9... | collective-permute-start | bytes 3932168 | tf_op jit(solution)/shard_map/ppermute | solution.py:25
  197.6 28.7 %collective-permute-done.4.keys = bf16[256,2560]{1,0:T(8,128)(2,1)S(1)} collective-permute-done((bf16[256,2560]{1,0:T(8,128)(2,1)}, bf16[256,2560]{1,0:T(8,128)(2,1)S(1)}, u32[]{:S(2)}, u32[]{:S(2)}) %collective-permute-start.4) | collective-permute-done | bytes 1310752 | tf_op jit(solution)/shard_map/ppermute | solution.py:25
  226.3 3.3 %join_values.1 = (bf16[256,2560]{1,0:T(8,128)(2,1)}, bf16[256,2560]{1,0:T(8,128)(2,1)}) custom-call(s32[96]{0:T(128)} %copy-done.7, bf16[256,2560]{1,0:T(8,128)(2,1)S(1)} %collective-permute-done.4.keys, bf16[128,2560]{1,0:T(8,128)(2,1)} %collective-permute-done.3.head_part, bf16[96,64,128]{2,1,0:T(8,128)(2,1)S(1)} %bitcast.31), custom_call_target="tpu_custom_call" | custom-call | tf_op jit(solution)/shard_map/join_values/pallas_call | solution.py:438
  (21 shorter events, 0.1 us)
Async XLA Ops:
  7.2 7.7 %copy-start.6 = (s32[96]{0:T(128)S(1)}, s32[96]{0:T(128)}, u32[]{:S(2)}) copy-start(s32[96]{0:T(128)} %reshape.173.codes) | copy-start | bytes 1156
  7.2 47.2 %all-to-all-start = ((bf16[32,3,128,128]{3,2,1,0:T(8,128)(2,1)}), bf16[32,3,128,128]{3,2,1,0:T(8,128)(2,1)S(1)}, u32[]{:S(2)}, u32[]{:S(2)}) async-start(bf16[32,3,128,128]{3,2,1,0:T(8,128)(2,1)} %bitcast.35), calls=%async_computation | async-start | bytes 6291456 | tf_op jit(solution)/shard_map/all_to_all | solution.py:358
  14.9 9.9 %collective-permute-start = (s32[96]{0:T(128)S(1)}, s32[96]{0:T(128)S(1)}, u32[]{:S(2)}, u32[]{:S(2)}) collective-permute-start(s32[96]{0:T(128)S(1)} %copy-done.6), channel_id=1, source_target_pairs={{0,7},{1,0},{2,1},{3,2},{4,3},{5,4},{6,5},{7,6},{8,15},{9,8},{10,9... | collective-permute-start | bytes 1160 | tf_op jit(solution)/shard_map/ppermute | solution.py:25
  24.8 29.6 %copy-start.7 = (s32[96]{0:T(128)}, s32[96]{0:T(128)S(1)}, u32[]{:S(2)}) copy-start(s32[96]{0:T(128)S(1)} %collective-permute-done.codes) | copy-start | bytes 1156
  54.4 1.7 copy-start
  54.4 7.0 %copy-start.4 = (s32[1,32,20]{1,0,2:T(1,128)S(1)}, s32[1,32,20]{1,0,2:T(1,128)}, u32[]{:S(2)}) copy-start(s32[1,32,20]{1,0,2:T(1,128)} %param.11) | copy-start | bytes 7684
  54.4 7.7 %copy-start.3 = (s32[1,32,20,4]{1,3,2,0:T(4,128)S(1)}, s32[1,32,20,4]{1,3,2,0:T(4,128)}, u32[]{:S(2)}) copy-start(s32[1,32,20,4]{1,3,2,0:T(4,128)} %param.10) | copy-start | bytes 30724
  56.1 44.9 %all-to-all-start.1 = ((bf16[32,3,128,128]{3,2,1,0:T(8,128)(2,1)}), bf16[32,3,128,128]{3,2,1,0:T(8,128)(2,1)}, u32[]{:S(2)}, u32[]{:S(2)}) async-start(bf16[32,3,128,128]{3,2,1,0:T(8,128)(2,1)} %bitcast.34), calls=%async_computation.1 | async-start | bytes 6291456 | tf_op jit(solution)/shard_map/all_to_all | solution.py:358
  61.9 3.8 %copy-start.5 = (s32[20]{0:T(128)}, s32[20]{0:T(128)S(1)}, u32[]{:S(2)}) copy-start(s32[20]{0:T(128)S(1)} %dynamic-slice_reduce_fusion.lengths) | copy-start | bytes 244
  77.4 47.2 %collective-permute-start.1 = (bf16[96,64,128]{2,1,0:T(8,128)(2,1)}, bf16[96,64,128]{2,1,0:T(8,128)(2,1)S(1)}, u32[]{:S(2)}, u32[]{:S(2)}) collective-permute-start(bf16[96,64,128]{2,1,0:T(8,128)(2,1)} %get-tuple-element.20), channel_id=1, source_target_pairs={{0,7},{1,0},{2,1},{3,2},{4,3},{5,4},{6,5},{7,6},{8,15},{9,8},{10,9... | collective-permute-start | bytes 4718600 | tf_op jit(solution)/shard_map/ppermute | solution.py:25
  100.9 26.3 %all-to-all-start.3 = ((bf16[32,3,64,128]{3,2,1,0:T(8,128)(2,1)}), bf16[32,3,64,128]{3,2,1,0:T(8,128)(2,1)S(1)}, u32[]{:S(2)}, u32[]{:S(2)}) async-start(bf16[32,3,64,128]{3,2,1,0:T(8,128)(2,1)} %bitcast.43), calls=%async_computation.3 | async-start | bytes 3145728 | tf_op jit(solution)/shard_map/all_to_all | solution.py:358
  124.6 2.7 %copy-start.2 = (bf16[96,64,128]{2,1,0:T(8,128)(2,1)}, bf16[96,64,128]{2,1,0:T(8,128)(2,1)S(1)}, u32[]{:S(2)}) copy-start(bf16[96,64,128]{2,1,0:T(8,128)(2,1)S(1)} %collective-permute-done.1) | copy-start | bytes 4718596
  127.2 1.2 copy-start.1
  128.4 54.7 %all-to-all-start.2 = ((bf16[32,3,128,128]{3,2,1,0:T(8,128)(2,1)}), bf16[32,3,128,128]{3,2,1,0:T(8,128)(2,1)S(1)}, u32[]{:S(2)}, u32[]{:S(2)}) async-start(bf16[32,3,128,128]{3,2,1,0:T(8,128)(2,1)} %bitcast.41), calls=%async_computation.2 | async-start | bytes 6291456 | tf_op jit(solution)/shard_map/all_to_all | solution.py:358
  134.4 35.4 %collective-permute-start.2 = (bf16[256,2560]{1,0:T(8,128)(2,1)}, bf16[256,2560]{1,0:T(8,128)(2,1)S(1)}, u32[]{:S(2)}, u32[]{:S(2)}) collective-permute-start(bf16[256,2560]{1,0:T(8,128)(2,1)} %get-tuple-element.22), channel_id=1, source_target_pairs={{0,7},{1,0},{2,1},{3,2},{4,3},{5,4},{6,5},{7,6},{8,15},{9,8},{10,9... | collective-permute-start | bytes 3932168 | tf_op jit(solution)/shard_map/ppermute | solution.py:25
  143.6 39.5 %collective-permute-start.3 = (bf16[128,2560]{1,0:T(8,128)(2,1)}, bf16[128,2560]{1,0:T(8,128)(2,1)}, u32[]{:S(2)}, u32[]{:S(2)}) collective-permute-start(bf16[128,2560]{1,0:T(8,128)(2,1)} %sum_values.1), channel_id=1, source_target_pairs={{0,7},{1,0},{2,1},{3,2},{4,3},{5,4},{6,5},{7,6},{8,15},{9,8},{10,9... | collective-permute-start | bytes 1966088 | tf_op jit(solution)/shard_map/ppermute | solution.py:25
  186.3 39.9 %all-to-all-start.4 = ((bf16[32,3,64,128]{3,2,1,0:T(8,128)(2,1)}), bf16[32,3,64,128]{3,2,1,0:T(8,128)(2,1)S(1)}, u32[]{:S(2)}, u32[]{:S(2)}) async-start(bf16[32,3,64,128]{3,2,1,0:T(8,128)(2,1)} %bitcast.42), calls=%async_computation.4 | async-start | bytes 3145728 | tf_op jit(solution)/shard_map/all_to_all | solution.py:358
  193.8 32.4 %collective-permute-start.4 = (bf16[256,2560]{1,0:T(8,128)(2,1)}, bf16[256,2560]{1,0:T(8,128)(2,1)S(1)}, u32[]{:S(2)}, u32[]{:S(2)}) collective-permute-start(bf16[256,2560]{1,0:T(8,128)(2,1)} %sum_keys.1), channel_id=1, source_target_pairs={{0,7},{1,0},{2,1},{3,2},{4,3},{5,4},{6,5},{7,6},{8,15},{9,8},{10,9... | collective-permute-start | bytes 3932168 | tf_op jit(solution)/shard_map/ppermute | solution.py:25

commit v4 on v3

--- a/solution.py
+++ b/solution.py
@@ -34,14 +34,27 @@
     )
 
 
-def pack_kernel(codes, source, packed):
+def pack_kernel(parts, codes, source, packed, held, made, got, sent):
     slots, rows, cols = packed.shape
-
-    def one(slot, carry):
-        packed[slot] = source[tile_of(jnp.maximum(codes[slot], 0), rows, cols)]
+    step = slots // parts
+    whole = copy(source, held, got)
+    whole.start()
+    whole.wait()
+
+    def part_of(part):
+        where = pl.ds(part * step, step)
+        return copy(made.at[where], packed.at[where], sent.at[part])
+
+    def one_part(part, carry):
+        for item in range(step):
+            slot = part * step + item
+            made[slot] = held[tile_of(jnp.maximum(codes[slot], 0), rows, cols)]
+        part_of(part).start()
         return carry
 
-    lax.fori_loop(0, slots, one, 0, unroll=4)
+    lax.fori_loop(0, parts, one_part, 0)
+    for part in range(parts):
+        part_of(part).wait()
 
 
 def add_slots(codes, terms, wide, first, count):
@@ -87,13 +100,17 @@
 
 
 def join_kernel(
-    parts, codes, keys, head_part, terms, key_out, total, wide, ready, head, sent, got, put
+    parts, codes, keys, head_part, terms, key_out, total,
+    wide, ready, head, key_held, sent, got, key_got, put,
 ):
     head_copy = copy(head_part, head, got)
     head_copy.start()
-    key_copy = copy(keys, key_out, put)
+    key_in = copy(keys, key_held, key_got)
+    key_in.start()
+    add_terms(codes, terms, wide, parts)
+    key_in.wait()
+    key_copy = copy(key_held, key_out, put)
     key_copy.start()
-    add_terms(codes, terms, wide, parts)
     head_copy.wait()
     tail_rows = terms.shape[1]
     head_rows = total.shape[0] // 2 - tail_rows
@@ -143,8 +160,13 @@
         columns = pl.ds(pl.multiple_of(index * width, width), width)
         return copy(source.at[:, columns], held.at[:, columns], sems.at[index])
 
-    def fetches(self, index, sources, tiles):
+    def block(self, index, source, held, sems):
+        where = pl.ds(index * self.group, self.group)
+        return copy(source.at[where], held.at[where], sems.at[index])
+
+    def fetches(self, index, sources, tiles, blocks):
         made = [self.wide(index, *source) for source in sources]
+        made += [self.block(index, *source) for source in blocks]
         count = self.group * self.list_size
         for item in range(count):
             entry = index * count + item
@@ -176,9 +198,9 @@
                 for one in self.puts(head * self.list_size + item, made, outs, sems):
                     act(one)
 
-    def run(self, sources, tiles, made, outs, sems, compute, finish=None):
+    def run(self, sources, tiles, blocks, made, outs, sems, compute, finish):
         def start(index):
-            for one in self.fetches(index, sources, tiles):
+            for one in self.fetches(index, sources, tiles, blocks):
                 one.start()
 
         start(0)
@@ -188,7 +210,7 @@
             def _():
                 start(index + 1)
 
-            for one in self.fetches(index, sources, tiles):
+            for one in self.fetches(index, sources, tiles, blocks):
                 one.wait()
             for item in range(self.group):
                 head = index * self.group + item
@@ -196,8 +218,7 @@
                 entries = pl.ds(head * self.list_size, self.list_size)
                 made[entries] = terms.reshape(self.list_size, -1, self.cols)
                 self.each_put(head, made, outs, sems, lambda one: one.start())
-            if finish is not None:
-                finish(index).start()
+            finish(index).start()
             return carry
 
         lax.fori_loop(0, self.groups, one_group, 0)
@@ -207,22 +228,24 @@
             return carry
 
         lax.fori_loop(0, self.lengths.shape[0], last, 0)
-        if finish is not None:
-            for index in range(self.groups):
-                finish(index).wait()
+        for index in range(self.groups):
+            finish(index).wait()
 
 
 def value_kernel(
-    list_size, group, scale, places, lengths, queries, grads, keys, first, last,
-    query_held, grad_held, key_held, made, query_sem, grad_sem, key_sem, out_sem,
+    list_size, group, scale, places, lengths, queries, grads, keys, first, last, weights_out,
+    query_held, grad_held, key_held, made, weights_made,
+    query_sem, grad_sem, key_sem, out_sem, weights_sem,
 ):
-    cols = keys.shape[2]
+    rows, cols = keys.shape[1:]
     walk = Grouped(places, lengths, list_size, group, cols)
 
     def compute(head):
         columns = walk.head(head)
         key = key_held[pl.ds(head * list_size, list_size)].reshape(-1, cols)
         weights = weights_of(query_held[:, columns], key, lengths[head], list_size, scale)
+        for item, part in enumerate(weights):
+            weights_made[head, item * rows : (item + 1) * rows] = part
         weights_low = jnp.concatenate([part.astype(jnp.bfloat16) for part in weights], axis=0)
         return lax.dot_general(
             weights_low, grad_held[:, columns], NN, preferred_element_type=jnp.float32
@@ -231,64 +254,52 @@
     walk.run(
         [(queries, query_held, query_sem), (grads, grad_held, grad_sem)],
         [(keys, key_held, key_sem)],
+        [],
         made,
         [first, last],
         out_sem,
         compute,
+        lambda index: walk.block(index, weights_made, weights_out, weights_sem),
     )
 
 
 def key_kernel(
-    list_size, group, scale, places, lengths, queries, grads, keys, values, query_grad, terms,
-    query_held, grad_held, key_held, value_held, made, query_made,
-    query_sem, grad_sem, key_sem, value_sem, out_sem, query_out_sem,
+    list_size, group, scale, places, lengths, queries, grads, keys, values, weights,
+    query_grad, terms,
+    query_held, grad_held, key_held, value_held, weights_held, made, query_made,
+    query_sem, grad_sem, key_sem, value_sem, weights_sem, out_sem, query_out_sem,
 ):
-    rows, cols = keys.shape[1:]
+    cols = keys.shape[2]
     walk = Grouped(places, lengths, list_size, group, cols)
 
     def compute(head):
         columns = walk.head(head)
         entries = pl.ds(head * list_size, list_size)
-        query = query_held[:, columns]
         key = key_held[entries].reshape(-1, cols)
         value = value_held[entries].reshape(-1, cols)
-        weights = weights_of(query, key, lengths[head], list_size, scale)
-        weights_low = [part.astype(jnp.bfloat16).astype(jnp.float32) for part in weights]
-        joined = lax.dot_general(
+        weight = weights_held[head]
+        weight_low = weight.astype(jnp.bfloat16).astype(jnp.float32)
+        dweights = lax.dot_general(
             value, grad_held[:, columns], NT, preferred_element_type=jnp.float32
         )
-        dweights = [joined[item * rows : (item + 1) * rows] for item in range(list_size)]
-        row_delta = sum(
-            jnp.sum(low * part, axis=0, keepdims=True)
-            for low, part in zip(weights_low, dweights)
-        )
-        dscores = jnp.concatenate(
-            [
-                (weight * (part - row_delta)).astype(jnp.bfloat16)
-                for weight, part in zip(weights, dweights)
-            ],
-            axis=0,
-        )
+        row_delta = jnp.sum(weight_low * dweights, axis=0, keepdims=True)
+        dscores = (weight * (dweights - row_delta)).astype(jnp.bfloat16)
         flipped = lax.dot_general(key, dscores, TN, preferred_element_type=jnp.float32)
         query_made[:, columns] = (flipped * scale).astype(jnp.bfloat16).T
-        made_terms = lax.dot_general(dscores, query, NN, preferred_element_type=jnp.float32)
+        made_terms = lax.dot_general(
+            dscores, query_held[:, columns], NN, preferred_element_type=jnp.float32
+        )
         return (made_terms * scale).astype(jnp.bfloat16)
-
-    def finish(index):
-        width = group * cols
-        columns = pl.ds(pl.multiple_of(index * width, width), width)
-        return copy(
-            query_made.at[:, columns], query_grad.at[:, columns], query_out_sem.at[index]
-        )
 
     walk.run(
         [(queries, query_held, query_sem), (grads, grad_held, grad_sem)],
         [(keys, key_held, key_sem), (values, value_held, value_sem)],
+        [(weights, weights_held, weights_sem)],
         made,
         [terms],
         out_sem,
         compute,
-        finish,
+        lambda index: walk.wide(index, query_made, query_grad, query_out_sem),
     )
 
 
@@ -340,7 +351,7 @@
     places = my_holder * capacity + my_rank
     places = jnp.where(my_used, places, places[:, :1]).reshape(entries)
 
-    first_rows = block_rows // 2
+    first_rows = 3 * block_rows // 8
     last_rows = block_rows - first_rows
     add_parts = 8 if slots % 8 == 0 else 1
     send_parts = 5 if head_count % 5 == 0 else 1
@@ -350,6 +361,8 @@
     def vmem(*shape):
         return pltpu.VMEM(shape, jnp.bfloat16)
 
+    flat = vmem(row_count, column_count)
+
     def packed_shape(rows):
         return jax.ShapeDtypeStruct((slots, rows, head_dim), jnp.bfloat16)
 
@@ -360,10 +373,11 @@
 
     def pack(name, source):
         return pl.pallas_call(
-            pack_kernel,
+            functools.partial(pack_kernel, add_parts),
             out_shape=packed_shape(block_rows),
-            in_specs=[SMEM, VMEM],
-            out_specs=VMEM,
+            in_specs=[SMEM, ANY],
+            out_specs=ANY,
+            scratch_shapes=[flat, vmem(slots, block_rows, head_dim), dma, dma((add_parts,))],
             compiler_params=PARAMS,
             name=name,
         )(codes, source)
@@ -386,7 +400,6 @@
             name=name,
         )(codes, returned)
 
-    flat = vmem(row_count, column_count)
     tiles = vmem(entries, block_rows, head_dim)
     wide_sem, tile_sem = dma((groups,)), dma((entries,))
     fetched_keys = exchanged(pack("pack_keys", keys[0]))
@@ -395,13 +408,19 @@
         (pack("pack_values", values[0]), handed_codes)
     )
     fetched_values = exchanged(packed_values)
-    first_terms, last_terms = pl.pallas_call(
+    weights_shape = (head_count, list_size * block_rows, row_count)
+    weights_tile = pltpu.VMEM(weights_shape, jnp.float32)
+    first_terms, last_terms, weights = pl.pallas_call(
         functools.partial(value_kernel, list_size, group, scale),
-        out_shape=(packed_shape(first_rows), packed_shape(last_rows)),
+        out_shape=(
+            packed_shape(first_rows),
+            packed_shape(last_rows),
+            jax.ShapeDtypeStruct(weights_shape, jnp.float32),
+        ),
         in_specs=[SMEM, SMEM, ANY, ANY, ANY],
-        out_specs=(ANY, ANY),
-        scratch_shapes=[flat, flat, tiles, tiles]
-        + [wide_sem, wide_sem, tile_sem, dma((2, entries))],
+        out_specs=(ANY, ANY, ANY),
+        scratch_shapes=[flat, flat, tiles, tiles, weights_tile]
+        + [wide_sem, wide_sem, tile_sem, dma((2, entries)), wide_sem],
         compiler_params=PARAMS,
         name="value_terms",
     )(places, my_lengths, queries[0], out_grad[0], fetched_keys)
@@ -409,13 +428,13 @@
     query_grad, key_terms = pl.pallas_call(
         functools.partial(key_kernel, list_size, group, scale),
         out_shape=(flat_shape, packed_shape(block_rows)),
-        in_specs=[SMEM, SMEM, ANY, ANY, ANY, ANY],
+        in_specs=[SMEM, SMEM, ANY, ANY, ANY, ANY, ANY],
         out_specs=(ANY, ANY),
-        scratch_shapes=[flat, flat, tiles, tiles, tiles, flat]
-        + [wide_sem, wide_sem, tile_sem, tile_sem, dma((1, entries)), wide_sem],
+        scratch_shapes=[flat, flat, tiles, tiles, weights_tile, tiles, flat]
+        + [wide_sem, wide_sem, tile_sem, tile_sem, wide_sem, dma((1, entries)), wide_sem],
         compiler_params=PARAMS,
         name="key_terms",
-    )(places, my_lengths, queries[0], out_grad[0], fetched_keys, fetched_values)
+    )(places, my_lengths, queries[0], out_grad[0], fetched_keys, fetched_values, weights)
     handed_queries = shifted(query_grad, "section", -1)
     first_values = add_up("sum_values", exchanged(first_terms))
     handed_first = shifted(first_values, "section", -1)
@@ -438,13 +457,13 @@
     handed_keys, handed_values = pl.pallas_call(
         functools.partial(join_kernel, add_parts),
         out_shape=(flat_shape, flat_shape),
-        in_specs=[SMEM, VMEM, ANY, VMEM],
+        in_specs=[SMEM, ANY, ANY, VMEM],
         out_specs=(ANY, ANY),
-        scratch_shapes=[wide_sum(last_rows), flat, vmem(2 * first_rows, column_count)]
-        + [dma((send_parts,)), dma, dma],
+        scratch_shapes=[wide_sum(last_rows), flat, vmem(2 * first_rows, column_count), flat]
+        + [dma((send_parts,)), dma, dma, dma],
         compiler_params=PARAMS,
         name="join_values",
-    )(handed_codes, near(handed_keys), handed_first, near(exchanged(handed_terms)))
+    )(handed_codes, handed_keys, handed_first, near(exchanged(handed_terms)))
     return (handed_queries[None], handed_keys[None], handed_values[None])
 
 

time: 231 us -> 227 us (0.983)
    all_to_all x5, waiting for transfers between devices: 50 us -> 45.4 us  [exchanged(): lax.all_to_all(parts, 'ctx', split_axis=0, concat_axis=0, tiled=True)]
    ppermute x5, starting transfers between devices: 22.6 us -> 19.4 us  [shifted(): return lax.ppermute(value, axis, pairs)]
    ppermute x5, waiting for transfers between devices: 65.7 us -> 68.9 us  [shifted(): return lax.ppermute(value, axis, pairs)]
where the time goes in v4:
time: 227 us; the launch traced here: 226 us
  waiting for transfers between devices  114 us (50%)
  starting transfers between devices  52.4 us (23%)
  Pallas kernels  48.2 us (21%)
  local copies, waits for them, and re-layouts  6.1 us (3%)
  other arithmetic  4 us (2%)
    ppermute x5, waiting for transfers between devices, shifted(): return lax.ppermute(value, axis, pairs)  68.9 us
    all_to_all x5, waiting for transfers between devices, exchanged(): lax.all_to_all(parts, 'ctx', split_axis=0, concat_axis=0, tiled=True)  45.4 us
    all_to_all x5, starting transfers between devices, exchanged(): lax.all_to_all(parts, 'ctx', split_axis=0, concat_axis=0, tiled=True)  33 us
    ppermute x5, starting transfers between devices, shifted(): return lax.ppermute(value, axis, pairs)  19.4 us
    pallas_call x1, Pallas kernels, local(): pl.pallas_call(functools.partial(key_kernel, list_size, group, scale), ou...  16.1 us
    pallas_call x1, Pallas kernels, local(): pl.pallas_call(functools.partial(value_kernel, list_size, group, scale),...  13.5 us
    pallas_call x2, Pallas kernels, pack(): pl.pallas_call(functools.partial(pack_kernel, add_parts), out_shape=packe...  7.69 us
    pallas_call x2, Pallas kernels, add_up(): pl.pallas_call(functools.partial(sum_kernel, add_parts), out_shape=jax.Sh...  6.19 us
  transfers between devices with their start and end apart: 10, of which 6 were waited for; matrix products, arithmetic and copies ran while one was open for 2% of the time, Pallas kernels for 17%

profile of v4, /device:TPU:8, one launch (start us, length us, event | category | flops | bytes accessed | tf_op | source)
XLA Modules:
  0.0 226.0 jit_solution(12779727146992097700)
XLA Ops:
  0.7 0.7 copy.40
  1.4 0.8 fusion
  2.2 0.2 select_reduce_fusion
  2.4 0.1 copy.37
  2.5 0.7 reshape.173.codes
  3.2 3.8 %pack_keys.1 = bf16[96,128,128]{2,1,0:T(8,128)(2,1)} custom-call(s32[96]{0:T(128)} %reshape.173.codes, bf16[256,2560]{1,0:T(8,128)(2,1)} %bitcast.43), custom_call_target="tpu_custom_call" | custom-call | tf_op jit(solution)/shard_map/pack_keys/pallas_call | solution.py:375
  7.0 7.5 %all-to-all-start = ((bf16[32,3,128,128]{3,2,1,0:T(8,128)(2,1)}), bf16[32,3,128,128]{3,2,1,0:T(8,128)(2,1)S(1)}, u32[]{:S(2)}, u32[]{:S(2)}) async-start(bf16[32,3,128,128]{3,2,1,0:T(8,128)(2,1)} %bitcast.35), calls=%async_computation | async-start | bytes 6291456 | tf_op jit(solution)/shard_map/all_to_all | solution.py:371
  14.6 5.9 %collective-permute-start = (s32[96]{0:T(128)S(1)}, s32[96]{0:T(128)S(1)}, u32[]{:S(2)}, u32[]{:S(2)}) collective-permute-start(s32[96]{0:T(128)S(1)} %copy-done.7), channel_id=1, source_target_pairs={{0,7},{1,0},{2,1},{3,2},{4,3},{5,4},{6,5},{7,6},{8,15},{9,8},{10,9... | collective-permute-start | bytes 1160 | tf_op jit(solution)/shard_map/ppermute | solution.py:25
  20.5 3.9 %pack_values.1 = bf16[96,128,128]{2,1,0:T(8,128)(2,1)} custom-call(s32[96]{0:T(128)} %reshape.173.codes, bf16[256,2560]{1,0:T(8,128)(2,1)} %bitcast.44), custom_call_target="tpu_custom_call" | custom-call | tf_op jit(solution)/shard_map/pack_values/pallas_call | solution.py:375
  24.4 29.6 %all-to-all-done = bf16[32,3,128,128]{3,2,1,0:T(8,128)(2,1)S(1)} async-done(((bf16[32,3,128,128]{3,2,1,0:T(8,128)(2,1)}), bf16[32,3,128,128]{3,2,1,0:T(8,128)(2,1)S(1)}, u32[]{:S(2)}, u32[]{:S(2)}) %all-to-all-start) | async-done | bytes 3145760 | tf_op jit(solution)/shard_map/all_to_all | solution.py:371
  54.1 1.6 copy-done
  55.7 5.3 %all-to-all-start.1 = ((bf16[32,3,128,128]{3,2,1,0:T(8,128)(2,1)}), bf16[32,3,128,128]{3,2,1,0:T(8,128)(2,1)}, u32[]{:S(2)}, u32[]{:S(2)}) async-start(bf16[32,3,128,128]{3,2,1,0:T(8,128)(2,1)} %bitcast.34), calls=%async_computation.1 | async-start | bytes 6291456 | tf_op jit(solution)/shard_map/all_to_all | solution.py:371
  61.0 0.5 dynamic-slice_reduce_fusion.lengths
  61.5 0.1 iota_compare_fusion.4
  61.6 0.1 lt.98
  61.7 0.5 fusion.6
  62.2 0.1 shift_right_arithmetic.24
  62.3 0.1 copy.35
  62.4 0.1 fusion.1
  62.5 0.1 copy.34
  62.6 0.1 copy.36
  62.7 0.1 broadcast_select_fusion
  62.8 1.6 select_reduce_fusion.1
  64.4 0.1 reduce_sum.30
  64.5 0.1 fusion.5
  64.6 0.1 broadcast_in_dim.82
  64.7 0.1 broadcast_in_dim.83
  64.8 0.5 add_select_fusion.places
  65.3 13.5 %value_terms.1 = (bf16[96,48,128]{2,1,0:T(8,128)(2,1)}, bf16[96,80,128]{2,1,0:T(8,128)(2,1)}, f32[20,512,256]{2,1,0:T(8,128)}) custom-call(s32[80]{0:T(128)} %add_select_fusion.places, s32[20]{0:T(128)} %copy-done.6, bf16[256,2560]{1,0:T(8,128)(2,1)} %bitcast.36, bf16[256,2560]{1,0:T(8,128)(2,1)} %bitcast.38, bf16[96,128,128]{2,1,0:T(8,128)(2,1)} %bitcast.32), custom_call_target="tpu_custom_call" | custom-call | tf_op jit(solution)/shard_map/value_terms/pallas_call | solution.py:413
  78.8 6.0 %collective-permute-start.1 = (bf16[96,80,128]{2,1,0:T(8,128)(2,1)}, bf16[96,80,128]{2,1,0:T(8,128)(2,1)S(1)}, u32[]{:S(2)}, u32[]{:S(2)}) collective-permute-start(bf16[96,80,128]{2,1,0:T(8,128)(2,1)} %get-tuple-element.22), channel_id=1, source_target_pairs={{0,7},{1,0},{2,1},{3,2},{4,3},{5,4},{6,5},{7,6},{8,15},{9,8},{10,9... | collective-permute-start | bytes 5898248 | tf_op jit(solution)/shard_map/ppermute | solution.py:25
  84.8 15.8 %all-to-all-done.1 = bf16[32,3,128,128]{3,2,1,0:T(8,128)(2,1)} async-done(((bf16[32,3,128,128]{3,2,1,0:T(8,128)(2,1)}), bf16[32,3,128,128]{3,2,1,0:T(8,128)(2,1)}, u32[]{:S(2)}, u32[]{:S(2)}) %all-to-all-start.1) | async-done | bytes 3145760 | tf_op jit(solution)/shard_map/all_to_all | solution.py:371
  100.6 5.2 %all-to-all-start.3 = ((bf16[32,3,48,128]{3,2,1,0:T(8,128)(2,1)}), bf16[32,3,48,128]{3,2,1,0:T(8,128)(2,1)S(1)}, u32[]{:S(2)}, u32[]{:S(2)}) async-start(bf16[32,3,48,128]{3,2,1,0:T(8,128)(2,1)} %bitcast.46), calls=%async_computation.3 | async-start | bytes 2359296 | tf_op jit(solution)/shard_map/all_to_all | solution.py:371
  105.8 16.1 %key_terms.1 = (bf16[256,2560]{1,0:T(8,128)(2,1)}, bf16[96,128,128]{2,1,0:T(8,128)(2,1)}) custom-call(s32[80]{0:T(128)} %add_select_fusion.places, s32[20]{0:T(128)} %copy-done.6, bf16[256,2560]{1,0:T(8,128)(2,1)} %bitcast.37, bf16[256,2560]{1,0:T(8,128)(2,1)} %bitcast.39, bf16[96,128,128]{2,1,0:T(8,128)(2,1)} %bitcast.33, ...), custom_call_target="tpu_custom_call" | custom-call | tf_op jit(solution)/shard_map/key_terms/pallas_call | solution.py:428
  121.9 5.5 %collective-permute-done.1 = bf16[96,80,128]{2,1,0:T(8,128)(2,1)S(1)} collective-permute-done((bf16[96,80,128]{2,1,0:T(8,128)(2,1)}, bf16[96,80,128]{2,1,0:T(8,128)(2,1)S(1)}, u32[]{:S(2)}, u32[]{:S(2)}) %collective-permute-start.1) | collective-permute-done | bytes 1966112 | tf_op jit(solution)/shard_map/ppermute | solution.py:25
  127.5 1.3 copy-done.2
  128.8 0.3 copy-done.1
  129.1 7.4 %all-to-all-start.2 = ((bf16[32,3,128,128]{3,2,1,0:T(8,128)(2,1)}), bf16[32,3,128,128]{3,2,1,0:T(8,128)(2,1)S(1)}, u32[]{:S(2)}, u32[]{:S(2)}) async-start(bf16[32,3,128,128]{3,2,1,0:T(8,128)(2,1)} %bitcast.41), calls=%async_computation.2 | async-start | bytes 6291456 | tf_op jit(solution)/shard_map/all_to_all | solution.py:371
  136.5 3.7 %collective-permute-start.2 = (bf16[256,2560]{1,0:T(8,128)(2,1)}, bf16[256,2560]{1,0:T(8,128)(2,1)S(1)}, u32[]{:S(2)}, u32[]{:S(2)}) collective-permute-start(bf16[256,2560]{1,0:T(8,128)(2,1)} %get-tuple-element.24), channel_id=1, source_target_pairs={{0,7},{1,0},{2,1},{3,2},{4,3},{5,4},{6,5},{7,6},{8,15},{9,8},{10,9... | collective-permute-start | bytes 3932168 | tf_op jit(solution)/shard_map/ppermute | solution.py:25
  140.1 2.9 %sum_values.1 = bf16[96,2560]{1,0:T(8,128)(2,1)} custom-call(s32[96]{0:T(128)} %reshape.173.codes, bf16[96,48,128]{2,1,0:T(8,128)(2,1)} %bitcast.40), custom_call_target="tpu_custom_call" | custom-call | tf_op jit(solution)/shard_map/sum_values/pallas_call | solution.py:393
  143.1 0.1 collective-permute-start.3
  143.2 26.4 %collective-permute-done.2.source = bf16[256,2560]{1,0:T(8,128)(2,1)S(1)} collective-permute-done((bf16[256,2560]{1,0:T(8,128)(2,1)}, bf16[256,2560]{1,0:T(8,128)(2,1)S(1)}, u32[]{:S(2)}, u32[]{:S(2)}) %collective-permute-start.2) | collective-permute-done | bytes 1310752 | tf_op jit(solution)/shard_map/ppermute | solution.py:25
  169.6 1.1 place_queries.1
  170.7 8.6 %collective-permute-done.3.head_part = bf16[96,2560]{1,0:T(8,128)(2,1)} collective-permute-done((bf16[96,2560]{1,0:T(8,128)(2,1)}, bf16[96,2560]{1,0:T(8,128)(2,1)}, u32[]{:S(2)}, u32[]{:S(2)}) %collective-permute-start.3) | collective-permute-done | bytes 491552 | tf_op jit(solution)/shard_map/ppermute | solution.py:25
  179.3 3.3 %sum_keys.1 = bf16[256,2560]{1,0:T(8,128)(2,1)} custom-call(s32[96]{0:T(128)} %reshape.173.codes, bf16[96,128,128]{2,1,0:T(8,128)(2,1)S(1)} %bitcast.30), custom_call_target="tpu_custom_call" | custom-call | tf_op jit(solution)/shard_map/sum_keys/pallas_call | solution.py:393
  182.6 7.5 %all-to-all-start.4 = ((bf16[32,3,80,128]{3,2,1,0:T(8,128)(2,1)}), bf16[32,3,80,128]{3,2,1,0:T(8,128)(2,1)S(1)}, u32[]{:S(2)}, u32[]{:S(2)}) async-start(bf16[32,3,80,128]{3,2,1,0:T(8,128)(2,1)} %bitcast.42), calls=%async_computation.4 | async-start | bytes 3932160 | tf_op jit(solution)/shard_map/all_to_all | solution.py:371
  190.2 3.8 %collective-permute-start.4 = (bf16[256,2560]{1,0:T(8,128)(2,1)S(1)}, bf16[256,2560]{1,0:T(8,128)(2,1)}, u32[]{:S(2)}, u32[]{:S(2)}) collective-permute-start(bf16[256,2560]{1,0:T(8,128)(2,1)S(1)} %copy-done.3), channel_id=1, source_target_pairs={{0,7},{1,0},{2,1},{3,2},{4,3},{5,4},{6,5},{7,6},{8,15},{9,8},{10,9... | collective-permute-start | bytes 3932168 | tf_op jit(solution)/shard_map/ppermute | solution.py:25
  193.9 28.3 %collective-permute-done.4.keys = bf16[256,2560]{1,0:T(8,128)(2,1)} collective-permute-done((bf16[256,2560]{1,0:T(8,128)(2,1)S(1)}, bf16[256,2560]{1,0:T(8,128)(2,1)}, u32[]{:S(2)}, u32[]{:S(2)}) %collective-permute-start.4) | collective-permute-done | bytes 1310752 | tf_op jit(solution)/shard_map/ppermute | solution.py:25
  222.3 3.7 %join_values.1 = (bf16[256,2560]{1,0:T(8,128)(2,1)}, bf16[256,2560]{1,0:T(8,128)(2,1)}) custom-call(s32[96]{0:T(128)} %copy-done.8, bf16[256,2560]{1,0:T(8,128)(2,1)} %collective-permute-done.4.keys, bf16[96,2560]{1,0:T(8,128)(2,1)} %collective-permute-done.3.head_part, bf16[96,80,128]{2,1,0:T(8,128)(2,1)S(1)} %bitcast.31), custom_call_target="tpu_custom_call" | custom-call | tf_op jit(solution)/shard_map/join_values/pallas_call | solution.py:457
  (23 shorter events, 0.1 us)
Async XLA Ops:
  7.0 7.6 %copy-start.7 = (s32[96]{0:T(128)S(1)}, s32[96]{0:T(128)}, u32[]{:S(2)}) copy-start(s32[96]{0:T(128)} %reshape.173.codes) | copy-start | bytes 1156
  7.0 47.1 %all-to-all-start = ((bf16[32,3,128,128]{3,2,1,0:T(8,128)(2,1)}), bf16[32,3,128,128]{3,2,1,0:T(8,128)(2,1)S(1)}, u32[]{:S(2)}, u32[]{:S(2)}) async-start(bf16[32,3,128,128]{3,2,1,0:T(8,128)(2,1)} %bitcast.35), calls=%async_computation | async-start | bytes 6291456 | tf_op jit(solution)/shard_map/all_to_all | solution.py:371
  14.6 9.8 %collective-permute-start = (s32[96]{0:T(128)S(1)}, s32[96]{0:T(128)S(1)}, u32[]{:S(2)}, u32[]{:S(2)}) collective-permute-start(s32[96]{0:T(128)S(1)} %copy-done.7), channel_id=1, source_target_pairs={{0,7},{1,0},{2,1},{3,2},{4,3},{5,4},{6,5},{7,6},{8,15},{9,8},{10,9... | collective-permute-start | bytes 1160 | tf_op jit(solution)/shard_map/ppermute | solution.py:25
  24.4 29.7 %copy-start.8 = (s32[96]{0:T(128)}, s32[96]{0:T(128)S(1)}, u32[]{:S(2)}) copy-start(s32[96]{0:T(128)S(1)} %collective-permute-done.codes) | copy-start | bytes 1156
  54.0 1.6 copy-start
  54.0 6.9 %copy-start.5 = (s32[1,32,20]{1,0,2:T(1,128)S(1)}, s32[1,32,20]{1,0,2:T(1,128)}, u32[]{:S(2)}) copy-start(s32[1,32,20]{1,0,2:T(1,128)} %param.11) | copy-start | bytes 7684
  54.1 7.7 %copy-start.4 = (s32[1,32,20,4]{1,3,2,0:T(4,128)S(1)}, s32[1,32,20,4]{1,3,2,0:T(4,128)}, u32[]{:S(2)}) copy-start(s32[1,32,20,4]{1,3,2,0:T(4,128)} %param.10) | copy-start | bytes 30724
  55.7 44.9 %all-to-all-start.1 = ((bf16[32,3,128,128]{3,2,1,0:T(8,128)(2,1)}), bf16[32,3,128,128]{3,2,1,0:T(8,128)(2,1)}, u32[]{:S(2)}, u32[]{:S(2)}) async-start(bf16[32,3,128,128]{3,2,1,0:T(8,128)(2,1)} %bitcast.34), calls=%async_computation.1 | async-start | bytes 6291456 | tf_op jit(solution)/shard_map/all_to_all | solution.py:371
  61.5 3.8 %copy-start.6 = (s32[20]{0:T(128)}, s32[20]{0:T(128)S(1)}, u32[]{:S(2)}) copy-start(s32[20]{0:T(128)S(1)} %dynamic-slice_reduce_fusion.lengths) | copy-start | bytes 244
  78.8 48.7 %collective-permute-start.1 = (bf16[96,80,128]{2,1,0:T(8,128)(2,1)}, bf16[96,80,128]{2,1,0:T(8,128)(2,1)S(1)}, u32[]{:S(2)}, u32[]{:S(2)}) collective-permute-start(bf16[96,80,128]{2,1,0:T(8,128)(2,1)} %get-tuple-element.22), channel_id=1, source_target_pairs={{0,7},{1,0},{2,1},{3,2},{4,3},{5,4},{6,5},{7,6},{8,15},{9,8},{10,9... | collective-permute-start | bytes 5898248 | tf_op jit(solution)/shard_map/ppermute | solution.py:25
  100.6 26.9 %all-to-all-start.3 = ((bf16[32,3,48,128]{3,2,1,0:T(8,128)(2,1)}), bf16[32,3,48,128]{3,2,1,0:T(8,128)(2,1)S(1)}, u32[]{:S(2)}, u32[]{:S(2)}) async-start(bf16[32,3,48,128]{3,2,1,0:T(8,128)(2,1)} %bitcast.46), calls=%async_computation.3 | async-start | bytes 2359296 | tf_op jit(solution)/shard_map/all_to_all | solution.py:371
  127.5 1.3 copy-start.2
  127.5 1.7 copy-start.1
  129.1 50.2 %all-to-all-start.2 = ((bf16[32,3,128,128]{3,2,1,0:T(8,128)(2,1)}), bf16[32,3,128,128]{3,2,1,0:T(8,128)(2,1)S(1)}, u32[]{:S(2)}, u32[]{:S(2)}) async-start(bf16[32,3,128,128]{3,2,1,0:T(8,128)(2,1)} %bitcast.41), calls=%async_computation.2 | async-start | bytes 6291456 | tf_op jit(solution)/shard_map/all_to_all | solution.py:371
  136.5 33.1 %collective-permute-start.2 = (bf16[256,2560]{1,0:T(8,128)(2,1)}, bf16[256,2560]{1,0:T(8,128)(2,1)S(1)}, u32[]{:S(2)}, u32[]{:S(2)}) collective-permute-start(bf16[256,2560]{1,0:T(8,128)(2,1)} %get-tuple-element.24), channel_id=1, source_target_pairs={{0,7},{1,0},{2,1},{3,2},{4,3},{5,4},{6,5},{7,6},{8,15},{9,8},{10,9... | collective-permute-start | bytes 3932168 | tf_op jit(solution)/shard_map/ppermute | solution.py:25
  143.1 36.3 %collective-permute-start.3 = (bf16[96,2560]{1,0:T(8,128)(2,1)}, bf16[96,2560]{1,0:T(8,128)(2,1)}, u32[]{:S(2)}, u32[]{:S(2)}) collective-permute-start(bf16[96,2560]{1,0:T(8,128)(2,1)} %sum_values.1), channel_id=1, source_target_pairs={{0,7},{1,0},{2,1},{3,2},{4,3},{5,4},{6,5},{7,6},{8,15},{9,8},{10,9... | collective-permute-start | bytes 1474568 | tf_op jit(solution)/shard_map/ppermute | solution.py:25
  182.6 7.5 %copy-start.3 = (bf16[256,2560]{1,0:T(8,128)(2,1)S(1)}, bf16[256,2560]{1,0:T(8,128)(2,1)}, u32[]{:S(2)}) copy-start(bf16[256,2560]{1,0:T(8,128)(2,1)} %sum_keys.1) | copy-start | bytes 3932164
  182.6 39.7 %all-to-all-start.4 = ((bf16[32,3,80,128]{3,2,1,0:T(8,128)(2,1)}), bf16[32,3,80,128]{3,2,1,0:T(8,128)(2,1)S(1)}, u32[]{:S(2)}, u32[]{:S(2)}) async-start(bf16[32,3,80,128]{3,2,1,0:T(8,128)(2,1)} %bitcast.42), calls=%async_computation.4 | async-start | bytes 3932160 | tf_op jit(solution)/shard_map/all_to_all | solution.py:371
  190.2 32.1 %collective-permute-start.4 = (bf16[256,2560]{1,0:T(8,128)(2,1)S(1)}, bf16[256,2560]{1,0:T(8,128)(2,1)}, u32[]{:S(2)}, u32[]{:S(2)}) collective-permute-start(bf16[256,2560]{1,0:T(8,128)(2,1)S(1)} %copy-done.3), channel_id=1, source_target_pairs={{0,7},{1,0},{2,1},{3,2},{4,3},{5,4},{6,5},{7,6},{8,15},{9,8},{10,9... | collective-permute-start | bytes 3932168 | tf_op jit(solution)/shard_map/ppermute | solution.py:25

commit v5 on v4

--- a/solution.py
+++ b/solution.py
@@ -99,32 +99,19 @@
     send_columns(ready, total, sent, sent.shape[0], fill)
 
 
-def join_kernel(
-    parts, codes, keys, head_part, terms, key_out, total,
-    wide, ready, head, key_held, sent, got, key_got, put,
+def last_kernel(
+    parts, codes, keys, terms, key_out, total, wide, ready, key_held, sent, key_got, put
 ):
-    head_copy = copy(head_part, head, got)
-    head_copy.start()
     key_in = copy(keys, key_held, key_got)
     key_in.start()
     add_terms(codes, terms, wide, parts)
     key_in.wait()
     key_copy = copy(key_held, key_out, put)
     key_copy.start()
-    head_copy.wait()
-    tail_rows = terms.shape[1]
-    head_rows = total.shape[0] // 2 - tail_rows
+    rows = total.shape[0]
 
     def fill(columns):
-        for block in range(2):
-            start = block * (head_rows + tail_rows)
-            middle = start + head_rows
-            ready[start:middle, columns] = head[
-                block * head_rows : (block + 1) * head_rows, columns
-            ]
-            ready[middle : middle + tail_rows, columns] = wide[
-                block * tail_rows : (block + 1) * tail_rows, columns
-            ].astype(ready.dtype)
+        ready[:, columns] = wide[:rows, columns].astype(ready.dtype)
 
     send_columns(ready, total, sent, sent.shape[0], fill)
     key_copy.wait()
@@ -266,17 +253,51 @@
 def key_kernel(
     list_size, group, scale, places, lengths, queries, grads, keys, values, weights,
     query_grad, terms,
-    query_held, grad_held, key_held, value_held, weights_held, made, query_made,
-    query_sem, grad_sem, key_sem, value_sem, weights_sem, out_sem, query_out_sem,
+    query_held, grad_held, key_held, weights_held, made, query_made,
+    query_sem, grad_sem, key_sem, weights_sem, out_sem, query_out_sem,
 ):
-    cols = keys.shape[2]
-    walk = Grouped(places, lengths, list_size, group, cols)
+    rows, cols = keys.shape[1:]
+    groups = lengths.shape[0] // group
+    parts = out_sem.shape[0]
+    step = keys.shape[0] // parts
+    width = group * cols
+
+    def columns_of(index):
+        return pl.ds(pl.multiple_of(index * width, width), width)
+
+    def fetches(index):
+        columns = columns_of(index)
+        heads = pl.ds(index * group, group)
+        return [
+            copy(grads.at[:, columns], grad_held.at[:, columns], grad_sem.at[index]),
+            copy(weights.at[heads], weights_held.at[heads], weights_sem.at[index]),
+            copy(queries.at[:, columns], query_held.at[:, columns], query_sem.at[index]),
+        ]
+
+    def key_part(part):
+        where = pl.ds(part * step, step)
+        return copy(keys.at[where], key_held.at[where], key_sem.at[part])
+
+    def made_part(part):
+        where = pl.ds(part * step, step)
+        return copy(made.at[where], terms.at[where], out_sem.at[part])
+
+    def query_part(index):
+        columns = columns_of(index)
+        return copy(
+            query_made.at[:, columns], query_grad.at[:, columns], query_out_sem.at[index]
+        )
+
+    for one in fetches(0):
+        one.start()
+    for part in range(parts):
+        key_part(part).start()
 
     def compute(head):
-        columns = walk.head(head)
-        entries = pl.ds(head * list_size, list_size)
-        key = key_held[entries].reshape(-1, cols)
-        value = value_held[entries].reshape(-1, cols)
+        columns = pl.ds(pl.multiple_of(head * cols, cols), cols)
+        where = [places[head * list_size + item] for item in range(list_size)]
+        key = jnp.concatenate([key_held[place] for place in where], axis=0)
+        value = jnp.concatenate([values[place] for place in where], axis=0)
         weight = weights_held[head]
         weight_low = weight.astype(jnp.bfloat16).astype(jnp.float32)
         dweights = lax.dot_general(
@@ -291,16 +312,41 @@
         )
         return (made_terms * scale).astype(jnp.bfloat16)
 
-    walk.run(
-        [(queries, query_held, query_sem), (grads, grad_held, grad_sem)],
-        [(keys, key_held, key_sem), (values, value_held, value_sem)],
-        [(weights, weights_held, weights_sem)],
-        made,
-        [terms],
-        out_sem,
-        compute,
-        lambda index: walk.wide(index, query_made, query_grad, query_out_sem),
-    )
+    def one_group(index, carry):
+        @pl.when(index + 1 < groups)
+        def _():
+            for one in fetches(index + 1):
+                one.start()
+
+        for one in fetches(index):
+            one.wait()
+
+        @pl.when(index == 0)
+        def _():
+            for part in range(parts):
+                key_part(part).wait()
+
+        results = [compute(index * group + item) for item in range(group)]
+        query_part(index).start()
+        for item, result in enumerate(results):
+            head = index * group + item
+            for entry in range(list_size):
+
+                @pl.when(entry < lengths[head])
+                def _():
+                    made[places[head * list_size + entry]] = result[
+                        entry * rows : (entry + 1) * rows
+                    ]
+
+        return carry
+
+    lax.fori_loop(0, groups, one_group, 0)
+    for part in range(parts):
+        made_part(part).start()
+    for index in range(groups):
+        query_part(index).wait()
+    for part in range(parts):
+        made_part(part).wait()
 
 
 def local(queries, keys, values, out_grad, key_blocks, list_lengths):
@@ -351,7 +397,7 @@
     places = my_holder * capacity + my_rank
     places = jnp.where(my_used, places, places[:, :1]).reshape(entries)
 
-    first_rows = 3 * block_rows // 8
+    first_rows = block_rows // 2
     last_rows = block_rows - first_rows
     add_parts = 8 if slots % 8 == 0 else 1
     send_parts = 5 if head_count % 5 == 0 else 1
@@ -401,6 +447,7 @@
         )(codes, returned)
 
     tiles = vmem(entries, block_rows, head_dim)
+    slot_tiles = vmem(slots, block_rows, head_dim)
     wide_sem, tile_sem = dma((groups,)), dma((entries,))
     fetched_keys = exchanged(pack("pack_keys", keys[0]))
     handed_codes = shifted(codes, "section", -1)
@@ -424,22 +471,22 @@
         compiler_params=PARAMS,
         name="value_terms",
     )(places, my_lengths, queries[0], out_grad[0], fetched_keys)
-    handed_terms = shifted(last_terms, "section", -1)
+    handed_first = shifted(first_terms, "section", -1)
     query_grad, key_terms = pl.pallas_call(
         functools.partial(key_kernel, list_size, group, scale),
         out_shape=(flat_shape, packed_shape(block_rows)),
-        in_specs=[SMEM, SMEM, ANY, ANY, ANY, ANY, ANY],
+        in_specs=[SMEM, SMEM, ANY, ANY, ANY, VMEM, ANY],
         out_specs=(ANY, ANY),
-        scratch_shapes=[flat, flat, tiles, tiles, weights_tile, tiles, flat]
-        + [wide_sem, wide_sem, tile_sem, tile_sem, wide_sem, dma((1, entries)), wide_sem],
+        scratch_shapes=[flat, flat, slot_tiles, weights_tile, slot_tiles, flat]
+        + [wide_sem, wide_sem, dma((add_parts,)), wide_sem, dma((add_parts,)), wide_sem],
         compiler_params=PARAMS,
         name="key_terms",
-    )(places, my_lengths, queries[0], out_grad[0], fetched_keys, fetched_values, weights)
+    )(places, my_lengths, queries[0], out_grad[0], fetched_keys, near(fetched_values), weights)
     handed_queries = shifted(query_grad, "section", -1)
-    first_values = add_up("sum_values", exchanged(first_terms))
-    handed_first = shifted(first_values, "section", -1)
-    key_terms, handed_terms = lax.optimization_barrier((key_terms, handed_terms))
+    handed_last = shifted(last_terms, "section", -1)
+    key_terms, handed_first = lax.optimization_barrier((key_terms, handed_first))
     returned_keys = exchanged(key_terms)
+    handed_terms = jnp.concatenate([handed_first, handed_last], axis=1)
     handed_queries = pl.pallas_call(
         place_kernel,
         out_shape=flat_shape,
@@ -448,22 +495,22 @@
         compiler_params=PARAMS,
         name="place_queries",
     )(near(handed_queries))
-    returned_keys, handed_queries, handed_first = lax.optimization_barrier(
-        (returned_keys, handed_queries, handed_first)
+    returned_keys, handed_queries, handed_terms = lax.optimization_barrier(
+        (returned_keys, handed_queries, handed_terms)
     )
     key_grad = add_up("sum_keys", near(returned_keys))
     key_grad, handed_terms = lax.optimization_barrier((key_grad, handed_terms))
     handed_keys = shifted(key_grad, "section", -1)
     handed_keys, handed_values = pl.pallas_call(
-        functools.partial(join_kernel, add_parts),
+        functools.partial(last_kernel, add_parts),
         out_shape=(flat_shape, flat_shape),
-        in_specs=[SMEM, ANY, ANY, VMEM],
+        in_specs=[SMEM, ANY, VMEM],
         out_specs=(ANY, ANY),
-        scratch_shapes=[wide_sum(last_rows), flat, vmem(2 * first_rows, column_count), flat]
-        + [dma((send_parts,)), dma, dma, dma],
+        scratch_shapes=[wide_sum(block_rows), flat, flat]
+        + [dma((send_parts,)), dma, dma],
         compiler_params=PARAMS,
-        name="join_values",
-    )(handed_codes, handed_keys, handed_first, near(exchanged(handed_terms)))
+        name="last_values",
+    )(handed_codes, handed_keys, near(exchanged(handed_terms)))
     return (handed_queries[None], handed_keys[None], handed_values[None])
 
 

time: 227 us -> 253 us (1.11)
  waiting for transfers between devices: 114 us -> 148 us
  starting transfers between devices: 52.4 us -> 46.8 us
  Pallas kernels: 48.2 us -> 43.9 us
  other arithmetic: 4 us -> 7.37 us
    ppermute x5, waiting for transfers between devices: 68.9 us -> 95.1 us  [shifted(): return lax.ppermute(value, axis, pairs)]
    all_to_all x5 -> x4, waiting for transfers between devices: 45.4 us -> 52.4 us  [exchanged(): lax.all_to_all(parts, 'ctx', split_axis=0, concat_axis=0, tiled=True)]
    all_to_all x5 -> x4, starting transfers between devices: 33 us -> 27.5 us  [exchanged(): lax.all_to_all(parts, 'ctx', split_axis=0, concat_axis=0, tiled=True)]
    concatenate x0 -> x1, other arithmetic: none -> 3.37 us  [local(): handed_terms = jnp.concatenate([handed_first, handed_last], axis=1)]
    pallas_call x2 -> x1, Pallas kernels: 6.19 us -> 3.26 us  [add_up(): pl.pallas_call(functools.partial(sum_kernel, add_parts), out_shape=jax.Sh...]
  transfers between devices with their start and end apart: 10 -> 9, of which waited for: 6 -> 6; matrix products, arithmetic and copies ran while one was open for 2% -> 3% of each run, Pallas kernels for 17% -> 13%
where the time goes in v5:
time: 253 us; the launch traced here: 251 us
  waiting for transfers between devices  148 us (58%)
  starting transfers between devices  46.8 us (18%)
  Pallas kernels  43.9 us (17%)
  other arithmetic  7.37 us (3%)
  local copies, waits for them, and re-layouts  4.42 us (2%)
    ppermute x5, waiting for transfers between devices, shifted(): return lax.ppermute(value, axis, pairs)  95.1 us
    all_to_all x4, waiting for transfers between devices, exchanged(): lax.all_to_all(parts, 'ctx', split_axis=0, concat_axis=0, tiled=True)  52.4 us
    all_to_all x4, starting transfers between devices, exchanged(): lax.all_to_all(parts, 'ctx', split_axis=0, concat_axis=0, tiled=True)  27.5 us
    ppermute x5, starting transfers between devices, shifted(): return lax.ppermute(value, axis, pairs)  19.3 us
    pallas_call x1, Pallas kernels, local(): pl.pallas_call(functools.partial(key_kernel, list_size, group, scale), ou...  14.5 us
    pallas_call x1, Pallas kernels, local(): pl.pallas_call(functools.partial(value_kernel, list_size, group, scale),...  13.7 us
    pallas_call x2, Pallas kernels, pack(): pl.pallas_call(functools.partial(pack_kernel, add_parts), out_shape=packe...  7.68 us
  transfers between devices with their start and end apart: 9, of which 6 were waited for; matrix products, arithmetic and copies ran while one was open for 3% of the time, Pallas kernels for 13%

profile of v5, /device:TPU:8, one launch (start us, length us, event | category | flops | bytes accessed | tf_op | source)
XLA Modules:
  0.0 250.9 jit_solution(13596459856564652350)
XLA Ops:
  0.7 0.7 copy.40
  1.4 0.8 fusion
  2.2 0.2 select_reduce_fusion
  2.4 0.1 copy.37
  2.5 0.7 reshape.167.codes
  3.2 3.8 %pack_keys.1 = bf16[96,128,128]{2,1,0:T(8,128)(2,1)} custom-call(s32[96]{0:T(128)} %reshape.167.codes, bf16[256,2560]{1,0:T(8,128)(2,1)} %bitcast.41), custom_call_target="tpu_custom_call" | custom-call | tf_op jit(solution)/shard_map/pack_keys/pallas_call | solution.py:421
  7.0 7.5 %all-to-all-start = ((bf16[32,3,128,128]{3,2,1,0:T(8,128)(2,1)}), bf16[32,3,128,128]{3,2,1,0:T(8,128)(2,1)S(1)}, u32[]{:S(2)}, u32[]{:S(2)}) async-start(bf16[32,3,128,128]{3,2,1,0:T(8,128)(2,1)} %bitcast.35), calls=%async_computation | async-start | bytes 6291456 | tf_op jit(solution)/shard_map/all_to_all | solution.py:417
  14.6 5.9 %collective-permute-start = (s32[96]{0:T(128)S(1)}, s32[96]{0:T(128)S(1)}, u32[]{:S(2)}, u32[]{:S(2)}) collective-permute-start(s32[96]{0:T(128)S(1)} %copy-done.4), channel_id=1, source_target_pairs={{0,7},{1,0},{2,1},{3,2},{4,3},{5,4},{6,5},{7,6},{8,15},{9,8},{10,9... | collective-permute-start | bytes 1160 | tf_op jit(solution)/shard_map/ppermute | solution.py:25
  20.5 3.9 %pack_values.1 = bf16[96,128,128]{2,1,0:T(8,128)(2,1)} custom-call(s32[96]{0:T(128)} %reshape.167.codes, bf16[256,2560]{1,0:T(8,128)(2,1)} %bitcast.42), custom_call_target="tpu_custom_call" | custom-call | tf_op jit(solution)/shard_map/pack_values/pallas_call | solution.py:421
  24.4 0.0 collective-permute-done.codes
  24.4 29.6 %all-to-all-done = bf16[32,3,128,128]{3,2,1,0:T(8,128)(2,1)S(1)} async-done(((bf16[32,3,128,128]{3,2,1,0:T(8,128)(2,1)}), bf16[32,3,128,128]{3,2,1,0:T(8,128)(2,1)S(1)}, u32[]{:S(2)}, u32[]{:S(2)}) %all-to-all-start) | async-done | bytes 3145760 | tf_op jit(solution)/shard_map/all_to_all | solution.py:417
  54.1 1.6 copy-done
  55.7 5.2 %all-to-all-start.1 = ((bf16[32,3,128,128]{3,2,1,0:T(8,128)(2,1)}), bf16[32,3,128,128]{3,2,1,0:T(8,128)(2,1)S(1)}, u32[]{:S(2)}, u32[]{:S(2)}) async-start(bf16[32,3,128,128]{3,2,1,0:T(8,128)(2,1)} %bitcast.33), calls=%async_computation.1 | async-start | bytes 6291456 | tf_op jit(solution)/shard_map/all_to_all | solution.py:417
  60.9 0.5 dynamic-slice_reduce_fusion.lengths
  61.5 0.1 iota_compare_fusion.4
  61.6 0.1 lt.98
  61.7 0.5 fusion.6
  62.2 0.1 shift_right_arithmetic.24
  62.3 0.1 copy.35
  62.4 0.1 fusion.1
  62.5 0.1 copy.34
  62.6 0.1 copy.36
  62.7 0.1 broadcast_select_fusion
  62.7 1.6 select_reduce_fusion.1
  64.4 0.1 reduce_sum.30
  64.5 0.1 fusion.5
  64.6 0.1 broadcast_in_dim.82
  64.6 0.1 broadcast_in_dim.83
  64.7 0.5 add_select_fusion.places
  65.3 13.7 %value_terms.1 = (bf16[96,64,128]{2,1,0:T(8,128)(2,1)}, bf16[96,64,128]{2,1,0:T(8,128)(2,1)}, f32[20,512,256]{2,1,0:T(8,128)}) custom-call(s32[80]{0:T(128)} %add_select_fusion.places, s32[20]{0:T(128)} %copy-done.3, bf16[256,2560]{1,0:T(8,128)(2,1)} %bitcast.36, bf16[256,2560]{1,0:T(8,128)(2,1)} %bitcast.38, bf16[96,128,128]{2,1,0:T(8,128)(2,1)} %bitcast.31), custom_call_target="tpu_custom_call" | custom-call | tf_op jit(solution)/shard_map/value_terms/pallas_call | solution.py:460
  79.0 5.8 %collective-permute-start.1 = (bf16[96,64,128]{2,1,0:T(8,128)(2,1)}, bf16[96,64,128]{2,1,0:T(8,128)(2,1)}, u32[]{:S(2)}, u32[]{:S(2)}) collective-permute-start(bf16[96,64,128]{2,1,0:T(8,128)(2,1)} %get-tuple-element.22), channel_id=1, source_target_pairs={{0,7},{1,0},{2,1},{3,2},{4,3},{5,4},{6,5},{7,6},{8,15},{9,8},{10,9... | collective-permute-start | bytes 4718600 | tf_op jit(solution)/shard_map/ppermute | solution.py:25
  84.8 15.6 %all-to-all-done.1 = bf16[32,3,128,128]{3,2,1,0:T(8,128)(2,1)S(1)} async-done(((bf16[32,3,128,128]{3,2,1,0:T(8,128)(2,1)}), bf16[32,3,128,128]{3,2,1,0:T(8,128)(2,1)S(1)}, u32[]{:S(2)}, u32[]{:S(2)}) %all-to-all-start.1) | async-done | bytes 3145760 | tf_op jit(solution)/shard_map/all_to_all | solution.py:417
  100.4 14.5 %key_terms.1 = (bf16[256,2560]{1,0:T(8,128)(2,1)}, bf16[96,128,128]{2,1,0:T(8,128)(2,1)}) custom-call(s32[80]{0:T(128)} %add_select_fusion.places, s32[20]{0:T(128)} %copy-done.3, bf16[256,2560]{1,0:T(8,128)(2,1)} %bitcast.37, bf16[256,2560]{1,0:T(8,128)(2,1)} %bitcast.39, bf16[96,128,128]{2,1,0:T(8,128)(2,1)} %bitcast.32, ...), custom_call_target="tpu_custom_call" | custom-call | tf_op jit(solution)/shard_map/key_terms/pallas_call | solution.py:475
  114.9 4.1 %collective-permute-done.1 = bf16[96,64,128]{2,1,0:T(8,128)(2,1)} collective-permute-done((bf16[96,64,128]{2,1,0:T(8,128)(2,1)}, bf16[96,64,128]{2,1,0:T(8,128)(2,1)}, u32[]{:S(2)}, u32[]{:S(2)}) %collective-permute-start.1) | collective-permute-done | bytes 1572896 | tf_op jit(solution)/shard_map/ppermute | solution.py:25
  119.1 7.3 %all-to-all-start.2 = ((bf16[32,3,128,128]{3,2,1,0:T(8,128)(2,1)}), bf16[32,3,128,128]{3,2,1,0:T(8,128)(2,1)S(1)}, u32[]{:S(2)}, u32[]{:S(2)}) async-start(bf16[32,3,128,128]{3,2,1,0:T(8,128)(2,1)} %bitcast.40), calls=%async_computation.2 | async-start | bytes 6291456 | tf_op jit(solution)/shard_map/all_to_all | solution.py:417
  126.4 3.8 %collective-permute-start.3 = (bf16[96,64,128]{2,1,0:T(8,128)(2,1)}, bf16[96,64,128]{2,1,0:T(8,128)(2,1)S(1)}, u32[]{:S(2)}, u32[]{:S(2)}) collective-permute-start(bf16[96,64,128]{2,1,0:T(8,128)(2,1)} %get-tuple-element.26), channel_id=1, source_target_pairs={{0,7},{1,0},{2,1},{3,2},{4,3},{5,4},{6,5},{7,6},{8,15},{9,8},{10,9... | collective-permute-start | bytes 4718600 | tf_op jit(solution)/shard_map/ppermute | solution.py:25
  130.2 0.1 collective-permute-start.2
  130.3 62.3 %collective-permute-done.2.source = bf16[256,2560]{1,0:T(8,128)(2,1)S(1)} collective-permute-done((bf16[256,2560]{1,0:T(8,128)(2,1)}, bf16[256,2560]{1,0:T(8,128)(2,1)S(1)}, u32[]{:S(2)}, u32[]{:S(2)}) %collective-permute-start.2) | collective-permute-done | bytes 1310752 | tf_op jit(solution)/shard_map/ppermute | solution.py:25
  192.6 1.1 place_queries.1
  193.7 0.0 collective-permute-done.3
  193.7 3.4 %pad_maximum_fusion = bf16[96,128,128]{2,1,0:T(8,128)(2,1)} fusion(bf16[96,64,128]{2,1,0:T(8,128)(2,1)S(1)} %collective-permute-done.3, bf16[96,64,128]{2,1,0:T(8,128)(2,1)} %collective-permute-done.1), kind=kLoop, calls=%fused_computation | loop fusion | flops 6291456 | bytes 6291456 | tf_op jit(solution)/shard_map/concatenate | solution.py:489
  197.1 0.0 all-to-all-done.2
  197.1 3.3 %sum_keys.1 = bf16[256,2560]{1,0:T(8,128)(2,1)} custom-call(s32[96]{0:T(128)} %reshape.167.codes, bf16[96,128,128]{2,1,0:T(8,128)(2,1)S(1)} %bitcast.29), custom_call_target="tpu_custom_call" | custom-call | tf_op jit(solution)/shard_map/sum_keys/pallas_call | solution.py:439
  200.3 7.4 %all-to-all-start.3 = ((bf16[32,3,128,128]{3,2,1,0:T(8,128)(2,1)}), bf16[32,3,128,128]{3,2,1,0:T(8,128)(2,1)S(1)}, u32[]{:S(2)}, u32[]{:S(2)}) async-start(bf16[32,3,128,128]{3,2,1,0:T(8,128)(2,1)} %bitcast.34), calls=%async_computation.3 | async-start | bytes 6291456 | tf_op jit(solution)/shard_map/all_to_all | solution.py:417
  207.7 3.7 %collective-permute-start.4 = (bf16[256,2560]{1,0:T(8,128)(2,1)}, bf16[256,2560]{1,0:T(8,128)(2,1)}, u32[]{:S(2)}, u32[]{:S(2)}) collective-permute-start(bf16[256,2560]{1,0:T(8,128)(2,1)} %sum_keys.1), channel_id=1, source_target_pairs={{0,7},{1,0},{2,1},{3,2},{4,3},{5,4},{6,5},{7,6},{8,15},{9,8},{10,9... | collective-permute-start | bytes 3932168 | tf_op jit(solution)/shard_map/ppermute | solution.py:25
  211.4 28.7 %collective-permute-done.4.keys = bf16[256,2560]{1,0:T(8,128)(2,1)} collective-permute-done((bf16[256,2560]{1,0:T(8,128)(2,1)}, bf16[256,2560]{1,0:T(8,128)(2,1)}, u32[]{:S(2)}, u32[]{:S(2)}) %collective-permute-start.4) | collective-permute-done | bytes 1310752 | tf_op jit(solution)/shard_map/ppermute | solution.py:25
  240.1 7.2 %all-to-all-done.3 = bf16[32,3,128,128]{3,2,1,0:T(8,128)(2,1)S(1)} async-done(((bf16[32,3,128,128]{3,2,1,0:T(8,128)(2,1)}), bf16[32,3,128,128]{3,2,1,0:T(8,128)(2,1)S(1)}, u32[]{:S(2)}, u32[]{:S(2)}) %all-to-all-start.3) | async-done | bytes 3145760 | tf_op jit(solution)/shard_map/all_to_all | solution.py:417
  247.2 3.6 %last_values.1 = (bf16[256,2560]{1,0:T(8,128)(2,1)}, bf16[256,2560]{1,0:T(8,128)(2,1)}) custom-call(s32[96]{0:T(128)} %copy-done.5, bf16[256,2560]{1,0:T(8,128)(2,1)} %collective-permute-done.4.keys, bf16[96,128,128]{2,1,0:T(8,128)(2,1)S(1)} %bitcast.30), custom_call_target="tpu_custom_call" | custom-call | tf_op jit(solution)/shard_map/last_values/pallas_call | solution.py:504
  (15 shorter events, 0.1 us)
Async XLA Ops:
  7.0 7.6 %copy-start.4 = (s32[96]{0:T(128)S(1)}, s32[96]{0:T(128)}, u32[]{:S(2)}) copy-start(s32[96]{0:T(128)} %reshape.167.codes) | copy-start | bytes 1156
  7.0 47.1 %all-to-all-start = ((bf16[32,3,128,128]{3,2,1,0:T(8,128)(2,1)}), bf16[32,3,128,128]{3,2,1,0:T(8,128)(2,1)S(1)}, u32[]{:S(2)}, u32[]{:S(2)}) async-start(bf16[32,3,128,128]{3,2,1,0:T(8,128)(2,1)} %bitcast.35), calls=%async_computation | async-start | bytes 6291456 | tf_op jit(solution)/shard_map/all_to_all | solution.py:417
  14.6 9.8 %collective-permute-start = (s32[96]{0:T(128)S(1)}, s32[96]{0:T(128)S(1)}, u32[]{:S(2)}, u32[]{:S(2)}) collective-permute-start(s32[96]{0:T(128)S(1)} %copy-done.4), channel_id=1, source_target_pairs={{0,7},{1,0},{2,1},{3,2},{4,3},{5,4},{6,5},{7,6},{8,15},{9,8},{10,9... | collective-permute-start | bytes 1160 | tf_op jit(solution)/shard_map/ppermute | solution.py:25
  24.4 31.3 %copy-start.5 = (s32[96]{0:T(128)}, s32[96]{0:T(128)S(1)}, u32[]{:S(2)}) copy-start(s32[96]{0:T(128)S(1)} %collective-permute-done.codes) | copy-start | bytes 1156
  54.0 1.6 copy-start
  54.1 6.9 %copy-start.2 = (s32[1,32,20]{1,0,2:T(1,128)S(1)}, s32[1,32,20]{1,0,2:T(1,128)}, u32[]{:S(2)}) copy-start(s32[1,32,20]{1,0,2:T(1,128)} %param.11) | copy-start | bytes 7684
  54.1 7.6 %copy-start.1 = (s32[1,32,20,4]{1,3,2,0:T(4,128)S(1)}, s32[1,32,20,4]{1,3,2,0:T(4,128)}, u32[]{:S(2)}) copy-start(s32[1,32,20,4]{1,3,2,0:T(4,128)} %param.10) | copy-start | bytes 30724
  55.7 44.8 %all-to-all-start.1 = ((bf16[32,3,128,128]{3,2,1,0:T(8,128)(2,1)}), bf16[32,3,128,128]{3,2,1,0:T(8,128)(2,1)S(1)}, u32[]{:S(2)}, u32[]{:S(2)}) async-start(bf16[32,3,128,128]{3,2,1,0:T(8,128)(2,1)} %bitcast.33), calls=%async_computation.1 | async-start | bytes 6291456 | tf_op jit(solution)/shard_map/all_to_all | solution.py:417
  61.5 3.8 %copy-start.3 = (s32[20]{0:T(128)}, s32[20]{0:T(128)S(1)}, u32[]{:S(2)}) copy-start(s32[20]{0:T(128)S(1)} %dynamic-slice_reduce_fusion.lengths) | copy-start | bytes 244
  79.0 40.1 %collective-permute-start.1 = (bf16[96,64,128]{2,1,0:T(8,128)(2,1)}, bf16[96,64,128]{2,1,0:T(8,128)(2,1)}, u32[]{:S(2)}, u32[]{:S(2)}) collective-permute-start(bf16[96,64,128]{2,1,0:T(8,128)(2,1)} %get-tuple-element.22), channel_id=1, source_target_pairs={{0,7},{1,0},{2,1},{3,2},{4,3},{5,4},{6,5},{7,6},{8,15},{9,8},{10,9... | collective-permute-start | bytes 4718600 | tf_op jit(solution)/shard_map/ppermute | solution.py:25
  119.1 78.0 %all-to-all-start.2 = ((bf16[32,3,128,128]{3,2,1,0:T(8,128)(2,1)}), bf16[32,3,128,128]{3,2,1,0:T(8,128)(2,1)S(1)}, u32[]{:S(2)}, u32[]{:S(2)}) async-start(bf16[32,3,128,128]{3,2,1,0:T(8,128)(2,1)} %bitcast.40), calls=%async_computation.2 | async-start | bytes 6291456 | tf_op jit(solution)/shard_map/all_to_all | solution.py:417
  126.4 67.3 %collective-permute-start.3 = (bf16[96,64,128]{2,1,0:T(8,128)(2,1)}, bf16[96,64,128]{2,1,0:T(8,128)(2,1)S(1)}, u32[]{:S(2)}, u32[]{:S(2)}) collective-permute-start(bf16[96,64,128]{2,1,0:T(8,128)(2,1)} %get-tuple-element.26), channel_id=1, source_target_pairs={{0,7},{1,0},{2,1},{3,2},{4,3},{5,4},{6,5},{7,6},{8,15},{9,8},{10,9... | collective-permute-start | bytes 4718600 | tf_op jit(solution)/shard_map/ppermute | solution.py:25
  130.2 62.4 %collective-permute-start.2 = (bf16[256,2560]{1,0:T(8,128)(2,1)}, bf16[256,2560]{1,0:T(8,128)(2,1)S(1)}, u32[]{:S(2)}, u32[]{:S(2)}) collective-permute-start(bf16[256,2560]{1,0:T(8,128)(2,1)} %get-tuple-element.24), channel_id=1, source_target_pairs={{0,7},{1,0},{2,1},{3,2},{4,3},{5,4},{6,5},{7,6},{8,15},{9,8},{10,9... | collective-permute-start | bytes 3932168 | tf_op jit(solution)/shard_map/ppermute | solution.py:25
  200.3 46.9 %all-to-all-start.3 = ((bf16[32,3,128,128]{3,2,1,0:T(8,128)(2,1)}), bf16[32,3,128,128]{3,2,1,0:T(8,128)(2,1)S(1)}, u32[]{:S(2)}, u32[]{:S(2)}) async-start(bf16[32,3,128,128]{3,2,1,0:T(8,128)(2,1)} %bitcast.34), calls=%async_computation.3 | async-start | bytes 6291456 | tf_op jit(solution)/shard_map/all_to_all | solution.py:417
  207.7 32.3 %collective-permute-start.4 = (bf16[256,2560]{1,0:T(8,128)(2,1)}, bf16[256,2560]{1,0:T(8,128)(2,1)}, u32[]{:S(2)}, u32[]{:S(2)}) collective-permute-start(bf16[256,2560]{1,0:T(8,128)(2,1)} %sum_keys.1), channel_id=1, source_target_pairs={{0,7},{1,0},{2,1},{3,2},{4,3},{5,4},{6,5},{7,6},{8,15},{9,8},{10,9... | collective-permute-start | bytes 3932168 | tf_op jit(solution)/shard_map/ppermute | solution.py:25

commit v6 on v5

--- a/solution.py
+++ b/solution.py
@@ -99,22 +99,28 @@
     send_columns(ready, total, sent, sent.shape[0], fill)
 
 
-def last_kernel(
-    parts, codes, keys, terms, key_out, total, wide, ready, key_held, sent, key_got, put
+def join_kernel(
+    parts, codes, head_part, terms, after, total, wide, ready, head, sent, got
 ):
-    key_in = copy(keys, key_held, key_got)
-    key_in.start()
+    head_copy = copy(head_part, head, got)
+    head_copy.start()
     add_terms(codes, terms, wide, parts)
-    key_in.wait()
-    key_copy = copy(key_held, key_out, put)
-    key_copy.start()
-    rows = total.shape[0]
+    head_copy.wait()
+    tail_rows = terms.shape[1]
+    head_rows = total.shape[0] // 2 - tail_rows
 
     def fill(columns):
-        ready[:, columns] = wide[:rows, columns].astype(ready.dtype)
+        for block in range(2):
+            start = block * (head_rows + tail_rows)
+            middle = start + head_rows
+            ready[start:middle, columns] = head[
+                block * head_rows : (block + 1) * head_rows, columns
+            ]
+            ready[middle : middle + tail_rows, columns] = wide[
+                block * tail_rows : (block + 1) * tail_rows, columns
+            ].astype(ready.dtype)
 
     send_columns(ready, total, sent, sent.shape[0], fill)
-    key_copy.wait()
 
 
 def place_kernel(source, out):
@@ -253,8 +259,8 @@
 def key_kernel(
     list_size, group, scale, places, lengths, queries, grads, keys, values, weights,
     query_grad, terms,
-    query_held, grad_held, key_held, weights_held, made, query_made,
-    query_sem, grad_sem, key_sem, weights_sem, out_sem, query_out_sem,
+    query_held, grad_held, key_held, value_held, weights_held, made, query_made,
+    query_sem, grad_sem, key_sem, value_sem, weights_sem, out_sem, query_out_sem,
 ):
     rows, cols = keys.shape[1:]
     groups = lengths.shape[0] // group
@@ -278,6 +284,10 @@
         where = pl.ds(part * step, step)
         return copy(keys.at[where], key_held.at[where], key_sem.at[part])
 
+    def value_part(part):
+        where = pl.ds(part * step, step)
+        return copy(values.at[where], value_held.at[where], value_sem.at[part])
+
     def made_part(part):
         where = pl.ds(part * step, step)
         return copy(made.at[where], terms.at[where], out_sem.at[part])
@@ -291,13 +301,15 @@
     for one in fetches(0):
         one.start()
     for part in range(parts):
+        value_part(part).start()
+    for part in range(parts):
         key_part(part).start()
 
     def compute(head):
         columns = pl.ds(pl.multiple_of(head * cols, cols), cols)
         where = [places[head * list_size + item] for item in range(list_size)]
         key = jnp.concatenate([key_held[place] for place in where], axis=0)
-        value = jnp.concatenate([values[place] for place in where], axis=0)
+        value = jnp.concatenate([value_held[place] for place in where], axis=0)
         weight = weights_held[head]
         weight_low = weight.astype(jnp.bfloat16).astype(jnp.float32)
         dweights = lax.dot_general(
@@ -324,6 +336,7 @@
         @pl.when(index == 0)
         def _():
             for part in range(parts):
+                value_part(part).wait()
                 key_part(part).wait()
 
         results = [compute(index * group + item) for item in range(group)]
@@ -397,7 +410,7 @@
     places = my_holder * capacity + my_rank
     places = jnp.where(my_used, places, places[:, :1]).reshape(entries)
 
-    first_rows = block_rows // 2
+    first_rows = 3 * block_rows // 8
     last_rows = block_rows - first_rows
     add_parts = 8 if slots % 8 == 0 else 1
     send_parts = 5 if head_count % 5 == 0 else 1
@@ -433,6 +446,17 @@
 
     def wide_sum(rows):
         return pltpu.VMEM((3 * rows, column_count), jnp.float32)
+
+    def placed(name, value, cost):
+        return pl.pallas_call(
+            place_kernel,
+            out_shape=flat_shape,
+            in_specs=[VMEM],
+            out_specs=VMEM,
+            compiler_params=PARAMS,
+            cost_estimate=pl.CostEstimate(flops=0, transcendentals=0, bytes_accessed=cost),
+            name=name,
+        )(near(value))
 
     def add_up(name, returned):
         rows = returned.shape[1]
@@ -448,7 +472,7 @@
 
     tiles = vmem(entries, block_rows, head_dim)
     slot_tiles = vmem(slots, block_rows, head_dim)
-    wide_sem, tile_sem = dma((groups,)), dma((entries,))
+    wide_sem, tile_sem, part_sem = dma((groups,)), dma((entries,)), dma((add_parts,))
     fetched_keys = exchanged(pack("pack_keys", keys[0]))
     handed_codes = shifted(codes, "section", -1)
     packed_values, handed_codes = lax.optimization_barrier(
@@ -471,46 +495,40 @@
         compiler_params=PARAMS,
         name="value_terms",
     )(places, my_lengths, queries[0], out_grad[0], fetched_keys)
-    handed_first = shifted(first_terms, "section", -1)
+    handed_terms = shifted(last_terms, "section", -1)
     query_grad, key_terms = pl.pallas_call(
         functools.partial(key_kernel, list_size, group, scale),
         out_shape=(flat_shape, packed_shape(block_rows)),
-        in_specs=[SMEM, SMEM, ANY, ANY, ANY, VMEM, ANY],
+        in_specs=[SMEM, SMEM, ANY, ANY, ANY, ANY, ANY],
         out_specs=(ANY, ANY),
-        scratch_shapes=[flat, flat, slot_tiles, weights_tile, slot_tiles, flat]
-        + [wide_sem, wide_sem, dma((add_parts,)), wide_sem, dma((add_parts,)), wide_sem],
+        scratch_shapes=[flat, flat, slot_tiles, slot_tiles, weights_tile, slot_tiles, flat]
+        + [wide_sem, wide_sem, part_sem, part_sem, wide_sem, part_sem, wide_sem],
         compiler_params=PARAMS,
         name="key_terms",
-    )(places, my_lengths, queries[0], out_grad[0], fetched_keys, near(fetched_values), weights)
-    handed_queries = shifted(query_grad, "section", -1)
-    handed_last = shifted(last_terms, "section", -1)
-    key_terms, handed_first = lax.optimization_barrier((key_terms, handed_first))
+    )(places, my_lengths, queries[0], out_grad[0], fetched_keys, fetched_values, weights)
+    first_values = add_up("sum_values", exchanged(first_terms))
+    handed_first = shifted(first_values, "section", -1)
+    key_terms, handed_terms = lax.optimization_barrier((key_terms, handed_terms))
     returned_keys = exchanged(key_terms)
-    handed_terms = jnp.concatenate([handed_first, handed_last], axis=1)
-    handed_queries = pl.pallas_call(
-        place_kernel,
+    handed_queries = placed("place_queries", shifted(query_grad, "section", -1), 5000000)
+    returned_keys, handed_queries, first_values = lax.optimization_barrier(
+        (returned_keys, handed_queries, first_values)
+    )
+    key_grad = add_up("sum_keys", near(returned_keys))
+    key_grad, handed_terms, handed_first = lax.optimization_barrier(
+        (key_grad, handed_terms, handed_first)
+    )
+    handed_keys = placed("place_keys", shifted(key_grad, "section", -1), 5000000)
+    handed_values = pl.pallas_call(
+        functools.partial(join_kernel, add_parts),
         out_shape=flat_shape,
-        in_specs=[VMEM],
-        out_specs=VMEM,
+        in_specs=[SMEM, ANY, VMEM, ANY],
+        out_specs=ANY,
+        scratch_shapes=[wide_sum(last_rows), flat, vmem(2 * first_rows, column_count)]
+        + [dma((send_parts,)), dma],
         compiler_params=PARAMS,
-        name="place_queries",
-    )(near(handed_queries))
-    returned_keys, handed_queries, handed_terms = lax.optimization_barrier(
-        (returned_keys, handed_queries, handed_terms)
-    )
-    key_grad = add_up("sum_keys", near(returned_keys))
-    key_grad, handed_terms = lax.optimization_barrier((key_grad, handed_terms))
-    handed_keys = shifted(key_grad, "section", -1)
-    handed_keys, handed_values = pl.pallas_call(
-        functools.partial(last_kernel, add_parts),
-        out_shape=(flat_shape, flat_shape),
-        in_specs=[SMEM, ANY, VMEM],
-        out_specs=(ANY, ANY),
-        scratch_shapes=[wide_sum(block_rows), flat, flat]
-        + [dma((send_parts,)), dma, dma],
-        compiler_params=PARAMS,
-        name="last_values",
-    )(handed_codes, handed_keys, near(exchanged(handed_terms)))
+        name="join_values",
+    )(handed_codes, handed_first, near(exchanged(handed_terms)), handed_keys)
     return (handed_queries[None], handed_keys[None], handed_values[None])
 
 

time: 253 us -> 225 us (0.89)
  waiting for transfers between devices: 148 us -> 111 us
  starting transfers between devices: 46.8 us -> 52.6 us
  Pallas kernels: 43.9 us -> 48.2 us
  other arithmetic: 7.37 us -> 4 us
    ppermute x5, waiting for transfers between devices: 95.1 us -> 60.8 us  [shifted(): return lax.ppermute(value, axis, pairs)]
    all_to_all x4 -> x5, starting transfers between devices: 27.5 us -> 33.1 us  [exchanged(): lax.all_to_all(parts, 'ctx', split_axis=0, concat_axis=0, tiled=True)]
    concatenate x1 -> x0, other arithmetic: 3.37 us -> none  [local(): handed_terms = jnp.concatenate([handed_first, handed_last], axis=1)]
    pallas_call x1 -> x2, Pallas kernels: 3.26 us -> 6.22 us  [add_up(): pl.pallas_call(functools.partial(sum_kernel, add_parts), out_shape=jax.Sh...]
    all_to_all x4 -> x5, waiting for transfers between devices: 52.4 us -> 50.6 us  [exchanged(): lax.all_to_all(parts, 'ctx', split_axis=0, concat_axis=0, tiled=True)]
    pallas_call x2 -> x3, Pallas kernels: 4.76 us -> 5.14 us  [the longest x1 2.86 us: local(): pl.pallas_call(functools.partial(join_kernel, add_parts), out_shape=flat_...]
  transfers between devices with their start and end apart: 9 -> 10, of which waited for: 6 -> 7; matrix products, arithmetic and copies ran while one was open for 3% -> 2% of each run, Pallas kernels for 13% -> 19%
where the time goes in v6:
time: 225 us; the launch traced here: 223 us
  waiting for transfers between devices  111 us (49%)
  starting transfers between devices  52.6 us (23%)
  Pallas kernels  48.2 us (21%)
  local copies, waits for them, and re-layouts  6.09 us (3%)
  other arithmetic  4 us (2%)
    ppermute x5, waiting for transfers between devices, shifted(): return lax.ppermute(value, axis, pairs)  60.8 us
    all_to_all x5, waiting for transfers between devices, exchanged(): lax.all_to_all(parts, 'ctx', split_axis=0, concat_axis=0, tiled=True)  50.6 us
    all_to_all x5, starting transfers between devices, exchanged(): lax.all_to_all(parts, 'ctx', split_axis=0, concat_axis=0, tiled=True)  33.1 us
    ppermute x5, starting transfers between devices, shifted(): return lax.ppermute(value, axis, pairs)  19.5 us
    pallas_call x1, Pallas kernels, local(): pl.pallas_call(functools.partial(key_kernel, list_size, group, scale), ou...  15.5 us
    pallas_call x1, Pallas kernels, local(): pl.pallas_call(functools.partial(value_kernel, list_size, group, scale),...  13.6 us
    pallas_call x2, Pallas kernels, pack(): pl.pallas_call(functools.partial(pack_kernel, add_parts), out_shape=packe...  7.68 us
    pallas_call x2, Pallas kernels, add_up(): pl.pallas_call(functools.partial(sum_kernel, add_parts), out_shape=jax.Sh...  6.22 us
  transfers between devices with their start and end apart: 10, of which 7 were waited for; matrix products, arithmetic and copies ran while one was open for 2% of the time, Pallas kernels for 19%

profile of v6, /device:TPU:8, one launch (start us, length us, event | category | flops | bytes accessed | tf_op | source)
XLA Modules:
  0.0 223.3 jit_solution(14868842172311725615)
XLA Ops:
  0.7 0.7 copy.40
  1.4 0.8 fusion
  2.2 0.2 select_reduce_fusion
  2.4 0.1 copy.37
  2.5 0.7 reshape.173.codes
  3.2 3.8 %pack_keys.1 = bf16[96,128,128]{2,1,0:T(8,128)(2,1)} custom-call(s32[96]{0:T(128)} %reshape.173.codes, bf16[256,2560]{1,0:T(8,128)(2,1)} %bitcast.44), custom_call_target="tpu_custom_call" | custom-call | tf_op jit(solution)/shard_map/pack_keys/pallas_call | solution.py:434
  7.0 7.5 %all-to-all-start = ((bf16[32,3,128,128]{3,2,1,0:T(8,128)(2,1)}), bf16[32,3,128,128]{3,2,1,0:T(8,128)(2,1)S(1)}, u32[]{:S(2)}, u32[]{:S(2)}) async-start(bf16[32,3,128,128]{3,2,1,0:T(8,128)(2,1)} %bitcast.35), calls=%async_computation | async-start | bytes 6291456 | tf_op jit(solution)/shard_map/all_to_all | solution.py:430
  14.5 5.9 %collective-permute-start = (s32[96]{0:T(128)S(1)}, s32[96]{0:T(128)S(1)}, u32[]{:S(2)}, u32[]{:S(2)}) collective-permute-start(s32[96]{0:T(128)S(1)} %copy-done.7), channel_id=1, source_target_pairs={{0,7},{1,0},{2,1},{3,2},{4,3},{5,4},{6,5},{7,6},{8,15},{9,8},{10,9... | collective-permute-start | bytes 1160 | tf_op jit(solution)/shard_map/ppermute | solution.py:25
  20.5 3.9 %pack_values.1 = bf16[96,128,128]{2,1,0:T(8,128)(2,1)} custom-call(s32[96]{0:T(128)} %reshape.173.codes, bf16[256,2560]{1,0:T(8,128)(2,1)} %bitcast.45), custom_call_target="tpu_custom_call" | custom-call | tf_op jit(solution)/shard_map/pack_values/pallas_call | solution.py:434
  24.4 29.6 %all-to-all-done = bf16[32,3,128,128]{3,2,1,0:T(8,128)(2,1)S(1)} async-done(((bf16[32,3,128,128]{3,2,1,0:T(8,128)(2,1)}), bf16[32,3,128,128]{3,2,1,0:T(8,128)(2,1)S(1)}, u32[]{:S(2)}, u32[]{:S(2)}) %all-to-all-start) | async-done | bytes 3145760 | tf_op jit(solution)/shard_map/all_to_all | solution.py:430
  54.1 1.6 copy-done
  55.7 5.3 %all-to-all-start.1 = ((bf16[32,3,128,128]{3,2,1,0:T(8,128)(2,1)}), bf16[32,3,128,128]{3,2,1,0:T(8,128)(2,1)}, u32[]{:S(2)}, u32[]{:S(2)}) async-start(bf16[32,3,128,128]{3,2,1,0:T(8,128)(2,1)} %bitcast.34), calls=%async_computation.1 | async-start | bytes 6291456 | tf_op jit(solution)/shard_map/all_to_all | solution.py:430
  61.0 0.5 dynamic-slice_reduce_fusion.lengths
  61.6 0.1 lt.98
  61.7 0.5 fusion.6
  62.2 0.1 shift_right_arithmetic.24
  62.3 0.1 copy.35
  62.4 0.1 fusion.1
  62.5 0.1 copy.34
  62.6 0.1 copy.36
  62.7 0.1 broadcast_select_fusion
  62.8 1.6 select_reduce_fusion.1
  64.4 0.1 reduce_sum.30
  64.5 0.1 fusion.5
  64.7 0.1 broadcast_in_dim.83
  64.8 0.5 add_select_fusion.places
  65.3 13.6 %value_terms.1 = (bf16[96,48,128]{2,1,0:T(8,128)(2,1)}, bf16[96,80,128]{2,1,0:T(8,128)(2,1)}, f32[20,512,256]{2,1,0:T(8,128)}) custom-call(s32[80]{0:T(128)} %add_select_fusion.places, s32[20]{0:T(128)} %copy-done.6, bf16[256,2560]{1,0:T(8,128)(2,1)} %bitcast.36, bf16[256,2560]{1,0:T(8,128)(2,1)} %bitcast.38, bf16[96,128,128]{2,1,0:T(8,128)(2,1)} %bitcast.32), custom_call_target="tpu_custom_call" | custom-call | tf_op jit(solution)/shard_map/value_terms/pallas_call | solution.py:484
  78.9 5.9 %collective-permute-start.1 = (bf16[96,80,128]{2,1,0:T(8,128)(2,1)}, bf16[96,80,128]{2,1,0:T(8,128)(2,1)S(1)}, u32[]{:S(2)}, u32[]{:S(2)}) collective-permute-start(bf16[96,80,128]{2,1,0:T(8,128)(2,1)} %get-tuple-element.20), channel_id=1, source_target_pairs={{0,7},{1,0},{2,1},{3,2},{4,3},{5,4},{6,5},{7,6},{8,15},{9,8},{10,9... | collective-permute-start | bytes 5898248 | tf_op jit(solution)/shard_map/ppermute | solution.py:25
  84.8 15.7 %all-to-all-done.1 = bf16[32,3,128,128]{3,2,1,0:T(8,128)(2,1)} async-done(((bf16[32,3,128,128]{3,2,1,0:T(8,128)(2,1)}), bf16[32,3,128,128]{3,2,1,0:T(8,128)(2,1)}, u32[]{:S(2)}, u32[]{:S(2)}) %all-to-all-start.1) | async-done | bytes 3145760 | tf_op jit(solution)/shard_map/all_to_all | solution.py:430
  100.5 5.2 %all-to-all-start.3 = ((bf16[32,3,48,128]{3,2,1,0:T(8,128)(2,1)}), bf16[32,3,48,128]{3,2,1,0:T(8,128)(2,1)S(1)}, u32[]{:S(2)}, u32[]{:S(2)}) async-start(bf16[32,3,48,128]{3,2,1,0:T(8,128)(2,1)} %bitcast.48), calls=%async_computation.3 | async-start | bytes 2359296 | tf_op jit(solution)/shard_map/all_to_all | solution.py:430
  105.8 15.5 %key_terms.1 = (bf16[256,2560]{1,0:T(8,128)(2,1)}, bf16[96,128,128]{2,1,0:T(8,128)(2,1)}) custom-call(s32[80]{0:T(128)} %add_select_fusion.places, s32[20]{0:T(128)} %copy-done.6, bf16[256,2560]{1,0:T(8,128)(2,1)} %bitcast.37, bf16[256,2560]{1,0:T(8,128)(2,1)} %bitcast.39, bf16[96,128,128]{2,1,0:T(8,128)(2,1)} %bitcast.33, ...), custom_call_target="tpu_custom_call" | custom-call | tf_op jit(solution)/shard_map/key_terms/pallas_call | solution.py:499
  121.3 6.2 %collective-permute-done.1 = bf16[96,80,128]{2,1,0:T(8,128)(2,1)S(1)} collective-permute-done((bf16[96,80,128]{2,1,0:T(8,128)(2,1)}, bf16[96,80,128]{2,1,0:T(8,128)(2,1)S(1)}, u32[]{:S(2)}, u32[]{:S(2)}) %collective-permute-start.1) | collective-permute-done | bytes 1966112 | tf_op jit(solution)/shard_map/ppermute | solution.py:25
  127.5 1.3 copy-done.2
  128.8 0.3 copy-done.1
  129.2 7.4 %all-to-all-start.2 = ((bf16[32,3,128,128]{3,2,1,0:T(8,128)(2,1)}), bf16[32,3,128,128]{3,2,1,0:T(8,128)(2,1)S(1)}, u32[]{:S(2)}, u32[]{:S(2)}) async-start(bf16[32,3,128,128]{3,2,1,0:T(8,128)(2,1)} %bitcast.42), calls=%async_computation.2 | async-start | bytes 6291456 | tf_op jit(solution)/shard_map/all_to_all | solution.py:430
  136.6 3.7 %collective-permute-start.2 = (bf16[256,2560]{1,0:T(8,128)(2,1)}, bf16[256,2560]{1,0:T(8,128)(2,1)S(1)}, u32[]{:S(2)}, u32[]{:S(2)}) collective-permute-start(bf16[256,2560]{1,0:T(8,128)(2,1)} %get-tuple-element.22), channel_id=1, source_target_pairs={{0,7},{1,0},{2,1},{3,2},{4,3},{5,4},{6,5},{7,6},{8,15},{9,8},{10,9... | collective-permute-start | bytes 3932168 | tf_op jit(solution)/shard_map/ppermute | solution.py:25
  140.3 3.0 %sum_values.1 = bf16[96,2560]{1,0:T(8,128)(2,1)} custom-call(s32[96]{0:T(128)} %reshape.173.codes, bf16[96,48,128]{2,1,0:T(8,128)(2,1)} %bitcast.41), custom_call_target="tpu_custom_call" | custom-call | tf_op jit(solution)/shard_map/sum_values/pallas_call | solution.py:463
  143.3 0.3 collective-permute-start.3
  143.5 26.2 %collective-permute-done.2.source = bf16[256,2560]{1,0:T(8,128)(2,1)S(1)} collective-permute-done((bf16[256,2560]{1,0:T(8,128)(2,1)}, bf16[256,2560]{1,0:T(8,128)(2,1)S(1)}, u32[]{:S(2)}, u32[]{:S(2)}) %collective-permute-start.2) | collective-permute-done | bytes 1310752 | tf_op jit(solution)/shard_map/ppermute | solution.py:25
  169.7 1.1 place_queries.1
  170.9 5.2 %all-to-all-done.2 = bf16[32,3,128,128]{3,2,1,0:T(8,128)(2,1)S(1)} async-done(((bf16[32,3,128,128]{3,2,1,0:T(8,128)(2,1)}), bf16[32,3,128,128]{3,2,1,0:T(8,128)(2,1)S(1)}, u32[]{:S(2)}, u32[]{:S(2)}) %all-to-all-start.2) | async-done | bytes 3145760 | tf_op jit(solution)/shard_map/all_to_all | solution.py:430
  176.1 3.3 %sum_keys.1 = bf16[256,2560]{1,0:T(8,128)(2,1)} custom-call(s32[96]{0:T(128)} %reshape.173.codes, bf16[96,128,128]{2,1,0:T(8,128)(2,1)S(1)} %bitcast.30), custom_call_target="tpu_custom_call" | custom-call | tf_op jit(solution)/shard_map/sum_keys/pallas_call | solution.py:463
  179.4 0.1 collective-permute-done.3.head_part
  179.5 7.5 %all-to-all-start.4 = ((bf16[32,3,80,128]{3,2,1,0:T(8,128)(2,1)}), bf16[32,3,80,128]{3,2,1,0:T(8,128)(2,1)S(1)}, u32[]{:S(2)}, u32[]{:S(2)}) async-start(bf16[32,3,80,128]{3,2,1,0:T(8,128)(2,1)} %bitcast.43), calls=%async_computation.4 | async-start | bytes 3932160 | tf_op jit(solution)/shard_map/all_to_all | solution.py:430
  187.0 3.8 %collective-permute-start.4 = (bf16[256,2560]{1,0:T(8,128)(2,1)S(1)}, bf16[256,2560]{1,0:T(8,128)(2,1)S(1)}, u32[]{:S(2)}, u32[]{:S(2)}) collective-permute-start(bf16[256,2560]{1,0:T(8,128)(2,1)S(1)} %copy-done.3), channel_id=1, source_target_pairs={{0,7},{1,0},{2,1},{3,2},{4,3},{5,4},{6,5},{7,6},{8,15},{9,8},{10,9... | collective-permute-start | bytes 3932168 | tf_op jit(solution)/shard_map/ppermute | solution.py:25
  190.8 28.3 %collective-permute-done.4.source = bf16[256,2560]{1,0:T(8,128)(2,1)S(1)} collective-permute-done((bf16[256,2560]{1,0:T(8,128)(2,1)S(1)}, bf16[256,2560]{1,0:T(8,128)(2,1)S(1)}, u32[]{:S(2)}, u32[]{:S(2)}) %collective-permute-start.4) | collective-permute-done | bytes 1310752 | tf_op jit(solution)/shard_map/ppermute | solution.py:25
  219.1 1.1 place_keys.1.after
  220.3 2.9 %join_values.1 = bf16[256,2560]{1,0:T(8,128)(2,1)} custom-call(s32[96]{0:T(128)} %copy-done.8, bf16[96,2560]{1,0:T(8,128)(2,1)} %collective-permute-done.3.head_part, bf16[96,80,128]{2,1,0:T(8,128)(2,1)S(1)} %bitcast.31, bf16[256,2560]{1,0:T(8,128)(2,1)} %place_keys.1.after), custom_call_target="tpu_custom_call" | custom-call | tf_op jit(solution)/shard_map/join_values/pallas_call | solution.py:522
  (24 shorter events, 0.2 us)
Async XLA Ops:
  7.0 7.6 %copy-start.7 = (s32[96]{0:T(128)S(1)}, s32[96]{0:T(128)}, u32[]{:S(2)}) copy-start(s32[96]{0:T(128)} %reshape.173.codes) | copy-start | bytes 1156
  7.0 47.1 %all-to-all-start = ((bf16[32,3,128,128]{3,2,1,0:T(8,128)(2,1)}), bf16[32,3,128,128]{3,2,1,0:T(8,128)(2,1)S(1)}, u32[]{:S(2)}, u32[]{:S(2)}) async-start(bf16[32,3,128,128]{3,2,1,0:T(8,128)(2,1)} %bitcast.35), calls=%async_computation | async-start | bytes 6291456 | tf_op jit(solution)/shard_map/all_to_all | solution.py:430
  14.5 9.8 %collective-permute-start = (s32[96]{0:T(128)S(1)}, s32[96]{0:T(128)S(1)}, u32[]{:S(2)}, u32[]{:S(2)}) collective-permute-start(s32[96]{0:T(128)S(1)} %copy-done.7), channel_id=1, source_target_pairs={{0,7},{1,0},{2,1},{3,2},{4,3},{5,4},{6,5},{7,6},{8,15},{9,8},{10,9... | collective-permute-start | bytes 1160 | tf_op jit(solution)/shard_map/ppermute | solution.py:25
  24.4 29.7 %copy-start.8 = (s32[96]{0:T(128)}, s32[96]{0:T(128)S(1)}, u32[]{:S(2)}) copy-start(s32[96]{0:T(128)S(1)} %collective-permute-done.codes) | copy-start | bytes 1156
  54.0 1.6 copy-start
  54.0 7.0 %copy-start.5 = (s32[1,32,20]{1,0,2:T(1,128)S(1)}, s32[1,32,20]{1,0,2:T(1,128)}, u32[]{:S(2)}) copy-start(s32[1,32,20]{1,0,2:T(1,128)} %param.11) | copy-start | bytes 7684
  54.0 7.7 %copy-start.4 = (s32[1,32,20,4]{1,3,2,0:T(4,128)S(1)}, s32[1,32,20,4]{1,3,2,0:T(4,128)}, u32[]{:S(2)}) copy-start(s32[1,32,20,4]{1,3,2,0:T(4,128)} %param.10) | copy-start | bytes 30724
  55.7 44.9 %all-to-all-start.1 = ((bf16[32,3,128,128]{3,2,1,0:T(8,128)(2,1)}), bf16[32,3,128,128]{3,2,1,0:T(8,128)(2,1)}, u32[]{:S(2)}, u32[]{:S(2)}) async-start(bf16[32,3,128,128]{3,2,1,0:T(8,128)(2,1)} %bitcast.34), calls=%async_computation.1 | async-start | bytes 6291456 | tf_op jit(solution)/shard_map/all_to_all | solution.py:430
  61.5 3.8 %copy-start.6 = (s32[20]{0:T(128)}, s32[20]{0:T(128)S(1)}, u32[]{:S(2)}) copy-start(s32[20]{0:T(128)S(1)} %dynamic-slice_reduce_fusion.lengths) | copy-start | bytes 244
  78.9 48.6 %collective-permute-start.1 = (bf16[96,80,128]{2,1,0:T(8,128)(2,1)}, bf16[96,80,128]{2,1,0:T(8,128)(2,1)S(1)}, u32[]{:S(2)}, u32[]{:S(2)}) collective-permute-start(bf16[96,80,128]{2,1,0:T(8,128)(2,1)} %get-tuple-element.20), channel_id=1, source_target_pairs={{0,7},{1,0},{2,1},{3,2},{4,3},{5,4},{6,5},{7,6},{8,15},{9,8},{10,9... | collective-permute-start | bytes 5898248 | tf_op jit(solution)/shard_map/ppermute | solution.py:25
  100.5 27.0 %all-to-all-start.3 = ((bf16[32,3,48,128]{3,2,1,0:T(8,128)(2,1)}), bf16[32,3,48,128]{3,2,1,0:T(8,128)(2,1)S(1)}, u32[]{:S(2)}, u32[]{:S(2)}) async-start(bf16[32,3,48,128]{3,2,1,0:T(8,128)(2,1)} %bitcast.48), calls=%async_computation.3 | async-start | bytes 2359296 | tf_op jit(solution)/shard_map/all_to_all | solution.py:430
  127.5 1.3 copy-start.2
  127.5 1.7 copy-start.1
  129.2 47.0 %all-to-all-start.2 = ((bf16[32,3,128,128]{3,2,1,0:T(8,128)(2,1)}), bf16[32,3,128,128]{3,2,1,0:T(8,128)(2,1)S(1)}, u32[]{:S(2)}, u32[]{:S(2)}) async-start(bf16[32,3,128,128]{3,2,1,0:T(8,128)(2,1)} %bitcast.42), calls=%async_computation.2 | async-start | bytes 6291456 | tf_op jit(solution)/shard_map/all_to_all | solution.py:430
  136.6 33.1 %collective-permute-start.2 = (bf16[256,2560]{1,0:T(8,128)(2,1)}, bf16[256,2560]{1,0:T(8,128)(2,1)S(1)}, u32[]{:S(2)}, u32[]{:S(2)}) collective-permute-start(bf16[256,2560]{1,0:T(8,128)(2,1)} %get-tuple-element.22), channel_id=1, source_target_pairs={{0,7},{1,0},{2,1},{3,2},{4,3},{5,4},{6,5},{7,6},{8,15},{9,8},{10,9... | collective-permute-start | bytes 3932168 | tf_op jit(solution)/shard_map/ppermute | solution.py:25
  143.3 36.2 %collective-permute-start.3 = (bf16[96,2560]{1,0:T(8,128)(2,1)}, bf16[96,2560]{1,0:T(8,128)(2,1)}, u32[]{:S(2)}, u32[]{:S(2)}) collective-permute-start(bf16[96,2560]{1,0:T(8,128)(2,1)} %sum_values.1), channel_id=1, source_target_pairs={{0,7},{1,0},{2,1},{3,2},{4,3},{5,4},{6,5},{7,6},{8,15},{9,8},{10,9... | collective-permute-start | bytes 1474568 | tf_op jit(solution)/shard_map/ppermute | solution.py:25
  179.5 7.5 %copy-start.3 = (bf16[256,2560]{1,0:T(8,128)(2,1)S(1)}, bf16[256,2560]{1,0:T(8,128)(2,1)}, u32[]{:S(2)}) copy-start(bf16[256,2560]{1,0:T(8,128)(2,1)} %sum_keys.1) | copy-start | bytes 3932164
  179.5 40.8 %all-to-all-start.4 = ((bf16[32,3,80,128]{3,2,1,0:T(8,128)(2,1)}), bf16[32,3,80,128]{3,2,1,0:T(8,128)(2,1)S(1)}, u32[]{:S(2)}, u32[]{:S(2)}) async-start(bf16[32,3,80,128]{3,2,1,0:T(8,128)(2,1)} %bitcast.43), calls=%async_computation.4 | async-start | bytes 3932160 | tf_op jit(solution)/shard_map/all_to_all | solution.py:430
  187.0 32.1 %collective-permute-start.4 = (bf16[256,2560]{1,0:T(8,128)(2,1)S(1)}, bf16[256,2560]{1,0:T(8,128)(2,1)S(1)}, u32[]{:S(2)}, u32[]{:S(2)}) collective-permute-start(bf16[256,2560]{1,0:T(8,128)(2,1)S(1)} %copy-done.3), channel_id=1, source_target_pairs={{0,7},{1,0},{2,1},{3,2},{4,3},{5,4},{6,5},{7,6},{8,15},{9,8},{10,9... | collective-permute-start | bytes 3932168 | tf_op jit(solution)/shard_map/ppermute | solution.py:25

commit v7 on v6

--- a/solution.py
+++ b/solution.py
@@ -100,7 +100,7 @@
 
 
 def join_kernel(
-    parts, codes, head_part, terms, after, total, wide, ready, head, sent, got
+    parts, codes, head_part, terms, total, wide, ready, head, sent, got
 ):
     head_copy = copy(head_part, head, got)
     head_copy.start()
@@ -123,6 +123,10 @@
     send_columns(ready, total, sent, sent.shape[0], fill)
 
 
+def place_last_kernel(source, after, out):
+    out[...] = source[...]
+
+
 def place_kernel(source, out):
     out[...] = source[...]
 
@@ -139,103 +143,57 @@
     return [part * (inverse * keep) for keep, part in zip(kept, parts)]
 
 
-class Grouped:
-    def __init__(self, places, lengths, list_size, group, cols):
-        self.places, self.lengths = places, lengths
-        self.list_size, self.group, self.cols = list_size, group, cols
-        self.groups = lengths.shape[0] // group
-
-    def head(self, head):
-        return pl.ds(pl.multiple_of(head * self.cols, self.cols), self.cols)
-
-    def wide(self, index, source, held, sems):
-        width = self.group * self.cols
-        columns = pl.ds(pl.multiple_of(index * width, width), width)
-        return copy(source.at[:, columns], held.at[:, columns], sems.at[index])
-
-    def block(self, index, source, held, sems):
-        where = pl.ds(index * self.group, self.group)
-        return copy(source.at[where], held.at[where], sems.at[index])
-
-    def fetches(self, index, sources, tiles, blocks):
-        made = [self.wide(index, *source) for source in sources]
-        made += [self.block(index, *source) for source in blocks]
-        count = self.group * self.list_size
-        for item in range(count):
-            entry = index * count + item
-            for source, held, sems in tiles:
-                made.append(
-                    copy(source.at[self.places[entry]], held.at[entry], sems.at[entry])
-                )
-        return made
-
-    def puts(self, entry, made, outs, sems):
-        start, copies = 0, []
-        for which, out in enumerate(outs):
-            count = out.shape[1]
-            copies.append(
-                copy(
-                    made.at[entry, pl.ds(start, count)],
-                    out.at[self.places[entry]],
-                    sems.at[which, entry],
-                )
-            )
-            start += count
-        return copies
-
-    def each_put(self, head, made, outs, sems, act):
-        for item in range(self.list_size):
-
-            @pl.when(item < self.lengths[head])
-            def _():
-                for one in self.puts(head * self.list_size + item, made, outs, sems):
-                    act(one)
-
-    def run(self, sources, tiles, blocks, made, outs, sems, compute, finish):
-        def start(index):
-            for one in self.fetches(index, sources, tiles, blocks):
-                one.start()
-
-        start(0)
-
-        def one_group(index, carry):
-            @pl.when(index + 1 < self.groups)
-            def _():
-                start(index + 1)
-
-            for one in self.fetches(index, sources, tiles, blocks):
-                one.wait()
-            for item in range(self.group):
-                head = index * self.group + item
-                terms = compute(head)
-                entries = pl.ds(head * self.list_size, self.list_size)
-                made[entries] = terms.reshape(self.list_size, -1, self.cols)
-                self.each_put(head, made, outs, sems, lambda one: one.start())
-            finish(index).start()
-            return carry
-
-        lax.fori_loop(0, self.groups, one_group, 0)
-
-        def last(head, carry):
-            self.each_put(head, made, outs, sems, lambda one: one.wait())
-            return carry
-
-        lax.fori_loop(0, self.lengths.shape[0], last, 0)
-        for index in range(self.groups):
-            finish(index).wait()
+def in_parts(source, target, sems):
+    parts = sems.shape[0]
+    step = source.shape[0] // parts
+    wheres = [pl.ds(part * step, step) for part in range(parts)]
+    return [
+        copy(source.at[where], target.at[where], sems.at[part])
+        for part, where in enumerate(wheres)
+    ]
+
+
+def put_terms(places, lengths, list_size, head, result, outs):
+    rows = result.shape[0] // list_size
+    for entry in range(list_size):
+
+        @pl.when(entry < lengths[head])
+        def _():
+            start = entry * rows
+            for out in outs:
+                count = out.shape[1]
+                out[places[head * list_size + entry]] = result[start : start + count]
+                start += count
 
 
 def value_kernel(
     list_size, group, scale, places, lengths, queries, grads, keys, first, last, weights_out,
-    query_held, grad_held, key_held, made, weights_made,
-    query_sem, grad_sem, key_sem, out_sem, weights_sem,
+    query_held, grad_held, key_held, first_made, last_made, weights_made,
+    query_sem, grad_sem, key_sem, first_sem, last_sem, weights_sem,
 ):
     rows, cols = keys.shape[1:]
-    walk = Grouped(places, lengths, list_size, group, cols)
+    groups = lengths.shape[0] // group
+    width = group * cols
+
+    def fetches(index):
+        columns = pl.ds(pl.multiple_of(index * width, width), width)
+        return [
+            copy(queries.at[:, columns], query_held.at[:, columns], query_sem.at[index]),
+            copy(grads.at[:, columns], grad_held.at[:, columns], grad_sem.at[index]),
+        ]
+
+    def weights_part(index):
+        heads = pl.ds(index * group, group)
+        return copy(weights_made.at[heads], weights_out.at[heads], weights_sem.at[index])
+
+    for one in fetches(0) + in_parts(keys, key_held, key_sem):
+        one.start()
 
     def compute(head):
-        columns = walk.head(head)
-        key = key_held[pl.ds(head * list_size, list_size)].reshape(-1, cols)
+        columns = pl.ds(pl.multiple_of(head * cols, cols), cols)
+        key = jnp.concatenate(
+            [key_held[places[head * list_size + item]] for item in range(list_size)], axis=0
+        )
         weights = weights_of(query_held[:, columns], key, lengths[head], list_size, scale)
         for item, part in enumerate(weights):
             weights_made[head, item * rows : (item + 1) * rows] = part
@@ -244,16 +202,36 @@
             weights_low, grad_held[:, columns], NN, preferred_element_type=jnp.float32
         ).astype(jnp.bfloat16)
 
-    walk.run(
-        [(queries, query_held, query_sem), (grads, grad_held, grad_sem)],
-        [(keys, key_held, key_sem)],
-        [],
-        made,
-        [first, last],
-        out_sem,
-        compute,
-        lambda index: walk.block(index, weights_made, weights_out, weights_sem),
-    )
+    def one_group(index, carry):
+        @pl.when(index + 1 < groups)
+        def _():
+            for one in fetches(index + 1):
+                one.start()
+
+        for one in fetches(index):
+            one.wait()
+
+        @pl.when(index == 0)
+        def _():
+            for one in in_parts(keys, key_held, key_sem):
+                one.wait()
+
+        results = [compute(index * group + item) for item in range(group)]
+        weights_part(index).start()
+        for item, result in enumerate(results):
+            put_terms(
+                places, lengths, list_size, index * group + item, result, [first_made, last_made]
+            )
+        return carry
+
+    lax.fori_loop(0, groups, one_group, 0)
+    ends = in_parts(last_made, last, last_sem) + in_parts(first_made, first, first_sem)
+    for one in ends:
+        one.start()
+    for index in range(groups):
+        weights_part(index).wait()
+    for one in ends:
+        one.wait()
 
 
 def key_kernel(
@@ -262,10 +240,8 @@
     query_held, grad_held, key_held, value_held, weights_held, made, query_made,
     query_sem, grad_sem, key_sem, value_sem, weights_sem, out_sem, query_out_sem,
 ):
-    rows, cols = keys.shape[1:]
+    cols = keys.shape[2]
     groups = lengths.shape[0] // group
-    parts = out_sem.shape[0]
-    step = keys.shape[0] // parts
     width = group * cols
 
     def columns_of(index):
@@ -280,17 +256,8 @@
             copy(queries.at[:, columns], query_held.at[:, columns], query_sem.at[index]),
         ]
 
-    def key_part(part):
-        where = pl.ds(part * step, step)
-        return copy(keys.at[where], key_held.at[where], key_sem.at[part])
-
-    def value_part(part):
-        where = pl.ds(part * step, step)
-        return copy(values.at[where], value_held.at[where], value_sem.at[part])
-
-    def made_part(part):
-        where = pl.ds(part * step, step)
-        return copy(made.at[where], terms.at[where], out_sem.at[part])
+    def tile_fetches():
+        return in_parts(values, value_held, value_sem) + in_parts(keys, key_held, key_sem)
 
     def query_part(index):
         columns = columns_of(index)
@@ -298,12 +265,8 @@
             query_made.at[:, columns], query_grad.at[:, columns], query_out_sem.at[index]
         )
 
-    for one in fetches(0):
+    for one in fetches(0) + tile_fetches():
         one.start()
-    for part in range(parts):
-        value_part(part).start()
-    for part in range(parts):
-        key_part(part).start()
 
     def compute(head):
         columns = pl.ds(pl.multiple_of(head * cols, cols), cols)
@@ -335,31 +298,23 @@
 
         @pl.when(index == 0)
         def _():
-            for part in range(parts):
-                value_part(part).wait()
-                key_part(part).wait()
+            for one in tile_fetches():
+                one.wait()
 
         results = [compute(index * group + item) for item in range(group)]
         query_part(index).start()
         for item, result in enumerate(results):
-            head = index * group + item
-            for entry in range(list_size):
-
-                @pl.when(entry < lengths[head])
-                def _():
-                    made[places[head * list_size + entry]] = result[
-                        entry * rows : (entry + 1) * rows
-                    ]
-
+            put_terms(places, lengths, list_size, index * group + item, result, [made])
         return carry
 
     lax.fori_loop(0, groups, one_group, 0)
-    for part in range(parts):
-        made_part(part).start()
+    ends = in_parts(made, terms, out_sem)
+    for one in ends:
+        one.start()
     for index in range(groups):
         query_part(index).wait()
-    for part in range(parts):
-        made_part(part).wait()
+    for one in ends:
+        one.wait()
 
 
 def local(queries, keys, values, out_grad, key_blocks, list_lengths):
@@ -470,13 +425,12 @@
             name=name,
         )(codes, returned)
 
-    tiles = vmem(entries, block_rows, head_dim)
     slot_tiles = vmem(slots, block_rows, head_dim)
-    wide_sem, tile_sem, part_sem = dma((groups,)), dma((entries,)), dma((add_parts,))
+    wide_sem, part_sem = dma((groups,)), dma((add_parts,))
     fetched_keys = exchanged(pack("pack_keys", keys[0]))
     handed_codes = shifted(codes, "section", -1)
-    packed_values, handed_codes = lax.optimization_barrier(
-        (pack("pack_values", values[0]), handed_codes)
+    packed_values, handed_codes, places, my_lengths = lax.optimization_barrier(
+        (pack("pack_values", values[0]), handed_codes, places, my_lengths)
     )
     fetched_values = exchanged(packed_values)
     weights_shape = (head_count, list_size * block_rows, row_count)
@@ -490,8 +444,9 @@
         ),
         in_specs=[SMEM, SMEM, ANY, ANY, ANY],
         out_specs=(ANY, ANY, ANY),
-        scratch_shapes=[flat, flat, tiles, tiles, weights_tile]
-        + [wide_sem, wide_sem, tile_sem, dma((2, entries)), wide_sem],
+        scratch_shapes=[flat, flat, slot_tiles]
+        + [vmem(slots, rows, head_dim) for rows in (first_rows, last_rows)]
+        + [weights_tile, wide_sem, wide_sem, part_sem, part_sem, part_sem, wide_sem],
         compiler_params=PARAMS,
         name="value_terms",
     )(places, my_lengths, queries[0], out_grad[0], fetched_keys)
@@ -518,17 +473,25 @@
     key_grad, handed_terms, handed_first = lax.optimization_barrier(
         (key_grad, handed_terms, handed_first)
     )
-    handed_keys = placed("place_keys", shifted(key_grad, "section", -1), 5000000)
+    handed_keys = shifted(key_grad, "section", -1)
     handed_values = pl.pallas_call(
         functools.partial(join_kernel, add_parts),
         out_shape=flat_shape,
-        in_specs=[SMEM, ANY, VMEM, ANY],
+        in_specs=[SMEM, ANY, VMEM],
         out_specs=ANY,
         scratch_shapes=[wide_sum(last_rows), flat, vmem(2 * first_rows, column_count)]
         + [dma((send_parts,)), dma],
         compiler_params=PARAMS,
         name="join_values",
-    )(handed_codes, handed_first, near(exchanged(handed_terms)), handed_keys)
+    )(handed_codes, handed_first, near(exchanged(handed_terms)))
+    handed_keys = pl.pallas_call(
+        place_last_kernel,
+        out_shape=flat_shape,
+        in_specs=[VMEM, ANY],
+        out_specs=VMEM,
+        compiler_params=PARAMS,
+        name="place_keys",
+    )(near(handed_keys), handed_values)
     return (handed_queries[None], handed_keys[None], handed_values[None])
 
 

time: 225 us -> 218 us (0.969)
  waiting for transfers between devices: 111 us -> 105 us
  starting transfers between devices: 52.6 us -> 54.9 us
    ppermute x5, waiting for transfers between devices: 60.8 us -> 32 us  [shifted(): return lax.ppermute(value, axis, pairs)]
    all_to_all x5, waiting for transfers between devices: 50.6 us -> 72.6 us  [exchanged(): lax.all_to_all(parts, 'ctx', split_axis=0, concat_axis=0, tiled=True)]
    ppermute x5, starting transfers between devices: 19.5 us -> 22 us  [shifted(): return lax.ppermute(value, axis, pairs)]
  transfers between devices with their start and end apart: 10 -> 10, of which waited for: 7 -> 9; matrix products, arithmetic and copies ran while one was open for 2% -> 2% of each run, Pallas kernels for 19% -> 19%
where the time goes in v7:
time: 218 us; the launch traced here: 217 us
  waiting for transfers between devices  105 us (48%)
  starting transfers between devices  54.9 us (25%)
  Pallas kernels  46.8 us (21%)
  local copies, waits for them, and re-layouts  5.42 us (2%)
  other arithmetic  4 us (2%)
    all_to_all x5, waiting for transfers between devices, exchanged(): lax.all_to_all(parts, 'ctx', split_axis=0, concat_axis=0, tiled=True)  72.6 us
    all_to_all x5, starting transfers between devices, exchanged(): lax.all_to_all(parts, 'ctx', split_axis=0, concat_axis=0, tiled=True)  32.9 us
    ppermute x5, waiting for transfers between devices, shifted(): return lax.ppermute(value, axis, pairs)  32 us
    ppermute x5, starting transfers between devices, shifted(): return lax.ppermute(value, axis, pairs)  22 us
    pallas_call x1, Pallas kernels, local(): pl.pallas_call(functools.partial(key_kernel, list_size, group, scale), ou...  15.4 us
    pallas_call x1, Pallas kernels, local(): pl.pallas_call(functools.partial(value_kernel, list_size, group, scale),...  12.3 us
    pallas_call x2, Pallas kernels, pack(): pl.pallas_call(functools.partial(pack_kernel, add_parts), out_shape=packe...  7.69 us
    pallas_call x2, Pallas kernels, add_up(): pl.pallas_call(functools.partial(sum_kernel, add_parts), out_shape=jax.Sh...  6.21 us
  transfers between devices with their start and end apart: 10, of which 9 were waited for; matrix products, arithmetic and copies ran while one was open for 2% of the time, Pallas kernels for 19%

profile of v7, /device:TPU:8, one launch (start us, length us, event | category | flops | bytes accessed | tf_op | source)
XLA Modules:
  0.0 216.6 jit_solution(3702672264580277854)
XLA Ops:
  0.7 0.7 copy.40
  1.4 0.8 fusion
  2.2 0.2 select_reduce_fusion
  2.4 0.1 copy.34
  2.5 0.6 reshape.173.codes
  3.1 3.8 %pack_keys.1 = bf16[96,128,128]{2,1,0:T(8,128)(2,1)} custom-call(s32[96]{0:T(128)} %reshape.173.codes, bf16[256,2560]{1,0:T(8,128)(2,1)} %bitcast.44), custom_call_target="tpu_custom_call" | custom-call | tf_op jit(solution)/shard_map/pack_keys/pallas_call | solution.py:389
  7.0 7.7 %all-to-all-start = ((bf16[32,3,128,128]{3,2,1,0:T(8,128)(2,1)}), bf16[32,3,128,128]{3,2,1,0:T(8,128)(2,1)S(1)}, u32[]{:S(2)}, u32[]{:S(2)}) async-start(bf16[32,3,128,128]{3,2,1,0:T(8,128)(2,1)} %bitcast.34), calls=%async_computation | async-start | bytes 6291456 | tf_op jit(solution)/shard_map/all_to_all | solution.py:385
  14.7 5.9 %collective-permute-start = (s32[96]{0:T(128)S(1)}, s32[96]{0:T(128)S(1)}, u32[]{:S(2)}, u32[]{:S(2)}) collective-permute-start(s32[96]{0:T(128)S(1)} %copy-done.6), channel_id=1, source_target_pairs={{0,7},{1,0},{2,1},{3,2},{4,3},{5,4},{6,5},{7,6},{8,15},{9,8},{10,9... | collective-permute-start | bytes 1160 | tf_op jit(solution)/shard_map/ppermute | solution.py:25
  20.6 0.5 dynamic-slice_reduce_fusion.lengths
  21.2 0.1 lt.105
  21.3 0.5 fusion.6
  21.8 0.1 shift_right_arithmetic.25
  21.9 0.1 copy.36
  22.1 0.1 copy.35
  22.2 0.1 copy.37
  22.4 1.6 select_reduce_fusion.1
  24.0 0.1 reduce_sum.32
  24.1 0.1 fusion.5
  24.3 0.1 broadcast_in_dim.88
  24.4 0.5 add_select_fusion.places
  24.9 3.9 %pack_values.1 = bf16[96,128,128]{2,1,0:T(8,128)(2,1)} custom-call(s32[96]{0:T(128)} %reshape.173.codes, bf16[256,2560]{1,0:T(8,128)(2,1)} %bitcast.45), custom_call_target="tpu_custom_call" | custom-call | tf_op jit(solution)/shard_map/pack_values/pallas_call | solution.py:389
  28.8 25.3 %all-to-all-done = bf16[32,3,128,128]{3,2,1,0:T(8,128)(2,1)S(1)} async-done(((bf16[32,3,128,128]{3,2,1,0:T(8,128)(2,1)}), bf16[32,3,128,128]{3,2,1,0:T(8,128)(2,1)S(1)}, u32[]{:S(2)}, u32[]{:S(2)}) %all-to-all-start) | async-done | bytes 3145760 | tf_op jit(solution)/shard_map/all_to_all | solution.py:385
  54.2 1.6 copy-done
  55.8 5.3 %all-to-all-start.1 = ((bf16[32,3,128,128]{3,2,1,0:T(8,128)(2,1)}), bf16[32,3,128,128]{3,2,1,0:T(8,128)(2,1)}, u32[]{:S(2)}, u32[]{:S(2)}) async-start(bf16[32,3,128,128]{3,2,1,0:T(8,128)(2,1)} %bitcast.35), calls=%async_computation.1 | async-start | bytes 6291456 | tf_op jit(solution)/shard_map/all_to_all | solution.py:385
  61.1 12.3 %value_terms.1 = (bf16[96,48,128]{2,1,0:T(8,128)(2,1)}, bf16[96,80,128]{2,1,0:T(8,128)(2,1)}, f32[20,512,256]{2,1,0:T(8,128)}) custom-call(s32[80]{0:T(128)} %add_select_fusion.places, s32[20]{0:T(128)} %copy-done.5, bf16[256,2560]{1,0:T(8,128)(2,1)} %bitcast.36, bf16[256,2560]{1,0:T(8,128)(2,1)} %bitcast.38, bf16[96,128,128]{2,1,0:T(8,128)(2,1)} %bitcast.32), custom_call_target="tpu_custom_call" | custom-call | tf_op jit(solution)/shard_map/value_terms/pallas_call | solution.py:438
  73.4 5.9 %collective-permute-start.1 = (bf16[96,80,128]{2,1,0:T(8,128)(2,1)}, bf16[96,80,128]{2,1,0:T(8,128)(2,1)S(1)}, u32[]{:S(2)}, u32[]{:S(2)}) collective-permute-start(bf16[96,80,128]{2,1,0:T(8,128)(2,1)} %get-tuple-element.24), channel_id=1, source_target_pairs={{0,7},{1,0},{2,1},{3,2},{4,3},{5,4},{6,5},{7,6},{8,15},{9,8},{10,9... | collective-permute-start | bytes 5898248 | tf_op jit(solution)/shard_map/ppermute | solution.py:25
  79.4 21.3 %all-to-all-done.1 = bf16[32,3,128,128]{3,2,1,0:T(8,128)(2,1)} async-done(((bf16[32,3,128,128]{3,2,1,0:T(8,128)(2,1)}), bf16[32,3,128,128]{3,2,1,0:T(8,128)(2,1)}, u32[]{:S(2)}, u32[]{:S(2)}) %all-to-all-start.1) | async-done | bytes 3145760 | tf_op jit(solution)/shard_map/all_to_all | solution.py:385
  100.7 5.2 %all-to-all-start.3 = ((bf16[32,3,48,128]{3,2,1,0:T(8,128)(2,1)}), bf16[32,3,48,128]{3,2,1,0:T(8,128)(2,1)S(1)}, u32[]{:S(2)}, u32[]{:S(2)}) async-start(bf16[32,3,48,128]{3,2,1,0:T(8,128)(2,1)} %bitcast.48), calls=%async_computation.3 | async-start | bytes 2359296 | tf_op jit(solution)/shard_map/all_to_all | solution.py:385
  105.9 15.4 %key_terms.1 = (bf16[256,2560]{1,0:T(8,128)(2,1)}, bf16[96,128,128]{2,1,0:T(8,128)(2,1)}) custom-call(s32[80]{0:T(128)} %add_select_fusion.places, s32[20]{0:T(128)} %copy-done.5, bf16[256,2560]{1,0:T(8,128)(2,1)} %bitcast.37, bf16[256,2560]{1,0:T(8,128)(2,1)} %bitcast.39, bf16[96,128,128]{2,1,0:T(8,128)(2,1)} %bitcast.33, ...), custom_call_target="tpu_custom_call" | custom-call | tf_op jit(solution)/shard_map/key_terms/pallas_call | solution.py:454
  121.4 0.7 collective-permute-done.1
  122.1 0.7 all-to-all-done.3
  122.8 0.6 copy-done.2
  123.4 0.4 copy-done.1
  123.8 7.3 %all-to-all-start.2 = ((bf16[32,3,128,128]{3,2,1,0:T(8,128)(2,1)}), bf16[32,3,128,128]{3,2,1,0:T(8,128)(2,1)S(1)}, u32[]{:S(2)}, u32[]{:S(2)}) async-start(bf16[32,3,128,128]{3,2,1,0:T(8,128)(2,1)} %bitcast.42), calls=%async_computation.2 | async-start | bytes 6291456 | tf_op jit(solution)/shard_map/all_to_all | solution.py:385
  131.1 5.3 %collective-permute-start.2 = (bf16[256,2560]{1,0:T(8,128)(2,1)}, bf16[256,2560]{1,0:T(8,128)(2,1)S(1)}, u32[]{:S(2)}, u32[]{:S(2)}) collective-permute-start(bf16[256,2560]{1,0:T(8,128)(2,1)} %get-tuple-element.26), channel_id=1, source_target_pairs={{0,7},{1,0},{2,1},{3,2},{4,3},{5,4},{6,5},{7,6},{8,15},{9,8},{10,9... | collective-permute-start | bytes 3932168 | tf_op jit(solution)/shard_map/ppermute | solution.py:25
  136.4 2.9 %sum_values.1 = bf16[96,2560]{1,0:T(8,128)(2,1)} custom-call(s32[96]{0:T(128)} %reshape.173.codes, bf16[96,48,128]{2,1,0:T(8,128)(2,1)} %bitcast.41), custom_call_target="tpu_custom_call" | custom-call | tf_op jit(solution)/shard_map/sum_values/pallas_call | solution.py:418
  139.4 1.1 collective-permute-start.3
  140.4 25.4 %collective-permute-done.2.source = bf16[256,2560]{1,0:T(8,128)(2,1)S(1)} collective-permute-done((bf16[256,2560]{1,0:T(8,128)(2,1)}, bf16[256,2560]{1,0:T(8,128)(2,1)S(1)}, u32[]{:S(2)}, u32[]{:S(2)}) %collective-permute-start.2) | collective-permute-done | bytes 1310752 | tf_op jit(solution)/shard_map/ppermute | solution.py:25
  165.9 1.1 place_queries.1
  167.0 3.6 %all-to-all-done.2 = bf16[32,3,128,128]{3,2,1,0:T(8,128)(2,1)S(1)} async-done(((bf16[32,3,128,128]{3,2,1,0:T(8,128)(2,1)}), bf16[32,3,128,128]{3,2,1,0:T(8,128)(2,1)S(1)}, u32[]{:S(2)}, u32[]{:S(2)}) %all-to-all-start.2) | async-done | bytes 3145760 | tf_op jit(solution)/shard_map/all_to_all | solution.py:385
  170.6 3.3 %sum_keys.1 = bf16[256,2560]{1,0:T(8,128)(2,1)} custom-call(s32[96]{0:T(128)} %reshape.173.codes, bf16[96,128,128]{2,1,0:T(8,128)(2,1)S(1)} %bitcast.30), custom_call_target="tpu_custom_call" | custom-call | tf_op jit(solution)/shard_map/sum_keys/pallas_call | solution.py:418
  173.9 1.7 collective-permute-done.3.head_part
  175.6 7.4 %all-to-all-start.4 = ((bf16[32,3,80,128]{3,2,1,0:T(8,128)(2,1)}), bf16[32,3,80,128]{3,2,1,0:T(8,128)(2,1)S(1)}, u32[]{:S(2)}, u32[]{:S(2)}) async-start(bf16[32,3,80,128]{3,2,1,0:T(8,128)(2,1)} %bitcast.43), calls=%async_computation.4 | async-start | bytes 3932160 | tf_op jit(solution)/shard_map/all_to_all | solution.py:385
  183.0 3.8 %collective-permute-start.4 = (bf16[256,2560]{1,0:T(8,128)(2,1)}, bf16[256,2560]{1,0:T(8,128)(2,1)S(1)}, u32[]{:S(2)}, u32[]{:S(2)}) collective-permute-start(bf16[256,2560]{1,0:T(8,128)(2,1)} %sum_keys.1), channel_id=1, source_target_pairs={{0,7},{1,0},{2,1},{3,2},{4,3},{5,4},{6,5},{7,6},{8,15},{9,8},{10,9... | collective-permute-start | bytes 3932168 | tf_op jit(solution)/shard_map/ppermute | solution.py:25
  186.8 21.6 %all-to-all-done.4 = bf16[32,3,80,128]{3,2,1,0:T(8,128)(2,1)S(1)} async-done(((bf16[32,3,80,128]{3,2,1,0:T(8,128)(2,1)}), bf16[32,3,80,128]{3,2,1,0:T(8,128)(2,1)S(1)}, u32[]{:S(2)}, u32[]{:S(2)}) %all-to-all-start.4) | async-done | bytes 1966112 | tf_op jit(solution)/shard_map/all_to_all | solution.py:385
  208.4 2.9 %join_values.1.after = bf16[256,2560]{1,0:T(8,128)(2,1)} custom-call(s32[96]{0:T(128)} %copy-done.7, bf16[96,2560]{1,0:T(8,128)(2,1)} %collective-permute-done.3.head_part, bf16[96,80,128]{2,1,0:T(8,128)(2,1)S(1)} %bitcast.31), custom_call_target="tpu_custom_call" | custom-call | tf_op jit(solution)/shard_map/join_values/pallas_call | solution.py:477
  211.2 4.2 %collective-permute-done.4.source = bf16[256,2560]{1,0:T(8,128)(2,1)S(1)} collective-permute-done((bf16[256,2560]{1,0:T(8,128)(2,1)}, bf16[256,2560]{1,0:T(8,128)(2,1)S(1)}, u32[]{:S(2)}, u32[]{:S(2)}) %collective-permute-start.4) | collective-permute-done | bytes 1310752 | tf_op jit(solution)/shard_map/ppermute | solution.py:25
  215.4 1.1 place_keys.1
  (22 shorter events, 0.4 us)
Async XLA Ops:
  6.9 7.7 %copy-start.6 = (s32[96]{0:T(128)S(1)}, s32[96]{0:T(128)}, u32[]{:S(2)}) copy-start(s32[96]{0:T(128)} %reshape.173.codes) | copy-start | bytes 1156
  6.9 13.7 %copy-start.4 = (s32[1,32,20]{1,0,2:T(1,128)S(1)}, s32[1,32,20]{1,0,2:T(1,128)}, u32[]{:S(2)}) copy-start(s32[1,32,20]{1,0,2:T(1,128)} %param.11) | copy-start | bytes 7684
  7.0 14.4 %copy-start.3 = (s32[1,32,20,4]{1,3,2,0:T(4,128)S(1)}, s32[1,32,20,4]{1,3,2,0:T(4,128)}, u32[]{:S(2)}) copy-start(s32[1,32,20,4]{1,3,2,0:T(4,128)} %param.10) | copy-start | bytes 30724
  7.0 47.2 %all-to-all-start = ((bf16[32,3,128,128]{3,2,1,0:T(8,128)(2,1)}), bf16[32,3,128,128]{3,2,1,0:T(8,128)(2,1)S(1)}, u32[]{:S(2)}, u32[]{:S(2)}) async-start(bf16[32,3,128,128]{3,2,1,0:T(8,128)(2,1)} %bitcast.34), calls=%async_computation | async-start | bytes 6291456 | tf_op jit(solution)/shard_map/all_to_all | solution.py:385
  14.7 14.2 %collective-permute-start = (s32[96]{0:T(128)S(1)}, s32[96]{0:T(128)S(1)}, u32[]{:S(2)}, u32[]{:S(2)}) collective-permute-start(s32[96]{0:T(128)S(1)} %copy-done.6), channel_id=1, source_target_pairs={{0,7},{1,0},{2,1},{3,2},{4,3},{5,4},{6,5},{7,6},{8,15},{9,8},{10,9... | collective-permute-start | bytes 1160 | tf_op jit(solution)/shard_map/ppermute | solution.py:25
  21.1 7.7 %copy-start.5 = (s32[20]{0:T(128)}, s32[20]{0:T(128)S(1)}, u32[]{:S(2)}) copy-start(s32[20]{0:T(128)S(1)} %dynamic-slice_reduce_fusion.lengths) | copy-start | bytes 244
  28.8 25.3 %copy-start.7 = (s32[96]{0:T(128)}, s32[96]{0:T(128)S(1)}, u32[]{:S(2)}) copy-start(s32[96]{0:T(128)S(1)} %collective-permute-done.codes) | copy-start | bytes 1156
  54.2 1.7 copy-start
  55.8 44.9 %all-to-all-start.1 = ((bf16[32,3,128,128]{3,2,1,0:T(8,128)(2,1)}), bf16[32,3,128,128]{3,2,1,0:T(8,128)(2,1)}, u32[]{:S(2)}, u32[]{:S(2)}) async-start(bf16[32,3,128,128]{3,2,1,0:T(8,128)(2,1)} %bitcast.35), calls=%async_computation.1 | async-start | bytes 6291456 | tf_op jit(solution)/shard_map/all_to_all | solution.py:385
  73.4 48.7 %collective-permute-start.1 = (bf16[96,80,128]{2,1,0:T(8,128)(2,1)}, bf16[96,80,128]{2,1,0:T(8,128)(2,1)S(1)}, u32[]{:S(2)}, u32[]{:S(2)}) collective-permute-start(bf16[96,80,128]{2,1,0:T(8,128)(2,1)} %get-tuple-element.24), channel_id=1, source_target_pairs={{0,7},{1,0},{2,1},{3,2},{4,3},{5,4},{6,5},{7,6},{8,15},{9,8},{10,9... | collective-permute-start | bytes 5898248 | tf_op jit(solution)/shard_map/ppermute | solution.py:25
  100.7 22.1 %all-to-all-start.3 = ((bf16[32,3,48,128]{3,2,1,0:T(8,128)(2,1)}), bf16[32,3,48,128]{3,2,1,0:T(8,128)(2,1)S(1)}, u32[]{:S(2)}, u32[]{:S(2)}) async-start(bf16[32,3,48,128]{3,2,1,0:T(8,128)(2,1)} %bitcast.48), calls=%async_computation.3 | async-start | bytes 2359296 | tf_op jit(solution)/shard_map/all_to_all | solution.py:385
  122.1 1.3 copy-start.2
  122.8 1.0 copy-start.1
  123.8 46.8 %all-to-all-start.2 = ((bf16[32,3,128,128]{3,2,1,0:T(8,128)(2,1)}), bf16[32,3,128,128]{3,2,1,0:T(8,128)(2,1)S(1)}, u32[]{:S(2)}, u32[]{:S(2)}) async-start(bf16[32,3,128,128]{3,2,1,0:T(8,128)(2,1)} %bitcast.42), calls=%async_computation.2 | async-start | bytes 6291456 | tf_op jit(solution)/shard_map/all_to_all | solution.py:385
  131.1 34.7 %collective-permute-start.2 = (bf16[256,2560]{1,0:T(8,128)(2,1)}, bf16[256,2560]{1,0:T(8,128)(2,1)S(1)}, u32[]{:S(2)}, u32[]{:S(2)}) collective-permute-start(bf16[256,2560]{1,0:T(8,128)(2,1)} %get-tuple-element.26), channel_id=1, source_target_pairs={{0,7},{1,0},{2,1},{3,2},{4,3},{5,4},{6,5},{7,6},{8,15},{9,8},{10,9... | collective-permute-start | bytes 3932168 | tf_op jit(solution)/shard_map/ppermute | solution.py:25
  139.4 36.2 %collective-permute-start.3 = (bf16[96,2560]{1,0:T(8,128)(2,1)}, bf16[96,2560]{1,0:T(8,128)(2,1)}, u32[]{:S(2)}, u32[]{:S(2)}) collective-permute-start(bf16[96,2560]{1,0:T(8,128)(2,1)} %sum_values.1), channel_id=1, source_target_pairs={{0,7},{1,0},{2,1},{3,2},{4,3},{5,4},{6,5},{7,6},{8,15},{9,8},{10,9... | collective-permute-start | bytes 1474568 | tf_op jit(solution)/shard_map/ppermute | solution.py:25
  175.6 32.8 %all-to-all-start.4 = ((bf16[32,3,80,128]{3,2,1,0:T(8,128)(2,1)}), bf16[32,3,80,128]{3,2,1,0:T(8,128)(2,1)S(1)}, u32[]{:S(2)}, u32[]{:S(2)}) async-start(bf16[32,3,80,128]{3,2,1,0:T(8,128)(2,1)} %bitcast.43), calls=%async_computation.4 | async-start | bytes 3932160 | tf_op jit(solution)/shard_map/all_to_all | solution.py:385
  183.0 32.4 %collective-permute-start.4 = (bf16[256,2560]{1,0:T(8,128)(2,1)}, bf16[256,2560]{1,0:T(8,128)(2,1)S(1)}, u32[]{:S(2)}, u32[]{:S(2)}) collective-permute-start(bf16[256,2560]{1,0:T(8,128)(2,1)} %sum_keys.1), channel_id=1, source_target_pairs={{0,7},{1,0},{2,1},{3,2},{4,3},{5,4},{6,5},{7,6},{8,15},{9,8},{10,9... | collective-permute-start | bytes 3932168 | tf_op jit(solution)/shard_map/ppermute | solution.py:25

commit v8 on v7

--- a/solution.py
+++ b/solution.py
@@ -57,24 +57,32 @@
         part_of(part).wait()
 
 
-def add_slots(codes, terms, wide, first, count):
-    rows, cols = terms.shape[1:]
-    for item in range(count):
-        slot = first + item
-        code = codes[slot]
-        code = jnp.where(code < 0, 2 << HEAD_BITS, code)
-        wide[tile_of(code, rows, cols)] += terms[slot].astype(jnp.float32)
-
-
-def add_terms(codes, terms, wide, parts):
-    wide[...] = jnp.zeros_like(wide)
+def add_terms(codes, terms, wide, heads, parts):
+    for index in range(2 * heads):
+        wide[index] = jnp.zeros_like(wide[index])
     step = terms.shape[0] // parts
 
     def one_part(part, carry):
-        add_slots(codes, terms, wide, part * step, step)
+        for item in range(step):
+            slot = part * step + item
+            code = codes[slot]
+            block = lax.shift_right_logical(code, HEAD_BITS)
+            head = lax.bitwise_and(code, (1 << HEAD_BITS) - 1)
+            index = jnp.where(code < 0, 2 * heads, block * heads + head)
+            wide[index] += terms[slot].astype(jnp.float32)
         return carry
 
     lax.fori_loop(0, parts, one_part, 0)
+
+
+def fill_block(wide, ready, block, start, part, parts):
+    heads = wide.shape[0] // 2
+    rows, cols = wide.shape[1:]
+    count = heads // parts
+    for head in range(part * count, (part + 1) * count):
+        ready[start : start + rows, head * cols : (head + 1) * cols] = wide[
+            block * heads + head
+        ].astype(ready.dtype)
 
 
 def send_columns(ready, total, sent, parts, fill):
@@ -82,7 +90,7 @@
     copies = []
     for part in range(parts):
         columns = pl.ds(part * width, width)
-        fill(columns)
+        fill(part, columns)
         copies.append(copy(ready.at[:, columns], total.at[:, columns], sent.at[part]))
         copies[-1].start()
     for one in copies:
@@ -90,11 +98,12 @@
 
 
 def sum_kernel(parts, codes, terms, total, wide, ready, sent):
-    add_terms(codes, terms, wide, parts)
-    rows = total.shape[0]
-
-    def fill(columns):
-        ready[:, columns] = wide[:rows, columns].astype(ready.dtype)
+    add_terms(codes, terms, wide, wide.shape[0] // 2, parts)
+    rows = terms.shape[1]
+
+    def fill(part, columns):
+        for block in range(2):
+            fill_block(wide, ready, block, block * rows, part, sent.shape[0])
 
     send_columns(ready, total, sent, sent.shape[0], fill)
 
@@ -104,27 +113,49 @@
 ):
     head_copy = copy(head_part, head, got)
     head_copy.start()
-    add_terms(codes, terms, wide, parts)
+    add_terms(codes, terms, wide, wide.shape[0] // 2, parts)
     head_copy.wait()
     tail_rows = terms.shape[1]
     head_rows = total.shape[0] // 2 - tail_rows
 
-    def fill(columns):
+    def fill(part, columns):
         for block in range(2):
             start = block * (head_rows + tail_rows)
-            middle = start + head_rows
-            ready[start:middle, columns] = head[
+            ready[start : start + head_rows, columns] = head[
                 block * head_rows : (block + 1) * head_rows, columns
             ]
-            ready[middle : middle + tail_rows, columns] = wide[
-                block * tail_rows : (block + 1) * tail_rows, columns
-            ].astype(ready.dtype)
+            fill_block(wide, ready, block, start + head_rows, part, sent.shape[0])
 
     send_columns(ready, total, sent, sent.shape[0], fill)
 
 
 def place_last_kernel(source, after, out):
     out[...] = source[...]
+
+
+def slot_kernel(list_size, places, lengths, listed, slotted, held, made, got, sent):
+    fetched = in_parts(listed, held, got)
+    for one in fetched:
+        one.start()
+    for one in fetched:
+        one.wait()
+
+    def one_head(head, carry):
+        for item in range(list_size):
+
+            @pl.when(item < lengths[head])
+            def _():
+                entry = head * list_size + item
+                made[places[entry]] = held[entry]
+
+        return carry
+
+    lax.fori_loop(0, lengths.shape[0], one_head, 0)
+    ends = in_parts(made, slotted, sent)
+    for one in ends:
+        one.start()
+    for one in ends:
+        one.wait()
 
 
 def place_kernel(source, out):
@@ -219,9 +250,11 @@
         results = [compute(index * group + item) for item in range(group)]
         weights_part(index).start()
         for item, result in enumerate(results):
-            put_terms(
-                places, lengths, list_size, index * group + item, result, [first_made, last_made]
-            )
+            head = index * group + item
+            put_terms(places, lengths, list_size, head, result, [first_made])
+            for entry in range(list_size):
+                start, stop = entry * rows + first_made.shape[1], (entry + 1) * rows
+                last_made[head * list_size + entry] = result[start:stop]
         return carry
 
     lax.fori_loop(0, groups, one_group, 0)
@@ -365,9 +398,9 @@
     places = my_holder * capacity + my_rank
     places = jnp.where(my_used, places, places[:, :1]).reshape(entries)
 
-    first_rows = 3 * block_rows // 8
+    first_rows = block_rows // 4
     last_rows = block_rows - first_rows
-    add_parts = 8 if slots % 8 == 0 else 1
+    add_parts = 8 if slots % 8 == 0 and entries % 8 == 0 else 1
     send_parts = 5 if head_count % 5 == 0 else 1
     flat_shape = jax.ShapeDtypeStruct((row_count, column_count), jnp.bfloat16)
     dma = pltpu.SemaphoreType.DMA
@@ -400,7 +433,7 @@
         return pltpu.with_memory_space_constraint(value, pltpu.VMEM)
 
     def wide_sum(rows):
-        return pltpu.VMEM((3 * rows, column_count), jnp.float32)
+        return pltpu.VMEM((2 * head_count + 1, rows, head_dim), jnp.float32)
 
     def placed(name, value, cost):
         return pl.pallas_call(
@@ -428,10 +461,13 @@
     slot_tiles = vmem(slots, block_rows, head_dim)
     wide_sem, part_sem = dma((groups,)), dma((add_parts,))
     fetched_keys = exchanged(pack("pack_keys", keys[0]))
-    handed_codes = shifted(codes, "section", -1)
-    packed_values, handed_codes, places, my_lengths = lax.optimization_barrier(
-        (pack("pack_values", values[0]), handed_codes, places, my_lengths)
-    )
+    handed_tables = shifted(jnp.concatenate([codes, places, my_lengths]), "section", -1)
+    packed_values, handed_tables, places, my_lengths = lax.optimization_barrier(
+        (pack("pack_values", values[0]), handed_tables, places, my_lengths)
+    )
+    handed_codes = handed_tables[:slots]
+    handed_places = handed_tables[slots : slots + entries]
+    handed_lengths = handed_tables[slots + entries :]
     fetched_values = exchanged(packed_values)
     weights_shape = (head_count, list_size * block_rows, row_count)
     weights_tile = pltpu.VMEM(weights_shape, jnp.float32)
@@ -439,13 +475,13 @@
         functools.partial(value_kernel, list_size, group, scale),
         out_shape=(
             packed_shape(first_rows),
-            packed_shape(last_rows),
+            jax.ShapeDtypeStruct((entries, last_rows, head_dim), jnp.bfloat16),
             jax.ShapeDtypeStruct(weights_shape, jnp.float32),
         ),
         in_specs=[SMEM, SMEM, ANY, ANY, ANY],
         out_specs=(ANY, ANY, ANY),
         scratch_shapes=[flat, flat, slot_tiles]
-        + [vmem(slots, rows, head_dim) for rows in (first_rows, last_rows)]
+        + [vmem(slots, first_rows, head_dim), vmem(entries, last_rows, head_dim)]
         + [weights_tile, wide_sem, wide_sem, part_sem, part_sem, part_sem, wide_sem],
         compiler_params=PARAMS,
         name="value_terms",
@@ -466,8 +502,18 @@
     key_terms, handed_terms = lax.optimization_barrier((key_terms, handed_terms))
     returned_keys = exchanged(key_terms)
     handed_queries = placed("place_queries", shifted(query_grad, "section", -1), 5000000)
-    returned_keys, handed_queries, first_values = lax.optimization_barrier(
-        (returned_keys, handed_queries, first_values)
+    handed_terms = pl.pallas_call(
+        functools.partial(slot_kernel, list_size),
+        out_shape=packed_shape(last_rows),
+        in_specs=[SMEM, SMEM, ANY],
+        out_specs=ANY,
+        scratch_shapes=[vmem(entries, last_rows, head_dim), vmem(slots, last_rows, head_dim)]
+        + [part_sem, part_sem],
+        compiler_params=PARAMS,
+        name="slot_values",
+    )(handed_places, handed_lengths, handed_terms)
+    returned_keys, handed_queries, first_values, handed_terms = lax.optimization_barrier(
+        (returned_keys, handed_queries, first_values, handed_terms)
     )
     key_grad = add_up("sum_keys", near(returned_keys))
     key_grad, handed_terms, handed_first = lax.optimization_barrier(

time: 218 us -> 221 us (1.014)
  waiting for transfers between devices: 105 us -> 98.4 us
  Pallas kernels: 46.8 us -> 51.6 us
  local copies, waits for them, and re-layouts: 5.42 us -> 8.43 us
    ppermute x5, waiting for transfers between devices: 32 us -> 25.3 us  [shifted(): return lax.ppermute(value, axis, pairs)]
    pallas_call x0 -> x1, Pallas kernels: none -> 4.72 us  [local(): pl.pallas_call(functools.partial(slot_kernel, list_size), out_shape=packe...]
    unnamed x17 -> x19, local copies, waits for them, and re-layouts: 3.4 us -> 4.63 us
  transfers between devices with their start and end apart: 10 -> 10, of which waited for: 9 -> 5; matrix products, arithmetic and copies ran while one was open for 2% -> 3% of each run, Pallas kernels for 19% -> 21%
where the time goes in v8:
time: 221 us; the launch traced here: 218 us
  waiting for transfers between devices  98.4 us (45%)
  starting transfers between devices  54.8 us (25%)
  Pallas kernels  51.6 us (23%)
  local copies, waits for them, and re-layouts  8.43 us (4%)
  other arithmetic  3.56 us (2%)
    all_to_all x5, waiting for transfers between devices, exchanged(): lax.all_to_all(parts, 'ctx', split_axis=0, concat_axis=0, tiled=True)  73 us
    all_to_all x5, starting transfers between devices, exchanged(): lax.all_to_all(parts, 'ctx', split_axis=0, concat_axis=0, tiled=True)  32.9 us
    ppermute x5, waiting for transfers between devices, shifted(): return lax.ppermute(value, axis, pairs)  25.3 us
    ppermute x5, starting transfers between devices, shifted(): return lax.ppermute(value, axis, pairs)  22 us
    pallas_call x1, Pallas kernels, local(): pl.pallas_call(functools.partial(key_kernel, list_size, group, scale), ou...  15.4 us
    pallas_call x1, Pallas kernels, local(): pl.pallas_call(functools.partial(value_kernel, list_size, group, scale),...  12.1 us
    pallas_call x2, Pallas kernels, pack(): pl.pallas_call(functools.partial(pack_kernel, add_parts), out_shape=packe...  7.68 us
    pallas_call x2, Pallas kernels, add_up(): pl.pallas_call(functools.partial(sum_kernel, add_parts), out_shape=jax.Sh...  5.27 us
  transfers between devices with their start and end apart: 10, of which 5 were waited for; matrix products, arithmetic and copies ran while one was open for 3% of the time, Pallas kernels for 21%

profile of v8, /device:TPU:8, one launch (start us, length us, event | category | flops | bytes accessed | tf_op | source)
XLA Modules:
  0.0 217.7 jit_solution(8615986510997675874)
XLA Ops:
  0.7 0.7 copy.40
  1.4 0.8 fusion
  2.2 0.2 select_reduce_fusion
  2.5 0.7 reshape.173.codes
  3.2 3.8 %pack_keys.1 = bf16[96,128,128]{2,1,0:T(8,128)(2,1)} custom-call(s32[96]{0:T(128)} %reshape.173.codes, bf16[256,2560]{1,0:T(8,128)(2,1)} %bitcast.44), custom_call_target="tpu_custom_call" | custom-call | tf_op jit(solution)/shard_map/pack_keys/pallas_call | solution.py:422
  7.0 7.5 %all-to-all-start = ((bf16[32,3,128,128]{3,2,1,0:T(8,128)(2,1)}), bf16[32,3,128,128]{3,2,1,0:T(8,128)(2,1)S(1)}, u32[]{:S(2)}, u32[]{:S(2)}) async-start(bf16[32,3,128,128]{3,2,1,0:T(8,128)(2,1)} %bitcast.34), calls=%async_computation | async-start | bytes 6291456 | tf_op jit(solution)/shard_map/all_to_all | solution.py:418
  14.6 0.5 fusion.6
  15.1 0.1 copy.36
  15.2 0.1 copy.37
  15.3 0.5 dynamic-slice_reduce_fusion.lengths
  15.8 0.1 fusion.3
  15.9 0.1 copy.35
  16.1 1.6 select_reduce_fusion.1
  17.7 0.1 reduce_sum.32
  17.8 0.1 fusion.5
  18.0 0.1 broadcast_in_dim.88
  18.2 0.1 lt.105
  18.3 0.1 shift_right_arithmetic.25
  18.5 5.9 %collective-permute-start = (s32[196]{0:T(256)S(1)}, s32[196]{0:T(256)S(1)}, u32[]{:S(2)}, u32[]{:S(2)}) collective-permute-start(s32[196]{0:T(256)S(1)} %pad_add_fusion), channel_id=1, source_target_pairs={{0,7},{1,0},{2,1},{3,2},{4,3},{5,4},{6,5},{7,6},{8,15},{9,8},{10,9... | collective-permute-start | bytes 2360 | tf_op jit(solution)/shard_map/ppermute | solution.py:25
  24.4 3.9 %pack_values.1 = bf16[96,128,128]{2,1,0:T(8,128)(2,1)} custom-call(s32[96]{0:T(128)} %reshape.173.codes, bf16[256,2560]{1,0:T(8,128)(2,1)} %bitcast.45), custom_call_target="tpu_custom_call" | custom-call | tf_op jit(solution)/shard_map/pack_values/pallas_call | solution.py:422
  28.3 25.8 %all-to-all-done = bf16[32,3,128,128]{3,2,1,0:T(8,128)(2,1)S(1)} async-done(((bf16[32,3,128,128]{3,2,1,0:T(8,128)(2,1)}), bf16[32,3,128,128]{3,2,1,0:T(8,128)(2,1)S(1)}, u32[]{:S(2)}, u32[]{:S(2)}) %all-to-all-start) | async-done | bytes 3145760 | tf_op jit(solution)/shard_map/all_to_all | solution.py:418
  54.1 1.6 copy-done
  55.7 5.3 %all-to-all-start.1 = ((bf16[32,3,128,128]{3,2,1,0:T(8,128)(2,1)}), bf16[32,3,128,128]{3,2,1,0:T(8,128)(2,1)}, u32[]{:S(2)}, u32[]{:S(2)}) async-start(bf16[32,3,128,128]{3,2,1,0:T(8,128)(2,1)} %bitcast.35), calls=%async_computation.1 | async-start | bytes 6291456 | tf_op jit(solution)/shard_map/all_to_all | solution.py:418
  61.0 12.1 %value_terms.1 = (bf16[96,32,128]{2,1,0:T(8,128)(2,1)}, bf16[80,96,128]{2,1,0:T(8,128)(2,1)}, f32[20,512,256]{2,1,0:T(8,128)}) custom-call(s32[80]{0:T(128)} %copy-done.8, s32[20]{0:T(128)} %copy-done.6, bf16[256,2560]{1,0:T(8,128)(2,1)} %bitcast.37, bf16[256,2560]{1,0:T(8,128)(2,1)} %bitcast.39, bf16[96,128,128]{2,1,0:T(8,128)(2,1)} %bitcast.32), custom_call_target="tpu_custom_call" | custom-call | tf_op jit(solution)/shard_map/value_terms/pallas_call | solution.py:474
  73.2 5.9 %collective-permute-start.1 = (bf16[80,96,128]{2,1,0:T(8,128)(2,1)}, bf16[80,96,128]{2,1,0:T(8,128)(2,1)S(1)}, u32[]{:S(2)}, u32[]{:S(2)}) collective-permute-start(bf16[80,96,128]{2,1,0:T(8,128)(2,1)} %get-tuple-element.25), channel_id=1, source_target_pairs={{0,7},{1,0},{2,1},{3,2},{4,3},{5,4},{6,5},{7,6},{8,15},{9,8},{10,9... | collective-permute-start | bytes 5898248 | tf_op jit(solution)/shard_map/ppermute | solution.py:25
  79.1 21.5 %all-to-all-done.1 = bf16[32,3,128,128]{3,2,1,0:T(8,128)(2,1)} async-done(((bf16[32,3,128,128]{3,2,1,0:T(8,128)(2,1)}), bf16[32,3,128,128]{3,2,1,0:T(8,128)(2,1)}, u32[]{:S(2)}, u32[]{:S(2)}) %all-to-all-start.1) | async-done | bytes 3145760 | tf_op jit(solution)/shard_map/all_to_all | solution.py:418
  100.6 5.2 %all-to-all-start.3 = ((bf16[32,3,32,128]{3,2,1,0:T(8,128)(2,1)}), bf16[32,3,32,128]{3,2,1,0:T(8,128)(2,1)S(1)}, u32[]{:S(2)}, u32[]{:S(2)}) async-start(bf16[32,3,32,128]{3,2,1,0:T(8,128)(2,1)} %bitcast.48), calls=%async_computation.3 | async-start | bytes 1572864 | tf_op jit(solution)/shard_map/all_to_all | solution.py:418
  105.8 15.4 %key_terms.1 = (bf16[256,2560]{1,0:T(8,128)(2,1)}, bf16[96,128,128]{2,1,0:T(8,128)(2,1)}) custom-call(s32[80]{0:T(128)} %copy-done.8, s32[20]{0:T(128)} %copy-done.6, bf16[256,2560]{1,0:T(8,128)(2,1)} %bitcast.38, bf16[256,2560]{1,0:T(8,128)(2,1)} %bitcast.40, bf16[96,128,128]{2,1,0:T(8,128)(2,1)} %bitcast.33, bf16[96,128,128]{2,1,0:T(8,128)(2,1)} %bitcast.11.values, ...), custom_call_target="tpu_custom_call" | custom-call | tf_op jit(solution)/shard_map/key_terms/pallas_call | solution.py:490
  121.3 0.5 collective-permute-done.1.listed
  121.8 1.3 copy-done.2
  123.1 0.2 copy-done.1
  123.3 7.4 %all-to-all-start.2 = ((bf16[32,3,128,128]{3,2,1,0:T(8,128)(2,1)}), bf16[32,3,128,128]{3,2,1,0:T(8,128)(2,1)S(1)}, u32[]{:S(2)}, u32[]{:S(2)}) async-start(bf16[32,3,128,128]{3,2,1,0:T(8,128)(2,1)} %bitcast.42), calls=%async_computation.2 | async-start | bytes 6291456 | tf_op jit(solution)/shard_map/all_to_all | solution.py:418
  130.7 5.5 %collective-permute-start.2 = (bf16[256,2560]{1,0:T(8,128)(2,1)}, bf16[256,2560]{1,0:T(8,128)(2,1)S(1)}, u32[]{:S(2)}, u32[]{:S(2)}) collective-permute-start(bf16[256,2560]{1,0:T(8,128)(2,1)} %get-tuple-element.27), channel_id=1, source_target_pairs={{0,7},{1,0},{2,1},{3,2},{4,3},{5,4},{6,5},{7,6},{8,15},{9,8},{10,9... | collective-permute-start | bytes 3932168 | tf_op jit(solution)/shard_map/ppermute | solution.py:25
  136.2 2.5 %sum_values.1 = bf16[64,2560]{1,0:T(8,128)(2,1)} custom-call(s32[96]{0:T(128)} %reshape.173.codes, bf16[96,32,128]{2,1,0:T(8,128)(2,1)} %bitcast.43), custom_call_target="tpu_custom_call" | custom-call | tf_op jit(solution)/shard_map/sum_values/pallas_call | solution.py:451
  138.7 1.0 collective-permute-start.3
  139.7 0.6 slice.13.places
  140.3 0.6 slice.14.lengths
  140.9 24.8 %collective-permute-done.2.source = bf16[256,2560]{1,0:T(8,128)(2,1)S(1)} collective-permute-done((bf16[256,2560]{1,0:T(8,128)(2,1)}, bf16[256,2560]{1,0:T(8,128)(2,1)S(1)}, u32[]{:S(2)}, u32[]{:S(2)}) %collective-permute-start.2) | collective-permute-done | bytes 1310752 | tf_op jit(solution)/shard_map/ppermute | solution.py:25
  165.6 1.1 place_queries.1
  166.8 4.7 %slot_values.1 = bf16[96,96,128]{2,1,0:T(8,128)(2,1)} custom-call(s32[80]{0:T(128)} %slice.13.places, s32[20]{0:T(128)} %slice.14.lengths, bf16[80,96,128]{2,1,0:T(8,128)(2,1)} %copy-done.2), custom_call_target="tpu_custom_call" | custom-call | tf_op jit(solution)/shard_map/slot_values/pallas_call | solution.py:505
  171.5 2.8 %sum_keys.1 = bf16[256,2560]{1,0:T(8,128)(2,1)} custom-call(s32[96]{0:T(128)} %reshape.173.codes, bf16[96,128,128]{2,1,0:T(8,128)(2,1)S(1)} %bitcast.30), custom_call_target="tpu_custom_call" | custom-call | tf_op jit(solution)/shard_map/sum_keys/pallas_call | solution.py:451
  174.3 0.7 copy-done.3
  175.1 7.4 %all-to-all-start.4 = ((bf16[32,3,96,128]{3,2,1,0:T(8,128)(2,1)}), bf16[32,3,96,128]{3,2,1,0:T(8,128)(2,1)S(1)}, u32[]{:S(2)}, u32[]{:S(2)}) async-start(bf16[32,3,96,128]{3,2,1,0:T(8,128)(2,1)} %bitcast.36), calls=%async_computation.4 | async-start | bytes 4718592 | tf_op jit(solution)/shard_map/all_to_all | solution.py:418
  182.5 3.7 %collective-permute-start.4 = (bf16[256,2560]{1,0:T(8,128)(2,1)}, bf16[256,2560]{1,0:T(8,128)(2,1)}, u32[]{:S(2)}, u32[]{:S(2)}) collective-permute-start(bf16[256,2560]{1,0:T(8,128)(2,1)} %sum_keys.1), channel_id=1, source_target_pairs={{0,7},{1,0},{2,1},{3,2},{4,3},{5,4},{6,5},{7,6},{8,15},{9,8},{10,9... | collective-permute-start | bytes 3932168 | tf_op jit(solution)/shard_map/ppermute | solution.py:25
  186.1 0.6 slice.15.codes
  186.7 25.8 %all-to-all-done.4 = bf16[32,3,96,128]{3,2,1,0:T(8,128)(2,1)S(1)} async-done(((bf16[32,3,96,128]{3,2,1,0:T(8,128)(2,1)}), bf16[32,3,96,128]{3,2,1,0:T(8,128)(2,1)S(1)}, u32[]{:S(2)}, u32[]{:S(2)}) %all-to-all-start.4) | async-done | bytes 2359328 | tf_op jit(solution)/shard_map/all_to_all | solution.py:418
  212.5 2.8 %join_values.1.after = bf16[256,2560]{1,0:T(8,128)(2,1)} custom-call(s32[96]{0:T(128)} %slice.15.codes, bf16[64,2560]{1,0:T(8,128)(2,1)} %copy-done.3, bf16[96,96,128]{2,1,0:T(8,128)(2,1)S(1)} %bitcast.31), custom_call_target="tpu_custom_call" | custom-call | tf_op jit(solution)/shard_map/join_values/pallas_call | solution.py:523
  215.3 2.5 %place_keys.1 = bf16[256,2560]{1,0:T(8,128)(2,1)} custom-call(bf16[256,2560]{1,0:T(8,128)(2,1)} %collective-permute-done.4.source, bf16[256,2560]{1,0:T(8,128)(2,1)} %join_values.1.after), custom_call_target="tpu_custom_call" | custom-call | tf_op jit(solution)/shard_map/place_keys/pallas_call | solution.py:533
  (29 shorter events, 0.5 us)
Async XLA Ops:
  7.0 7.6 %copy-start.4 = (s32[1,32,20,4]{1,3,2,0:T(4,128)S(1)}, s32[1,32,20,4]{1,3,2,0:T(4,128)}, u32[]{:S(2)}) copy-start(s32[1,32,20,4]{1,3,2,0:T(4,128)} %param.10) | copy-start | bytes 30724
  7.0 8.3 %copy-start.5 = (s32[1,32,20]{1,0,2:T(1,128)S(1)}, s32[1,32,20]{1,0,2:T(1,128)}, u32[]{:S(2)}) copy-start(s32[1,32,20]{1,0,2:T(1,128)} %param.11) | copy-start | bytes 7684
  7.0 11.4 %copy-start.7 = (s32[96]{0:T(128)S(1)}, s32[96]{0:T(128)}, u32[]{:S(2)}) copy-start(s32[96]{0:T(128)} %reshape.173.codes) | copy-start | bytes 1156
  7.0 47.1 %all-to-all-start = ((bf16[32,3,128,128]{3,2,1,0:T(8,128)(2,1)}), bf16[32,3,128,128]{3,2,1,0:T(8,128)(2,1)S(1)}, u32[]{:S(2)}, u32[]{:S(2)}) async-start(bf16[32,3,128,128]{3,2,1,0:T(8,128)(2,1)} %bitcast.34), calls=%async_computation | async-start | bytes 6291456 | tf_op jit(solution)/shard_map/all_to_all | solution.py:418
  15.8 12.4 %copy-start.6 = (s32[20]{0:T(128)}, s32[20]{0:T(128)S(1)}, u32[]{:S(2)}) copy-start(s32[20]{0:T(128)S(1)} %dynamic-slice_reduce_fusion.lengths) | copy-start | bytes 244
  18.4 9.9 %copy-start.8 = (s32[80]{0:T(128)}, s32[80]{0:T(128)S(1)}, u32[]{:S(2)}) copy-start(s32[80]{0:T(128)S(1)} %add_select_fusion.places) | copy-start | bytes 964
  18.5 9.8 %collective-permute-start = (s32[196]{0:T(256)S(1)}, s32[196]{0:T(256)S(1)}, u32[]{:S(2)}, u32[]{:S(2)}) collective-permute-start(s32[196]{0:T(256)S(1)} %pad_add_fusion), channel_id=1, source_target_pairs={{0,7},{1,0},{2,1},{3,2},{4,3},{5,4},{6,5},{7,6},{8,15},{9,8},{10,9... | collective-permute-start | bytes 2360 | tf_op jit(solution)/shard_map/ppermute | solution.py:25
  54.1 1.6 copy-start
  55.7 44.9 %all-to-all-start.1 = ((bf16[32,3,128,128]{3,2,1,0:T(8,128)(2,1)}), bf16[32,3,128,128]{3,2,1,0:T(8,128)(2,1)}, u32[]{:S(2)}, u32[]{:S(2)}) async-start(bf16[32,3,128,128]{3,2,1,0:T(8,128)(2,1)} %bitcast.35), calls=%async_computation.1 | async-start | bytes 6291456 | tf_op jit(solution)/shard_map/all_to_all | solution.py:418
  73.2 48.7 %collective-permute-start.1 = (bf16[80,96,128]{2,1,0:T(8,128)(2,1)}, bf16[80,96,128]{2,1,0:T(8,128)(2,1)S(1)}, u32[]{:S(2)}, u32[]{:S(2)}) collective-permute-start(bf16[80,96,128]{2,1,0:T(8,128)(2,1)} %get-tuple-element.25), channel_id=1, source_target_pairs={{0,7},{1,0},{2,1},{3,2},{4,3},{5,4},{6,5},{7,6},{8,15},{9,8},{10,9... | collective-permute-start | bytes 5898248 | tf_op jit(solution)/shard_map/ppermute | solution.py:25
  100.6 21.2 %all-to-all-start.3 = ((bf16[32,3,32,128]{3,2,1,0:T(8,128)(2,1)}), bf16[32,3,32,128]{3,2,1,0:T(8,128)(2,1)S(1)}, u32[]{:S(2)}, u32[]{:S(2)}) async-start(bf16[32,3,32,128]{3,2,1,0:T(8,128)(2,1)} %bitcast.48), calls=%async_computation.3 | async-start | bytes 1572864 | tf_op jit(solution)/shard_map/all_to_all | solution.py:418
  121.8 1.3 copy-start.2
  121.8 1.5 copy-start.1
  123.3 48.2 %all-to-all-start.2 = ((bf16[32,3,128,128]{3,2,1,0:T(8,128)(2,1)}), bf16[32,3,128,128]{3,2,1,0:T(8,128)(2,1)S(1)}, u32[]{:S(2)}, u32[]{:S(2)}) async-start(bf16[32,3,128,128]{3,2,1,0:T(8,128)(2,1)} %bitcast.42), calls=%async_computation.2 | async-start | bytes 6291456 | tf_op jit(solution)/shard_map/all_to_all | solution.py:418
  130.7 34.9 %collective-permute-start.2 = (bf16[256,2560]{1,0:T(8,128)(2,1)}, bf16[256,2560]{1,0:T(8,128)(2,1)S(1)}, u32[]{:S(2)}, u32[]{:S(2)}) collective-permute-start(bf16[256,2560]{1,0:T(8,128)(2,1)} %get-tuple-element.27), channel_id=1, source_target_pairs={{0,7},{1,0},{2,1},{3,2},{4,3},{5,4},{6,5},{7,6},{8,15},{9,8},{10,9... | collective-permute-start | bytes 3932168 | tf_op jit(solution)/shard_map/ppermute | solution.py:25
  138.7 35.7 %collective-permute-start.3 = (bf16[64,2560]{1,0:T(8,128)(2,1)}, bf16[64,2560]{1,0:T(8,128)(2,1)S(1)}, u32[]{:S(2)}, u32[]{:S(2)}) collective-permute-start(bf16[64,2560]{1,0:T(8,128)(2,1)} %sum_values.1), channel_id=1, source_target_pairs={{0,7},{1,0},{2,1},{3,2},{4,3},{5,4},{6,5},{7,6},{8,15},{9,8},{10,9... | collective-permute-start | bytes 983048 | tf_op jit(solution)/shard_map/ppermute | solution.py:25
  174.3 0.7 copy-start.3
  175.1 37.4 %all-to-all-start.4 = ((bf16[32,3,96,128]{3,2,1,0:T(8,128)(2,1)}), bf16[32,3,96,128]{3,2,1,0:T(8,128)(2,1)S(1)}, u32[]{:S(2)}, u32[]{:S(2)}) async-start(bf16[32,3,96,128]{3,2,1,0:T(8,128)(2,1)} %bitcast.36), calls=%async_computation.4 | async-start | bytes 4718592 | tf_op jit(solution)/shard_map/all_to_all | solution.py:418
  182.5 32.8 %collective-permute-start.4 = (bf16[256,2560]{1,0:T(8,128)(2,1)}, bf16[256,2560]{1,0:T(8,128)(2,1)}, u32[]{:S(2)}, u32[]{:S(2)}) collective-permute-start(bf16[256,2560]{1,0:T(8,128)(2,1)} %sum_keys.1), channel_id=1, source_target_pairs={{0,7},{1,0},{2,1},{3,2},{4,3},{5,4},{6,5},{7,6},{8,15},{9,8},{10,9... | collective-permute-start | bytes 3932168 | tf_op jit(solution)/shard_map/ppermute | solution.py:25

commit v9 on v7

--- a/solution.py
+++ b/solution.py
@@ -57,24 +57,32 @@
         part_of(part).wait()
 
 
-def add_slots(codes, terms, wide, first, count):
-    rows, cols = terms.shape[1:]
-    for item in range(count):
-        slot = first + item
-        code = codes[slot]
-        code = jnp.where(code < 0, 2 << HEAD_BITS, code)
-        wide[tile_of(code, rows, cols)] += terms[slot].astype(jnp.float32)
-
-
-def add_terms(codes, terms, wide, parts):
-    wide[...] = jnp.zeros_like(wide)
+def add_terms(codes, terms, wide, heads, parts):
+    for index in range(2 * heads):
+        wide[index] = jnp.zeros_like(wide[index])
     step = terms.shape[0] // parts
 
     def one_part(part, carry):
-        add_slots(codes, terms, wide, part * step, step)
+        for item in range(step):
+            slot = part * step + item
+            code = codes[slot]
+            block = lax.shift_right_logical(code, HEAD_BITS)
+            head = lax.bitwise_and(code, (1 << HEAD_BITS) - 1)
+            index = jnp.where(code < 0, 2 * heads, block * heads + head)
+            wide[index] += terms[slot].astype(jnp.float32)
         return carry
 
     lax.fori_loop(0, parts, one_part, 0)
+
+
+def fill_block(wide, ready, block, start, part, parts):
+    heads = wide.shape[0] // 2
+    rows, cols = wide.shape[1:]
+    count = heads // parts
+    for head in range(part * count, (part + 1) * count):
+        ready[start : start + rows, head * cols : (head + 1) * cols] = wide[
+            block * heads + head
+        ].astype(ready.dtype)
 
 
 def send_columns(ready, total, sent, parts, fill):
@@ -82,7 +90,7 @@
     copies = []
     for part in range(parts):
         columns = pl.ds(part * width, width)
-        fill(columns)
+        fill(part, columns)
         copies.append(copy(ready.at[:, columns], total.at[:, columns], sent.at[part]))
         copies[-1].start()
     for one in copies:
@@ -90,11 +98,12 @@
 
 
 def sum_kernel(parts, codes, terms, total, wide, ready, sent):
-    add_terms(codes, terms, wide, parts)
-    rows = total.shape[0]
-
-    def fill(columns):
-        ready[:, columns] = wide[:rows, columns].astype(ready.dtype)
+    add_terms(codes, terms, wide, wide.shape[0] // 2, parts)
+    rows = terms.shape[1]
+
+    def fill(part, columns):
+        for block in range(2):
+            fill_block(wide, ready, block, block * rows, part, sent.shape[0])
 
     send_columns(ready, total, sent, sent.shape[0], fill)
 
@@ -104,21 +113,18 @@
 ):
     head_copy = copy(head_part, head, got)
     head_copy.start()
-    add_terms(codes, terms, wide, parts)
+    add_terms(codes, terms, wide, wide.shape[0] // 2, parts)
     head_copy.wait()
     tail_rows = terms.shape[1]
     head_rows = total.shape[0] // 2 - tail_rows
 
-    def fill(columns):
+    def fill(part, columns):
         for block in range(2):
             start = block * (head_rows + tail_rows)
-            middle = start + head_rows
-            ready[start:middle, columns] = head[
+            ready[start : start + head_rows, columns] = head[
                 block * head_rows : (block + 1) * head_rows, columns
             ]
-            ready[middle : middle + tail_rows, columns] = wide[
-                block * tail_rows : (block + 1) * tail_rows, columns
-            ].astype(ready.dtype)
+            fill_block(wide, ready, block, start + head_rows, part, sent.shape[0])
 
     send_columns(ready, total, sent, sent.shape[0], fill)
 
@@ -168,25 +174,16 @@
 
 def value_kernel(
     list_size, group, scale, places, lengths, queries, grads, keys, first, last, weights_out,
-    query_held, grad_held, key_held, first_made, last_made, weights_made,
-    query_sem, grad_sem, key_sem, first_sem, last_sem, weights_sem,
+    key_held, first_made, last_made, weights_made, key_sem, first_sem, last_sem, weights_sem,
 ):
     rows, cols = keys.shape[1:]
     groups = lengths.shape[0] // group
-    width = group * cols
-
-    def fetches(index):
-        columns = pl.ds(pl.multiple_of(index * width, width), width)
-        return [
-            copy(queries.at[:, columns], query_held.at[:, columns], query_sem.at[index]),
-            copy(grads.at[:, columns], grad_held.at[:, columns], grad_sem.at[index]),
-        ]
 
     def weights_part(index):
         heads = pl.ds(index * group, group)
         return copy(weights_made.at[heads], weights_out.at[heads], weights_sem.at[index])
 
-    for one in fetches(0) + in_parts(keys, key_held, key_sem):
+    for one in in_parts(keys, key_held, key_sem):
         one.start()
 
     def compute(head):
@@ -194,23 +191,15 @@
         key = jnp.concatenate(
             [key_held[places[head * list_size + item]] for item in range(list_size)], axis=0
         )
-        weights = weights_of(query_held[:, columns], key, lengths[head], list_size, scale)
+        weights = weights_of(queries[:, columns], key, lengths[head], list_size, scale)
         for item, part in enumerate(weights):
             weights_made[head, item * rows : (item + 1) * rows] = part
         weights_low = jnp.concatenate([part.astype(jnp.bfloat16) for part in weights], axis=0)
         return lax.dot_general(
-            weights_low, grad_held[:, columns], NN, preferred_element_type=jnp.float32
+            weights_low, grads[:, columns], NN, preferred_element_type=jnp.float32
         ).astype(jnp.bfloat16)
 
     def one_group(index, carry):
-        @pl.when(index + 1 < groups)
-        def _():
-            for one in fetches(index + 1):
-                one.start()
-
-        for one in fetches(index):
-            one.wait()
-
         @pl.when(index == 0)
         def _():
             for one in in_parts(keys, key_held, key_sem):
@@ -237,8 +226,8 @@
 def key_kernel(
     list_size, group, scale, places, lengths, queries, grads, keys, values, weights,
     query_grad, terms,
-    query_held, grad_held, key_held, value_held, weights_held, made, query_made,
-    query_sem, grad_sem, key_sem, value_sem, weights_sem, out_sem, query_out_sem,
+    key_held, value_held, weights_held, made, query_made,
+    key_sem, value_sem, weights_sem, out_sem, query_out_sem,
 ):
     cols = keys.shape[2]
     groups = lengths.shape[0] // group
@@ -247,14 +236,9 @@
     def columns_of(index):
         return pl.ds(pl.multiple_of(index * width, width), width)
 
-    def fetches(index):
-        columns = columns_of(index)
+    def weights_part(index):
         heads = pl.ds(index * group, group)
-        return [
-            copy(grads.at[:, columns], grad_held.at[:, columns], grad_sem.at[index]),
-            copy(weights.at[heads], weights_held.at[heads], weights_sem.at[index]),
-            copy(queries.at[:, columns], query_held.at[:, columns], query_sem.at[index]),
-        ]
+        return copy(weights.at[heads], weights_held.at[heads], weights_sem.at[index])
 
     def tile_fetches():
         return in_parts(values, value_held, value_sem) + in_parts(keys, key_held, key_sem)
@@ -265,7 +249,7 @@
             query_made.at[:, columns], query_grad.at[:, columns], query_out_sem.at[index]
         )
 
-    for one in fetches(0) + tile_fetches():
+    for one in tile_fetches() + [weights_part(index) for index in range(groups)]:
         one.start()
 
     def compute(head):
@@ -276,25 +260,19 @@
         weight = weights_held[head]
         weight_low = weight.astype(jnp.bfloat16).astype(jnp.float32)
         dweights = lax.dot_general(
-            value, grad_held[:, columns], NT, preferred_element_type=jnp.float32
+            value, grads[:, columns], NT, preferred_element_type=jnp.float32
         )
         row_delta = jnp.sum(weight_low * dweights, axis=0, keepdims=True)
         dscores = (weight * (dweights - row_delta)).astype(jnp.bfloat16)
         flipped = lax.dot_general(key, dscores, TN, preferred_element_type=jnp.float32)
         query_made[:, columns] = (flipped * scale).astype(jnp.bfloat16).T
         made_terms = lax.dot_general(
-            dscores, query_held[:, columns], NN, preferred_element_type=jnp.float32
+            dscores, queries[:, columns], NN, preferred_element_type=jnp.float32
         )
         return (made_terms * scale).astype(jnp.bfloat16)
 
     def one_group(index, carry):
-        @pl.when(index + 1 < groups)
-        def _():
-            for one in fetches(index + 1):
-                one.start()
-
-        for one in fetches(index):
-            one.wait()
+        weights_part(index).wait()
 
         @pl.when(index == 0)
         def _():
@@ -385,6 +363,9 @@
         parts = lax.all_to_all(parts, "ctx", split_axis=0, concat_axis=0, tiled=True)
         return parts.reshape(packed.shape)
 
+    def near(value):
+        return pltpu.with_memory_space_constraint(value, pltpu.VMEM)
+
     def pack(name, source):
         return pl.pallas_call(
             functools.partial(pack_kernel, add_parts),
@@ -396,11 +377,8 @@
             name=name,
         )(codes, source)
 
-    def near(value):
-        return pltpu.with_memory_space_constraint(value, pltpu.VMEM)
-
     def wide_sum(rows):
-        return pltpu.VMEM((3 * rows, column_count), jnp.float32)
+        return pltpu.VMEM((2 * head_count + 1, rows, head_dim), jnp.float32)
 
     def placed(name, value, cost):
         return pl.pallas_call(
@@ -430,7 +408,7 @@
     fetched_keys = exchanged(pack("pack_keys", keys[0]))
     handed_codes = shifted(codes, "section", -1)
     packed_values, handed_codes, places, my_lengths = lax.optimization_barrier(
-        (pack("pack_values", values[0]), handed_codes, places, my_lengths)
+        (pack("pack_values", near(values[0])), handed_codes, places, my_lengths)
     )
     fetched_values = exchanged(packed_values)
     weights_shape = (head_count, list_size * block_rows, row_count)
@@ -442,25 +420,33 @@
             packed_shape(last_rows),
             jax.ShapeDtypeStruct(weights_shape, jnp.float32),
         ),
-        in_specs=[SMEM, SMEM, ANY, ANY, ANY],
+        in_specs=[SMEM, SMEM, VMEM, VMEM, ANY],
         out_specs=(ANY, ANY, ANY),
-        scratch_shapes=[flat, flat, slot_tiles]
+        scratch_shapes=[slot_tiles]
         + [vmem(slots, rows, head_dim) for rows in (first_rows, last_rows)]
-        + [weights_tile, wide_sem, wide_sem, part_sem, part_sem, part_sem, wide_sem],
+        + [weights_tile, part_sem, part_sem, part_sem, wide_sem],
         compiler_params=PARAMS,
         name="value_terms",
-    )(places, my_lengths, queries[0], out_grad[0], fetched_keys)
+    )(places, my_lengths, near(queries[0]), near(out_grad[0]), fetched_keys)
     handed_terms = shifted(last_terms, "section", -1)
     query_grad, key_terms = pl.pallas_call(
         functools.partial(key_kernel, list_size, group, scale),
         out_shape=(flat_shape, packed_shape(block_rows)),
-        in_specs=[SMEM, SMEM, ANY, ANY, ANY, ANY, ANY],
+        in_specs=[SMEM, SMEM, VMEM, VMEM, ANY, ANY, ANY],
         out_specs=(ANY, ANY),
-        scratch_shapes=[flat, flat, slot_tiles, slot_tiles, weights_tile, slot_tiles, flat]
-        + [wide_sem, wide_sem, part_sem, part_sem, wide_sem, part_sem, wide_sem],
+        scratch_shapes=[slot_tiles, slot_tiles, weights_tile, slot_tiles, flat]
+        + [part_sem, part_sem, wide_sem, part_sem, wide_sem],
         compiler_params=PARAMS,
         name="key_terms",
-    )(places, my_lengths, queries[0], out_grad[0], fetched_keys, fetched_values, weights)
+    )(
+        places,
+        my_lengths,
+        near(queries[0]),
+        near(out_grad[0]),
+        fetched_keys,
+        fetched_values,
+        weights,
+    )
     first_values = add_up("sum_values", exchanged(first_terms))
     handed_first = shifted(first_values, "section", -1)
     key_terms, handed_terms = lax.optimization_barrier((key_terms, handed_terms))

time: 218 us -> 216 us (level)
  local copies, waits for them, and re-layouts: 5.42 us -> 2.81 us
    unnamed x17, local copies, waits for them, and re-layouts: 3.4 us -> 0.74 us
  transfers between devices with their start and end apart: 10 -> 10, of which waited for: 9 -> 7; matrix products, arithmetic and copies ran while one was open for 2% -> 2% of each run, Pallas kernels for 19% -> 19%
where the time goes in v9:
time: 216 us; the launch traced here: 215 us
  waiting for transfers between devices  106 us (49%)
  starting transfers between devices  56 us (26%)
  Pallas kernels  46 us (21%)
  other arithmetic  4 us (2%)
  local copies, waits for them, and re-layouts  2.81 us (1%)
    all_to_all x5, waiting for transfers between devices, exchanged(): lax.all_to_all(parts, 'ctx', split_axis=0, concat_axis=0, tiled=True)  72.8 us
    all_to_all x5, starting transfers between devices, exchanged(): lax.all_to_all(parts, 'ctx', split_axis=0, concat_axis=0, tiled=True)  33.4 us
    ppermute x5, waiting for transfers between devices, shifted(): return lax.ppermute(value, axis, pairs)  32.7 us
    ppermute x5, starting transfers between devices, shifted(): return lax.ppermute(value, axis, pairs)  22.6 us
    pallas_call x1, Pallas kernels, local(): pl.pallas_call(functools.partial(key_kernel, list_size, group, scale), ou...  17 us
    pallas_call x1, Pallas kernels, local(): pl.pallas_call(functools.partial(value_kernel, list_size, group, scale),...  12.1 us
    pallas_call x2, Pallas kernels, pack(): pl.pallas_call(functools.partial(pack_kernel, add_parts), out_shape=packe...  6.37 us
    pallas_call x2, Pallas kernels, add_up(): pl.pallas_call(functools.partial(sum_kernel, add_parts), out_shape=jax.Sh...  5.51 us
  transfers between devices with their start and end apart: 10, of which 7 were waited for; matrix products, arithmetic and copies ran while one was open for 2% of the time, Pallas kernels for 19%

profile of v9, /device:TPU:8, one launch (start us, length us, event | category | flops | bytes accessed | tf_op | source)
XLA Modules:
  0.0 215.2 jit_solution(5277454763326655588)
XLA Ops:
  0.7 0.7 copy.40
  1.4 0.8 fusion
  2.2 0.2 select_reduce_fusion
  2.4 0.1 copy.34
  2.5 0.7 reshape.173.codes
  3.2 3.8 %pack_keys.1 = bf16[96,128,128]{2,1,0:T(8,128)(2,1)} custom-call(s32[96]{0:T(128)} %reshape.173.codes, bf16[256,2560]{1,0:T(8,128)(2,1)} %bitcast.41), custom_call_target="tpu_custom_call" | custom-call | tf_op jit(solution)/shard_map/pack_keys/pallas_call | solution.py:370
  7.0 0.0 copy-start.4
  7.0 7.7 %all-to-all-start = ((bf16[32,3,128,128]{3,2,1,0:T(8,128)(2,1)}), bf16[32,3,128,128]{3,2,1,0:T(8,128)(2,1)}, u32[]{:S(2)}, u32[]{:S(2)}) async-start(bf16[32,3,128,128]{3,2,1,0:T(8,128)(2,1)} %bitcast.37), calls=%async_computation | async-start | bytes 6291456 | tf_op jit(solution)/shard_map/all_to_all | solution.py:363
  14.7 5.9 %collective-permute-start = (s32[96]{0:T(128)S(1)}, s32[96]{0:T(128)S(1)}, u32[]{:S(2)}, u32[]{:S(2)}) collective-permute-start(s32[96]{0:T(128)S(1)} %copy-done.6), channel_id=1, source_target_pairs={{0,7},{1,0},{2,1},{3,2},{4,3},{5,4},{6,5},{7,6},{8,15},{9,8},{10,9... | collective-permute-start | bytes 1160 | tf_op jit(solution)/shard_map/ppermute | solution.py:25
  20.7 0.5 dynamic-slice_reduce_fusion.lengths
  21.2 0.1 iota_compare_fusion.3
  21.3 0.1 lt.105
  21.4 0.5 fusion.6
  21.9 0.1 shift_right_arithmetic.25
  22.0 0.1 copy.36
  22.1 0.1 fusion.3
  22.2 0.1 copy.35
  22.3 0.1 copy.37
  22.4 0.1 broadcast_select_fusion
  22.5 1.6 select_reduce_fusion.1
  24.1 0.1 reduce_sum.32
  24.2 0.1 fusion.5
  24.3 0.1 broadcast_in_dim.87
  24.4 0.1 broadcast_in_dim.88
  24.5 0.5 add_select_fusion.places
  25.0 2.6 %pack_values.1 = bf16[96,128,128]{2,1,0:T(8,128)(2,1)} custom-call(s32[96]{0:T(128)} %reshape.173.codes, bf16[256,2560]{1,0:T(8,128)(2,1)S(1)} %bitcast.36), custom_call_target="tpu_custom_call" | custom-call | tf_op jit(solution)/shard_map/pack_values/pallas_call | solution.py:370
  27.6 26.7 %all-to-all-done = bf16[32,3,128,128]{3,2,1,0:T(8,128)(2,1)} async-done(((bf16[32,3,128,128]{3,2,1,0:T(8,128)(2,1)}), bf16[32,3,128,128]{3,2,1,0:T(8,128)(2,1)}, u32[]{:S(2)}, u32[]{:S(2)}) %all-to-all-start) | async-done | bytes 3145760 | tf_op jit(solution)/shard_map/all_to_all | solution.py:363
  54.3 5.6 %all-to-all-start.1 = ((bf16[32,3,128,128]{3,2,1,0:T(8,128)(2,1)}), bf16[32,3,128,128]{3,2,1,0:T(8,128)(2,1)}, u32[]{:S(2)}, u32[]{:S(2)}) async-start(bf16[32,3,128,128]{3,2,1,0:T(8,128)(2,1)} %bitcast.38), calls=%async_computation.1 | async-start | bytes 6291456 | tf_op jit(solution)/shard_map/all_to_all | solution.py:363
  59.9 12.1 %value_terms.1 = (bf16[96,48,128]{2,1,0:T(8,128)(2,1)}, bf16[96,80,128]{2,1,0:T(8,128)(2,1)}, f32[20,512,256]{2,1,0:T(8,128)}) custom-call(s32[80]{0:T(128)} %add_select_fusion.places, s32[20]{0:T(128)} %copy-done.5, bf16[256,2560]{1,0:T(8,128)(2,1)S(1)} %bitcast.32, bf16[256,2560]{1,0:T(8,128)(2,1)S(1)} %bitcast.34, bf16[96,128,128]{2,1,0:T(8,128)(2,1)} %bitcast.9.keys), custom_call_target="tpu_custom_call" | custom-call | tf_op jit(solution)/shard_map/value_terms/pallas_call | solution.py:416
  72.0 5.9 %collective-permute-start.1 = (bf16[96,80,128]{2,1,0:T(8,128)(2,1)}, bf16[96,80,128]{2,1,0:T(8,128)(2,1)}, u32[]{:S(2)}, u32[]{:S(2)}) collective-permute-start(bf16[96,80,128]{2,1,0:T(8,128)(2,1)} %get-tuple-element.24), channel_id=1, source_target_pairs={{0,7},{1,0},{2,1},{3,2},{4,3},{5,4},{6,5},{7,6},{8,15},{9,8},{10,9... | collective-permute-start | bytes 5898248 | tf_op jit(solution)/shard_map/ppermute | solution.py:25
  77.9 21.6 %all-to-all-done.1 = bf16[32,3,128,128]{3,2,1,0:T(8,128)(2,1)} async-done(((bf16[32,3,128,128]{3,2,1,0:T(8,128)(2,1)}), bf16[32,3,128,128]{3,2,1,0:T(8,128)(2,1)}, u32[]{:S(2)}, u32[]{:S(2)}) %all-to-all-start.1) | async-done | bytes 3145760 | tf_op jit(solution)/shard_map/all_to_all | solution.py:363
  99.4 5.3 %all-to-all-start.3 = ((bf16[32,3,48,128]{3,2,1,0:T(8,128)(2,1)}), bf16[32,3,48,128]{3,2,1,0:T(8,128)(2,1)}, u32[]{:S(2)}, u32[]{:S(2)}) async-start(bf16[32,3,48,128]{3,2,1,0:T(8,128)(2,1)} %bitcast.44), calls=%async_computation.3 | async-start | bytes 2359296 | tf_op jit(solution)/shard_map/all_to_all | solution.py:363
  104.7 17.0 %key_terms.1 = (bf16[256,2560]{1,0:T(8,128)(2,1)}, bf16[96,128,128]{2,1,0:T(8,128)(2,1)}) custom-call(s32[80]{0:T(128)} %add_select_fusion.places, s32[20]{0:T(128)} %copy-done.5, bf16[256,2560]{1,0:T(8,128)(2,1)S(1)} %bitcast.33, bf16[256,2560]{1,0:T(8,128)(2,1)S(1)} %bitcast.35, bf16[96,128,128]{2,1,0:T(8,128)(2,1)} %bitcast.9.keys, ...), custom_call_target="tpu_custom_call" | custom-call | tf_op jit(solution)/shard_map/key_terms/pallas_call | solution.py:432
  121.8 7.4 %all-to-all-start.2 = ((bf16[32,3,128,128]{3,2,1,0:T(8,128)(2,1)}), bf16[32,3,128,128]{3,2,1,0:T(8,128)(2,1)S(1)}, u32[]{:S(2)}, u32[]{:S(2)}) async-start(bf16[32,3,128,128]{3,2,1,0:T(8,128)(2,1)} %bitcast.40), calls=%async_computation.2 | async-start | bytes 6291456 | tf_op jit(solution)/shard_map/all_to_all | solution.py:363
  129.1 5.9 %collective-permute-start.2 = (bf16[256,2560]{1,0:T(8,128)(2,1)}, bf16[256,2560]{1,0:T(8,128)(2,1)S(1)}, u32[]{:S(2)}, u32[]{:S(2)}) collective-permute-start(bf16[256,2560]{1,0:T(8,128)(2,1)} %get-tuple-element.26), channel_id=1, source_target_pairs={{0,7},{1,0},{2,1},{3,2},{4,3},{5,4},{6,5},{7,6},{8,15},{9,8},{10,9... | collective-permute-start | bytes 3932168 | tf_op jit(solution)/shard_map/ppermute | solution.py:25
  135.1 2.7 %sum_values.1 = bf16[96,2560]{1,0:T(8,128)(2,1)} custom-call(s32[96]{0:T(128)} %reshape.173.codes, bf16[96,48,128]{2,1,0:T(8,128)(2,1)} %bitcast.15.terms), custom_call_target="tpu_custom_call" | custom-call | tf_op jit(solution)/shard_map/sum_values/pallas_call | solution.py:396
  137.8 1.1 collective-permute-start.3
  138.9 25.7 %collective-permute-done.2.source = bf16[256,2560]{1,0:T(8,128)(2,1)S(1)} collective-permute-done((bf16[256,2560]{1,0:T(8,128)(2,1)}, bf16[256,2560]{1,0:T(8,128)(2,1)S(1)}, u32[]{:S(2)}, u32[]{:S(2)}) %collective-permute-start.2) | collective-permute-done | bytes 1310752 | tf_op jit(solution)/shard_map/ppermute | solution.py:25
  164.5 1.1 place_queries.1
  165.7 3.0 %all-to-all-done.2 = bf16[32,3,128,128]{3,2,1,0:T(8,128)(2,1)S(1)} async-done(((bf16[32,3,128,128]{3,2,1,0:T(8,128)(2,1)}), bf16[32,3,128,128]{3,2,1,0:T(8,128)(2,1)S(1)}, u32[]{:S(2)}, u32[]{:S(2)}) %all-to-all-start.2) | async-done | bytes 3145760 | tf_op jit(solution)/shard_map/all_to_all | solution.py:363
  168.6 2.8 %sum_keys.1 = bf16[256,2560]{1,0:T(8,128)(2,1)} custom-call(s32[96]{0:T(128)} %reshape.173.codes, bf16[96,128,128]{2,1,0:T(8,128)(2,1)S(1)} %bitcast.30), custom_call_target="tpu_custom_call" | custom-call | tf_op jit(solution)/shard_map/sum_keys/pallas_call | solution.py:396
  171.5 2.8 %collective-permute-done.3.head_part = bf16[96,2560]{1,0:T(8,128)(2,1)} collective-permute-done((bf16[96,2560]{1,0:T(8,128)(2,1)}, bf16[96,2560]{1,0:T(8,128)(2,1)}, u32[]{:S(2)}, u32[]{:S(2)}) %collective-permute-start.3) | collective-permute-done | bytes 491552 | tf_op jit(solution)/shard_map/ppermute | solution.py:25
  174.3 7.4 %all-to-all-start.4 = ((bf16[32,3,80,128]{3,2,1,0:T(8,128)(2,1)}), bf16[32,3,80,128]{3,2,1,0:T(8,128)(2,1)S(1)}, u32[]{:S(2)}, u32[]{:S(2)}) async-start(bf16[32,3,80,128]{3,2,1,0:T(8,128)(2,1)} %bitcast.17), calls=%async_computation.4 | async-start | bytes 3932160 | tf_op jit(solution)/shard_map/all_to_all | solution.py:363
  181.7 3.8 %collective-permute-start.4 = (bf16[256,2560]{1,0:T(8,128)(2,1)}, bf16[256,2560]{1,0:T(8,128)(2,1)S(1)}, u32[]{:S(2)}, u32[]{:S(2)}) collective-permute-start(bf16[256,2560]{1,0:T(8,128)(2,1)} %sum_keys.1), channel_id=1, source_target_pairs={{0,7},{1,0},{2,1},{3,2},{4,3},{5,4},{6,5},{7,6},{8,15},{9,8},{10,9... | collective-permute-start | bytes 3932168 | tf_op jit(solution)/shard_map/ppermute | solution.py:25
  185.4 21.6 %all-to-all-done.4 = bf16[32,3,80,128]{3,2,1,0:T(8,128)(2,1)S(1)} async-done(((bf16[32,3,80,128]{3,2,1,0:T(8,128)(2,1)}), bf16[32,3,80,128]{3,2,1,0:T(8,128)(2,1)S(1)}, u32[]{:S(2)}, u32[]{:S(2)}) %all-to-all-start.4) | async-done | bytes 1966112 | tf_op jit(solution)/shard_map/all_to_all | solution.py:363
  207.0 2.8 %join_values.1.after = bf16[256,2560]{1,0:T(8,128)(2,1)} custom-call(s32[96]{0:T(128)} %copy-done.7, bf16[96,2560]{1,0:T(8,128)(2,1)} %collective-permute-done.3.head_part, bf16[96,80,128]{2,1,0:T(8,128)(2,1)S(1)} %bitcast.31), custom_call_target="tpu_custom_call" | custom-call | tf_op jit(solution)/shard_map/join_values/pallas_call | solution.py:463
  209.9 4.2 %collective-permute-done.4.source = bf16[256,2560]{1,0:T(8,128)(2,1)S(1)} collective-permute-done((bf16[256,2560]{1,0:T(8,128)(2,1)}, bf16[256,2560]{1,0:T(8,128)(2,1)S(1)}, u32[]{:S(2)}, u32[]{:S(2)}) %collective-permute-start.4) | collective-permute-done | bytes 1310752 | tf_op jit(solution)/shard_map/ppermute | solution.py:25
  214.1 1.1 place_keys.1
  (22 shorter events, 0.1 us)
Async XLA Ops:
  7.0 7.8 %copy-start.6 = (s32[96]{0:T(128)S(1)}, s32[96]{0:T(128)}, u32[]{:S(2)}) copy-start(s32[96]{0:T(128)} %reshape.173.codes) | copy-start | bytes 1156
  7.0 13.7 %copy-start.4 = (s32[1,32,20]{1,0,2:T(1,128)S(1)}, s32[1,32,20]{1,0,2:T(1,128)}, u32[]{:S(2)}) copy-start(s32[1,32,20]{1,0,2:T(1,128)} %param.11) | copy-start | bytes 7684
  7.0 14.4 %copy-start.3 = (s32[1,32,20,4]{1,3,2,0:T(4,128)S(1)}, s32[1,32,20,4]{1,3,2,0:T(4,128)}, u32[]{:S(2)}) copy-start(s32[1,32,20,4]{1,3,2,0:T(4,128)} %param.10) | copy-start | bytes 30724
  7.0 18.0 %copy-start.2 = (bf16[1,256,2560]{2,1,0:T(8,128)(2,1)S(1)}, bf16[1,256,2560]{2,1,0:T(8,128)(2,1)}, u32[]{:S(2)}) copy-start(bf16[1,256,2560]{2,1,0:T(8,128)(2,1)} %param.8) | copy-start | bytes 3932164
  7.0 47.3 %all-to-all-start = ((bf16[32,3,128,128]{3,2,1,0:T(8,128)(2,1)}), bf16[32,3,128,128]{3,2,1,0:T(8,128)(2,1)}, u32[]{:S(2)}, u32[]{:S(2)}) async-start(bf16[32,3,128,128]{3,2,1,0:T(8,128)(2,1)} %bitcast.37), calls=%async_computation | async-start | bytes 6291456 | tf_op jit(solution)/shard_map/all_to_all | solution.py:363
  14.7 12.9 %collective-permute-start = (s32[96]{0:T(128)S(1)}, s32[96]{0:T(128)S(1)}, u32[]{:S(2)}, u32[]{:S(2)}) collective-permute-start(s32[96]{0:T(128)S(1)} %copy-done.6), channel_id=1, source_target_pairs={{0,7},{1,0},{2,1},{3,2},{4,3},{5,4},{6,5},{7,6},{8,15},{9,8},{10,9... | collective-permute-start | bytes 1160 | tf_op jit(solution)/shard_map/ppermute | solution.py:25
  21.2 6.4 %copy-start.5 = (s32[20]{0:T(128)}, s32[20]{0:T(128)S(1)}, u32[]{:S(2)}) copy-start(s32[20]{0:T(128)S(1)} %dynamic-slice_reduce_fusion.lengths) | copy-start | bytes 244
  27.6 26.7 %copy-start.7 = (s32[96]{0:T(128)}, s32[96]{0:T(128)S(1)}, u32[]{:S(2)}) copy-start(s32[96]{0:T(128)S(1)} %collective-permute-done.codes) | copy-start | bytes 1156
  54.3 5.6 %copy-start = (bf16[1,256,2560]{2,1,0:T(8,128)(2,1)S(1)}, bf16[1,256,2560]{2,1,0:T(8,128)(2,1)}, u32[]{:S(2)}) copy-start(bf16[1,256,2560]{2,1,0:T(8,128)(2,1)} %param.6) | copy-start | bytes 3932164
  54.3 5.6 %copy-start.1 = (bf16[1,256,2560]{2,1,0:T(8,128)(2,1)S(1)}, bf16[1,256,2560]{2,1,0:T(8,128)(2,1)}, u32[]{:S(2)}) copy-start(bf16[1,256,2560]{2,1,0:T(8,128)(2,1)} %param.9) | copy-start | bytes 3932164
  54.3 45.1 %all-to-all-start.1 = ((bf16[32,3,128,128]{3,2,1,0:T(8,128)(2,1)}), bf16[32,3,128,128]{3,2,1,0:T(8,128)(2,1)}, u32[]{:S(2)}, u32[]{:S(2)}) async-start(bf16[32,3,128,128]{3,2,1,0:T(8,128)(2,1)} %bitcast.38), calls=%async_computation.1 | async-start | bytes 6291456 | tf_op jit(solution)/shard_map/all_to_all | solution.py:363
  72.0 49.8 %collective-permute-start.1 = (bf16[96,80,128]{2,1,0:T(8,128)(2,1)}, bf16[96,80,128]{2,1,0:T(8,128)(2,1)}, u32[]{:S(2)}, u32[]{:S(2)}) collective-permute-start(bf16[96,80,128]{2,1,0:T(8,128)(2,1)} %get-tuple-element.24), channel_id=1, source_target_pairs={{0,7},{1,0},{2,1},{3,2},{4,3},{5,4},{6,5},{7,6},{8,15},{9,8},{10,9... | collective-permute-start | bytes 5898248 | tf_op jit(solution)/shard_map/ppermute | solution.py:25
  99.4 22.3 %all-to-all-start.3 = ((bf16[32,3,48,128]{3,2,1,0:T(8,128)(2,1)}), bf16[32,3,48,128]{3,2,1,0:T(8,128)(2,1)}, u32[]{:S(2)}, u32[]{:S(2)}) async-start(bf16[32,3,48,128]{3,2,1,0:T(8,128)(2,1)} %bitcast.44), calls=%async_computation.3 | async-start | bytes 2359296 | tf_op jit(solution)/shard_map/all_to_all | solution.py:363
  121.8 46.9 %all-to-all-start.2 = ((bf16[32,3,128,128]{3,2,1,0:T(8,128)(2,1)}), bf16[32,3,128,128]{3,2,1,0:T(8,128)(2,1)S(1)}, u32[]{:S(2)}, u32[]{:S(2)}) async-start(bf16[32,3,128,128]{3,2,1,0:T(8,128)(2,1)} %bitcast.40), calls=%async_computation.2 | async-start | bytes 6291456 | tf_op jit(solution)/shard_map/all_to_all | solution.py:363
  129.1 35.4 %collective-permute-start.2 = (bf16[256,2560]{1,0:T(8,128)(2,1)}, bf16[256,2560]{1,0:T(8,128)(2,1)S(1)}, u32[]{:S(2)}, u32[]{:S(2)}) collective-permute-start(bf16[256,2560]{1,0:T(8,128)(2,1)} %get-tuple-element.26), channel_id=1, source_target_pairs={{0,7},{1,0},{2,1},{3,2},{4,3},{5,4},{6,5},{7,6},{8,15},{9,8},{10,9... | collective-permute-start | bytes 3932168 | tf_op jit(solution)/shard_map/ppermute | solution.py:25
  137.8 36.5 %collective-permute-start.3 = (bf16[96,2560]{1,0:T(8,128)(2,1)}, bf16[96,2560]{1,0:T(8,128)(2,1)}, u32[]{:S(2)}, u32[]{:S(2)}) collective-permute-start(bf16[96,2560]{1,0:T(8,128)(2,1)} %sum_values.1), channel_id=1, source_target_pairs={{0,7},{1,0},{2,1},{3,2},{4,3},{5,4},{6,5},{7,6},{8,15},{9,8},{10,9... | collective-permute-start | bytes 1474568 | tf_op jit(solution)/shard_map/ppermute | solution.py:25
  174.3 32.8 %all-to-all-start.4 = ((bf16[32,3,80,128]{3,2,1,0:T(8,128)(2,1)}), bf16[32,3,80,128]{3,2,1,0:T(8,128)(2,1)S(1)}, u32[]{:S(2)}, u32[]{:S(2)}) async-start(bf16[32,3,80,128]{3,2,1,0:T(8,128)(2,1)} %bitcast.17), calls=%async_computation.4 | async-start | bytes 3932160 | tf_op jit(solution)/shard_map/all_to_all | solution.py:363
  181.7 32.4 %collective-permute-start.4 = (bf16[256,2560]{1,0:T(8,128)(2,1)}, bf16[256,2560]{1,0:T(8,128)(2,1)S(1)}, u32[]{:S(2)}, u32[]{:S(2)}) collective-permute-start(bf16[256,2560]{1,0:T(8,128)(2,1)} %sum_keys.1), channel_id=1, source_target_pairs={{0,7},{1,0},{2,1},{3,2},{4,3},{5,4},{6,5},{7,6},{8,15},{9,8},{10,9... | collective-permute-start | bytes 3932168 | tf_op jit(solution)/shard_map/ppermute | solution.py:25

commit v10 on v9

--- a/solution.py
+++ b/solution.py
@@ -34,12 +34,9 @@
     )
 
 
-def pack_kernel(parts, codes, source, packed, held, made, got, sent):
+def pack_kernel(parts, codes, source, packed, made, sent):
     slots, rows, cols = packed.shape
     step = slots // parts
-    whole = copy(source, held, got)
-    whole.start()
-    whole.wait()
 
     def part_of(part):
         where = pl.ds(part * step, step)
@@ -48,7 +45,7 @@
     def one_part(part, carry):
         for item in range(step):
             slot = part * step + item
-            made[slot] = held[tile_of(jnp.maximum(codes[slot], 0), rows, cols)]
+            made[slot] = source[tile_of(jnp.maximum(codes[slot], 0), rows, cols)]
         part_of(part).start()
         return carry
 
@@ -249,7 +246,9 @@
             query_made.at[:, columns], query_grad.at[:, columns], query_out_sem.at[index]
         )
 
-    for one in tile_fetches() + [weights_part(index) for index in range(groups)]:
+    parts = key_sem.shape[0]
+    tile_starts = tile_fetches()
+    for one in tile_starts[:parts] + [weights_part(0)] + tile_starts[parts:]:
         one.start()
 
     def compute(head):
@@ -272,6 +271,10 @@
         return (made_terms * scale).astype(jnp.bfloat16)
 
     def one_group(index, carry):
+        @pl.when(index + 1 < groups)
+        def _():
+            weights_part(index + 1).start()
+
         weights_part(index).wait()
 
         @pl.when(index == 0)
@@ -370,9 +373,9 @@
         return pl.pallas_call(
             functools.partial(pack_kernel, add_parts),
             out_shape=packed_shape(block_rows),
-            in_specs=[SMEM, ANY],
+            in_specs=[SMEM, VMEM],
             out_specs=ANY,
-            scratch_shapes=[flat, vmem(slots, block_rows, head_dim), dma, dma((add_parts,))],
+            scratch_shapes=[vmem(slots, block_rows, head_dim), dma((add_parts,))],
             compiler_params=PARAMS,
             name=name,
         )(codes, source)
@@ -405,7 +408,7 @@
 
     slot_tiles = vmem(slots, block_rows, head_dim)
     wide_sem, part_sem = dma((groups,)), dma((add_parts,))
-    fetched_keys = exchanged(pack("pack_keys", keys[0]))
+    fetched_keys = exchanged(pack("pack_keys", near(keys[0])))
     handed_codes = shifted(codes, "section", -1)
     packed_values, handed_codes, places, my_lengths = lax.optimization_barrier(
         (pack("pack_values", near(values[0])), handed_codes, places, my_lengths)

time: 216 us -> 215 us (level)
  Pallas kernels: 46 us -> 42.8 us
  transfers between devices with their start and end apart: 10 -> 10, of which waited for: 7 -> 9; matrix products, arithmetic and copies ran while one was open for 2% -> 2% of each run, Pallas kernels for 19% -> 18%
where the time goes in v10:
time: 215 us; the launch traced here: 214 us
  waiting for transfers between devices  107 us (50%)
  starting transfers between devices  54.4 us (25%)
  Pallas kernels  42.8 us (20%)
  local copies, waits for them, and re-layouts  4.15 us (2%)
  other arithmetic  4 us (2%)
    all_to_all x5, waiting for transfers between devices, exchanged(): lax.all_to_all(parts, 'ctx', split_axis=0, concat_axis=0, tiled=True)  74.5 us
    ppermute x5, waiting for transfers between devices, shifted(): return lax.ppermute(value, axis, pairs)  32.8 us
    all_to_all x5, starting transfers between devices, exchanged(): lax.all_to_all(parts, 'ctx', split_axis=0, concat_axis=0, tiled=True)  32.3 us
    ppermute x5, starting transfers between devices, shifted(): return lax.ppermute(value, axis, pairs)  22.1 us
    pallas_call x1, Pallas kernels, local(): pl.pallas_call(functools.partial(key_kernel, list_size, group, scale), ou...  15.2 us
    pallas_call x1, Pallas kernels, local(): pl.pallas_call(functools.partial(value_kernel, list_size, group, scale),...  12 us
    pallas_call x2, Pallas kernels, add_up(): pl.pallas_call(functools.partial(sum_kernel, add_parts), out_shape=jax.Sh...  5.5 us
    pallas_call x2, Pallas kernels, pack(): pl.pallas_call(functools.partial(pack_kernel, add_parts), out_shape=packe...  4.95 us
  transfers between devices with their start and end apart: 10, of which 9 were waited for; matrix products, arithmetic and copies ran while one was open for 2% of the time, Pallas kernels for 18%

profile of v10, /device:TPU:8, one launch (start us, length us, event | category | flops | bytes accessed | tf_op | source)
XLA Modules:
  0.0 213.6 jit_solution(8269155501809536905)
XLA Ops:
  0.7 0.7 copy.40
  1.4 0.8 fusion
  2.2 0.2 select_reduce_fusion
  2.4 0.1 copy.34
  2.5 0.7 reshape.173.codes
  3.2 1.3 copy-done.2
  4.5 2.5 %pack_keys.1 = bf16[96,128,128]{2,1,0:T(8,128)(2,1)} custom-call(s32[96]{0:T(128)} %reshape.173.codes, bf16[256,2560]{1,0:T(8,128)(2,1)S(1)} %bitcast.36), custom_call_target="tpu_custom_call" | custom-call | tf_op jit(solution)/shard_map/pack_keys/pallas_call | solution.py:373
  7.0 7.7 %all-to-all-start = ((bf16[32,3,128,128]{3,2,1,0:T(8,128)(2,1)}), bf16[32,3,128,128]{3,2,1,0:T(8,128)(2,1)}, u32[]{:S(2)}, u32[]{:S(2)}) async-start(bf16[32,3,128,128]{3,2,1,0:T(8,128)(2,1)} %bitcast.38), calls=%async_computation | async-start | bytes 6291456 | tf_op jit(solution)/shard_map/all_to_all | solution.py:366
  14.8 5.9 %collective-permute-start = (s32[96]{0:T(128)S(1)}, s32[96]{0:T(128)S(1)}, u32[]{:S(2)}, u32[]{:S(2)}) collective-permute-start(s32[96]{0:T(128)S(1)} %copy-done.7), channel_id=1, source_target_pairs={{0,7},{1,0},{2,1},{3,2},{4,3},{5,4},{6,5},{7,6},{8,15},{9,8},{10,9... | collective-permute-start | bytes 1160 | tf_op jit(solution)/shard_map/ppermute | solution.py:25
  20.7 0.5 dynamic-slice_reduce_fusion.lengths
  21.3 0.1 lt.105
  21.4 0.5 fusion.6
  21.9 0.1 shift_right_arithmetic.25
  22.0 0.1 copy.36
  22.1 0.1 fusion.3
  22.2 0.1 copy.35
  22.3 0.1 copy.37
  22.4 0.1 broadcast_select_fusion
  22.5 1.6 select_reduce_fusion.1
  24.1 0.1 reduce_sum.32
  24.2 0.1 fusion.5
  24.4 0.1 broadcast_in_dim.88
  24.5 0.5 add_select_fusion.places
  25.0 2.5 %pack_values.1 = bf16[96,128,128]{2,1,0:T(8,128)(2,1)} custom-call(s32[96]{0:T(128)} %reshape.173.codes, bf16[256,2560]{1,0:T(8,128)(2,1)S(1)} %bitcast.37), custom_call_target="tpu_custom_call" | custom-call | tf_op jit(solution)/shard_map/pack_values/pallas_call | solution.py:373
  27.6 26.8 %all-to-all-done = bf16[32,3,128,128]{3,2,1,0:T(8,128)(2,1)} async-done(((bf16[32,3,128,128]{3,2,1,0:T(8,128)(2,1)}), bf16[32,3,128,128]{3,2,1,0:T(8,128)(2,1)}, u32[]{:S(2)}, u32[]{:S(2)}) %all-to-all-start) | async-done | bytes 3145760 | tf_op jit(solution)/shard_map/all_to_all | solution.py:366
  54.3 5.6 %all-to-all-start.1 = ((bf16[32,3,128,128]{3,2,1,0:T(8,128)(2,1)}), bf16[32,3,128,128]{3,2,1,0:T(8,128)(2,1)}, u32[]{:S(2)}, u32[]{:S(2)}) async-start(bf16[32,3,128,128]{3,2,1,0:T(8,128)(2,1)} %bitcast.39), calls=%async_computation.1 | async-start | bytes 6291456 | tf_op jit(solution)/shard_map/all_to_all | solution.py:366
  59.9 12.0 %value_terms.1 = (bf16[96,48,128]{2,1,0:T(8,128)(2,1)}, bf16[96,80,128]{2,1,0:T(8,128)(2,1)}, f32[20,512,256]{2,1,0:T(8,128)}) custom-call(s32[80]{0:T(128)} %add_select_fusion.places, s32[20]{0:T(128)} %copy-done.6, bf16[256,2560]{1,0:T(8,128)(2,1)S(1)} %bitcast.32, bf16[256,2560]{1,0:T(8,128)(2,1)S(1)} %bitcast.34, bf16[96,128,128]{2,1,0:T(8,128)(2,1)} %bitcast.9.keys), custom_call_target="tpu_custom_call" | custom-call | tf_op jit(solution)/shard_map/value_terms/pallas_call | solution.py:419
  72.0 5.9 %collective-permute-start.1 = (bf16[96,80,128]{2,1,0:T(8,128)(2,1)}, bf16[96,80,128]{2,1,0:T(8,128)(2,1)}, u32[]{:S(2)}, u32[]{:S(2)}) collective-permute-start(bf16[96,80,128]{2,1,0:T(8,128)(2,1)} %get-tuple-element.24), channel_id=1, source_target_pairs={{0,7},{1,0},{2,1},{3,2},{4,3},{5,4},{6,5},{7,6},{8,15},{9,8},{10,9... | collective-permute-start | bytes 5898248 | tf_op jit(solution)/shard_map/ppermute | solution.py:25
  77.9 21.5 %all-to-all-done.1 = bf16[32,3,128,128]{3,2,1,0:T(8,128)(2,1)} async-done(((bf16[32,3,128,128]{3,2,1,0:T(8,128)(2,1)}), bf16[32,3,128,128]{3,2,1,0:T(8,128)(2,1)}, u32[]{:S(2)}, u32[]{:S(2)}) %all-to-all-start.1) | async-done | bytes 3145760 | tf_op jit(solution)/shard_map/all_to_all | solution.py:366
  99.5 5.3 %all-to-all-start.3 = ((bf16[32,3,48,128]{3,2,1,0:T(8,128)(2,1)}), bf16[32,3,48,128]{3,2,1,0:T(8,128)(2,1)}, u32[]{:S(2)}, u32[]{:S(2)}) async-start(bf16[32,3,48,128]{3,2,1,0:T(8,128)(2,1)} %bitcast.44), calls=%async_computation.3 | async-start | bytes 2359296 | tf_op jit(solution)/shard_map/all_to_all | solution.py:366
  104.8 15.2 %key_terms.1 = (bf16[256,2560]{1,0:T(8,128)(2,1)}, bf16[96,128,128]{2,1,0:T(8,128)(2,1)}) custom-call(s32[80]{0:T(128)} %add_select_fusion.places, s32[20]{0:T(128)} %copy-done.6, bf16[256,2560]{1,0:T(8,128)(2,1)S(1)} %bitcast.33, bf16[256,2560]{1,0:T(8,128)(2,1)S(1)} %bitcast.35, bf16[96,128,128]{2,1,0:T(8,128)(2,1)} %bitcast.9.keys, ...), custom_call_target="tpu_custom_call" | custom-call | tf_op jit(solution)/shard_map/key_terms/pallas_call | solution.py:435
  120.0 0.6 collective-permute-done.1
  120.6 1.1 all-to-all-done.3
  121.7 6.3 %all-to-all-start.2 = ((bf16[32,3,128,128]{3,2,1,0:T(8,128)(2,1)}), bf16[32,3,128,128]{3,2,1,0:T(8,128)(2,1)S(1)}, u32[]{:S(2)}, u32[]{:S(2)}) async-start(bf16[32,3,128,128]{3,2,1,0:T(8,128)(2,1)} %bitcast.41), calls=%async_computation.2 | async-start | bytes 6291456 | tf_op jit(solution)/shard_map/all_to_all | solution.py:366
  128.0 5.4 %collective-permute-start.2 = (bf16[256,2560]{1,0:T(8,128)(2,1)}, bf16[256,2560]{1,0:T(8,128)(2,1)S(1)}, u32[]{:S(2)}, u32[]{:S(2)}) collective-permute-start(bf16[256,2560]{1,0:T(8,128)(2,1)} %get-tuple-element.26), channel_id=1, source_target_pairs={{0,7},{1,0},{2,1},{3,2},{4,3},{5,4},{6,5},{7,6},{8,15},{9,8},{10,9... | collective-permute-start | bytes 3932168 | tf_op jit(solution)/shard_map/ppermute | solution.py:25
  133.4 2.7 %sum_values.1 = bf16[96,2560]{1,0:T(8,128)(2,1)} custom-call(s32[96]{0:T(128)} %reshape.173.codes, bf16[96,48,128]{2,1,0:T(8,128)(2,1)} %bitcast.15.terms), custom_call_target="tpu_custom_call" | custom-call | tf_op jit(solution)/shard_map/sum_values/pallas_call | solution.py:399
  136.1 1.1 collective-permute-start.3
  137.2 25.7 %collective-permute-done.2.source = bf16[256,2560]{1,0:T(8,128)(2,1)S(1)} collective-permute-done((bf16[256,2560]{1,0:T(8,128)(2,1)}, bf16[256,2560]{1,0:T(8,128)(2,1)S(1)}, u32[]{:S(2)}, u32[]{:S(2)}) %collective-permute-start.2) | collective-permute-done | bytes 1310752 | tf_op jit(solution)/shard_map/ppermute | solution.py:25
  162.9 1.1 place_queries.1
  164.0 3.5 %all-to-all-done.2 = bf16[32,3,128,128]{3,2,1,0:T(8,128)(2,1)S(1)} async-done(((bf16[32,3,128,128]{3,2,1,0:T(8,128)(2,1)}), bf16[32,3,128,128]{3,2,1,0:T(8,128)(2,1)S(1)}, u32[]{:S(2)}, u32[]{:S(2)}) %all-to-all-start.2) | async-done | bytes 3145760 | tf_op jit(solution)/shard_map/all_to_all | solution.py:366
  167.5 2.8 %sum_keys.1 = bf16[256,2560]{1,0:T(8,128)(2,1)} custom-call(s32[96]{0:T(128)} %reshape.173.codes, bf16[96,128,128]{2,1,0:T(8,128)(2,1)S(1)} %bitcast.30), custom_call_target="tpu_custom_call" | custom-call | tf_op jit(solution)/shard_map/sum_keys/pallas_call | solution.py:399
  170.3 2.3 %collective-permute-done.3.head_part = bf16[96,2560]{1,0:T(8,128)(2,1)} collective-permute-done((bf16[96,2560]{1,0:T(8,128)(2,1)}, bf16[96,2560]{1,0:T(8,128)(2,1)}, u32[]{:S(2)}, u32[]{:S(2)}) %collective-permute-start.3) | collective-permute-done | bytes 491552 | tf_op jit(solution)/shard_map/ppermute | solution.py:25
  172.6 7.4 %all-to-all-start.4 = ((bf16[32,3,80,128]{3,2,1,0:T(8,128)(2,1)}), bf16[32,3,80,128]{3,2,1,0:T(8,128)(2,1)S(1)}, u32[]{:S(2)}, u32[]{:S(2)}) async-start(bf16[32,3,80,128]{3,2,1,0:T(8,128)(2,1)} %bitcast.17), calls=%async_computation.4 | async-start | bytes 3932160 | tf_op jit(solution)/shard_map/all_to_all | solution.py:366
  180.0 3.8 %collective-permute-start.4 = (bf16[256,2560]{1,0:T(8,128)(2,1)}, bf16[256,2560]{1,0:T(8,128)(2,1)S(1)}, u32[]{:S(2)}, u32[]{:S(2)}) collective-permute-start(bf16[256,2560]{1,0:T(8,128)(2,1)} %sum_keys.1), channel_id=1, source_target_pairs={{0,7},{1,0},{2,1},{3,2},{4,3},{5,4},{6,5},{7,6},{8,15},{9,8},{10,9... | collective-permute-start | bytes 3932168 | tf_op jit(solution)/shard_map/ppermute | solution.py:25
  183.8 21.6 %all-to-all-done.4 = bf16[32,3,80,128]{3,2,1,0:T(8,128)(2,1)S(1)} async-done(((bf16[32,3,80,128]{3,2,1,0:T(8,128)(2,1)}), bf16[32,3,80,128]{3,2,1,0:T(8,128)(2,1)S(1)}, u32[]{:S(2)}, u32[]{:S(2)}) %all-to-all-start.4) | async-done | bytes 1966112 | tf_op jit(solution)/shard_map/all_to_all | solution.py:366
  205.4 2.8 %join_values.1.after = bf16[256,2560]{1,0:T(8,128)(2,1)} custom-call(s32[96]{0:T(128)} %copy-done.8, bf16[96,2560]{1,0:T(8,128)(2,1)} %collective-permute-done.3.head_part, bf16[96,80,128]{2,1,0:T(8,128)(2,1)S(1)} %bitcast.31), custom_call_target="tpu_custom_call" | custom-call | tf_op jit(solution)/shard_map/join_values/pallas_call | solution.py:466
  208.2 4.2 %collective-permute-done.4.source = bf16[256,2560]{1,0:T(8,128)(2,1)S(1)} collective-permute-done((bf16[256,2560]{1,0:T(8,128)(2,1)}, bf16[256,2560]{1,0:T(8,128)(2,1)S(1)}, u32[]{:S(2)}, u32[]{:S(2)}) %collective-permute-start.4) | collective-permute-done | bytes 1310752 | tf_op jit(solution)/shard_map/ppermute | solution.py:25
  212.4 1.1 place_keys.1
  (24 shorter events, 0.2 us)
Async XLA Ops:
  3.2 1.3 copy-start.2
  7.0 7.8 %copy-start.7 = (s32[96]{0:T(128)S(1)}, s32[96]{0:T(128)}, u32[]{:S(2)}) copy-start(s32[96]{0:T(128)} %reshape.173.codes) | copy-start | bytes 1156
  7.0 13.7 %copy-start.5 = (s32[1,32,20]{1,0,2:T(1,128)S(1)}, s32[1,32,20]{1,0,2:T(1,128)}, u32[]{:S(2)}) copy-start(s32[1,32,20]{1,0,2:T(1,128)} %param.11) | copy-start | bytes 7684
  7.0 14.4 %copy-start.4 = (s32[1,32,20,4]{1,3,2,0:T(4,128)S(1)}, s32[1,32,20,4]{1,3,2,0:T(4,128)}, u32[]{:S(2)}) copy-start(s32[1,32,20,4]{1,3,2,0:T(4,128)} %param.10) | copy-start | bytes 30724
  7.0 18.0 %copy-start.3 = (bf16[1,256,2560]{2,1,0:T(8,128)(2,1)S(1)}, bf16[1,256,2560]{2,1,0:T(8,128)(2,1)}, u32[]{:S(2)}) copy-start(bf16[1,256,2560]{2,1,0:T(8,128)(2,1)} %param.8) | copy-start | bytes 3932164
  7.0 47.3 %all-to-all-start = ((bf16[32,3,128,128]{3,2,1,0:T(8,128)(2,1)}), bf16[32,3,128,128]{3,2,1,0:T(8,128)(2,1)}, u32[]{:S(2)}, u32[]{:S(2)}) async-start(bf16[32,3,128,128]{3,2,1,0:T(8,128)(2,1)} %bitcast.38), calls=%async_computation | async-start | bytes 6291456 | tf_op jit(solution)/shard_map/all_to_all | solution.py:366
  14.8 12.8 %collective-permute-start = (s32[96]{0:T(128)S(1)}, s32[96]{0:T(128)S(1)}, u32[]{:S(2)}, u32[]{:S(2)}) collective-permute-start(s32[96]{0:T(128)S(1)} %copy-done.7), channel_id=1, source_target_pairs={{0,7},{1,0},{2,1},{3,2},{4,3},{5,4},{6,5},{7,6},{8,15},{9,8},{10,9... | collective-permute-start | bytes 1160 | tf_op jit(solution)/shard_map/ppermute | solution.py:25
  21.2 6.3 %copy-start.6 = (s32[20]{0:T(128)}, s32[20]{0:T(128)S(1)}, u32[]{:S(2)}) copy-start(s32[20]{0:T(128)S(1)} %dynamic-slice_reduce_fusion.lengths) | copy-start | bytes 244
  27.5 26.8 %copy-start.8 = (s32[96]{0:T(128)}, s32[96]{0:T(128)S(1)}, u32[]{:S(2)}) copy-start(s32[96]{0:T(128)S(1)} %collective-permute-done.codes) | copy-start | bytes 1156
  54.3 5.6 %copy-start = (bf16[1,256,2560]{2,1,0:T(8,128)(2,1)S(1)}, bf16[1,256,2560]{2,1,0:T(8,128)(2,1)}, u32[]{:S(2)}) copy-start(bf16[1,256,2560]{2,1,0:T(8,128)(2,1)} %param.6) | copy-start | bytes 3932164
  54.3 5.6 %copy-start.1 = (bf16[1,256,2560]{2,1,0:T(8,128)(2,1)S(1)}, bf16[1,256,2560]{2,1,0:T(8,128)(2,1)}, u32[]{:S(2)}) copy-start(bf16[1,256,2560]{2,1,0:T(8,128)(2,1)} %param.9) | copy-start | bytes 3932164
  54.3 45.1 %all-to-all-start.1 = ((bf16[32,3,128,128]{3,2,1,0:T(8,128)(2,1)}), bf16[32,3,128,128]{3,2,1,0:T(8,128)(2,1)}, u32[]{:S(2)}, u32[]{:S(2)}) async-start(bf16[32,3,128,128]{3,2,1,0:T(8,128)(2,1)} %bitcast.39), calls=%async_computation.1 | async-start | bytes 6291456 | tf_op jit(solution)/shard_map/all_to_all | solution.py:366
  72.0 48.6 %collective-permute-start.1 = (bf16[96,80,128]{2,1,0:T(8,128)(2,1)}, bf16[96,80,128]{2,1,0:T(8,128)(2,1)}, u32[]{:S(2)}, u32[]{:S(2)}) collective-permute-start(bf16[96,80,128]{2,1,0:T(8,128)(2,1)} %get-tuple-element.24), channel_id=1, source_target_pairs={{0,7},{1,0},{2,1},{3,2},{4,3},{5,4},{6,5},{7,6},{8,15},{9,8},{10,9... | collective-permute-start | bytes 5898248 | tf_op jit(solution)/shard_map/ppermute | solution.py:25
  99.5 22.2 %all-to-all-start.3 = ((bf16[32,3,48,128]{3,2,1,0:T(8,128)(2,1)}), bf16[32,3,48,128]{3,2,1,0:T(8,128)(2,1)}, u32[]{:S(2)}, u32[]{:S(2)}) async-start(bf16[32,3,48,128]{3,2,1,0:T(8,128)(2,1)} %bitcast.44), calls=%async_computation.3 | async-start | bytes 2359296 | tf_op jit(solution)/shard_map/all_to_all | solution.py:366
  121.7 45.8 %all-to-all-start.2 = ((bf16[32,3,128,128]{3,2,1,0:T(8,128)(2,1)}), bf16[32,3,128,128]{3,2,1,0:T(8,128)(2,1)S(1)}, u32[]{:S(2)}, u32[]{:S(2)}) async-start(bf16[32,3,128,128]{3,2,1,0:T(8,128)(2,1)} %bitcast.41), calls=%async_computation.2 | async-start | bytes 6291456 | tf_op jit(solution)/shard_map/all_to_all | solution.py:366
  128.0 34.9 %collective-permute-start.2 = (bf16[256,2560]{1,0:T(8,128)(2,1)}, bf16[256,2560]{1,0:T(8,128)(2,1)S(1)}, u32[]{:S(2)}, u32[]{:S(2)}) collective-permute-start(bf16[256,2560]{1,0:T(8,128)(2,1)} %get-tuple-element.26), channel_id=1, source_target_pairs={{0,7},{1,0},{2,1},{3,2},{4,3},{5,4},{6,5},{7,6},{8,15},{9,8},{10,9... | collective-permute-start | bytes 3932168 | tf_op jit(solution)/shard_map/ppermute | solution.py:25
  136.1 36.5 %collective-permute-start.3 = (bf16[96,2560]{1,0:T(8,128)(2,1)}, bf16[96,2560]{1,0:T(8,128)(2,1)}, u32[]{:S(2)}, u32[]{:S(2)}) collective-permute-start(bf16[96,2560]{1,0:T(8,128)(2,1)} %sum_values.1), channel_id=1, source_target_pairs={{0,7},{1,0},{2,1},{3,2},{4,3},{5,4},{6,5},{7,6},{8,15},{9,8},{10,9... | collective-permute-start | bytes 1474568 | tf_op jit(solution)/shard_map/ppermute | solution.py:25
  172.6 32.8 %all-to-all-start.4 = ((bf16[32,3,80,128]{3,2,1,0:T(8,128)(2,1)}), bf16[32,3,80,128]{3,2,1,0:T(8,128)(2,1)S(1)}, u32[]{:S(2)}, u32[]{:S(2)}) async-start(bf16[32,3,80,128]{3,2,1,0:T(8,128)(2,1)} %bitcast.17), calls=%async_computation.4 | async-start | bytes 3932160 | tf_op jit(solution)/shard_map/all_to_all | solution.py:366
  180.0 32.4 %collective-permute-start.4 = (bf16[256,2560]{1,0:T(8,128)(2,1)}, bf16[256,2560]{1,0:T(8,128)(2,1)S(1)}, u32[]{:S(2)}, u32[]{:S(2)}) collective-permute-start(bf16[256,2560]{1,0:T(8,128)(2,1)} %sum_keys.1), channel_id=1, source_target_pairs={{0,7},{1,0},{2,1},{3,2},{4,3},{5,4},{6,5},{7,6},{8,15},{9,8},{10,9... | collective-permute-start | bytes 3932168 | tf_op jit(solution)/shard_map/ppermute | solution.py:25

commit v11 on v10

--- a/solution.py
+++ b/solution.py
@@ -34,6 +34,11 @@
     )
 
 
+def code_at(codes, part, step, item):
+    capacity = codes.shape[1]
+    return codes[part * (step // capacity) + item // capacity, item % capacity]
+
+
 def pack_kernel(parts, codes, source, packed, made, sent):
     slots, rows, cols = packed.shape
     step = slots // parts
@@ -44,8 +49,8 @@
 
     def one_part(part, carry):
         for item in range(step):
-            slot = part * step + item
-            made[slot] = source[tile_of(jnp.maximum(codes[slot], 0), rows, cols)]
+            code = jnp.maximum(code_at(codes, part, step, item), 0)
+            made[part * step + item] = source[tile_of(code, rows, cols)]
         part_of(part).start()
         return carry
 
@@ -62,7 +67,7 @@
     def one_part(part, carry):
         for item in range(step):
             slot = part * step + item
-            code = codes[slot]
+            code = code_at(codes, part, step, item)
             block = lax.shift_right_logical(code, HEAD_BITS)
             head = lax.bitwise_and(code, (1 << HEAD_BITS) - 1)
             index = jnp.where(code < 0, 2 * heads, block * heads + head)
@@ -237,8 +242,11 @@
         heads = pl.ds(index * group, group)
         return copy(weights.at[heads], weights_held.at[heads], weights_sem.at[index])
 
-    def tile_fetches():
-        return in_parts(values, value_held, value_sem) + in_parts(keys, key_held, key_sem)
+    def value_fetches():
+        return in_parts(values, value_held, value_sem)
+
+    def key_fetches():
+        return in_parts(keys, key_held, key_sem)
 
     def query_part(index):
         columns = columns_of(index)
@@ -246,31 +254,44 @@
             query_made.at[:, columns], query_grad.at[:, columns], query_out_sem.at[index]
         )
 
-    parts = key_sem.shape[0]
-    tile_starts = tile_fetches()
-    for one in tile_starts[:parts] + [weights_part(0)] + tile_starts[parts:]:
+    for one in value_fetches() + [weights_part(0)] + key_fetches():
         one.start()
 
-    def compute(head):
-        columns = pl.ds(pl.multiple_of(head * cols, cols), cols)
-        where = [places[head * list_size + item] for item in range(list_size)]
-        key = jnp.concatenate([key_held[place] for place in where], axis=0)
-        value = jnp.concatenate([value_held[place] for place in where], axis=0)
+    def listed(head, tiles):
+        return jnp.concatenate(
+            [tiles[places[head * list_size + item]] for item in range(list_size)], axis=0
+        )
+
+    def columns_at(head):
+        return pl.ds(pl.multiple_of(head * cols, cols), cols)
+
+    def dscores_of(head):
         weight = weights_held[head]
         weight_low = weight.astype(jnp.bfloat16).astype(jnp.float32)
         dweights = lax.dot_general(
-            value, grads[:, columns], NT, preferred_element_type=jnp.float32
+            listed(head, value_held),
+            grads[:, columns_at(head)],
+            NT,
+            preferred_element_type=jnp.float32,
         )
         row_delta = jnp.sum(weight_low * dweights, axis=0, keepdims=True)
-        dscores = (weight * (dweights - row_delta)).astype(jnp.bfloat16)
-        flipped = lax.dot_general(key, dscores, TN, preferred_element_type=jnp.float32)
-        query_made[:, columns] = (flipped * scale).astype(jnp.bfloat16).T
+        return (weight * (dweights - row_delta)).astype(jnp.bfloat16)
+
+    def terms_of(head, dscores):
         made_terms = lax.dot_general(
-            dscores, queries[:, columns], NN, preferred_element_type=jnp.float32
+            dscores, queries[:, columns_at(head)], NN, preferred_element_type=jnp.float32
         )
         return (made_terms * scale).astype(jnp.bfloat16)
 
+    def put_query(head, dscores):
+        flipped = lax.dot_general(
+            listed(head, key_held), dscores, TN, preferred_element_type=jnp.float32
+        )
+        query_made[:, columns_at(head)] = (flipped * scale).astype(jnp.bfloat16).T
+
     def one_group(index, carry):
+        heads = [index * group + item for item in range(group)]
+
         @pl.when(index + 1 < groups)
         def _():
             weights_part(index + 1).start()
@@ -279,10 +300,19 @@
 
         @pl.when(index == 0)
         def _():
-            for one in tile_fetches():
+            for one in value_fetches():
                 one.wait()
 
-        results = [compute(index * group + item) for item in range(group)]
+        dscores = [dscores_of(head) for head in heads]
+        results = [terms_of(head, part) for head, part in zip(heads, dscores)]
+
+        @pl.when(index == 0)
+        def _():
+            for one in key_fetches():
+                one.wait()
+
+        for head, part in zip(heads, dscores):
+            put_query(head, part)
         query_part(index).start()
         for item, result in enumerate(results):
             put_terms(places, lengths, list_size, index * group + item, result, [made])
@@ -333,7 +363,7 @@
             -1,
         ),
         axis=2,
-    ).reshape(slots)
+    )
 
     my_lengths = lax.dynamic_index_in_dim(lengths, my_index, 0, keepdims=False)
     my_chosen = lax.dynamic_index_in_dim(chosen, my_index, 0, keepdims=False)
@@ -348,7 +378,7 @@
 
     first_rows = 3 * block_rows // 8
     last_rows = block_rows - first_rows
-    add_parts = 8 if slots % 8 == 0 else 1
+    add_parts = 8 if ctx_count % 8 == 0 else 1
     send_parts = 5 if head_count % 5 == 0 else 1
     flat_shape = jax.ShapeDtypeStruct((row_count, column_count), jnp.bfloat16)
     dma = pltpu.SemaphoreType.DMA

time: 215 us -> 215 us (level)
  no operation moved by 1% of the time
where the time goes in v11:
time: 215 us; the launch traced here: 214 us
  waiting for transfers between devices  108 us (50%)
  starting transfers between devices  54.2 us (25%)
  Pallas kernels  42.6 us (20%)
  local copies, waits for them, and re-layouts  4.05 us (2%)
  other arithmetic  4 us (2%)
    all_to_all x5, waiting for transfers between devices, exchanged(): lax.all_to_all(parts, 'ctx', split_axis=0, concat_axis=0, tiled=True)  74.5 us
    ppermute x5, waiting for transfers between devices, shifted(): return lax.ppermute(value, axis, pairs)  33.3 us
    all_to_all x5, starting transfers between devices, exchanged(): lax.all_to_all(parts, 'ctx', split_axis=0, concat_axis=0, tiled=True)  32.4 us
    ppermute x5, starting transfers between devices, shifted(): return lax.ppermute(value, axis, pairs)  21.9 us
    pallas_call x1, Pallas kernels, local(): pl.pallas_call(functools.partial(key_kernel, list_size, group, scale), ou...  14 us
    pallas_call x1, Pallas kernels, local(): pl.pallas_call(functools.partial(value_kernel, list_size, group, scale),...  12 us
    pallas_call x2, Pallas kernels, add_up(): pl.pallas_call(functools.partial(sum_kernel, add_parts), out_shape=jax.Sh...  5.73 us
    pallas_call x2, Pallas kernels, pack(): pl.pallas_call(functools.partial(pack_kernel, add_parts), out_shape=packe...  5.47 us
  transfers between devices with their start and end apart: 10, of which 9 were waited for; matrix products, arithmetic and copies ran while one was open for 2% of the time, Pallas kernels for 18%

profile of v11, /device:TPU:8, one launch (start us, length us, event | category | flops | bytes accessed | tf_op | source)
XLA Modules:
  0.0 213.5 jit_solution(8990101944211013760)
XLA Ops:
  0.7 0.7 copy.48
  1.4 0.8 fusion
  2.2 0.2 select_reduce_fusion
  2.4 0.7 copy.38.codes
  3.1 1.3 copy-done.2
  4.4 2.7 %pack_keys.1 = bf16[96,128,128]{2,1,0:T(8,128)(2,1)} custom-call(s32[32,3]{1,0:T(8,128)} %copy.38.codes, bf16[256,2560]{1,0:T(8,128)(2,1)S(1)} %bitcast.36), custom_call_target="tpu_custom_call" | custom-call | tf_op jit(solution)/shard_map/pack_keys/pallas_call | solution.py:403
  7.2 7.7 %all-to-all-start = ((bf16[32,3,128,128]{3,2,1,0:T(8,128)(2,1)}), bf16[32,3,128,128]{3,2,1,0:T(8,128)(2,1)}, u32[]{:S(2)}, u32[]{:S(2)}) async-start(bf16[32,3,128,128]{3,2,1,0:T(8,128)(2,1)} %bitcast.38), calls=%async_computation | async-start | bytes 6291456 | tf_op jit(solution)/shard_map/all_to_all | solution.py:396
  14.9 5.9 %collective-permute-start = (s32[32,3]{1,0:T(8,128)S(1)}, s32[32,3]{1,0:T(8,128)S(1)}, u32[]{:S(2)}, u32[]{:S(2)}) collective-permute-start(s32[32,3]{1,0:T(8,128)S(1)} %copy-done.4), channel_id=1, source_target_pairs={{0,7},{1,0},{2,1},{3,2},{4,3},{5,4},{6,5},{7,6},{8,15},{9,8},{10,9... | collective-permute-start | bytes 1160 | tf_op jit(solution)/shard_map/ppermute | solution.py:25
  20.9 0.5 dynamic-slice_reduce_fusion.lengths
  21.4 0.1 iota_compare_fusion.3
  21.5 0.1 lt.105
  21.6 0.5 fusion.6
  22.1 0.1 shift_right_arithmetic.25
  22.2 0.1 copy.41
  22.3 0.1 fusion.3
  22.4 0.1 copy.40
  22.5 0.1 copy.42
  22.6 0.1 broadcast_select_fusion
  22.7 1.6 select_reduce_fusion.1
  24.3 0.1 reduce_sum.32
  24.4 0.1 fusion.5
  24.6 0.1 broadcast_in_dim.88
  24.7 0.5 add_select_fusion.places
  25.2 2.7 %pack_values.1 = bf16[96,128,128]{2,1,0:T(8,128)(2,1)} custom-call(s32[32,3]{1,0:T(8,128)} %copy.38.codes, bf16[256,2560]{1,0:T(8,128)(2,1)S(1)} %bitcast.37), custom_call_target="tpu_custom_call" | custom-call | tf_op jit(solution)/shard_map/pack_values/pallas_call | solution.py:403
  28.0 26.5 %all-to-all-done = bf16[32,3,128,128]{3,2,1,0:T(8,128)(2,1)} async-done(((bf16[32,3,128,128]{3,2,1,0:T(8,128)(2,1)}), bf16[32,3,128,128]{3,2,1,0:T(8,128)(2,1)}, u32[]{:S(2)}, u32[]{:S(2)}) %all-to-all-start) | async-done | bytes 3145760 | tf_op jit(solution)/shard_map/all_to_all | solution.py:396
  54.5 5.6 %all-to-all-start.1 = ((bf16[32,3,128,128]{3,2,1,0:T(8,128)(2,1)}), bf16[32,3,128,128]{3,2,1,0:T(8,128)(2,1)}, u32[]{:S(2)}, u32[]{:S(2)}) async-start(bf16[32,3,128,128]{3,2,1,0:T(8,128)(2,1)} %bitcast.39), calls=%async_computation.1 | async-start | bytes 6291456 | tf_op jit(solution)/shard_map/all_to_all | solution.py:396
  60.1 12.0 %value_terms.1 = (bf16[96,48,128]{2,1,0:T(8,128)(2,1)}, bf16[96,80,128]{2,1,0:T(8,128)(2,1)}, f32[20,512,256]{2,1,0:T(8,128)}) custom-call(s32[80]{0:T(128)} %add_select_fusion.places, s32[20]{0:T(128)} %copy-done.7, bf16[256,2560]{1,0:T(8,128)(2,1)S(1)} %bitcast.32, bf16[256,2560]{1,0:T(8,128)(2,1)S(1)} %bitcast.34, bf16[96,128,128]{2,1,0:T(8,128)(2,1)} %bitcast.9.keys), custom_call_target="tpu_custom_call" | custom-call | tf_op jit(solution)/shard_map/value_terms/pallas_call | solution.py:449
  72.1 6.0 %collective-permute-start.1 = (bf16[96,80,128]{2,1,0:T(8,128)(2,1)}, bf16[96,80,128]{2,1,0:T(8,128)(2,1)}, u32[]{:S(2)}, u32[]{:S(2)}) collective-permute-start(bf16[96,80,128]{2,1,0:T(8,128)(2,1)} %get-tuple-element.24), channel_id=1, source_target_pairs={{0,7},{1,0},{2,1},{3,2},{4,3},{5,4},{6,5},{7,6},{8,15},{9,8},{10,9... | collective-permute-start | bytes 5898248 | tf_op jit(solution)/shard_map/ppermute | solution.py:25
  78.1 21.5 %all-to-all-done.1 = bf16[32,3,128,128]{3,2,1,0:T(8,128)(2,1)} async-done(((bf16[32,3,128,128]{3,2,1,0:T(8,128)(2,1)}), bf16[32,3,128,128]{3,2,1,0:T(8,128)(2,1)}, u32[]{:S(2)}, u32[]{:S(2)}) %all-to-all-start.1) | async-done | bytes 3145760 | tf_op jit(solution)/shard_map/all_to_all | solution.py:396
  99.6 5.3 %all-to-all-start.3 = ((bf16[32,3,48,128]{3,2,1,0:T(8,128)(2,1)}), bf16[32,3,48,128]{3,2,1,0:T(8,128)(2,1)}, u32[]{:S(2)}, u32[]{:S(2)}) async-start(bf16[32,3,48,128]{3,2,1,0:T(8,128)(2,1)} %bitcast.44), calls=%async_computation.3 | async-start | bytes 2359296 | tf_op jit(solution)/shard_map/all_to_all | solution.py:396
  104.9 14.0 %key_terms.1 = (bf16[256,2560]{1,0:T(8,128)(2,1)}, bf16[96,128,128]{2,1,0:T(8,128)(2,1)}) custom-call(s32[80]{0:T(128)} %add_select_fusion.places, s32[20]{0:T(128)} %copy-done.7, bf16[256,2560]{1,0:T(8,128)(2,1)S(1)} %bitcast.33, bf16[256,2560]{1,0:T(8,128)(2,1)S(1)} %bitcast.35, bf16[96,128,128]{2,1,0:T(8,128)(2,1)} %bitcast.9.keys, ...), custom_call_target="tpu_custom_call" | custom-call | tf_op jit(solution)/shard_map/key_terms/pallas_call | solution.py:465
  118.9 1.9 collective-permute-done.1
  120.8 1.1 all-to-all-done.3
  121.8 6.3 %all-to-all-start.2 = ((bf16[32,3,128,128]{3,2,1,0:T(8,128)(2,1)}), bf16[32,3,128,128]{3,2,1,0:T(8,128)(2,1)S(1)}, u32[]{:S(2)}, u32[]{:S(2)}) async-start(bf16[32,3,128,128]{3,2,1,0:T(8,128)(2,1)} %bitcast.41), calls=%async_computation.2 | async-start | bytes 6291456 | tf_op jit(solution)/shard_map/all_to_all | solution.py:396
  128.2 5.1 %collective-permute-start.2 = (bf16[256,2560]{1,0:T(8,128)(2,1)}, bf16[256,2560]{1,0:T(8,128)(2,1)S(1)}, u32[]{:S(2)}, u32[]{:S(2)}) collective-permute-start(bf16[256,2560]{1,0:T(8,128)(2,1)} %get-tuple-element.26), channel_id=1, source_target_pairs={{0,7},{1,0},{2,1},{3,2},{4,3},{5,4},{6,5},{7,6},{8,15},{9,8},{10,9... | collective-permute-start | bytes 3932168 | tf_op jit(solution)/shard_map/ppermute | solution.py:25
  133.3 2.7 %sum_values.1 = bf16[96,2560]{1,0:T(8,128)(2,1)} custom-call(s32[32,3]{1,0:T(8,128)} %copy.38.codes, bf16[96,48,128]{2,1,0:T(8,128)(2,1)} %bitcast.15.terms), custom_call_target="tpu_custom_call" | custom-call | tf_op jit(solution)/shard_map/sum_values/pallas_call | solution.py:429
  136.0 1.1 collective-permute-start.3
  137.1 25.6 %collective-permute-done.2.source = bf16[256,2560]{1,0:T(8,128)(2,1)S(1)} collective-permute-done((bf16[256,2560]{1,0:T(8,128)(2,1)}, bf16[256,2560]{1,0:T(8,128)(2,1)S(1)}, u32[]{:S(2)}, u32[]{:S(2)}) %collective-permute-start.2) | collective-permute-done | bytes 1310752 | tf_op jit(solution)/shard_map/ppermute | solution.py:25
  162.7 1.1 place_queries.1
  163.9 3.8 %all-to-all-done.2 = bf16[32,3,128,128]{3,2,1,0:T(8,128)(2,1)S(1)} async-done(((bf16[32,3,128,128]{3,2,1,0:T(8,128)(2,1)}), bf16[32,3,128,128]{3,2,1,0:T(8,128)(2,1)S(1)}, u32[]{:S(2)}, u32[]{:S(2)}) %all-to-all-start.2) | async-done | bytes 3145760 | tf_op jit(solution)/shard_map/all_to_all | solution.py:396
  167.7 3.0 %sum_keys.1 = bf16[256,2560]{1,0:T(8,128)(2,1)} custom-call(s32[32,3]{1,0:T(8,128)} %copy.38.codes, bf16[96,128,128]{2,1,0:T(8,128)(2,1)S(1)} %bitcast.30), custom_call_target="tpu_custom_call" | custom-call | tf_op jit(solution)/shard_map/sum_keys/pallas_call | solution.py:429
  170.7 1.8 collective-permute-done.3.head_part
  172.5 7.5 %all-to-all-start.4 = ((bf16[32,3,80,128]{3,2,1,0:T(8,128)(2,1)}), bf16[32,3,80,128]{3,2,1,0:T(8,128)(2,1)S(1)}, u32[]{:S(2)}, u32[]{:S(2)}) async-start(bf16[32,3,80,128]{3,2,1,0:T(8,128)(2,1)} %bitcast.17), calls=%async_computation.4 | async-start | bytes 3932160 | tf_op jit(solution)/shard_map/all_to_all | solution.py:396
  179.9 3.8 %collective-permute-start.4 = (bf16[256,2560]{1,0:T(8,128)(2,1)}, bf16[256,2560]{1,0:T(8,128)(2,1)S(1)}, u32[]{:S(2)}, u32[]{:S(2)}) collective-permute-start(bf16[256,2560]{1,0:T(8,128)(2,1)} %sum_keys.1), channel_id=1, source_target_pairs={{0,7},{1,0},{2,1},{3,2},{4,3},{5,4},{6,5},{7,6},{8,15},{9,8},{10,9... | collective-permute-start | bytes 3932168 | tf_op jit(solution)/shard_map/ppermute | solution.py:25
  183.7 21.6 %all-to-all-done.4 = bf16[32,3,80,128]{3,2,1,0:T(8,128)(2,1)S(1)} async-done(((bf16[32,3,80,128]{3,2,1,0:T(8,128)(2,1)}), bf16[32,3,80,128]{3,2,1,0:T(8,128)(2,1)S(1)}, u32[]{:S(2)}, u32[]{:S(2)}) %all-to-all-start.4) | async-done | bytes 1966112 | tf_op jit(solution)/shard_map/all_to_all | solution.py:396
  205.3 3.1 %join_values.1.after = bf16[256,2560]{1,0:T(8,128)(2,1)} custom-call(s32[32,3]{1,0:T(8,128)} %copy-done.8, bf16[96,2560]{1,0:T(8,128)(2,1)} %collective-permute-done.3.head_part, bf16[96,80,128]{2,1,0:T(8,128)(2,1)S(1)} %bitcast.31), custom_call_target="tpu_custom_call" | custom-call | tf_op jit(solution)/shard_map/join_values/pallas_call | solution.py:496
  208.4 4.0 %collective-permute-done.4.source = bf16[256,2560]{1,0:T(8,128)(2,1)S(1)} collective-permute-done((bf16[256,2560]{1,0:T(8,128)(2,1)}, bf16[256,2560]{1,0:T(8,128)(2,1)S(1)}, u32[]{:S(2)}, u32[]{:S(2)}) %collective-permute-start.4) | collective-permute-done | bytes 1310752 | tf_op jit(solution)/shard_map/ppermute | solution.py:25
  212.4 1.1 place_keys.1
  (23 shorter events, 0.2 us)
Async XLA Ops:
  3.1 1.3 copy-start.2
  7.2 7.8 %copy-start.4 = (s32[32,3]{1,0:T(8,128)S(1)}, s32[32,3]{1,0:T(8,128)}, u32[]{:S(2)}) copy-start(s32[32,3]{1,0:T(8,128)} %copy.38.codes) | copy-start | bytes 1156
  7.2 13.7 %copy-start.6 = (s32[1,32,20]{1,0,2:T(1,128)S(1)}, s32[1,32,20]{1,0,2:T(1,128)}, u32[]{:S(2)}) copy-start(s32[1,32,20]{1,0,2:T(1,128)} %param.11) | copy-start | bytes 7684
  7.2 14.4 %copy-start.5 = (s32[1,32,20,4]{1,3,2,0:T(4,128)S(1)}, s32[1,32,20,4]{1,3,2,0:T(4,128)}, u32[]{:S(2)}) copy-start(s32[1,32,20,4]{1,3,2,0:T(4,128)} %param.10) | copy-start | bytes 30724
  7.2 18.0 %copy-start.3 = (bf16[1,256,2560]{2,1,0:T(8,128)(2,1)S(1)}, bf16[1,256,2560]{2,1,0:T(8,128)(2,1)}, u32[]{:S(2)}) copy-start(bf16[1,256,2560]{2,1,0:T(8,128)(2,1)} %param.8) | copy-start | bytes 3932164
  7.2 47.3 %all-to-all-start = ((bf16[32,3,128,128]{3,2,1,0:T(8,128)(2,1)}), bf16[32,3,128,128]{3,2,1,0:T(8,128)(2,1)}, u32[]{:S(2)}, u32[]{:S(2)}) async-start(bf16[32,3,128,128]{3,2,1,0:T(8,128)(2,1)} %bitcast.38), calls=%async_computation | async-start | bytes 6291456 | tf_op jit(solution)/shard_map/all_to_all | solution.py:396
  14.9 13.0 %collective-permute-start = (s32[32,3]{1,0:T(8,128)S(1)}, s32[32,3]{1,0:T(8,128)S(1)}, u32[]{:S(2)}, u32[]{:S(2)}) collective-permute-start(s32[32,3]{1,0:T(8,128)S(1)} %copy-done.4), channel_id=1, source_target_pairs={{0,7},{1,0},{2,1},{3,2},{4,3},{5,4},{6,5},{7,6},{8,15},{9,8},{10,9... | collective-permute-start | bytes 1160 | tf_op jit(solution)/shard_map/ppermute | solution.py:25
  21.4 6.6 %copy-start.7 = (s32[20]{0:T(128)}, s32[20]{0:T(128)S(1)}, u32[]{:S(2)}) copy-start(s32[20]{0:T(128)S(1)} %dynamic-slice_reduce_fusion.lengths) | copy-start | bytes 244
  28.0 26.5 %copy-start.8 = (s32[32,3]{1,0:T(8,128)}, s32[32,3]{1,0:T(8,128)S(1)}, u32[]{:S(2)}) copy-start(s32[32,3]{1,0:T(8,128)S(1)} %collective-permute-done.codes) | copy-start | bytes 1156
  54.5 5.6 %copy-start = (bf16[1,256,2560]{2,1,0:T(8,128)(2,1)S(1)}, bf16[1,256,2560]{2,1,0:T(8,128)(2,1)}, u32[]{:S(2)}) copy-start(bf16[1,256,2560]{2,1,0:T(8,128)(2,1)} %param.6) | copy-start | bytes 3932164
  54.5 5.6 %copy-start.1 = (bf16[1,256,2560]{2,1,0:T(8,128)(2,1)S(1)}, bf16[1,256,2560]{2,1,0:T(8,128)(2,1)}, u32[]{:S(2)}) copy-start(bf16[1,256,2560]{2,1,0:T(8,128)(2,1)} %param.9) | copy-start | bytes 3932164
  54.5 45.1 %all-to-all-start.1 = ((bf16[32,3,128,128]{3,2,1,0:T(8,128)(2,1)}), bf16[32,3,128,128]{3,2,1,0:T(8,128)(2,1)}, u32[]{:S(2)}, u32[]{:S(2)}) async-start(bf16[32,3,128,128]{3,2,1,0:T(8,128)(2,1)} %bitcast.39), calls=%async_computation.1 | async-start | bytes 6291456 | tf_op jit(solution)/shard_map/all_to_all | solution.py:396
  72.1 48.6 %collective-permute-start.1 = (bf16[96,80,128]{2,1,0:T(8,128)(2,1)}, bf16[96,80,128]{2,1,0:T(8,128)(2,1)}, u32[]{:S(2)}, u32[]{:S(2)}) collective-permute-start(bf16[96,80,128]{2,1,0:T(8,128)(2,1)} %get-tuple-element.24), channel_id=1, source_target_pairs={{0,7},{1,0},{2,1},{3,2},{4,3},{5,4},{6,5},{7,6},{8,15},{9,8},{10,9... | collective-permute-start | bytes 5898248 | tf_op jit(solution)/shard_map/ppermute | solution.py:25
  99.6 22.2 %all-to-all-start.3 = ((bf16[32,3,48,128]{3,2,1,0:T(8,128)(2,1)}), bf16[32,3,48,128]{3,2,1,0:T(8,128)(2,1)}, u32[]{:S(2)}, u32[]{:S(2)}) async-start(bf16[32,3,48,128]{3,2,1,0:T(8,128)(2,1)} %bitcast.44), calls=%async_computation.3 | async-start | bytes 2359296 | tf_op jit(solution)/shard_map/all_to_all | solution.py:396
  121.8 45.8 %all-to-all-start.2 = ((bf16[32,3,128,128]{3,2,1,0:T(8,128)(2,1)}), bf16[32,3,128,128]{3,2,1,0:T(8,128)(2,1)S(1)}, u32[]{:S(2)}, u32[]{:S(2)}) async-start(bf16[32,3,128,128]{3,2,1,0:T(8,128)(2,1)} %bitcast.41), calls=%async_computation.2 | async-start | bytes 6291456 | tf_op jit(solution)/shard_map/all_to_all | solution.py:396
  128.2 34.5 %collective-permute-start.2 = (bf16[256,2560]{1,0:T(8,128)(2,1)}, bf16[256,2560]{1,0:T(8,128)(2,1)S(1)}, u32[]{:S(2)}, u32[]{:S(2)}) collective-permute-start(bf16[256,2560]{1,0:T(8,128)(2,1)} %get-tuple-element.26), channel_id=1, source_target_pairs={{0,7},{1,0},{2,1},{3,2},{4,3},{5,4},{6,5},{7,6},{8,15},{9,8},{10,9... | collective-permute-start | bytes 3932168 | tf_op jit(solution)/shard_map/ppermute | solution.py:25
  136.0 36.5 %collective-permute-start.3 = (bf16[96,2560]{1,0:T(8,128)(2,1)}, bf16[96,2560]{1,0:T(8,128)(2,1)}, u32[]{:S(2)}, u32[]{:S(2)}) collective-permute-start(bf16[96,2560]{1,0:T(8,128)(2,1)} %sum_values.1), channel_id=1, source_target_pairs={{0,7},{1,0},{2,1},{3,2},{4,3},{5,4},{6,5},{7,6},{8,15},{9,8},{10,9... | collective-permute-start | bytes 1474568 | tf_op jit(solution)/shard_map/ppermute | solution.py:25
  172.5 32.9 %all-to-all-start.4 = ((bf16[32,3,80,128]{3,2,1,0:T(8,128)(2,1)}), bf16[32,3,80,128]{3,2,1,0:T(8,128)(2,1)S(1)}, u32[]{:S(2)}, u32[]{:S(2)}) async-start(bf16[32,3,80,128]{3,2,1,0:T(8,128)(2,1)} %bitcast.17), calls=%async_computation.4 | async-start | bytes 3932160 | tf_op jit(solution)/shard_map/all_to_all | solution.py:396
  179.9 32.4 %collective-permute-start.4 = (bf16[256,2560]{1,0:T(8,128)(2,1)}, bf16[256,2560]{1,0:T(8,128)(2,1)S(1)}, u32[]{:S(2)}, u32[]{:S(2)}) collective-permute-start(bf16[256,2560]{1,0:T(8,128)(2,1)} %sum_keys.1), channel_id=1, source_target_pairs={{0,7},{1,0},{2,1},{3,2},{4,3},{5,4},{6,5},{7,6},{8,15},{9,8},{10,9... | collective-permute-start | bytes 3932168 | tf_op jit(solution)/shard_map/ppermute | solution.py:25

commit v12 on v11

--- a/solution.py
+++ b/solution.py
@@ -34,11 +34,6 @@
     )
 
 
-def code_at(codes, part, step, item):
-    capacity = codes.shape[1]
-    return codes[part * (step // capacity) + item // capacity, item % capacity]
-
-
 def pack_kernel(parts, codes, source, packed, made, sent):
     slots, rows, cols = packed.shape
     step = slots // parts
@@ -49,8 +44,8 @@
 
     def one_part(part, carry):
         for item in range(step):
-            code = jnp.maximum(code_at(codes, part, step, item), 0)
-            made[part * step + item] = source[tile_of(code, rows, cols)]
+            slot = part * step + item
+            made[slot] = source[tile_of(jnp.maximum(codes[slot], 0), rows, cols)]
         part_of(part).start()
         return carry
 
@@ -67,7 +62,7 @@
     def one_part(part, carry):
         for item in range(step):
             slot = part * step + item
-            code = code_at(codes, part, step, item)
+            code = codes[slot]
             block = lax.shift_right_logical(code, HEAD_BITS)
             head = lax.bitwise_and(code, (1 << HEAD_BITS) - 1)
             index = jnp.where(code < 0, 2 * heads, block * heads + head)
@@ -363,7 +358,7 @@
             -1,
         ),
         axis=2,
-    )
+    ).reshape(slots)
 
     my_lengths = lax.dynamic_index_in_dim(lengths, my_index, 0, keepdims=False)
     my_chosen = lax.dynamic_index_in_dim(chosen, my_index, 0, keepdims=False)
@@ -378,7 +373,7 @@
 
     first_rows = 3 * block_rows // 8
     last_rows = block_rows - first_rows
-    add_parts = 8 if ctx_count % 8 == 0 else 1
+    add_parts = 8 if slots % 8 == 0 else 1
     send_parts = 5 if head_count % 5 == 0 else 1
     flat_shape = jax.ShapeDtypeStruct((row_count, column_count), jnp.bfloat16)
     dma = pltpu.SemaphoreType.DMA

time: 215 us -> 215 us (level)
  no operation moved by 1% of the time
where the time goes in v12:
time: 215 us; the launch traced here: 213 us
  waiting for transfers between devices  109 us (51%)
  starting transfers between devices  54.2 us (25%)
  Pallas kernels  41.5 us (19%)
  local copies, waits for them, and re-layouts  4.15 us (2%)
  other arithmetic  4 us (2%)
    all_to_all x5, waiting for transfers between devices, exchanged(): lax.all_to_all(parts, 'ctx', split_axis=0, concat_axis=0, tiled=True)  74.8 us
    ppermute x5, waiting for transfers between devices, shifted(): return lax.ppermute(value, axis, pairs)  33.8 us
    all_to_all x5, starting transfers between devices, exchanged(): lax.all_to_all(parts, 'ctx', split_axis=0, concat_axis=0, tiled=True)  32.4 us
    ppermute x5, starting transfers between devices, shifted(): return lax.ppermute(value, axis, pairs)  21.8 us
    pallas_call x1, Pallas kernels, local(): pl.pallas_call(functools.partial(key_kernel, list_size, group, scale), ou...  13.9 us
    pallas_call x1, Pallas kernels, local(): pl.pallas_call(functools.partial(value_kernel, list_size, group, scale),...  12 us
    pallas_call x2, Pallas kernels, add_up(): pl.pallas_call(functools.partial(sum_kernel, add_parts), out_shape=jax.Sh...  5.48 us
    pallas_call x2, Pallas kernels, pack(): pl.pallas_call(functools.partial(pack_kernel, add_parts), out_shape=packe...  4.95 us
  transfers between devices with their start and end apart: 10, of which 9 were waited for; matrix products, arithmetic and copies ran while one was open for 2% of the time, Pallas kernels for 18%

profile of v12, /device:TPU:8, one launch (start us, length us, event | category | flops | bytes accessed | tf_op | source)
XLA Modules:
  0.0 213.4 jit_solution(1392346430568657103)
XLA Ops:
  0.7 0.7 copy.40
  1.4 0.8 fusion
  2.2 0.2 select_reduce_fusion
  2.4 0.1 copy.34
  2.5 0.7 reshape.173.codes
  3.2 1.3 copy-done.2
  4.5 2.5 %pack_keys.1 = bf16[96,128,128]{2,1,0:T(8,128)(2,1)} custom-call(s32[96]{0:T(128)} %reshape.173.codes, bf16[256,2560]{1,0:T(8,128)(2,1)S(1)} %bitcast.36), custom_call_target="tpu_custom_call" | custom-call | tf_op jit(solution)/shard_map/pack_keys/pallas_call | solution.py:398
  7.0 7.7 %all-to-all-start = ((bf16[32,3,128,128]{3,2,1,0:T(8,128)(2,1)}), bf16[32,3,128,128]{3,2,1,0:T(8,128)(2,1)}, u32[]{:S(2)}, u32[]{:S(2)}) async-start(bf16[32,3,128,128]{3,2,1,0:T(8,128)(2,1)} %bitcast.38), calls=%async_computation | async-start | bytes 6291456 | tf_op jit(solution)/shard_map/all_to_all | solution.py:391
  14.8 5.9 %collective-permute-start = (s32[96]{0:T(128)S(1)}, s32[96]{0:T(128)S(1)}, u32[]{:S(2)}, u32[]{:S(2)}) collective-permute-start(s32[96]{0:T(128)S(1)} %copy-done.7), channel_id=1, source_target_pairs={{0,7},{1,0},{2,1},{3,2},{4,3},{5,4},{6,5},{7,6},{8,15},{9,8},{10,9... | collective-permute-start | bytes 1160 | tf_op jit(solution)/shard_map/ppermute | solution.py:25
  20.7 0.5 dynamic-slice_reduce_fusion.lengths
  21.3 0.1 lt.105
  21.4 0.5 fusion.6
  21.9 0.1 shift_right_arithmetic.25
  22.0 0.1 copy.36
  22.1 0.1 fusion.3
  22.2 0.1 copy.35
  22.3 0.1 copy.37
  22.4 0.1 broadcast_select_fusion
  22.5 1.6 select_reduce_fusion.1
  24.1 0.1 reduce_sum.32
  24.2 0.1 fusion.5
  24.4 0.1 broadcast_in_dim.88
  24.5 0.5 add_select_fusion.places
  25.0 2.5 %pack_values.1 = bf16[96,128,128]{2,1,0:T(8,128)(2,1)} custom-call(s32[96]{0:T(128)} %reshape.173.codes, bf16[256,2560]{1,0:T(8,128)(2,1)S(1)} %bitcast.37), custom_call_target="tpu_custom_call" | custom-call | tf_op jit(solution)/shard_map/pack_values/pallas_call | solution.py:398
  27.6 26.8 %all-to-all-done = bf16[32,3,128,128]{3,2,1,0:T(8,128)(2,1)} async-done(((bf16[32,3,128,128]{3,2,1,0:T(8,128)(2,1)}), bf16[32,3,128,128]{3,2,1,0:T(8,128)(2,1)}, u32[]{:S(2)}, u32[]{:S(2)}) %all-to-all-start) | async-done | bytes 3145760 | tf_op jit(solution)/shard_map/all_to_all | solution.py:391
  54.3 5.6 %all-to-all-start.1 = ((bf16[32,3,128,128]{3,2,1,0:T(8,128)(2,1)}), bf16[32,3,128,128]{3,2,1,0:T(8,128)(2,1)}, u32[]{:S(2)}, u32[]{:S(2)}) async-start(bf16[32,3,128,128]{3,2,1,0:T(8,128)(2,1)} %bitcast.39), calls=%async_computation.1 | async-start | bytes 6291456 | tf_op jit(solution)/shard_map/all_to_all | solution.py:391
  59.9 12.0 %value_terms.1 = (bf16[96,48,128]{2,1,0:T(8,128)(2,1)}, bf16[96,80,128]{2,1,0:T(8,128)(2,1)}, f32[20,512,256]{2,1,0:T(8,128)}) custom-call(s32[80]{0:T(128)} %add_select_fusion.places, s32[20]{0:T(128)} %copy-done.6, bf16[256,2560]{1,0:T(8,128)(2,1)S(1)} %bitcast.32, bf16[256,2560]{1,0:T(8,128)(2,1)S(1)} %bitcast.34, bf16[96,128,128]{2,1,0:T(8,128)(2,1)} %bitcast.9.keys), custom_call_target="tpu_custom_call" | custom-call | tf_op jit(solution)/shard_map/value_terms/pallas_call | solution.py:444
  72.0 6.0 %collective-permute-start.1 = (bf16[96,80,128]{2,1,0:T(8,128)(2,1)}, bf16[96,80,128]{2,1,0:T(8,128)(2,1)}, u32[]{:S(2)}, u32[]{:S(2)}) collective-permute-start(bf16[96,80,128]{2,1,0:T(8,128)(2,1)} %get-tuple-element.24), channel_id=1, source_target_pairs={{0,7},{1,0},{2,1},{3,2},{4,3},{5,4},{6,5},{7,6},{8,15},{9,8},{10,9... | collective-permute-start | bytes 5898248 | tf_op jit(solution)/shard_map/ppermute | solution.py:25
  77.9 21.6 %all-to-all-done.1 = bf16[32,3,128,128]{3,2,1,0:T(8,128)(2,1)} async-done(((bf16[32,3,128,128]{3,2,1,0:T(8,128)(2,1)}), bf16[32,3,128,128]{3,2,1,0:T(8,128)(2,1)}, u32[]{:S(2)}, u32[]{:S(2)}) %all-to-all-start.1) | async-done | bytes 3145760 | tf_op jit(solution)/shard_map/all_to_all | solution.py:391
  99.5 5.3 %all-to-all-start.3 = ((bf16[32,3,48,128]{3,2,1,0:T(8,128)(2,1)}), bf16[32,3,48,128]{3,2,1,0:T(8,128)(2,1)}, u32[]{:S(2)}, u32[]{:S(2)}) async-start(bf16[32,3,48,128]{3,2,1,0:T(8,128)(2,1)} %bitcast.44), calls=%async_computation.3 | async-start | bytes 2359296 | tf_op jit(solution)/shard_map/all_to_all | solution.py:391
  104.8 13.9 %key_terms.1 = (bf16[256,2560]{1,0:T(8,128)(2,1)}, bf16[96,128,128]{2,1,0:T(8,128)(2,1)}) custom-call(s32[80]{0:T(128)} %add_select_fusion.places, s32[20]{0:T(128)} %copy-done.6, bf16[256,2560]{1,0:T(8,128)(2,1)S(1)} %bitcast.33, bf16[256,2560]{1,0:T(8,128)(2,1)S(1)} %bitcast.35, bf16[96,128,128]{2,1,0:T(8,128)(2,1)} %bitcast.9.keys, ...), custom_call_target="tpu_custom_call" | custom-call | tf_op jit(solution)/shard_map/key_terms/pallas_call | solution.py:460
  118.7 1.9 collective-permute-done.1
  120.6 1.1 all-to-all-done.3
  121.7 6.3 %all-to-all-start.2 = ((bf16[32,3,128,128]{3,2,1,0:T(8,128)(2,1)}), bf16[32,3,128,128]{3,2,1,0:T(8,128)(2,1)S(1)}, u32[]{:S(2)}, u32[]{:S(2)}) async-start(bf16[32,3,128,128]{3,2,1,0:T(8,128)(2,1)} %bitcast.41), calls=%async_computation.2 | async-start | bytes 6291456 | tf_op jit(solution)/shard_map/all_to_all | solution.py:391
  128.0 5.1 %collective-permute-start.2 = (bf16[256,2560]{1,0:T(8,128)(2,1)}, bf16[256,2560]{1,0:T(8,128)(2,1)S(1)}, u32[]{:S(2)}, u32[]{:S(2)}) collective-permute-start(bf16[256,2560]{1,0:T(8,128)(2,1)} %get-tuple-element.26), channel_id=1, source_target_pairs={{0,7},{1,0},{2,1},{3,2},{4,3},{5,4},{6,5},{7,6},{8,15},{9,8},{10,9... | collective-permute-start | bytes 3932168 | tf_op jit(solution)/shard_map/ppermute | solution.py:25
  133.1 2.7 %sum_values.1 = bf16[96,2560]{1,0:T(8,128)(2,1)} custom-call(s32[96]{0:T(128)} %reshape.173.codes, bf16[96,48,128]{2,1,0:T(8,128)(2,1)} %bitcast.15.terms), custom_call_target="tpu_custom_call" | custom-call | tf_op jit(solution)/shard_map/sum_values/pallas_call | solution.py:424
  135.8 1.1 collective-permute-start.3
  136.9 25.7 %collective-permute-done.2.source = bf16[256,2560]{1,0:T(8,128)(2,1)S(1)} collective-permute-done((bf16[256,2560]{1,0:T(8,128)(2,1)}, bf16[256,2560]{1,0:T(8,128)(2,1)S(1)}, u32[]{:S(2)}, u32[]{:S(2)}) %collective-permute-start.2) | collective-permute-done | bytes 1310752 | tf_op jit(solution)/shard_map/ppermute | solution.py:25
  162.5 1.1 place_queries.1
  163.7 3.8 %all-to-all-done.2 = bf16[32,3,128,128]{3,2,1,0:T(8,128)(2,1)S(1)} async-done(((bf16[32,3,128,128]{3,2,1,0:T(8,128)(2,1)}), bf16[32,3,128,128]{3,2,1,0:T(8,128)(2,1)S(1)}, u32[]{:S(2)}, u32[]{:S(2)}) %all-to-all-start.2) | async-done | bytes 3145760 | tf_op jit(solution)/shard_map/all_to_all | solution.py:391
  167.5 2.8 %sum_keys.1 = bf16[256,2560]{1,0:T(8,128)(2,1)} custom-call(s32[96]{0:T(128)} %reshape.173.codes, bf16[96,128,128]{2,1,0:T(8,128)(2,1)S(1)} %bitcast.30), custom_call_target="tpu_custom_call" | custom-call | tf_op jit(solution)/shard_map/sum_keys/pallas_call | solution.py:424
  170.3 2.0 collective-permute-done.3.head_part
  172.3 7.5 %all-to-all-start.4 = ((bf16[32,3,80,128]{3,2,1,0:T(8,128)(2,1)}), bf16[32,3,80,128]{3,2,1,0:T(8,128)(2,1)S(1)}, u32[]{:S(2)}, u32[]{:S(2)}) async-start(bf16[32,3,80,128]{3,2,1,0:T(8,128)(2,1)} %bitcast.17), calls=%async_computation.4 | async-start | bytes 3932160 | tf_op jit(solution)/shard_map/all_to_all | solution.py:391
  179.8 3.8 %collective-permute-start.4 = (bf16[256,2560]{1,0:T(8,128)(2,1)}, bf16[256,2560]{1,0:T(8,128)(2,1)S(1)}, u32[]{:S(2)}, u32[]{:S(2)}) collective-permute-start(bf16[256,2560]{1,0:T(8,128)(2,1)} %sum_keys.1), channel_id=1, source_target_pairs={{0,7},{1,0},{2,1},{3,2},{4,3},{5,4},{6,5},{7,6},{8,15},{9,8},{10,9... | collective-permute-start | bytes 3932168 | tf_op jit(solution)/shard_map/ppermute | solution.py:25
  183.5 21.6 %all-to-all-done.4 = bf16[32,3,80,128]{3,2,1,0:T(8,128)(2,1)S(1)} async-done(((bf16[32,3,80,128]{3,2,1,0:T(8,128)(2,1)}), bf16[32,3,80,128]{3,2,1,0:T(8,128)(2,1)S(1)}, u32[]{:S(2)}, u32[]{:S(2)}) %all-to-all-start.4) | async-done | bytes 1966112 | tf_op jit(solution)/shard_map/all_to_all | solution.py:391
  205.1 2.8 %join_values.1.after = bf16[256,2560]{1,0:T(8,128)(2,1)} custom-call(s32[96]{0:T(128)} %copy-done.8, bf16[96,2560]{1,0:T(8,128)(2,1)} %collective-permute-done.3.head_part, bf16[96,80,128]{2,1,0:T(8,128)(2,1)S(1)} %bitcast.31), custom_call_target="tpu_custom_call" | custom-call | tf_op jit(solution)/shard_map/join_values/pallas_call | solution.py:491
  208.0 4.2 %collective-permute-done.4.source = bf16[256,2560]{1,0:T(8,128)(2,1)S(1)} collective-permute-done((bf16[256,2560]{1,0:T(8,128)(2,1)}, bf16[256,2560]{1,0:T(8,128)(2,1)S(1)}, u32[]{:S(2)}, u32[]{:S(2)}) %collective-permute-start.4) | collective-permute-done | bytes 1310752 | tf_op jit(solution)/shard_map/ppermute | solution.py:25
  212.2 1.1 place_keys.1
  (24 shorter events, 0.2 us)
Async XLA Ops:
  3.2 1.3 copy-start.2
  7.0 7.8 %copy-start.7 = (s32[96]{0:T(128)S(1)}, s32[96]{0:T(128)}, u32[]{:S(2)}) copy-start(s32[96]{0:T(128)} %reshape.173.codes) | copy-start | bytes 1156
  7.0 13.7 %copy-start.5 = (s32[1,32,20]{1,0,2:T(1,128)S(1)}, s32[1,32,20]{1,0,2:T(1,128)}, u32[]{:S(2)}) copy-start(s32[1,32,20]{1,0,2:T(1,128)} %param.11) | copy-start | bytes 7684
  7.0 14.4 %copy-start.4 = (s32[1,32,20,4]{1,3,2,0:T(4,128)S(1)}, s32[1,32,20,4]{1,3,2,0:T(4,128)}, u32[]{:S(2)}) copy-start(s32[1,32,20,4]{1,3,2,0:T(4,128)} %param.10) | copy-start | bytes 30724
  7.0 18.0 %copy-start.3 = (bf16[1,256,2560]{2,1,0:T(8,128)(2,1)S(1)}, bf16[1,256,2560]{2,1,0:T(8,128)(2,1)}, u32[]{:S(2)}) copy-start(bf16[1,256,2560]{2,1,0:T(8,128)(2,1)} %param.8) | copy-start | bytes 3932164
  7.0 47.3 %all-to-all-start = ((bf16[32,3,128,128]{3,2,1,0:T(8,128)(2,1)}), bf16[32,3,128,128]{3,2,1,0:T(8,128)(2,1)}, u32[]{:S(2)}, u32[]{:S(2)}) async-start(bf16[32,3,128,128]{3,2,1,0:T(8,128)(2,1)} %bitcast.38), calls=%async_computation | async-start | bytes 6291456 | tf_op jit(solution)/shard_map/all_to_all | solution.py:391
  14.8 12.8 %collective-permute-start = (s32[96]{0:T(128)S(1)}, s32[96]{0:T(128)S(1)}, u32[]{:S(2)}, u32[]{:S(2)}) collective-permute-start(s32[96]{0:T(128)S(1)} %copy-done.7), channel_id=1, source_target_pairs={{0,7},{1,0},{2,1},{3,2},{4,3},{5,4},{6,5},{7,6},{8,15},{9,8},{10,9... | collective-permute-start | bytes 1160 | tf_op jit(solution)/shard_map/ppermute | solution.py:25
  21.2 6.3 %copy-start.6 = (s32[20]{0:T(128)}, s32[20]{0:T(128)S(1)}, u32[]{:S(2)}) copy-start(s32[20]{0:T(128)S(1)} %dynamic-slice_reduce_fusion.lengths) | copy-start | bytes 244
  27.5 26.8 %copy-start.8 = (s32[96]{0:T(128)}, s32[96]{0:T(128)S(1)}, u32[]{:S(2)}) copy-start(s32[96]{0:T(128)S(1)} %collective-permute-done.codes) | copy-start | bytes 1156
  54.3 5.6 %copy-start = (bf16[1,256,2560]{2,1,0:T(8,128)(2,1)S(1)}, bf16[1,256,2560]{2,1,0:T(8,128)(2,1)}, u32[]{:S(2)}) copy-start(bf16[1,256,2560]{2,1,0:T(8,128)(2,1)} %param.6) | copy-start | bytes 3932164
  54.3 5.6 %copy-start.1 = (bf16[1,256,2560]{2,1,0:T(8,128)(2,1)S(1)}, bf16[1,256,2560]{2,1,0:T(8,128)(2,1)}, u32[]{:S(2)}) copy-start(bf16[1,256,2560]{2,1,0:T(8,128)(2,1)} %param.9) | copy-start | bytes 3932164
  54.3 45.1 %all-to-all-start.1 = ((bf16[32,3,128,128]{3,2,1,0:T(8,128)(2,1)}), bf16[32,3,128,128]{3,2,1,0:T(8,128)(2,1)}, u32[]{:S(2)}, u32[]{:S(2)}) async-start(bf16[32,3,128,128]{3,2,1,0:T(8,128)(2,1)} %bitcast.39), calls=%async_computation.1 | async-start | bytes 6291456 | tf_op jit(solution)/shard_map/all_to_all | solution.py:391
  72.0 48.7 %collective-permute-start.1 = (bf16[96,80,128]{2,1,0:T(8,128)(2,1)}, bf16[96,80,128]{2,1,0:T(8,128)(2,1)}, u32[]{:S(2)}, u32[]{:S(2)}) collective-permute-start(bf16[96,80,128]{2,1,0:T(8,128)(2,1)} %get-tuple-element.24), channel_id=1, source_target_pairs={{0,7},{1,0},{2,1},{3,2},{4,3},{5,4},{6,5},{7,6},{8,15},{9,8},{10,9... | collective-permute-start | bytes 5898248 | tf_op jit(solution)/shard_map/ppermute | solution.py:25
  99.5 22.2 %all-to-all-start.3 = ((bf16[32,3,48,128]{3,2,1,0:T(8,128)(2,1)}), bf16[32,3,48,128]{3,2,1,0:T(8,128)(2,1)}, u32[]{:S(2)}, u32[]{:S(2)}) async-start(bf16[32,3,48,128]{3,2,1,0:T(8,128)(2,1)} %bitcast.44), calls=%async_computation.3 | async-start | bytes 2359296 | tf_op jit(solution)/shard_map/all_to_all | solution.py:391
  121.7 45.8 %all-to-all-start.2 = ((bf16[32,3,128,128]{3,2,1,0:T(8,128)(2,1)}), bf16[32,3,128,128]{3,2,1,0:T(8,128)(2,1)S(1)}, u32[]{:S(2)}, u32[]{:S(2)}) async-start(bf16[32,3,128,128]{3,2,1,0:T(8,128)(2,1)} %bitcast.41), calls=%async_computation.2 | async-start | bytes 6291456 | tf_op jit(solution)/shard_map/all_to_all | solution.py:391
  128.0 34.5 %collective-permute-start.2 = (bf16[256,2560]{1,0:T(8,128)(2,1)}, bf16[256,2560]{1,0:T(8,128)(2,1)S(1)}, u32[]{:S(2)}, u32[]{:S(2)}) collective-permute-start(bf16[256,2560]{1,0:T(8,128)(2,1)} %get-tuple-element.26), channel_id=1, source_target_pairs={{0,7},{1,0},{2,1},{3,2},{4,3},{5,4},{6,5},{7,6},{8,15},{9,8},{10,9... | collective-permute-start | bytes 3932168 | tf_op jit(solution)/shard_map/ppermute | solution.py:25
  135.8 36.5 %collective-permute-start.3 = (bf16[96,2560]{1,0:T(8,128)(2,1)}, bf16[96,2560]{1,0:T(8,128)(2,1)}, u32[]{:S(2)}, u32[]{:S(2)}) collective-permute-start(bf16[96,2560]{1,0:T(8,128)(2,1)} %sum_values.1), channel_id=1, source_target_pairs={{0,7},{1,0},{2,1},{3,2},{4,3},{5,4},{6,5},{7,6},{8,15},{9,8},{10,9... | collective-permute-start | bytes 1474568 | tf_op jit(solution)/shard_map/ppermute | solution.py:25
  172.3 32.9 %all-to-all-start.4 = ((bf16[32,3,80,128]{3,2,1,0:T(8,128)(2,1)}), bf16[32,3,80,128]{3,2,1,0:T(8,128)(2,1)S(1)}, u32[]{:S(2)}, u32[]{:S(2)}) async-start(bf16[32,3,80,128]{3,2,1,0:T(8,128)(2,1)} %bitcast.17), calls=%async_computation.4 | async-start | bytes 3932160 | tf_op jit(solution)/shard_map/all_to_all | solution.py:391
  179.8 32.4 %collective-permute-start.4 = (bf16[256,2560]{1,0:T(8,128)(2,1)}, bf16[256,2560]{1,0:T(8,128)(2,1)S(1)}, u32[]{:S(2)}, u32[]{:S(2)}) collective-permute-start(bf16[256,2560]{1,0:T(8,128)(2,1)} %sum_keys.1), channel_id=1, source_target_pairs={{0,7},{1,0},{2,1},{3,2},{4,3},{5,4},{6,5},{7,6},{8,15},{9,8},{10,9... | collective-permute-start | bytes 3932168 | tf_op jit(solution)/shard_map/ppermute | solution.py:25

commit v13 on v11

--- a/solution.py
+++ b/solution.py
@@ -340,7 +340,7 @@
     capacity = (entries + ctx_count - 1) // ctx_count
     slots = ctx_count * capacity
     scale = 1.0 / math.sqrt(head_dim)
-    group = 4 if head_count % 4 == 0 else 1
+    group = 5 if head_count % 5 == 0 else 1
     groups = head_count // group
 
     chosen = key_blocks[0]

time: 215 us -> 215 us (level)
  no operation moved by 1% of the time
where the time goes in v13:
time: 215 us; the launch traced here: 214 us
  waiting for transfers between devices  108 us (50%)
  starting transfers between devices  54.2 us (25%)
  Pallas kernels  42.2 us (20%)
  local copies, waits for them, and re-layouts  4.05 us (2%)
  other arithmetic  4 us (2%)
    all_to_all x5, waiting for transfers between devices, exchanged(): lax.all_to_all(parts, 'ctx', split_axis=0, concat_axis=0, tiled=True)  74.8 us
    ppermute x5, waiting for transfers between devices, shifted(): return lax.ppermute(value, axis, pairs)  33.4 us
    all_to_all x5, starting transfers between devices, exchanged(): lax.all_to_all(parts, 'ctx', split_axis=0, concat_axis=0, tiled=True)  32.1 us
    ppermute x5, starting transfers between devices, shifted(): return lax.ppermute(value, axis, pairs)  22.2 us
    pallas_call x1, Pallas kernels, local(): pl.pallas_call(functools.partial(key_kernel, list_size, group, scale), ou...  13.9 us
    pallas_call x1, Pallas kernels, local(): pl.pallas_call(functools.partial(value_kernel, list_size, group, scale),...  11.7 us
    pallas_call x2, Pallas kernels, add_up(): pl.pallas_call(functools.partial(sum_kernel, add_parts), out_shape=jax.Sh...  5.74 us
    pallas_call x2, Pallas kernels, pack(): pl.pallas_call(functools.partial(pack_kernel, add_parts), out_shape=packe...  5.47 us
  transfers between devices with their start and end apart: 10, of which 9 were waited for; matrix products, arithmetic and copies ran while one was open for 2% of the time, Pallas kernels for 18%

profile of v13, /device:TPU:8, one launch (start us, length us, event | category | flops | bytes accessed | tf_op | source)
XLA Modules:
  0.0 213.5 jit_solution(12679669438182595520)
XLA Ops:
  0.7 0.7 copy.48
  1.4 0.8 fusion
  2.2 0.2 select_reduce_fusion
  2.4 0.7 copy.38.codes
  3.1 1.3 copy-done.2
  4.4 2.7 %pack_keys.1 = bf16[96,128,128]{2,1,0:T(8,128)(2,1)} custom-call(s32[32,3]{1,0:T(8,128)} %copy.38.codes, bf16[256,2560]{1,0:T(8,128)(2,1)S(1)} %bitcast.36), custom_call_target="tpu_custom_call" | custom-call | tf_op jit(solution)/shard_map/pack_keys/pallas_call | solution.py:403
  7.2 7.7 %all-to-all-start = ((bf16[32,3,128,128]{3,2,1,0:T(8,128)(2,1)}), bf16[32,3,128,128]{3,2,1,0:T(8,128)(2,1)}, u32[]{:S(2)}, u32[]{:S(2)}) async-start(bf16[32,3,128,128]{3,2,1,0:T(8,128)(2,1)} %bitcast.38), calls=%async_computation | async-start | bytes 6291456 | tf_op jit(solution)/shard_map/all_to_all | solution.py:396
  14.9 5.9 %collective-permute-start = (s32[32,3]{1,0:T(8,128)S(1)}, s32[32,3]{1,0:T(8,128)S(1)}, u32[]{:S(2)}, u32[]{:S(2)}) collective-permute-start(s32[32,3]{1,0:T(8,128)S(1)} %copy-done.4), channel_id=1, source_target_pairs={{0,7},{1,0},{2,1},{3,2},{4,3},{5,4},{6,5},{7,6},{8,15},{9,8},{10,9... | collective-permute-start | bytes 1160 | tf_op jit(solution)/shard_map/ppermute | solution.py:25
  20.9 0.5 dynamic-slice_reduce_fusion.lengths
  21.4 0.1 iota_compare_fusion.3
  21.5 0.1 lt.105
  21.6 0.5 fusion.6
  22.1 0.1 shift_right_arithmetic.25
  22.2 0.1 copy.41
  22.3 0.1 fusion.3
  22.4 0.1 copy.40
  22.5 0.1 copy.42
  22.6 0.1 broadcast_select_fusion
  22.7 1.6 select_reduce_fusion.1
  24.3 0.1 reduce_sum.32
  24.4 0.1 fusion.5
  24.6 0.1 broadcast_in_dim.88
  24.7 0.5 add_select_fusion.places
  25.2 2.7 %pack_values.1 = bf16[96,128,128]{2,1,0:T(8,128)(2,1)} custom-call(s32[32,3]{1,0:T(8,128)} %copy.38.codes, bf16[256,2560]{1,0:T(8,128)(2,1)S(1)} %bitcast.37), custom_call_target="tpu_custom_call" | custom-call | tf_op jit(solution)/shard_map/pack_values/pallas_call | solution.py:403
  28.0 26.5 %all-to-all-done = bf16[32,3,128,128]{3,2,1,0:T(8,128)(2,1)} async-done(((bf16[32,3,128,128]{3,2,1,0:T(8,128)(2,1)}), bf16[32,3,128,128]{3,2,1,0:T(8,128)(2,1)}, u32[]{:S(2)}, u32[]{:S(2)}) %all-to-all-start) | async-done | bytes 3145760 | tf_op jit(solution)/shard_map/all_to_all | solution.py:396
  54.5 5.6 %all-to-all-start.1 = ((bf16[32,3,128,128]{3,2,1,0:T(8,128)(2,1)}), bf16[32,3,128,128]{3,2,1,0:T(8,128)(2,1)}, u32[]{:S(2)}, u32[]{:S(2)}) async-start(bf16[32,3,128,128]{3,2,1,0:T(8,128)(2,1)} %bitcast.39), calls=%async_computation.1 | async-start | bytes 6291456 | tf_op jit(solution)/shard_map/all_to_all | solution.py:396
  60.1 11.7 %value_terms.1 = (bf16[96,48,128]{2,1,0:T(8,128)(2,1)}, bf16[96,80,128]{2,1,0:T(8,128)(2,1)}, f32[20,512,256]{2,1,0:T(8,128)}) custom-call(s32[80]{0:T(128)} %add_select_fusion.places, s32[20]{0:T(128)} %copy-done.7, bf16[256,2560]{1,0:T(8,128)(2,1)S(1)} %bitcast.32, bf16[256,2560]{1,0:T(8,128)(2,1)S(1)} %bitcast.34, bf16[96,128,128]{2,1,0:T(8,128)(2,1)} %bitcast.9.keys), custom_call_target="tpu_custom_call" | custom-call | tf_op jit(solution)/shard_map/value_terms/pallas_call | solution.py:449
  71.8 6.0 %collective-permute-start.1 = (bf16[96,80,128]{2,1,0:T(8,128)(2,1)}, bf16[96,80,128]{2,1,0:T(8,128)(2,1)}, u32[]{:S(2)}, u32[]{:S(2)}) collective-permute-start(bf16[96,80,128]{2,1,0:T(8,128)(2,1)} %get-tuple-element.24), channel_id=1, source_target_pairs={{0,7},{1,0},{2,1},{3,2},{4,3},{5,4},{6,5},{7,6},{8,15},{9,8},{10,9... | collective-permute-start | bytes 5898248 | tf_op jit(solution)/shard_map/ppermute | solution.py:25
  77.8 21.9 %all-to-all-done.1 = bf16[32,3,128,128]{3,2,1,0:T(8,128)(2,1)} async-done(((bf16[32,3,128,128]{3,2,1,0:T(8,128)(2,1)}), bf16[32,3,128,128]{3,2,1,0:T(8,128)(2,1)}, u32[]{:S(2)}, u32[]{:S(2)}) %all-to-all-start.1) | async-done | bytes 3145760 | tf_op jit(solution)/shard_map/all_to_all | solution.py:396
  99.6 5.3 %all-to-all-start.3 = ((bf16[32,3,48,128]{3,2,1,0:T(8,128)(2,1)}), bf16[32,3,48,128]{3,2,1,0:T(8,128)(2,1)}, u32[]{:S(2)}, u32[]{:S(2)}) async-start(bf16[32,3,48,128]{3,2,1,0:T(8,128)(2,1)} %bitcast.44), calls=%async_computation.3 | async-start | bytes 2359296 | tf_op jit(solution)/shard_map/all_to_all | solution.py:396
  104.9 13.9 %key_terms.1 = (bf16[256,2560]{1,0:T(8,128)(2,1)}, bf16[96,128,128]{2,1,0:T(8,128)(2,1)}) custom-call(s32[80]{0:T(128)} %add_select_fusion.places, s32[20]{0:T(128)} %copy-done.7, bf16[256,2560]{1,0:T(8,128)(2,1)S(1)} %bitcast.33, bf16[256,2560]{1,0:T(8,128)(2,1)S(1)} %bitcast.35, bf16[96,128,128]{2,1,0:T(8,128)(2,1)} %bitcast.9.keys, ...), custom_call_target="tpu_custom_call" | custom-call | tf_op jit(solution)/shard_map/key_terms/pallas_call | solution.py:465
  118.8 1.6 collective-permute-done.1
  120.5 1.4 all-to-all-done.3
  121.8 6.0 %all-to-all-start.2 = ((bf16[32,3,128,128]{3,2,1,0:T(8,128)(2,1)}), bf16[32,3,128,128]{3,2,1,0:T(8,128)(2,1)S(1)}, u32[]{:S(2)}, u32[]{:S(2)}) async-start(bf16[32,3,128,128]{3,2,1,0:T(8,128)(2,1)} %bitcast.41), calls=%async_computation.2 | async-start | bytes 6291456 | tf_op jit(solution)/shard_map/all_to_all | solution.py:396
  127.8 5.4 %collective-permute-start.2 = (bf16[256,2560]{1,0:T(8,128)(2,1)}, bf16[256,2560]{1,0:T(8,128)(2,1)S(1)}, u32[]{:S(2)}, u32[]{:S(2)}) collective-permute-start(bf16[256,2560]{1,0:T(8,128)(2,1)} %get-tuple-element.26), channel_id=1, source_target_pairs={{0,7},{1,0},{2,1},{3,2},{4,3},{5,4},{6,5},{7,6},{8,15},{9,8},{10,9... | collective-permute-start | bytes 3932168 | tf_op jit(solution)/shard_map/ppermute | solution.py:25
  133.3 2.7 %sum_values.1 = bf16[96,2560]{1,0:T(8,128)(2,1)} custom-call(s32[32,3]{1,0:T(8,128)} %copy.38.codes, bf16[96,48,128]{2,1,0:T(8,128)(2,1)} %bitcast.15.terms), custom_call_target="tpu_custom_call" | custom-call | tf_op jit(solution)/shard_map/sum_values/pallas_call | solution.py:429
  136.0 1.1 collective-permute-start.3
  137.1 25.7 %collective-permute-done.2.source = bf16[256,2560]{1,0:T(8,128)(2,1)S(1)} collective-permute-done((bf16[256,2560]{1,0:T(8,128)(2,1)}, bf16[256,2560]{1,0:T(8,128)(2,1)S(1)}, u32[]{:S(2)}, u32[]{:S(2)}) %collective-permute-start.2) | collective-permute-done | bytes 1310752 | tf_op jit(solution)/shard_map/ppermute | solution.py:25
  162.7 1.1 place_queries.1
  163.9 3.5 %all-to-all-done.2 = bf16[32,3,128,128]{3,2,1,0:T(8,128)(2,1)S(1)} async-done(((bf16[32,3,128,128]{3,2,1,0:T(8,128)(2,1)}), bf16[32,3,128,128]{3,2,1,0:T(8,128)(2,1)S(1)}, u32[]{:S(2)}, u32[]{:S(2)}) %all-to-all-start.2) | async-done | bytes 3145760 | tf_op jit(solution)/shard_map/all_to_all | solution.py:396
  167.3 3.0 %sum_keys.1 = bf16[256,2560]{1,0:T(8,128)(2,1)} custom-call(s32[32,3]{1,0:T(8,128)} %copy.38.codes, bf16[96,128,128]{2,1,0:T(8,128)(2,1)S(1)} %bitcast.30), custom_call_target="tpu_custom_call" | custom-call | tf_op jit(solution)/shard_map/sum_keys/pallas_call | solution.py:429
  170.4 2.1 collective-permute-done.3.head_part
  172.5 7.5 %all-to-all-start.4 = ((bf16[32,3,80,128]{3,2,1,0:T(8,128)(2,1)}), bf16[32,3,80,128]{3,2,1,0:T(8,128)(2,1)S(1)}, u32[]{:S(2)}, u32[]{:S(2)}) async-start(bf16[32,3,80,128]{3,2,1,0:T(8,128)(2,1)} %bitcast.17), calls=%async_computation.4 | async-start | bytes 3932160 | tf_op jit(solution)/shard_map/all_to_all | solution.py:396
  179.9 3.8 %collective-permute-start.4 = (bf16[256,2560]{1,0:T(8,128)(2,1)}, bf16[256,2560]{1,0:T(8,128)(2,1)S(1)}, u32[]{:S(2)}, u32[]{:S(2)}) collective-permute-start(bf16[256,2560]{1,0:T(8,128)(2,1)} %sum_keys.1), channel_id=1, source_target_pairs={{0,7},{1,0},{2,1},{3,2},{4,3},{5,4},{6,5},{7,6},{8,15},{9,8},{10,9... | collective-permute-start | bytes 3932168 | tf_op jit(solution)/shard_map/ppermute | solution.py:25
  183.7 21.6 %all-to-all-done.4 = bf16[32,3,80,128]{3,2,1,0:T(8,128)(2,1)S(1)} async-done(((bf16[32,3,80,128]{3,2,1,0:T(8,128)(2,1)}), bf16[32,3,80,128]{3,2,1,0:T(8,128)(2,1)S(1)}, u32[]{:S(2)}, u32[]{:S(2)}) %all-to-all-start.4) | async-done | bytes 1966112 | tf_op jit(solution)/shard_map/all_to_all | solution.py:396
  205.3 3.1 %join_values.1.after = bf16[256,2560]{1,0:T(8,128)(2,1)} custom-call(s32[32,3]{1,0:T(8,128)} %copy-done.8, bf16[96,2560]{1,0:T(8,128)(2,1)} %collective-permute-done.3.head_part, bf16[96,80,128]{2,1,0:T(8,128)(2,1)S(1)} %bitcast.31), custom_call_target="tpu_custom_call" | custom-call | tf_op jit(solution)/shard_map/join_values/pallas_call | solution.py:496
  208.4 4.0 %collective-permute-done.4.source = bf16[256,2560]{1,0:T(8,128)(2,1)S(1)} collective-permute-done((bf16[256,2560]{1,0:T(8,128)(2,1)}, bf16[256,2560]{1,0:T(8,128)(2,1)S(1)}, u32[]{:S(2)}, u32[]{:S(2)}) %collective-permute-start.4) | collective-permute-done | bytes 1310752 | tf_op jit(solution)/shard_map/ppermute | solution.py:25
  212.4 1.1 place_keys.1
  (23 shorter events, 0.2 us)
Async XLA Ops:
  3.1 1.3 copy-start.2
  7.2 7.8 %copy-start.4 = (s32[32,3]{1,0:T(8,128)S(1)}, s32[32,3]{1,0:T(8,128)}, u32[]{:S(2)}) copy-start(s32[32,3]{1,0:T(8,128)} %copy.38.codes) | copy-start | bytes 1156
  7.2 13.7 %copy-start.6 = (s32[1,32,20]{1,0,2:T(1,128)S(1)}, s32[1,32,20]{1,0,2:T(1,128)}, u32[]{:S(2)}) copy-start(s32[1,32,20]{1,0,2:T(1,128)} %param.11) | copy-start | bytes 7684
  7.2 14.4 %copy-start.5 = (s32[1,32,20,4]{1,3,2,0:T(4,128)S(1)}, s32[1,32,20,4]{1,3,2,0:T(4,128)}, u32[]{:S(2)}) copy-start(s32[1,32,20,4]{1,3,2,0:T(4,128)} %param.10) | copy-start | bytes 30724
  7.2 18.0 %copy-start.3 = (bf16[1,256,2560]{2,1,0:T(8,128)(2,1)S(1)}, bf16[1,256,2560]{2,1,0:T(8,128)(2,1)}, u32[]{:S(2)}) copy-start(bf16[1,256,2560]{2,1,0:T(8,128)(2,1)} %param.8) | copy-start | bytes 3932164
  7.2 47.3 %all-to-all-start = ((bf16[32,3,128,128]{3,2,1,0:T(8,128)(2,1)}), bf16[32,3,128,128]{3,2,1,0:T(8,128)(2,1)}, u32[]{:S(2)}, u32[]{:S(2)}) async-start(bf16[32,3,128,128]{3,2,1,0:T(8,128)(2,1)} %bitcast.38), calls=%async_computation | async-start | bytes 6291456 | tf_op jit(solution)/shard_map/all_to_all | solution.py:396
  14.9 13.0 %collective-permute-start = (s32[32,3]{1,0:T(8,128)S(1)}, s32[32,3]{1,0:T(8,128)S(1)}, u32[]{:S(2)}, u32[]{:S(2)}) collective-permute-start(s32[32,3]{1,0:T(8,128)S(1)} %copy-done.4), channel_id=1, source_target_pairs={{0,7},{1,0},{2,1},{3,2},{4,3},{5,4},{6,5},{7,6},{8,15},{9,8},{10,9... | collective-permute-start | bytes 1160 | tf_op jit(solution)/shard_map/ppermute | solution.py:25
  21.4 6.6 %copy-start.7 = (s32[20]{0:T(128)}, s32[20]{0:T(128)S(1)}, u32[]{:S(2)}) copy-start(s32[20]{0:T(128)S(1)} %dynamic-slice_reduce_fusion.lengths) | copy-start | bytes 244
  28.0 26.5 %copy-start.8 = (s32[32,3]{1,0:T(8,128)}, s32[32,3]{1,0:T(8,128)S(1)}, u32[]{:S(2)}) copy-start(s32[32,3]{1,0:T(8,128)S(1)} %collective-permute-done.codes) | copy-start | bytes 1156
  54.5 5.6 %copy-start = (bf16[1,256,2560]{2,1,0:T(8,128)(2,1)S(1)}, bf16[1,256,2560]{2,1,0:T(8,128)(2,1)}, u32[]{:S(2)}) copy-start(bf16[1,256,2560]{2,1,0:T(8,128)(2,1)} %param.6) | copy-start | bytes 3932164
  54.5 5.6 %copy-start.1 = (bf16[1,256,2560]{2,1,0:T(8,128)(2,1)S(1)}, bf16[1,256,2560]{2,1,0:T(8,128)(2,1)}, u32[]{:S(2)}) copy-start(bf16[1,256,2560]{2,1,0:T(8,128)(2,1)} %param.9) | copy-start | bytes 3932164
  54.5 45.1 %all-to-all-start.1 = ((bf16[32,3,128,128]{3,2,1,0:T(8,128)(2,1)}), bf16[32,3,128,128]{3,2,1,0:T(8,128)(2,1)}, u32[]{:S(2)}, u32[]{:S(2)}) async-start(bf16[32,3,128,128]{3,2,1,0:T(8,128)(2,1)} %bitcast.39), calls=%async_computation.1 | async-start | bytes 6291456 | tf_op jit(solution)/shard_map/all_to_all | solution.py:396
  71.8 48.7 %collective-permute-start.1 = (bf16[96,80,128]{2,1,0:T(8,128)(2,1)}, bf16[96,80,128]{2,1,0:T(8,128)(2,1)}, u32[]{:S(2)}, u32[]{:S(2)}) collective-permute-start(bf16[96,80,128]{2,1,0:T(8,128)(2,1)} %get-tuple-element.24), channel_id=1, source_target_pairs={{0,7},{1,0},{2,1},{3,2},{4,3},{5,4},{6,5},{7,6},{8,15},{9,8},{10,9... | collective-permute-start | bytes 5898248 | tf_op jit(solution)/shard_map/ppermute | solution.py:25
  99.6 22.2 %all-to-all-start.3 = ((bf16[32,3,48,128]{3,2,1,0:T(8,128)(2,1)}), bf16[32,3,48,128]{3,2,1,0:T(8,128)(2,1)}, u32[]{:S(2)}, u32[]{:S(2)}) async-start(bf16[32,3,48,128]{3,2,1,0:T(8,128)(2,1)} %bitcast.44), calls=%async_computation.3 | async-start | bytes 2359296 | tf_op jit(solution)/shard_map/all_to_all | solution.py:396
  121.8 45.5 %all-to-all-start.2 = ((bf16[32,3,128,128]{3,2,1,0:T(8,128)(2,1)}), bf16[32,3,128,128]{3,2,1,0:T(8,128)(2,1)S(1)}, u32[]{:S(2)}, u32[]{:S(2)}) async-start(bf16[32,3,128,128]{3,2,1,0:T(8,128)(2,1)} %bitcast.41), calls=%async_computation.2 | async-start | bytes 6291456 | tf_op jit(solution)/shard_map/all_to_all | solution.py:396
  127.8 34.9 %collective-permute-start.2 = (bf16[256,2560]{1,0:T(8,128)(2,1)}, bf16[256,2560]{1,0:T(8,128)(2,1)S(1)}, u32[]{:S(2)}, u32[]{:S(2)}) collective-permute-start(bf16[256,2560]{1,0:T(8,128)(2,1)} %get-tuple-element.26), channel_id=1, source_target_pairs={{0,7},{1,0},{2,1},{3,2},{4,3},{5,4},{6,5},{7,6},{8,15},{9,8},{10,9... | collective-permute-start | bytes 3932168 | tf_op jit(solution)/shard_map/ppermute | solution.py:25
  136.0 36.5 %collective-permute-start.3 = (bf16[96,2560]{1,0:T(8,128)(2,1)}, bf16[96,2560]{1,0:T(8,128)(2,1)}, u32[]{:S(2)}, u32[]{:S(2)}) collective-permute-start(bf16[96,2560]{1,0:T(8,128)(2,1)} %sum_values.1), channel_id=1, source_target_pairs={{0,7},{1,0},{2,1},{3,2},{4,3},{5,4},{6,5},{7,6},{8,15},{9,8},{10,9... | collective-permute-start | bytes 1474568 | tf_op jit(solution)/shard_map/ppermute | solution.py:25
  172.5 32.9 %all-to-all-start.4 = ((bf16[32,3,80,128]{3,2,1,0:T(8,128)(2,1)}), bf16[32,3,80,128]{3,2,1,0:T(8,128)(2,1)S(1)}, u32[]{:S(2)}, u32[]{:S(2)}) async-start(bf16[32,3,80,128]{3,2,1,0:T(8,128)(2,1)} %bitcast.17), calls=%async_computation.4 | async-start | bytes 3932160 | tf_op jit(solution)/shard_map/all_to_all | solution.py:396
  179.9 32.4 %collective-permute-start.4 = (bf16[256,2560]{1,0:T(8,128)(2,1)}, bf16[256,2560]{1,0:T(8,128)(2,1)S(1)}, u32[]{:S(2)}, u32[]{:S(2)}) collective-permute-start(bf16[256,2560]{1,0:T(8,128)(2,1)} %sum_keys.1), channel_id=1, source_target_pairs={{0,7},{1,0},{2,1},{3,2},{4,3},{5,4},{6,5},{7,6},{8,15},{9,8},{10,9... | collective-permute-start | bytes 3932168 | tf_op jit(solution)/shard_map/ppermute | solution.py:25
